TPU v7x, 128 devices: a whole 4x4x4 slice. The times are simulated.
128 devices in a mesh: fsdp: 8 (over x, core), tensor: 2 (over y_lo), context: 8 (over z, y_hi).
Axes of the slice: x: 4, y: 4 (y_hi: 2, y_lo: 2; y = y_hi * 2 + y_lo), z: 4, core: 2. Of those that a mesh axis runs over, the one named last changes fastest.
Arguments:
- block_input: bfloat16 [16384, 768], P(('fsdp', 'context')), may hold values from -6 to 6
- seq_lengths: int32 [8, 3], P('fsdp'), may hold values from 1 to 1536, 2048 in all within a row
- attn_gain: bfloat16 [768], P('fsdp'), may hold values from 0.5 to 1.5
- qkv_weight: bfloat16 [768, 3, 768], P('fsdp', None, 'tensor'), may hold values from -0.3969283 to 0.3969283
- proj_weight: bfloat16 [768, 768], P('tensor', 'fsdp'), may hold values from -4 to 4
- mlp_gain: bfloat16 [768], P('fsdp'), may hold values from 0.5 to 1.5
- gelu_weight: bfloat16 [768, 2, 1152], P('fsdp', None, 'tensor'), may hold values from -0.21875 to 0.21875
- down_weight: bfloat16 [1152, 768], P('tensor', 'fsdp'), may hold values from -0.1875 to 0.1875
- out_cotangent: bfloat16 [16384, 768], P(('fsdp', 'context')), may hold values from -6 to 6
Outputs:
- block_output: bfloat16 [16384, 768], P(('fsdp', 'context'))
- input_grad: float32 [16384, 768], P(('fsdp', 'context'))
- attngain_grad: float32 [768], P('fsdp')
- qkv_grad: float32 [768, 3, 768], P('fsdp', None, 'tensor')
- proj_grad: float32 [768, 768], P('tensor', 'fsdp')
- mlpgain_grad: float32 [768], P('fsdp')
- gelu_grad: float32 [768, 2, 1152], P('fsdp', None, 'tensor')
- down_grad: float32 [1152, 768], P('tensor', 'fsdp')
All inputs are finite; a program needn't handle non-finite values.
Results may differ from a plain program's by a relative error of at most 0.02.
Values may be sent and summed in bfloat16 or wider, within the bound.
A program may use at most 128 MiB of HBM per device.

v0:
```python
import jax
import jax.numpy as jnp
from jax import lax
from jax.sharding import PartitionSpec as P

HD = 64


EPSILON = 1e-05
THETA = 160000.0
MASKED_LOW = -1e30


def layer_norm(values):
    centre = values - jnp.mean(values, axis=-1, keepdims=True)
    spread = lax.rsqrt(jnp.mean(centre * centre, axis=-1, keepdims=True) + EPSILON)
    return (centre * spread, spread)


def norm_back(grad_out, normed, spread, gain):
    scaled = grad_out * gain
    inner = jnp.mean(scaled, axis=-1, keepdims=True) + normed * jnp.mean(
        scaled * normed, axis=-1, keepdims=True
    )
    return spread * (scaled - inner)


def segments_of(row_ids, lengths):
    ends = jnp.cumsum(lengths)
    segment = jnp.sum((row_ids[:, None] >= ends[None, :]).astype(jnp.int32), axis=1)
    starts = ends - lengths
    picked = segment[:, None] == jnp.arange(lengths.shape[0], dtype=jnp.int32)[None, :]
    begin = jnp.sum(jnp.where(picked, starts[None, :], 0), axis=1)
    return (segment, row_ids - begin)


def rope_tables(positions, head_dim):
    half_dim = head_dim // 2
    exponent = jnp.arange(half_dim, dtype=jnp.float32) * (-2.0 / head_dim)
    frequency = jnp.power(jnp.float32(THETA), exponent)
    angles = positions.astype(jnp.float32)[:, None] * frequency[None, :]
    return (jnp.cos(angles)[:, None, :], jnp.sin(angles)[:, None, :])


def rotate(values, cosine, sine_tab):
    half_dim = values.shape[-1] // 2
    lower_half, upper_half = (values[..., :half_dim], values[..., half_dim:])
    return jnp.concatenate(
        [lower_half * cosine - upper_half * sine_tab, upper_half * cosine + lower_half * sine_tab],
        axis=-1,
    )


def rotate_back(grads, cosine, sine_tab):
    half_dim = grads.shape[-1] // 2
    lower_half, upper_half = (grads[..., :half_dim], grads[..., half_dim:])
    return jnp.concatenate(
        [lower_half * cosine + upper_half * sine_tab, upper_half * cosine - lower_half * sine_tab],
        axis=-1,
    )


def gelu_parts(gate_pre):
    normal_cdf = 0.5 * (1.0 + jax.scipy.special.erf(gate_pre * 0.7071067811865476))
    density = jnp.exp(-0.5 * gate_pre * gate_pre) * 0.3989422804014327
    return (gate_pre * normal_cdf, normal_cdf + gate_pre * density)


def split_count(row_count):
    pieces = 1
    while row_count // pieces > 1024 and row_count % (2 * pieces) == 0:
        pieces = pieces * 2
    return pieces


def over_blocks(step, running, members):
    row_count = members[0].shape[0]
    pieces = split_count(row_count)
    stride = row_count // pieces

    def one_block(counter, current):
        offset = counter * stride
        sliced = tuple((lax.dynamic_slice_in_dim(member, offset, stride, 0) for member in members))
        return step(current, sliced, offset)

    return lax.fori_loop(0, pieces, one_block, running)


def guarded(step):

    def wrapped(running, members, first_row):
        return step(running, members, first_row)

    def folded(running, members, first_row):
        return over_blocks(wrapped, running, members)

    return folded


def on_device(
    block_input,
    seq_lengths,
    attn_gain,
    qkv_weight,
    proj_weight,
    mlp_gain,
    gelu_weight,
    down_weight,
    out_cotangent,
):
    row_count = block_input.shape[0]
    feature_count = block_input.shape[1]
    lengths = seq_lengths[0]
    group_rows = row_count * lax.axis_size("context")
    own_first = lax.axis_index("context") * row_count
    own_rows = own_first + jnp.arange(row_count, dtype=jnp.int32)
    own_segment, positions = segments_of(own_rows, lengths)
    cosine, sine_tab = rope_tables(positions, HD)
    gathered = (
        lax.all_gather(qkv_weight, "fsdp", axis=0, tiled=True),
        lax.all_gather(proj_weight, "fsdp", axis=1, tiled=True),
        lax.all_gather(gelu_weight, "fsdp", axis=0, tiled=True),
        lax.all_gather(down_weight, "fsdp", axis=1, tiled=True),
        lax.all_gather(attn_gain, "fsdp", axis=0, tiled=True),
        lax.all_gather(mlp_gain, "fsdp", axis=0, tiled=True),
    )
    qkv_full, proj_full, gelu_full, down_full, attn_full, mlp_full = gathered
    local_width = qkv_full.shape[2]
    head_count = local_width // HD
    hidden = gelu_full.shape[2]
    attn_scale = attn_full.astype(jnp.float32)
    mlp_scale = mlp_full.astype(jnp.float32)
    inputs = block_input.astype(jnp.float32)
    normed_attn, spread_attn = layer_norm(inputs)
    hidden_attn = (normed_attn * attn_scale).astype(jnp.bfloat16)
    qkv_flat = qkv_full.reshape(feature_count, 3 * local_width)
    projected = jnp.dot(hidden_attn, qkv_flat, preferred_element_type=jnp.float32).reshape(
        row_count, 3, head_count, HD
    )
    query_bf = rotate(projected[:, 0], cosine, sine_tab).astype(jnp.bfloat16)
    key_bf = rotate(projected[:, 1], cosine, sine_tab).astype(jnp.bfloat16)
    value_bf = projected[:, 2].astype(jnp.bfloat16)
    key_flat = key_bf.reshape(row_count, local_width)
    value_flat = value_bf.reshape(row_count, local_width)
    keys_group, values_group = (
        lax.all_gather(key_flat, "context", axis=0, tiled=True),
        lax.all_gather(value_flat, "context", axis=0, tiled=True),
    )
    keys_heads = keys_group.reshape(group_rows, head_count, HD)
    values_heads = values_group.reshape(group_rows, head_count, HD)
    group_segment, unused_pos = segments_of(jnp.arange(group_rows, dtype=jnp.int32), lengths)
    same_group = (own_segment[:, None] == group_segment[None, :])[None]
    fwd_scores = (
        jnp.einsum("qhd,khd->hqk", query_bf, keys_heads, preferred_element_type=jnp.float32) * 0.125
    )
    row_max = jnp.max(jnp.where(same_group, fwd_scores, MASKED_LOW), axis=2)
    denom_sum = jnp.sum(
        jnp.where(same_group, jnp.exp(fwd_scores - row_max[:, :, None]), 0.0), axis=2
    )
    log_total = row_max + jnp.log(denom_sum)
    fwd_weights = jnp.where(same_group, jnp.exp(fwd_scores - log_total[:, :, None]), 0.0).astype(
        jnp.bfloat16
    )
    mixed = jnp.einsum(
        "hqk,khd->qhd", fwd_weights, values_heads, preferred_element_type=jnp.float32
    ).astype(jnp.bfloat16)
    mixed_flat = mixed.reshape(row_count, local_width)
    attn_part = jnp.dot(mixed_flat, proj_full, preferred_element_type=jnp.float32)
    residual = inputs + lax.psum(attn_part, "tensor")
    normed_mlp, spread_mlp = layer_norm(residual)
    hidden_mlp = (normed_mlp * mlp_scale).astype(jnp.bfloat16)
    gelu_flat = gelu_full.reshape(feature_count, 2 * hidden)
    gate_up = jnp.dot(hidden_mlp, gelu_flat, preferred_element_type=jnp.float32).reshape(
        row_count, 2, hidden
    )
    gate_pre, up_pre = (gate_up[:, 0], gate_up[:, 1])
    gelu_val, gelu_slope = gelu_parts(gate_pre)
    activ = (gelu_val * up_pre).astype(jnp.bfloat16)
    mlp_part = jnp.dot(activ, down_full, preferred_element_type=jnp.float32)
    block_output = (
        residual + lax.psum(mlp_part.astype(jnp.bfloat16), "tensor").astype(jnp.float32)
    ).astype(jnp.bfloat16)
    act_grad = jnp.dot(out_cotangent, down_full.T, preferred_element_type=jnp.float32)
    down_grad = jnp.dot(activ.T, out_cotangent, preferred_element_type=jnp.float32)
    gate_up_grad = (
        jnp.stack([act_grad * up_pre * gelu_slope, act_grad * gelu_val], axis=1)
        .astype(jnp.bfloat16)
        .reshape(row_count, 2 * hidden)
    )
    gelu_grad = jnp.dot(hidden_mlp.T, gate_up_grad, preferred_element_type=jnp.float32).reshape(
        feature_count, 2, hidden
    )
    mlp_in_grad = lax.psum(
        jnp.dot(gate_up_grad, gelu_flat.T, preferred_element_type=jnp.float32), "tensor"
    )
    mlpgain_grad = jnp.sum(mlp_in_grad * normed_mlp, axis=0)
    resid_grad = out_cotangent.astype(jnp.float32) + norm_back(
        mlp_in_grad, normed_mlp, spread_mlp, mlp_scale
    )
    resid_bf = resid_grad.astype(jnp.bfloat16)
    out_grad = jnp.dot(resid_bf, proj_full.T, preferred_element_type=jnp.float32).astype(
        jnp.bfloat16
    )
    proj_grad = jnp.dot(mixed_flat.T, resid_bf, preferred_element_type=jnp.float32)
    out_heads = out_grad.reshape(row_count, head_count, HD)
    delta = jnp.transpose(
        jnp.sum(out_heads.astype(jnp.float32) * mixed.astype(jnp.float32), axis=2)
    )

    def key_terms(members, first_row):
        key_count = members[0].shape[0]
        key_part = members[0].reshape(key_count, head_count, HD)
        value_part = members[1].reshape(key_count, head_count, HD)
        key_segment, unused = segments_of(
            first_row + jnp.arange(key_count, dtype=jnp.int32), lengths
        )
        same_doc = (own_segment[:, None] == key_segment[None, :])[None]
        scores = (
            jnp.einsum("qhd,khd->hqk", query_bf, key_part, preferred_element_type=jnp.float32)
            * 0.125
        )
        weights = jnp.where(same_doc, jnp.exp(scores - log_total[:, :, None]), 0.0)
        prob_grad = jnp.einsum(
            "qhd,khd->hqk", out_heads, value_part, preferred_element_type=jnp.float32
        )
        score_grad = (weights * (prob_grad - delta[:, :, None])).astype(jnp.bfloat16)
        return (key_part, weights, score_grad)

    def owner_step(running, members, first_row):
        query_grad, key_all, value_all = running
        key_part, weights, score_grad = key_terms(members, first_row)
        key_count = key_part.shape[0]
        query_grad = (
            query_grad
            + jnp.einsum("hqk,khd->qhd", score_grad, key_part, preferred_element_type=jnp.float32)
            * 0.125
        )
        key_piece = (
            jnp.einsum(
                "hqk,qhd->khd", score_grad, query_bf, preferred_element_type=jnp.float32
            ).reshape(key_count, local_width)
            * 0.125
        )
        value_piece = jnp.einsum(
            "hqk,qhd->khd",
            weights.astype(jnp.bfloat16),
            out_heads,
            preferred_element_type=jnp.float32,
        ).reshape(key_count, local_width)
        key_all = lax.dynamic_update_slice_in_dim(
            key_all,
            lax.dynamic_slice_in_dim(key_all, first_row, key_count, 0) + key_piece,
            first_row,
            0,
        )
        value_all = lax.dynamic_update_slice_in_dim(
            value_all,
            lax.dynamic_slice_in_dim(value_all, first_row, key_count, 0) + value_piece,
            first_row,
            0,
        )
        return (query_grad, key_all, value_all)

    grad_start = jnp.zeros((row_count, head_count, HD), jnp.float32)
    back_state = (
        grad_start,
        jnp.zeros((group_rows, local_width), jnp.float32),
        jnp.zeros((group_rows, local_width), jnp.float32),
    )
    back_result = guarded(owner_step)(
        back_state,
        (
            lax.all_gather(key_flat, "context", axis=0, tiled=True),
            lax.all_gather(value_flat, "context", axis=0, tiled=True),
        ),
        jnp.int32(0),
    )
    query_grad = back_result[0]
    key_grad, value_grad = (
        lax.psum_scatter(
            back_result[1].astype(jnp.bfloat16), "context", scatter_dimension=0, tiled=True
        ).astype(jnp.float32),
        lax.psum_scatter(
            back_result[2].astype(jnp.bfloat16), "context", scatter_dimension=0, tiled=True
        ).astype(jnp.float32),
    )
    key_grad = key_grad.reshape(row_count, head_count, HD)
    value_grad = value_grad.reshape(row_count, head_count, HD)
    qkv_rows = (
        jnp.stack(
            [
                rotate_back(query_grad, cosine, sine_tab),
                rotate_back(key_grad, cosine, sine_tab),
                value_grad,
            ],
            axis=1,
        )
        .astype(jnp.bfloat16)
        .reshape(row_count, 3 * local_width)
    )
    qkv_grad = jnp.dot(hidden_attn.T, qkv_rows, preferred_element_type=jnp.float32).reshape(
        feature_count, 3, local_width
    )
    attn_in_grad = lax.psum(
        jnp.dot(qkv_rows, qkv_flat.T, preferred_element_type=jnp.float32).astype(jnp.bfloat16),
        "tensor",
    ).astype(jnp.float32)
    attngain_grad = jnp.sum(attn_in_grad * normed_attn, axis=0)
    input_grad = resid_grad + norm_back(attn_in_grad, normed_attn, spread_attn, attn_scale)
    grads = (attngain_grad, qkv_grad, proj_grad, mlpgain_grad, gelu_grad, down_grad)
    shares = (
        lax.psum_scatter(grads[0], ("fsdp", "context"), scatter_dimension=0, tiled=True),
        lax.psum_scatter(grads[1], ("fsdp", "context"), scatter_dimension=0, tiled=True),
        lax.psum_scatter(grads[2], ("fsdp", "context"), scatter_dimension=1, tiled=True),
        lax.psum_scatter(grads[3], ("fsdp", "context"), scatter_dimension=0, tiled=True),
        lax.psum_scatter(grads[4], ("fsdp", "context"), scatter_dimension=0, tiled=True),
        lax.psum_scatter(grads[5], ("fsdp", "context"), scatter_dimension=1, tiled=True),
    )
    shares = (
        lax.all_gather(shares[0].astype(jnp.bfloat16), "context", axis=0, tiled=True).astype(
            jnp.float32
        ),
        lax.all_gather(shares[1].astype(jnp.bfloat16), "context", axis=0, tiled=True).astype(
            jnp.float32
        ),
        lax.all_gather(shares[2].astype(jnp.bfloat16), "context", axis=1, tiled=True).astype(
            jnp.float32
        ),
        lax.all_gather(shares[3].astype(jnp.bfloat16), "context", axis=0, tiled=True).astype(
            jnp.float32
        ),
        lax.all_gather(shares[4].astype(jnp.bfloat16), "context", axis=0, tiled=True).astype(
            jnp.float32
        ),
        lax.all_gather(shares[5].astype(jnp.bfloat16), "context", axis=1, tiled=True).astype(
            jnp.float32
        ),
    )
    return (
        block_output,
        input_grad,
        shares[0],
        shares[1],
        shares[2],
        shares[3],
        shares[4],
        shares[5],
    )


def solution(mesh):
    in_specs = (
        P(("fsdp", "context"), None),
        P("fsdp", None),
        P("fsdp"),
        P("fsdp", None, "tensor"),
        P("tensor", "fsdp"),
        P("fsdp"),
        P("fsdp", None, "tensor"),
        P("tensor", "fsdp"),
        P(("fsdp", "context"), None),
    )
    out_specs = (
        P(("fsdp", "context"), None),
        P(("fsdp", "context"), None),
        P("fsdp"),
        P("fsdp", None, "tensor"),
        P("tensor", "fsdp"),
        P("fsdp"),
        P("fsdp", None, "tensor"),
        P("tensor", "fsdp"),
    )
    return jax.shard_map(
        on_device, mesh=mesh, in_specs=in_specs, out_specs=out_specs, check_vma=False
    )
```

profile of v0, /device:TPU:0, one launch (start us, length us, event | category | flops | bytes accessed | tf_op | source)
XLA Modules:
  0.0 1200.9 jit_solution(9545804989500354648)
XLA Ops:
  11.6 14.7 %all-reduce.14 = (bf16[768]{0:T(1024)(128)(2,1)S(1)}, bf16[768]{0:T(1024)(128)(2,1)S(1)}) all-reduce(bf16[768]{0:T(1024)(128)(2,1)S(1)} %dynamic-update-slice, bf16[768]{0:T(1024)(128)(2,1)S(1)} %dynamic-update-slice.1), channel_id=1, replica_groups=mesh['fsdp'=8,'tensor'=2,'context'=8] {'fsdp'}, use_global_device_ids=true, to_apply=%add | all-reduce | flops 1536 | bytes 6144
  30.6 6.5 all-gather.7.cloned.1.call-done
  37.1 2.6 copy.50
  45.6 13.2 %all_gather.48 = bf16[384,768]{0,1:T(8,128)(2,1)S(1)} all-gather(bf16[384,96]{0,1:T(8,128)(2,1)S(1)} %copy-done.49), channel_id=1, replica_groups=mesh['fsdp'=8,'tensor'=2,'context'=8] {'fsdp'}, dimensions={1}, use_global_device_ids=true | all-gather | bytes 663552 | tf_op jit(solution)/shard_map/all_gather | solution.py:121
  58.8 33.9 %all-gather.11.cloned.1.call-done = bf16[2048,384]{0,1:T(8,128)(2,1)} async-done(((bf16[256,384]{0,1:T(8,128)(2,1)}), bf16[2048,384]{0,1:T(8,128)(2,1)}) %all-gather.11.cloned.1.call-update) | async-done | bytes 1572880 | tf_op jit(solution)/shard_map/all_gather | solution.py:146
  92.7 3.9 select_reduce_fusion.1
  96.6 3.9 select_reduce_fusion
  101.2 42.1 %all-gather.9.cloned.1.call-done = bf16[2048,384]{0,1:T(8,128)(2,1)} async-done(((bf16[256,384]{0,1:T(8,128)(2,1)}), bf16[2048,384]{0,1:T(8,128)(2,1)}) %all-gather.9.cloned.1.call-update) | async-done | bytes 1572880 | tf_op jit(solution)/shard_map/all_gather | solution.py:147
  143.3 7.7 fusion.15
  152.4 16.8 %all_gather.51 = bf16[576,768]{0,1:T(8,128)(2,1)} all-gather(bf16[576,96]{0,1:T(8,128)(2,1)S(1)} %copy-done.48), channel_id=1, replica_groups=mesh['fsdp'=8,'tensor'=2,'context'=8] {'fsdp'}, dimensions={1}, use_global_device_ids=true | all-gather | bytes 995328 | tf_op jit(solution)/shard_map/all_gather | solution.py:123
  170.0 2.7 copy.52
  172.7 40.8 %all-reduce.22.cloned.1.call-done = f32[256,768]{1,0:T(8,128)} async-done(((f32[256,768]{1,0:T(8,128)}), f32[256,768]{1,0:T(8,128)}) %all-reduce.22.cloned.1.call-update) | async-done | bytes 786448 | tf_op jit(solution)/shard_map/psum | solution.py:169
  219.9 41.8 %all-reduce.24.cloned.1.call-done = f32[256,768]{1,0:T(8,128)} async-done(((f32[256,768]{1,0:T(8,128)}), f32[256,768]{1,0:T(8,128)}) %all-reduce.24.cloned.1.call-update) | async-done | bytes 786448 | tf_op jit(solution)/shard_map/psum | solution.py:193
  270.7 40.5 %while.20 = (s32[]{:T(128)}, f32[256,6,64]{0,2,1:T(8,128)}, f32[2048,384]{0,1:T(8,128)}, f32[2048,384]{0,1:T(8,128)}, bf16[2048,384]{0,1:T(8,128)(2,1)}, /*index...) while((s32[]{:T(128)}, f32[256,6,64]{0,2,1:T(8,128)}, ...), condition=%wide.region_19.20_spmd.clone, body=%wide.region_17.19_spmd.clone.sunk | while | flops 1024107520 | bytes 131182336 | solution.py:86
  275.2 3.3 fusion.118
  278.6 2.6 fusion.119
  281.1 4.3 fusion.120
  295.4 3.3 fusion.118
  298.8 2.7 fusion.119
  301.5 4.3 fusion.120
  311.2 3.4 convert_element_type.196
  325.5 194.8 %fusion.59 = (f32[384,16]{0,1:T(8,128)S(1)}, f32[576,16]{0,1:T(8,128)S(1)}) fusion(f32[384,768]{0,1:T(8,128)} %fusion.44, f32[576,768]{0,1:T(8,128)} %fusion.66), kind=kCustom, calls=%all-reduce-scatter.2 | all-reduce-scatter fusion | flops 983041 | bytes 3011072
  522.2 2.9 collective-permute-start.13
  525.1 5.9 collective-permute-start.12
  531.1 9.4 collective-permute-start.11
  545.7 3.4 collective-permute-start.9
  549.1 4.9 collective-permute-start.8
  554.0 2.6 collective-permute-start.7
  556.6 5.9 collective-permute-start.6
  567.7 3.3 collective-permute-start.3
  573.2 2.5 collective-permute-start.1
  575.7 4.0 collective-permute-start
  594.0 4.9 copy.57
  599.0 7.7 concatenate.18
  609.0 3.4 collective-permute-start.24
  613.7 4.3 collective-permute-start.22
  620.1 2.7 collective-permute-start.20
  622.8 2.9 collective-permute-start.19
  625.8 2.8 collective-permute-start.18
  631.0 4.3 collective-permute-start.16
  635.3 34.2 %all-gather = bf16[8,12,384]{2,1,0:T(8,128)(2,1)S(1)} all-gather(bf16[1,12,384]{2,1,0:T(8,128)(2,1)S(1)} %fusion.48), channel_id=1, replica_groups=mesh['fsdp'=8,'tensor'=2,'context'=8] {'context'}, dimensions={0}, use_global_device_ids=true | all-gather | bytes 82944 | tf_op jit(solution)/shard_map/all_gather | solution.py:326
  670.3 2.6 concatenate.19
  672.9 34.7 %all-gather.1 = bf16[8,12,576]{2,1,0:T(8,128)(2,1)S(1)} all-gather(bf16[1,12,576]{2,1,0:T(8,128)(2,1)S(1)} %fusion.47), channel_id=1, replica_groups=mesh['fsdp'=8,'tensor'=2,'context'=8] {'context'}, dimensions={0}, use_global_device_ids=true | all-gather | bytes 124416 | tf_op jit(solution)/shard_map/all_gather | solution.py:335
  708.3 2.6 fusion.42
  714.3 384.3 %all-reduce.27 = (bf16[768,3,384]{2,0,1:T(8,128)(2,1)S(1)}, bf16[768]{0:T(1024)(128)(2,1)S(1)}, bf16[768]{0:T(1024)(128)(2,1)S(1)}, bf16[768,2,576]{2,1,0:T(2,128)(2,1)}) all-reduce(f32[768,3,384]{2,0,1:T(8,128)} %fusion.42, ...), channel_id=5, replica_groups=mesh['fsdp'=8,'tensor'=2,'context'=8] {'fsdp','context'}, use_global_device_ids=true, to_apply=%region_27.28.clone | all-reduce | flops 1771008 | bytes 10626048
  1099.1 20.4 %all-reduce.13 = (bf16[96]{0:T(256)(128)(2,1)S(1)}, bf16[96]{0:T(256)(128)(2,1)S(1)}) all-reduce(bf16[96]{0:T(256)(128)(2,1)S(1)} %dynamic-update-slice.2, bf16[96]{0:T(256)(128)(2,1)S(1)} %dynamic-update-slice.3), channel_id=1, replica_groups=mesh['fsdp'=8,'tensor'=2,'context'=8] {'context'}, use_global_device_ids=true, to_apply=%add.2 | all-reduce | flops 192 | bytes 768
  1120.1 34.9 %all_gather.53 = bf16[96,3,384]{2,1,0:T(4,128)(2,1)S(1)} all-gather(bf16[12,3,384]{2,1,0:T(4,128)(2,1)S(1)} %copy.55), channel_id=1, replica_groups=mesh['fsdp'=8,'tensor'=2,'context'=8] {'context'}, dimensions={0}, use_global_device_ids=true | all-gather | bytes 248832 | tf_op jit(solution)/shard_map/all_gather | solution.py:323
  1157.1 34.6 %all_gather.56 = bf16[96,2,576]{2,1,0:T(2,128)(2,1)S(1)} all-gather(bf16[12,2,576]{2,1,0:T(2,128)(2,1)S(1)} %dynamic-slice_convert_fusion.1), channel_id=1, replica_groups=mesh['fsdp'=8,'tensor'=2,'context'=8] {'context'}, dimensions={0}, use_global_device_ids=true | all-gather | bytes 248832 | tf_op jit(solution)/shard_map/all_gather | solution.py:332
  (355 shorter events, 106.8 us)
Async XLA Ops:
  7.2 29.9 %all-gather.7.cloned.1.call-start = ((), (), s32[]{:S(2)}) async-start(), calls=%async_computation.2 | async-start | bytes 1990656 | tf_op jit(solution)/shard_map/all_gather | solution.py:120
  7.9 84.8 %all-gather.11.cloned.1.call-start = ((), (), s32[]{:S(2)}) async-start(), calls=%async_computation.4 | async-start | bytes 1769472 | tf_op jit(solution)/shard_map/all_gather | solution.py:146
  42.5 100.8 %all-gather.9.cloned.1.call-start = ((), (), s32[]{:S(2)}) async-start(), calls=%async_computation.3 | async-start | bytes 1769472 | tf_op jit(solution)/shard_map/all_gather | solution.py:147
  44.3 125.7 %all-gather.13.cloned.1.call-start = ((), (), s32[]{:S(2)}) async-start(), calls=%async_computation.6 | async-start | bytes 2211840 | tf_op jit(solution)/shard_map/all_gather | solution.py:122
  45.1 168.4 %all-reduce.22.cloned.1.call-start = ((), (), s32[]{:S(2)}) async-start(), calls=%async_computation.5 | async-start | bytes 1572864 | tf_op jit(solution)/shard_map/psum | solution.py:169
  152.3 109.4 %all-reduce.24.cloned.1.call-start = ((), (), s32[]{:S(2)}) async-start(), calls=%async_computation.7 | async-start | bytes 1572864 | tf_op jit(solution)/shard_map/psum | solution.py:193
  219.6 323.4 %reduce-scatter.8.cloned.1.call-start = ((), (), s32[]{:S(2)}) async-start(), calls=%async_computation.8 | async-start | bytes 1769472 | tf_op jit(solution)/shard_map/reduce_scatter | solution.py:280
  314.7 252.0 %reduce-scatter.10.cloned.1.call-start = ((), (), s32[]{:S(2)}) async-start(), calls=%async_computation.9 | async-start | bytes 1769472 | tf_op jit(solution)/shard_map/reduce_scatter | solution.py:283
  316.1 394.8 %all-reduce.26.cloned.1.call-start = ((), (), s32[]{:S(2)}) async-start(), calls=%async_computation.10 | async-start | bytes 1572864 | tf_op jit(solution)/shard_map/psum | solution.py:304
  324.0 219.9 %copy-start.14 = (f32[256,6,64]{0,2,1:T(8,128)S(1)}, f32[256,6,64]{0,2,1:T(8,128)}, u32[]{:S(2)}) copy-start(f32[256,6,64]{0,2,1:T(8,128)} %get-tuple-element.285) | copy-start | bytes 1179652
  324.1 219.9 %copy-start.44 = (f32[256,32]{0,1:T(8,128)S(1)}, f32[256,32]{0,1:T(8,128)}, u32[]{:S(2)}) copy-start(f32[256,32]{0,1:T(8,128)} %copy-done.43) | copy-start | bytes 98308
  324.1 219.9 %copy-start.46 = (f32[256,32]{0,1:T(8,128)S(1)}, f32[256,32]{0,1:T(8,128)}, u32[]{:S(2)}) copy-start(f32[256,32]{0,1:T(8,128)} %copy-done.45) | copy-start | bytes 98308
  325.5 255.5 %copy-start.13 = (bf16[768,3,384]{0,2,1:T(8,128)(2,1)S(1)}, bf16[768,3,384]{0,2,1:T(8,128)(2,1)}, u32[]{:S(2)}) copy-start(bf16[768,3,384]{0,2,1:T(8,128)(2,1)} %copy-done.12) | copy-start | bytes 5308420
  520.9 24.7 %collective-permute-start.14 = (bf16[384,16]{0,1:T(8,128)(2,1)}, bf16[384,16]{0,1:T(8,128)(2,1)S(1)}, u32[]{:S(2)}, u32[]{:S(2)}) collective-permute-start(bf16[384,16]{0,1:T(8,128)(2,1)} %convert.105), channel_id=1, source_target_pairs={{0,23},{1,32},{2,33},{3,34},{4,35},{5,36},{6,37},{7,38},{16,39},{1... | collective-permute-start | bytes 36872
  522.2 26.8 %collective-permute-start.13 = (bf16[384,16]{0,1:T(8,128)(2,1)}, bf16[384,16]{0,1:T(8,128)(2,1)}, u32[]{:S(2)}, u32[]{:S(2)}) collective-permute-start(bf16[384,16]{0,1:T(8,128)(2,1)} %convert.105), channel_id=1, source_target_pairs={{0,22},{1,23},{2,32},{3,33},{4,34},{5,35},{6,36},{7,37},{16,38},{1... | collective-permute-start | bytes 36872
  525.1 28.9 %collective-permute-start.12 = (bf16[384,16]{0,1:T(8,128)(2,1)}, bf16[384,16]{0,1:T(8,128)(2,1)}, u32[]{:S(2)}, u32[]{:S(2)}) collective-permute-start(bf16[384,16]{0,1:T(8,128)(2,1)} %convert.105), channel_id=1, source_target_pairs={{0,21},{1,22},{2,23},{3,32},{4,33},{5,34},{6,35},{7,36},{16,37},{1... | collective-permute-start | bytes 36872
  531.1 25.6 %collective-permute-start.11 = (bf16[384,16]{0,1:T(8,128)(2,1)}, bf16[384,16]{0,1:T(8,128)(2,1)}, u32[]{:S(2)}, u32[]{:S(2)}) collective-permute-start(bf16[384,16]{0,1:T(8,128)(2,1)} %convert.105), channel_id=1, source_target_pairs={{0,20},{1,21},{2,22},{3,23},{4,32},{5,33},{6,34},{7,35},{16,36},{1... | collective-permute-start | bytes 36872
  541.7 2.7 collective-permute-start.15
  544.3 18.2 %collective-permute-start.10 = (bf16[384,16]{0,1:T(8,128)(2,1)}, bf16[384,16]{0,1:T(8,128)(2,1)S(1)}, u32[]{:S(2)}, u32[]{:S(2)}) collective-permute-start(bf16[384,16]{0,1:T(8,128)(2,1)} %convert.105), channel_id=1, source_target_pairs={{0,19},{1,20},{2,21},{3,22},{4,23},{5,32},{6,33},{7,34},{16,35},{1... | collective-permute-start | bytes 36872
  545.7 18.7 %collective-permute-start.9 = (bf16[384,16]{0,1:T(8,128)(2,1)}, bf16[384,16]{0,1:T(8,128)(2,1)S(1)}, u32[]{:S(2)}, u32[]{:S(2)}) collective-permute-start(bf16[384,16]{0,1:T(8,128)(2,1)} %convert.105), channel_id=1, source_target_pairs={{0,18},{1,19},{2,20},{3,21},{4,22},{5,23},{6,32},{7,33},{16,34},{1... | collective-permute-start | bytes 36872
  549.1 18.6 %collective-permute-start.8 = (bf16[384,16]{0,1:T(8,128)(2,1)}, bf16[384,16]{0,1:T(8,128)(2,1)}, u32[]{:S(2)}, u32[]{:S(2)}) collective-permute-start(bf16[384,16]{0,1:T(8,128)(2,1)} %convert.105), channel_id=1, source_target_pairs={{0,17},{1,18},{2,19},{3,20},{4,21},{5,22},{6,23},{7,32},{16,33},{1... | collective-permute-start | bytes 36872
  554.0 17.0 %collective-permute-start.7 = (bf16[384,16]{0,1:T(8,128)(2,1)}, bf16[384,16]{0,1:T(8,128)(2,1)}, u32[]{:S(2)}, u32[]{:S(2)}) collective-permute-start(bf16[384,16]{0,1:T(8,128)(2,1)} %convert.105), channel_id=1, source_target_pairs={{0,16},{1,17},{2,18},{3,19},{4,20},{5,21},{6,22},{7,23},{16,32},{1... | collective-permute-start | bytes 36872
  556.6 16.6 %collective-permute-start.6 = (bf16[384,16]{0,1:T(8,128)(2,1)}, bf16[384,16]{0,1:T(8,128)(2,1)}, u32[]{:S(2)}, u32[]{:S(2)}) collective-permute-start(bf16[384,16]{0,1:T(8,128)(2,1)} %convert.105), channel_id=1, source_target_pairs={{0,7},{1,16},{2,17},{3,18},{4,19},{5,20},{6,21},{7,22},{16,23},{17... | collective-permute-start | bytes 36872
  562.5 13.2 %collective-permute-start.5 = (bf16[384,16]{0,1:T(8,128)(2,1)}, bf16[384,16]{0,1:T(8,128)(2,1)}, u32[]{:S(2)}, u32[]{:S(2)}) collective-permute-start(bf16[384,16]{0,1:T(8,128)(2,1)} %convert.105), channel_id=1, source_target_pairs={{0,6},{1,7},{2,16},{3,17},{4,18},{5,19},{6,20},{7,21},{16,22},{17,... | collective-permute-start | bytes 36872
  564.4 15.4 %collective-permute-start.4 = (bf16[384,16]{0,1:T(8,128)(2,1)}, bf16[384,16]{0,1:T(8,128)(2,1)}, u32[]{:S(2)}, u32[]{:S(2)}) collective-permute-start(bf16[384,16]{0,1:T(8,128)(2,1)} %convert.105), channel_id=1, source_target_pairs={{0,5},{1,6},{2,7},{3,16},{4,17},{5,18},{6,19},{7,20},{16,21},{17,2... | collective-permute-start | bytes 36872
  567.7 14.9 %collective-permute-start.3 = (bf16[384,16]{0,1:T(8,128)(2,1)}, bf16[384,16]{0,1:T(8,128)(2,1)S(1)}, u32[]{:S(2)}, u32[]{:S(2)}) collective-permute-start(bf16[384,16]{0,1:T(8,128)(2,1)} %convert.105), channel_id=1, source_target_pairs={{0,4},{1,5},{2,6},{3,7},{4,16},{5,17},{6,18},{7,19},{16,20},{17,21... | collective-permute-start | bytes 36872
  571.0 13.8 %collective-permute-start.2 = (bf16[384,16]{0,1:T(8,128)(2,1)}, bf16[384,16]{0,1:T(8,128)(2,1)S(1)}, u32[]{:S(2)}, u32[]{:S(2)}) collective-permute-start(bf16[384,16]{0,1:T(8,128)(2,1)} %convert.105), channel_id=1, source_target_pairs={{0,3},{1,4},{2,5},{3,6},{4,7},{5,16},{6,17},{7,18},{16,19},{17,20}... | collective-permute-start | bytes 36872
  573.2 12.9 %collective-permute-start.1 = (bf16[384,16]{0,1:T(8,128)(2,1)}, bf16[384,16]{0,1:T(8,128)(2,1)S(1)}, u32[]{:S(2)}, u32[]{:S(2)}) collective-permute-start(bf16[384,16]{0,1:T(8,128)(2,1)} %convert.105), channel_id=1, source_target_pairs={{0,2},{1,3},{2,4},{3,5},{4,6},{5,7},{6,16},{7,17},{16,18},{17,19},... | collective-permute-start | bytes 36872
  575.7 12.6 %collective-permute-start = (bf16[384,16]{0,1:T(8,128)(2,1)}, bf16[384,16]{0,1:T(8,128)(2,1)S(1)}, u32[]{:S(2)}, u32[]{:S(2)}) collective-permute-start(bf16[384,16]{0,1:T(8,128)(2,1)} %convert.105), channel_id=1, source_target_pairs={{0,1},{1,2},{2,3},{3,4},{4,5},{5,6},{6,7},{7,16},{16,17},{17,18},{... | collective-permute-start | bytes 36872
  579.8 9.9 collective-permute-start.31
  582.6 24.1 %collective-permute-start.30 = (bf16[576,16]{0,1:T(8,128)(2,1)}, bf16[576,16]{0,1:T(8,128)(2,1)S(1)}, u32[]{:S(2)}, u32[]{:S(2)}) collective-permute-start(bf16[576,16]{0,1:T(8,128)(2,1)} %convert.104), channel_id=1, source_target_pairs={{0,23},{1,32},{2,33},{3,34},{4,35},{5,36},{6,37},{7,38},{16,39},{1... | collective-permute-start | bytes 55304
  584.8 24.2 %collective-permute-start.29 = (bf16[576,16]{0,1:T(8,128)(2,1)}, bf16[576,16]{0,1:T(8,128)(2,1)S(1)}, u32[]{:S(2)}, u32[]{:S(2)}) collective-permute-start(bf16[576,16]{0,1:T(8,128)(2,1)} %convert.104), channel_id=1, source_target_pairs={{0,22},{1,23},{2,32},{3,33},{4,34},{5,35},{6,36},{7,37},{16,38},{1... | collective-permute-start | bytes 55304
  586.1 26.2 %collective-permute-start.28 = (bf16[576,16]{0,1:T(8,128)(2,1)}, bf16[576,16]{0,1:T(8,128)(2,1)S(1)}, u32[]{:S(2)}, u32[]{:S(2)}) collective-permute-start(bf16[576,16]{0,1:T(8,128)(2,1)} %convert.104), channel_id=1, source_target_pairs={{0,21},{1,22},{2,23},{3,32},{4,33},{5,34},{6,35},{7,36},{16,37},{1... | collective-permute-start | bytes 55304
  588.4 25.3 %collective-permute-start.27 = (bf16[576,16]{0,1:T(8,128)(2,1)}, bf16[576,16]{0,1:T(8,128)(2,1)S(1)}, u32[]{:S(2)}, u32[]{:S(2)}) collective-permute-start(bf16[576,16]{0,1:T(8,128)(2,1)} %convert.104), channel_id=1, source_target_pairs={{0,20},{1,21},{2,22},{3,23},{4,32},{5,33},{6,34},{7,35},{16,36},{1... | collective-permute-start | bytes 55304
  589.7 28.3 %collective-permute-start.26 = (bf16[576,16]{0,1:T(8,128)(2,1)}, bf16[576,16]{0,1:T(8,128)(2,1)S(1)}, u32[]{:S(2)}, u32[]{:S(2)}) collective-permute-start(bf16[576,16]{0,1:T(8,128)(2,1)} %convert.104), channel_id=1, source_target_pairs={{0,19},{1,20},{2,21},{3,22},{4,23},{5,32},{6,33},{7,34},{16,35},{1... | collective-permute-start | bytes 55304
  594.0 114.3 %copy-start.11 = (bf16[256,768]{1,0:T(8,128)(2,1)S(1)}, bf16[256,768]{1,0:T(8,128)(2,1)}, u32[]{:S(2)}) copy-start(bf16[256,768]{1,0:T(8,128)(2,1)} %param.11) | copy-start | bytes 1179652
  606.7 13.3 %collective-permute-start.25 = (bf16[576,16]{0,1:T(8,128)(2,1)S(1)}, bf16[576,16]{0,1:T(8,128)(2,1)S(1)}, u32[]{:S(2)}, u32[]{:S(2)}) collective-permute-start(bf16[576,16]{0,1:T(8,128)(2,1)S(1)} %copy-done.57), channel_id=1, source_target_pairs={{0,18},{1,19},{2,20},{3,21},{4,22},{5,23},{6,32},{7,33},{16,34},{1... | collective-permute-start | bytes 55304
  609.0 13.8 %collective-permute-start.24 = (bf16[576,16]{0,1:T(8,128)(2,1)S(1)}, bf16[576,16]{0,1:T(8,128)(2,1)S(1)}, u32[]{:S(2)}, u32[]{:S(2)}) collective-permute-start(bf16[576,16]{0,1:T(8,128)(2,1)S(1)} %copy-done.57), channel_id=1, source_target_pairs={{0,17},{1,18},{2,19},{3,20},{4,21},{5,22},{6,23},{7,32},{16,33},{1... | collective-permute-start | bytes 55304
  612.3 13.4 %collective-permute-start.23 = (bf16[576,16]{0,1:T(8,128)(2,1)S(1)}, bf16[576,16]{0,1:T(8,128)(2,1)S(1)}, u32[]{:S(2)}, u32[]{:S(2)}) collective-permute-start(bf16[576,16]{0,1:T(8,128)(2,1)S(1)} %copy-done.57), channel_id=1, source_target_pairs={{0,16},{1,17},{2,18},{3,19},{4,20},{5,21},{6,22},{7,23},{16,32},{1... | collective-permute-start | bytes 55304
  613.7 14.9 %collective-permute-start.22 = (bf16[576,16]{0,1:T(8,128)(2,1)S(1)}, bf16[576,16]{0,1:T(8,128)(2,1)S(1)}, u32[]{:S(2)}, u32[]{:S(2)}) collective-permute-start(bf16[576,16]{0,1:T(8,128)(2,1)S(1)} %copy-done.57), channel_id=1, source_target_pairs={{0,7},{1,16},{2,17},{3,18},{4,19},{5,20},{6,21},{7,22},{16,23},{17... | collective-permute-start | bytes 55304
  618.0 13.0 %collective-permute-start.21 = (bf16[576,16]{0,1:T(8,128)(2,1)S(1)}, bf16[576,16]{0,1:T(8,128)(2,1)S(1)}, u32[]{:S(2)}, u32[]{:S(2)}) collective-permute-start(bf16[576,16]{0,1:T(8,128)(2,1)S(1)} %copy-done.57), channel_id=1, source_target_pairs={{0,6},{1,7},{2,16},{3,17},{4,18},{5,19},{6,20},{7,21},{16,22},{17,... | collective-permute-start | bytes 55304
  620.1 50.2 %collective-permute-start.20 = (bf16[576,16]{0,1:T(8,128)(2,1)S(1)}, bf16[576,16]{0,1:T(8,128)(2,1)S(1)}, u32[]{:S(2)}, u32[]{:S(2)}) collective-permute-start(bf16[576,16]{0,1:T(8,128)(2,1)S(1)} %copy-done.57), channel_id=1, source_target_pairs={{0,5},{1,6},{2,7},{3,16},{4,17},{5,18},{6,19},{7,20},{16,21},{17,2... | collective-permute-start | bytes 55304
  622.8 47.4 %collective-permute-start.19 = (bf16[576,16]{0,1:T(8,128)(2,1)S(1)}, bf16[576,16]{0,1:T(8,128)(2,1)S(1)}, u32[]{:S(2)}, u32[]{:S(2)}) collective-permute-start(bf16[576,16]{0,1:T(8,128)(2,1)S(1)} %copy-done.57), channel_id=1, source_target_pairs={{0,4},{1,5},{2,6},{3,7},{4,16},{5,17},{6,18},{7,19},{16,20},{17,21... | collective-permute-start | bytes 55304
  625.8 44.5 %collective-permute-start.18 = (bf16[576,16]{0,1:T(8,128)(2,1)S(1)}, bf16[576,16]{0,1:T(8,128)(2,1)S(1)}, u32[]{:S(2)}, u32[]{:S(2)}) collective-permute-start(bf16[576,16]{0,1:T(8,128)(2,1)S(1)} %copy-done.57), channel_id=1, source_target_pairs={{0,3},{1,4},{2,5},{3,6},{4,7},{5,16},{6,17},{7,18},{16,19},{17,20}... | collective-permute-start | bytes 55304
  628.5 41.7 %collective-permute-start.17 = (bf16[576,16]{0,1:T(8,128)(2,1)S(1)}, bf16[576,16]{0,1:T(8,128)(2,1)S(1)}, u32[]{:S(2)}, u32[]{:S(2)}) collective-permute-start(bf16[576,16]{0,1:T(8,128)(2,1)S(1)} %copy-done.57), channel_id=1, source_target_pairs={{0,2},{1,3},{2,4},{3,5},{4,6},{5,7},{6,16},{7,17},{16,18},{17,19},... | collective-permute-start | bytes 55304
  631.0 39.3 %collective-permute-start.16 = (bf16[576,16]{0,1:T(8,128)(2,1)S(1)}, bf16[576,16]{0,1:T(8,128)(2,1)S(1)}, u32[]{:S(2)}, u32[]{:S(2)}) collective-permute-start(bf16[576,16]{0,1:T(8,128)(2,1)S(1)} %copy-done.57), channel_id=1, source_target_pairs={{0,1},{1,2},{2,3},{3,4},{4,5},{5,6},{6,7},{7,16},{16,17},{17,18},{... | collective-permute-start | bytes 55304
  714.3 478.5 %copy-start.17 = (f32[256,768]{1,0:T(8,128)S(1)}, f32[256,768]{1,0:T(8,128)}, u32[]{:S(2)}) copy-start(f32[256,768]{1,0:T(8,128)} %copy-done.15) | copy-start | bytes 2359300
  714.3 478.5 %copy-start.27 = (bf16[256,768]{1,0:T(8,128)(2,1)S(1)}, bf16[256,768]{1,0:T(8,128)(2,1)}, u32[]{:S(2)}) copy-start(bf16[256,768]{1,0:T(8,128)(2,1)} %get-tuple-element.397) | copy-start | bytes 1179652
  (84 other events, 1241.7 us)
Sparse Core Ops, SparseCore 0:
  9.7 27.3 all-gather.6
  42.7 50.0 all-gather.10
  95.5 47.7 all-gather.8
  145.4 24.5 all-gather.12
  172.8 40.6 all-reduce.21
  219.7 41.8 all-reduce.23
  314.8 78.5 reduce-scatter.7
  397.5 75.9 reduce-scatter.9
  582.7 38.3 all-reduce.25
where the time goes:
time: 1220 us; the launch traced here: 1200 us
  blocking collectives  783 us (64%)
  waiting for transfers between devices  167 us (14%)
  starting transfers between devices  94.6 us (8%)
  matrix products  52.3 us (4%)
  local copies, waits for them, and re-layouts  52.1 us (4%)
  other arithmetic  33.6 us (3%)
  between operations  18.2 us (1%)
    unnamed x4, blocking collectives  614 us
    unnamed x32, starting transfers between devices  94 us
    all_gather x1, waiting for transfers between devices, on_device(): lax.all_gather(value_flat, 'context', axis=0, tiled=True)  42.1 us
    psum x1, waiting for transfers between devices, on_device(): lax.psum(jnp.dot(gate_up_grad, gelu_flat.T, preferred_element_type=jnp.fl...  41.8 us
    psum x1, waiting for transfers between devices, on_device(): residual = inputs + lax.psum(attn_part, 'tensor')  40.8 us
    all_gather x1, blocking collectives, on_device(): lax.all_gather(shares[1].astype(jnp.bfloat16), 'context', axis=0, tiled=T...  34.9 us
    all_gather x1, blocking collectives, on_device(): lax.all_gather(shares[5].astype(jnp.bfloat16), 'context', axis=1, tiled=T...  34.7 us
    all_gather x1, blocking collectives, on_device(): lax.all_gather(shares[4].astype(jnp.bfloat16), 'context', axis=0, tiled=T...  34.6 us
  transfers between devices with their start and end apart: 41, of which 7 were waited for; matrix products, arithmetic and copies ran while one was open for 22% of the time, Pallas kernels for 0%

commit v1 on v0

--- a/solution.py
+++ b/solution.py
@@ -181,7 +181,7 @@
         residual + lax.psum(mlp_part.astype(jnp.bfloat16), "tensor").astype(jnp.float32)
     ).astype(jnp.bfloat16)
     act_grad = jnp.dot(out_cotangent, down_full.T, preferred_element_type=jnp.float32)
-    down_grad = jnp.dot(activ.T, out_cotangent, preferred_element_type=jnp.float32)
+    down_grad_t = jnp.dot(out_cotangent.T, activ, preferred_element_type=jnp.float32)
     gate_up_grad = (
         jnp.stack([act_grad * up_pre * gelu_slope, act_grad * gelu_val], axis=1)
         .astype(jnp.bfloat16)
@@ -201,7 +201,7 @@
     out_grad = jnp.dot(resid_bf, proj_full.T, preferred_element_type=jnp.float32).astype(
         jnp.bfloat16
     )
-    proj_grad = jnp.dot(mixed_flat.T, resid_bf, preferred_element_type=jnp.float32)
+    proj_grad_t = jnp.dot(resid_bf.T, mixed_flat, preferred_element_type=jnp.float32)
     out_heads = out_grad.reshape(row_count, head_count, HD)
     delta = jnp.transpose(
         jnp.sum(out_heads.astype(jnp.float32) * mixed.astype(jnp.float32), axis=2)
@@ -307,34 +307,31 @@
     ).astype(jnp.float32)
     attngain_grad = jnp.sum(attn_in_grad * normed_attn, axis=0)
     input_grad = resid_grad + norm_back(attn_in_grad, normed_attn, spread_attn, attn_scale)
-    grads = (attngain_grad, qkv_grad, proj_grad, mlpgain_grad, gelu_grad, down_grad)
+    grads = (
+        attngain_grad[:, None],
+        mlpgain_grad[:, None],
+        qkv_grad.reshape(feature_count, 3 * local_width),
+        gelu_grad.reshape(feature_count, 2 * hidden),
+        proj_grad_t,
+        down_grad_t,
+    )
+    widths = [g.shape[1] for g in grads]
+    packed = jnp.concatenate(grads, axis=1)
+    packed = lax.psum_scatter(packed, "fsdp", scatter_dimension=0, tiled=True)
+    packed = lax.psum(packed, "context")
+    pieces = []
+    start = 0
+    for width in widths:
+        pieces.append(packed[:, start : start + width])
+        start += width
+    shard_rows = packed.shape[0]
     shares = (
-        lax.psum_scatter(grads[0], ("fsdp", "context"), scatter_dimension=0, tiled=True),
-        lax.psum_scatter(grads[1], ("fsdp", "context"), scatter_dimension=0, tiled=True),
-        lax.psum_scatter(grads[2], ("fsdp", "context"), scatter_dimension=1, tiled=True),
-        lax.psum_scatter(grads[3], ("fsdp", "context"), scatter_dimension=0, tiled=True),
-        lax.psum_scatter(grads[4], ("fsdp", "context"), scatter_dimension=0, tiled=True),
-        lax.psum_scatter(grads[5], ("fsdp", "context"), scatter_dimension=1, tiled=True),
-    )
-    shares = (
-        lax.all_gather(shares[0].astype(jnp.bfloat16), "context", axis=0, tiled=True).astype(
-            jnp.float32
-        ),
-        lax.all_gather(shares[1].astype(jnp.bfloat16), "context", axis=0, tiled=True).astype(
-            jnp.float32
-        ),
-        lax.all_gather(shares[2].astype(jnp.bfloat16), "context", axis=1, tiled=True).astype(
-            jnp.float32
-        ),
-        lax.all_gather(shares[3].astype(jnp.bfloat16), "context", axis=0, tiled=True).astype(
-            jnp.float32
-        ),
-        lax.all_gather(shares[4].astype(jnp.bfloat16), "context", axis=0, tiled=True).astype(
-            jnp.float32
-        ),
-        lax.all_gather(shares[5].astype(jnp.bfloat16), "context", axis=1, tiled=True).astype(
-            jnp.float32
-        ),
+        pieces[0][:, 0],
+        pieces[2].reshape(shard_rows, 3, local_width),
+        pieces[4].T,
+        pieces[1][:, 0],
+        pieces[3].reshape(shard_rows, 2, hidden),
+        pieces[5].T,
     )
     return (
         block_output,

time: 1220 us -> 700 us (0.57); the launches traced: 1200 us -> 698 us
  blocking collectives: 783 us -> 44.7 us
  waiting for transfers between devices: 167 us -> 499 us
  starting transfers between devices: 94.6 us -> 0.67 us
    unnamed x4 -> x1, blocking collectives: 614 us -> 14.7 us
    all_gather x4 -> x0, blocking collectives: 138 us -> none  [the longest x1 34.9 us: on_device(): lax.all_gather(shares[1].astype(jnp.bfloat16), 'context', axis=0, tiled=T...]
    psum x1 -> x2, waiting for transfers between devices: 0.01 us -> 128 us  [the longest x1 94.9 us: on_device(): packed = lax.psum(packed, 'context')]
    unnamed x32 -> x0, starting transfers between devices: 94 us -> none
    reduce_scatter x1, waiting for transfers between devices: 0.01 us -> 74.7 us  [on_device(): lax.psum_scatter(back_result[2].astype(jnp.bfloat16), 'context', scatter_...]
    reduce_scatter x1, waiting for transfers between devices: 0.02 us -> 67.5 us  [on_device(): lax.psum_scatter(back_result[1].astype(jnp.bfloat16), 'context', scatter_...]
    reduce_scatter x0 -> x1, waiting for transfers between devices: none -> 62.2 us  [on_device(): packed = lax.psum_scatter(packed, 'fsdp', scatter_dimension=0, tiled=True)]
    concatenate x0 -> x1, local copies, waits for them, and re-layouts: none -> 13.5 us  [on_device(): packed = jnp.concatenate(grads, axis=1)]
  transfers between devices with their start and end apart: 41 -> 11, of which waited for: 7 -> 11; matrix products, arithmetic and copies ran while one was open for 22% -> 7% of each run, Pallas kernels for 0% -> 0%
where the time goes in v1:
time: 700 us; the launch traced here: 698 us
  waiting for transfers between devices  499 us (71%)
  matrix products  54.2 us (8%)
  local copies, waits for them, and re-layouts  54.1 us (8%)
  blocking collectives  44.7 us (6%)
  other arithmetic  30.3 us (4%)
  between operations  15.2 us (2%)
    psum x1, waiting for transfers between devices, on_device(): packed = lax.psum(packed, 'context')  94.9 us
    reduce_scatter x1, waiting for transfers between devices, on_device(): lax.psum_scatter(back_result[2].astype(jnp.bfloat16), 'context', scatter_...  74.7 us
    reduce_scatter x1, waiting for transfers between devices, on_device(): lax.psum_scatter(back_result[1].astype(jnp.bfloat16), 'context', scatter_...  67.5 us
    reduce_scatter x1, waiting for transfers between devices, on_device(): packed = lax.psum_scatter(packed, 'fsdp', scatter_dimension=0, tiled=True)  62.2 us
    all_gather x1, waiting for transfers between devices, on_device(): lax.all_gather(value_flat, 'context', axis=0, tiled=True)  42.2 us
    psum x1, waiting for transfers between devices, on_device(): lax.psum(jnp.dot(gate_up_grad, gelu_flat.T, preferred_element_type=jnp.fl...  41.8 us
    psum x1, waiting for transfers between devices, on_device(): residual = inputs + lax.psum(attn_part, 'tensor')  40.8 us
    all_gather x1, waiting for transfers between devices, on_device(): lax.all_gather(key_flat, 'context', axis=0, tiled=True)  33.9 us
  transfers between devices with their start and end apart: 11, of which 11 were waited for; matrix products, arithmetic and copies ran while one was open for 7% of the time, Pallas kernels for 0%

profile of v1, /device:TPU:0, one launch (start us, length us, event | category | flops | bytes accessed | tf_op | source)
XLA Modules:
  0.0 698.4 jit_solution(5407401806397029626)
XLA Ops:
  11.6 14.7 %all-reduce.2 = (bf16[768]{0:T(1024)(128)(2,1)S(1)}, bf16[768]{0:T(1024)(128)(2,1)S(1)}) all-reduce(bf16[768]{0:T(1024)(128)(2,1)S(1)} %dynamic-update-slice, bf16[768]{0:T(1024)(128)(2,1)S(1)} %dynamic-update-slice.1), channel_id=1, replica_groups=mesh['fsdp'=8,'tensor'=2,'context'=8] {'fsdp'}, use_global_device_ids=true, to_apply=%add | all-reduce | flops 1536 | bytes 6144
  30.6 6.5 all-gather.5.cloned.1.call-done
  37.1 2.6 copy.52
  42.6 1.7 slice.139
  45.6 13.2 %all_gather.30 = bf16[384,768]{0,1:T(8,128)(2,1)S(1)} all-gather(bf16[384,96]{0,1:T(8,128)(2,1)S(1)} %copy-done.46), channel_id=1, replica_groups=mesh['fsdp'=8,'tensor'=2,'context'=8] {'fsdp'}, dimensions={1}, use_global_device_ids=true | all-gather | bytes 663552 | tf_op jit(solution)/shard_map/all_gather | solution.py:121
  58.8 33.9 %all-gather.9.cloned.1.call-done = bf16[2048,384]{0,1:T(8,128)(2,1)} async-done(((bf16[256,384]{0,1:T(8,128)(2,1)}), bf16[2048,384]{0,1:T(8,128)(2,1)}) %all-gather.9.cloned.1.call-update) | async-done | bytes 1572880 | tf_op jit(solution)/shard_map/all_gather | solution.py:146
  92.7 3.9 select_reduce_fusion.1
  96.6 3.9 select_reduce_fusion
  101.1 42.2 %all-gather.7.cloned.1.call-done = bf16[2048,384]{0,1:T(8,128)(2,1)} async-done(((bf16[256,384]{0,1:T(8,128)(2,1)}), bf16[2048,384]{0,1:T(8,128)(2,1)}) %all-gather.7.cloned.1.call-update) | async-done | bytes 1572880 | tf_op jit(solution)/shard_map/all_gather | solution.py:147
  143.3 7.7 %fusion.13 = bf16[6,64,256]{2,1,0:T(8,128)(2,1)S(1)} fusion(bf16[2048,6,64]{0,2,1:T(8,128)(2,1)} %bitcast.184, f32[6,256,2048]{2,1,0:T(8,128)} %copy-done.7, f32[6,256]{1,0:T(8,128)S(1)} %log_add_fusion, pred[256,2048]{1,0:T(8,128)(4,1)S(1)} %broadcast_compare_fusion.1), kind=kOutput, calls=%fused_computation.37 | convolution fusion | flops 415334400 | bytes 14882816 | tf_op jit(solution)/shard_map/hqk,khd->qhd/dot_general | solution.py:164
  152.4 16.8 %all_gather.33 = bf16[576,768]{0,1:T(8,128)(2,1)} all-gather(bf16[576,96]{0,1:T(8,128)(2,1)S(1)} %copy-done.45), channel_id=1, replica_groups=mesh['fsdp'=8,'tensor'=2,'context'=8] {'fsdp'}, dimensions={1}, use_global_device_ids=true | all-gather | bytes 995328 | tf_op jit(solution)/shard_map/all_gather | solution.py:123
  170.0 2.7 copy.54
  172.7 40.8 %all-reduce.9.cloned.1.call-done = f32[256,768]{1,0:T(8,128)} async-done(((f32[256,768]{1,0:T(8,128)}), f32[256,768]{1,0:T(8,128)}) %all-reduce.9.cloned.1.call-update) | async-done | bytes 786448 | tf_op jit(solution)/shard_map/psum | solution.py:169
  217.8 1.7 convolution_bitcast_fusion.1
  219.8 41.8 %all-reduce.11.cloned.1.call-done = f32[256,768]{1,0:T(8,128)} async-done(((f32[256,768]{1,0:T(8,128)}), f32[256,768]{1,0:T(8,128)}) %all-reduce.11.cloned.1.call-update) | async-done | bytes 786448 | tf_op jit(solution)/shard_map/psum | solution.py:193
  261.6 2.1 multiply_reduce_fusion
  263.8 1.4 multiply_add_fusion
  266.4 2.1 broadcast.210
  268.5 2.0 broadcast.210.clone
  270.5 40.4 %while.20 = (s32[]{:T(128)}, f32[256,6,64]{0,2,1:T(8,128)}, f32[2048,384]{0,1:T(8,128)}, f32[2048,384]{0,1:T(8,128)}, bf16[2048,384]{0,1:T(8,128)(2,1)}, /*index...) while((s32[]{:T(128)}, f32[256,6,64]{0,2,1:T(8,128)}, ...), condition=%wide.region_19.20_spmd.clone, body=%wide.region_17.19_spmd.clone.sunk | while | flops 1024107520 | bytes 131182336 | solution.py:86
  273.2 1.8 constant_dynamic-slice_fusion.5
  275.0 3.3 fusion.105
  278.4 2.6 fusion.106
  281.0 4.3 fusion.107
  288.1 1.7 copy-done.3
  293.4 1.8 constant_dynamic-slice_fusion.5
  295.2 3.3 fusion.105
  298.6 2.7 fusion.106
  301.2 4.3 fusion.107
  308.3 1.7 copy-done.3
  310.9 3.4 convert_element_type.160
  314.4 1.4 convert_element_type.161
  318.9 2.7 fusion.48
  321.6 67.5 %reduce-scatter.4.cloned.1.call-done = bf16[256,384]{0,1:T(8,128)(2,1)} async-done(((bf16[2048,384]{0,1:T(8,128)(2,1)}), bf16[256,384]{0,1:T(8,128)(2,1)}) %reduce-scatter.4.cloned.1.call-update) | async-done | bytes 196624 | tf_op jit(solution)/shard_map/reduce_scatter | solution.py:280
  391.1 74.7 %reduce-scatter.6.cloned.1.call-done = bf16[256,384]{0,1:T(8,128)(2,1)} async-done(((bf16[2048,384]{0,1:T(8,128)(2,1)}), bf16[256,384]{0,1:T(8,128)(2,1)}) %reduce-scatter.6.cloned.1.call-update) | async-done | bytes 196624 | tf_op jit(solution)/shard_map/reduce_scatter | solution.py:283
  467.6 1.5 convolution_convert_fusion
  469.1 3.0 convolution_bitcast_fusion
  472.3 1.4 fusion.38
  473.7 2.6 fusion.45
  476.3 32.8 %all-reduce.15.cloned.1.call-done = (bf16[256,768]{1,0:T(8,128)(2,1)}, bf16[256,768]{1,0:T(8,128)(2,1)}) async-done(((bf16[256,768]{1,0:T(8,128)(2,1)}, bf16[256,768]{1,0:T(8,128)(2,1)}), (bf16[256,768]{1,0:T(8,128)(2,1)}, bf16[256,768]{1,0:T(8,128)(2,1)})) %all-reduce.15.cloned.1.call-update) | async-done | bytes 786448 | tf_op jit(solution)/shard_map/psum | solution.py:181
  509.1 1.4 fusion.27
  510.7 13.5 %concatenate.21 = f32[768,3266]{1,0:T(8,128)} concatenate(f32[768,1]{1,0:T(8,128)S(1)} %broadcast_in_dim.141, f32[768,1]{1,0:T(8,128)S(1)} %broadcast_in_dim.142, f32[768,1152]{1,0:T(8,128)} %fusion.45, f32[768,1152]{1,0:T(8,128)} %fusion.48, f32[768,384]{1,0:T(8,128)} %fusion.38, f32[768,576]{1,0:T(8,128)} %convolution_bitcast_fusion), dimensions={1} | concatenate | bytes 20066304 | tf_op jit(solution)/shard_map/concatenate | solution.py:319
  524.3 62.2 %reduce-scatter.8.cloned.1.call-done = f32[96,3266]{1,0:T(8,128)} async-done(((f32[768,3266]{1,0:T(8,128)}), f32[96,3266]{1,0:T(8,128)}) %reduce-scatter.8.cloned.1.call-update) | async-done | bytes 1254160 | tf_op jit(solution)/shard_map/reduce_scatter | solution.py:320
  588.6 94.9 %all-reduce.13.cloned.1.call-done = f32[96,3266]{1,0:T(8,128)} async-done(((f32[96,3266]{1,0:T(8,128)}), f32[96,3266]{1,0:T(8,128)}) %all-reduce.13.cloned.1.call-update) | async-done | bytes 1254160 | tf_op jit(solution)/shard_map/psum | solution.py:321
  683.4 1.5 fusion.50
  686.8 1.6 slice_reduce_fusion
  688.4 1.7 slice_bitcast_fusion.5
  690.1 1.8 slice_bitcast_fusion.4
  (248 shorter events, 44.2 us)
Async XLA Ops:
  7.2 32.6 %copy-start.10 = (bf16[256,768]{1,0:T(8,128)(2,1)S(1)}, bf16[256,768]{1,0:T(8,128)(2,1)}, u32[]{:S(2)}) copy-start(bf16[256,768]{1,0:T(8,128)(2,1)} %param.11) | copy-start | bytes 1179652
  7.2 29.9 %all-gather.5.cloned.1.call-start = ((), (), s32[]{:S(2)}) async-start(), calls=%async_computation.3 | async-start | bytes 1990656 | tf_op jit(solution)/shard_map/all_gather | solution.py:120
  7.9 84.8 %all-gather.9.cloned.1.call-start = ((), (), s32[]{:S(2)}) async-start(), calls=%async_computation.5 | async-start | bytes 1769472 | tf_op jit(solution)/shard_map/all_gather | solution.py:146
  30.3 10.2 %copy-start.50 = (f32[256]{0:T(256)}, f32[256]{0:T(256)S(1)}, u32[]{:S(2)}) copy-start(f32[256]{0:T(256)S(1)} %add_rsqrt_fusion.1) | copy-start | bytes 3076
  30.6 11.1 %copy-start.40 = (f32[256,32]{0,1:T(8,128)}, f32[256,32]{0,1:T(8,128)S(1)}, u32[]{:S(2)}) copy-start(f32[256,32]{0,1:T(8,128)S(1)} %get-tuple-element.417) | copy-start | bytes 98308
  30.6 11.1 %copy-start.41 = (f32[256,32]{0,1:T(8,128)}, f32[256,32]{0,1:T(8,128)S(1)}, u32[]{:S(2)}) copy-start(f32[256,32]{0,1:T(8,128)S(1)} %get-tuple-element.418) | copy-start | bytes 98308
  39.7 4.6 copy-start.44
  41.6 4.1 copy-start.46
  41.8 54.8 %copy-start.33 = (bf16[256,6,32]{0,2,1:T(8,128)(2,1)}, bf16[256,6,32]{0,2,1:T(8,128)(2,1)S(1)}, u32[]{:S(2)}) copy-start(bf16[256,6,32]{0,2,1:T(8,128)(2,1)S(1)} %get-tuple-element.409) | copy-start | bytes 294916
  41.8 54.8 %copy-start.35 = (bf16[256,6,32]{0,2,1:T(8,128)(2,1)}, bf16[256,6,32]{0,2,1:T(8,128)(2,1)S(1)}, u32[]{:S(2)}) copy-start(bf16[256,6,32]{0,2,1:T(8,128)(2,1)S(1)} %get-tuple-element.410) | copy-start | bytes 294916
  42.5 100.8 %all-gather.7.cloned.1.call-start = ((), (), s32[]{:S(2)}) async-start(), calls=%async_computation.4 | async-start | bytes 1769472 | tf_op jit(solution)/shard_map/all_gather | solution.py:147
  44.3 125.7 %all-gather.11.cloned.1.call-start = ((), (), s32[]{:S(2)}) async-start(), calls=%async_computation.7 | async-start | bytes 2211840 | tf_op jit(solution)/shard_map/all_gather | solution.py:122
  45.1 168.4 %all-reduce.9.cloned.1.call-start = ((), (), s32[]{:S(2)}) async-start(), calls=%async_computation.6 | async-start | bytes 1572864 | tf_op jit(solution)/shard_map/psum | solution.py:169
  58.8 92.1 %copy-start.19 = (bf16[384,768]{0,1:T(8,128)(2,1)}, bf16[384,768]{0,1:T(8,128)(2,1)S(1)}, u32[]{:S(2)}) copy-start(bf16[384,768]{0,1:T(8,128)(2,1)S(1)} %all_gather.30) | copy-start | bytes 1769476
  96.6 4.5 copy-start.7
  101.1 49.8 %copy-start.58 = (f32[6,256]{1,0:T(8,128)}, f32[6,256]{1,0:T(8,128)S(1)}, u32[]{:S(2)}) copy-start(f32[6,256]{1,0:T(8,128)S(1)} %log_add_fusion) | copy-start | bytes 18436
  143.3 9.1 %copy-start.45 = (bf16[576,96]{0,1:T(8,128)(2,1)S(1)}, bf16[576,96]{0,1:T(8,128)(2,1)}, u32[]{:S(2)}) copy-start(bf16[576,96]{0,1:T(8,128)(2,1)} %param.18) | copy-start | bytes 331780
  152.3 109.3 %all-reduce.11.cloned.1.call-start = ((), (), s32[]{:S(2)}) async-start(), calls=%async_computation.8 | async-start | bytes 1572864 | tf_op jit(solution)/shard_map/psum | solution.py:193
  172.7 44.1 %copy-start.31 = (bf16[256,768]{1,0:T(8,128)(2,1)S(1)}, bf16[256,768]{1,0:T(8,128)(2,1)}, u32[]{:S(2)}) copy-start(bf16[256,768]{1,0:T(8,128)(2,1)} %param.19) | copy-start | bytes 1179652
  214.9 48.9 %copy-start.8 = (f32[256,768]{1,0:T(8,128)}, f32[256,768]{1,0:T(8,128)S(1)}, u32[]{:S(2)}) copy-start(f32[256,768]{1,0:T(8,128)S(1)} %get-tuple-element.396) | copy-start | bytes 2359300
  217.5 46.2 %copy-start.42 = (bf16[256,1,576]{0,2,1:T(8,128)(2,1)}, bf16[256,1,576]{0,2,1:T(8,128)(2,1)S(1)}, u32[]{:S(2)}) copy-start(bf16[256,1,576]{0,2,1:T(8,128)(2,1)S(1)} %get-tuple-element.399) | copy-start | bytes 884740
  217.5 46.2 %copy-start.43 = (bf16[256,1,576]{0,2,1:T(8,128)(2,1)}, bf16[256,1,576]{0,2,1:T(8,128)(2,1)S(1)}, u32[]{:S(2)}) copy-start(bf16[256,1,576]{0,2,1:T(8,128)(2,1)S(1)} %get-tuple-element.400) | copy-start | bytes 884740
  217.5 44.1 %copy-start.48 = (f32[256]{0:T(256)S(1)}, f32[256]{0:T(256)}, u32[]{:S(2)}) copy-start(f32[256]{0:T(256)} %copy-done.47) | copy-start | bytes 3076
  217.5 44.1 %copy-start.53 = (f32[256]{0:T(256)S(1)}, f32[256]{0:T(256)}, u32[]{:S(2)}) copy-start(f32[256]{0:T(256)} %copy-done.52) | copy-start | bytes 3076
  217.8 45.9 %copy-start.32 = (bf16[256,768]{1,0:T(8,128)(2,1)S(1)}, bf16[256,768]{1,0:T(8,128)(2,1)}, u32[]{:S(2)}) copy-start(bf16[256,768]{1,0:T(8,128)(2,1)} %param.19) | copy-start | bytes 1179652
  219.6 45.6 %copy-start.20 = (bf16[384,768]{0,1:T(8,128)(2,1)S(1)}, bf16[384,768]{0,1:T(8,128)(2,1)}, u32[]{:S(2)}) copy-start(bf16[384,768]{0,1:T(8,128)(2,1)} %copy-done.19) | copy-start | bytes 1769476
  219.6 169.6 %reduce-scatter.4.cloned.1.call-start = ((), (), s32[]{:S(2)}) async-start(), calls=%async_computation.9 | async-start | bytes 1769472 | tf_op jit(solution)/shard_map/reduce_scatter | solution.py:280
  265.2 5.4 copy-start.15
  272.9 5.5 copy-start.1
  273.2 5.2 copy-start.17
  281.0 5.4 copy-start.4
  293.0 5.5 copy-start.1
  293.4 5.2 copy-start.17
  301.2 5.4 copy-start.4
  310.9 3.5 copy-start.6
  314.4 151.4 %reduce-scatter.6.cloned.1.call-start = ((), (), s32[]{:S(2)}) async-start(), calls=%async_computation.10 | async-start | bytes 1769472 | tf_op jit(solution)/shard_map/reduce_scatter | solution.py:283
  315.9 193.2 %all-reduce.15.cloned.1.call-start = ((), (), s32[]{:S(2)}) async-start(), calls=%async_computation.13 | async-start | bytes 1572864 | tf_op jit(solution)/shard_map/psum | solution.py:181
  318.9 71.2 %copy-start.14 = (f32[256,6,64]{0,2,1:T(8,128)S(1)}, f32[256,6,64]{0,2,1:T(8,128)}, u32[]{:S(2)}) copy-start(f32[256,6,64]{0,2,1:T(8,128)} %get-tuple-element.285) | copy-start | bytes 1179652
  318.9 148.7 %copy-start.13 = (bf16[768,3,384]{0,2,1:T(8,128)(2,1)S(1)}, bf16[768,3,384]{0,2,1:T(8,128)(2,1)}, u32[]{:S(2)}) copy-start(bf16[768,3,384]{0,2,1:T(8,128)(2,1)} %copy-done.12) | copy-start | bytes 5308420
  466.8 5.3 copy-start.55
  467.6 4.7 copy-start.16
  469.0 4.7 copy-start.11
  469.0 4.7 copy-start.22
  469.0 4.7 copy-start.51
  469.1 117.4 %reduce-scatter.8.cloned.1.call-start = ((), (), s32[]{:S(2)}) async-start(), calls=%async_computation.11 | async-start | bytes 11501568 | tf_op jit(solution)/shard_map/reduce_scatter | solution.py:320
  524.2 62.3 %copy-start.39 = (bf16[256,768]{1,0:T(8,128)(2,1)S(1)}, bf16[256,768]{1,0:T(8,128)(2,1)}, u32[]{:S(2)}) copy-start(bf16[256,768]{1,0:T(8,128)(2,1)} %get-tuple-element.393) | copy-start | bytes 1179652
  524.2 63.2 %copy-start.30 = (bf16[256,768]{1,0:T(8,128)(2,1)S(1)}, bf16[256,768]{1,0:T(8,128)(2,1)}, u32[]{:S(2)}) copy-start(bf16[256,768]{1,0:T(8,128)(2,1)} %get-tuple-element.394) | copy-start | bytes 1179652
  524.3 159.2 %all-reduce.13.cloned.1.call-start = ((), (), s32[]{:S(2)}) async-start(), calls=%async_computation.12 | async-start | bytes 2555904 | tf_op jit(solution)/shard_map/psum | solution.py:321
  (41 other events, 95.8 us)
Sparse Core Ops, SparseCore 0:
  9.7 27.3 all-gather.4
  42.7 50.0 all-gather.8
  95.5 47.7 all-gather.6
  145.4 24.5 all-gather.10
  172.8 40.5 all-reduce.8
  219.7 41.8 all-reduce.10
  314.5 74.6 reduce-scatter.3
  393.3 72.4 reduce-scatter.5
  469.2 39.8 all-reduce.14
  524.4 62.0 reduce-scatter.7
  589.2 94.2 all-reduce.12

commit v2 on v1

--- a/solution.py
+++ b/solution.py
@@ -64,6 +64,13 @@
     normal_cdf = 0.5 * (1.0 + jax.scipy.special.erf(gate_pre * 0.7071067811865476))
     density = jnp.exp(-0.5 * gate_pre * gate_pre) * 0.3989422804014327
     return (gate_pre * normal_cdf, normal_cdf + gate_pre * density)
+
+
+def pair_sum(values, axis_name):
+    if lax.axis_size(axis_name) != 2:
+        return lax.psum(values, axis_name)
+    other = lax.ppermute(values, axis_name, perm=[(0, 1), (1, 0)])
+    return values.astype(jnp.float32) + other.astype(jnp.float32)
 
 
 def split_count(row_count):
@@ -142,10 +149,10 @@
     value_bf = projected[:, 2].astype(jnp.bfloat16)
     key_flat = key_bf.reshape(row_count, local_width)
     value_flat = value_bf.reshape(row_count, local_width)
-    keys_group, values_group = (
-        lax.all_gather(key_flat, "context", axis=0, tiled=True),
-        lax.all_gather(value_flat, "context", axis=0, tiled=True),
-    )
+    kv_group = lax.all_gather(
+        jnp.concatenate([key_flat, value_flat], axis=1), "context", axis=0, tiled=True
+    )
+    keys_group, values_group = (kv_group[:, :local_width], kv_group[:, local_width:])
     keys_heads = keys_group.reshape(group_rows, head_count, HD)
     values_heads = values_group.reshape(group_rows, head_count, HD)
     group_segment, unused_pos = segments_of(jnp.arange(group_rows, dtype=jnp.int32), lengths)
@@ -166,7 +173,7 @@
     ).astype(jnp.bfloat16)
     mixed_flat = mixed.reshape(row_count, local_width)
     attn_part = jnp.dot(mixed_flat, proj_full, preferred_element_type=jnp.float32)
-    residual = inputs + lax.psum(attn_part, "tensor")
+    residual = inputs + pair_sum(attn_part, "tensor")
     normed_mlp, spread_mlp = layer_norm(residual)
     hidden_mlp = (normed_mlp * mlp_scale).astype(jnp.bfloat16)
     gelu_flat = gelu_full.reshape(feature_count, 2 * hidden)
@@ -178,7 +185,7 @@
     activ = (gelu_val * up_pre).astype(jnp.bfloat16)
     mlp_part = jnp.dot(activ, down_full, preferred_element_type=jnp.float32)
     block_output = (
-        residual + lax.psum(mlp_part.astype(jnp.bfloat16), "tensor").astype(jnp.float32)
+        residual + pair_sum(mlp_part.astype(jnp.bfloat16), "tensor")
     ).astype(jnp.bfloat16)
     act_grad = jnp.dot(out_cotangent, down_full.T, preferred_element_type=jnp.float32)
     down_grad_t = jnp.dot(out_cotangent.T, activ, preferred_element_type=jnp.float32)
@@ -190,7 +197,7 @@
     gelu_grad = jnp.dot(hidden_mlp.T, gate_up_grad, preferred_element_type=jnp.float32).reshape(
         feature_count, 2, hidden
     )
-    mlp_in_grad = lax.psum(
+    mlp_in_grad = pair_sum(
         jnp.dot(gate_up_grad, gelu_flat.T, preferred_element_type=jnp.float32), "tensor"
     )
     mlpgain_grad = jnp.sum(mlp_in_grad * normed_mlp, axis=0)
@@ -269,21 +276,17 @@
     )
     back_result = guarded(owner_step)(
         back_state,
-        (
-            lax.all_gather(key_flat, "context", axis=0, tiled=True),
-            lax.all_gather(value_flat, "context", axis=0, tiled=True),
-        ),
+        (keys_group, values_group),
         jnp.int32(0),
     )
     query_grad = back_result[0]
-    key_grad, value_grad = (
-        lax.psum_scatter(
-            back_result[1].astype(jnp.bfloat16), "context", scatter_dimension=0, tiled=True
-        ).astype(jnp.float32),
-        lax.psum_scatter(
-            back_result[2].astype(jnp.bfloat16), "context", scatter_dimension=0, tiled=True
-        ).astype(jnp.float32),
-    )
+    kv_grad = lax.psum_scatter(
+        jnp.concatenate([back_result[1], back_result[2]], axis=1).astype(jnp.bfloat16),
+        "context",
+        scatter_dimension=0,
+        tiled=True,
+    ).astype(jnp.float32)
+    key_grad, value_grad = (kv_grad[:, :local_width], kv_grad[:, local_width:])
     key_grad = key_grad.reshape(row_count, head_count, HD)
     value_grad = value_grad.reshape(row_count, head_count, HD)
     qkv_rows = (
@@ -301,10 +304,10 @@
     qkv_grad = jnp.dot(hidden_attn.T, qkv_rows, preferred_element_type=jnp.float32).reshape(
         feature_count, 3, local_width
     )
-    attn_in_grad = lax.psum(
+    attn_in_grad = pair_sum(
         jnp.dot(qkv_rows, qkv_flat.T, preferred_element_type=jnp.float32).astype(jnp.bfloat16),
         "tensor",
-    ).astype(jnp.float32)
+    )
     attngain_grad = jnp.sum(attn_in_grad * normed_attn, axis=0)
     input_grad = resid_grad + norm_back(attn_in_grad, normed_attn, spread_attn, attn_scale)
     grads = (

time: 700 us -> 503 us (0.72)
  waiting for transfers between devices: 499 us -> 308 us
  matrix products: 54.2 us -> 45.8 us
    psum x3 -> x0, waiting for transfers between devices: 115 us -> none  [the longest x1 41.8 us: on_device(): lax.psum(jnp.dot(gate_up_grad, gelu_flat.T, preferred_element_type=jnp.fl...]
    reduce_scatter x2 -> x1, waiting for transfers between devices: 142 us -> 72 us  [on_device(): lax.psum_scatter(jnp.concatenate([back_result[1], back_result[2]], axis=1...]
    all_gather x2 -> x1, waiting for transfers between devices: 76.1 us -> 50 us  [on_device(): lax.all_gather(jnp.concatenate([key_flat, value_flat], axis=1), 'context'...]
    ppermute x0 -> x4, waiting for transfers between devices: none -> 24 us  [pair_sum(): other = lax.ppermute(values, axis_name, perm=[(0, 1), (1, 0)])]
  transfers between devices with their start and end apart: 11 -> 10, of which waited for: 11 -> 8; matrix products, arithmetic and copies ran while one was open for 7% -> 8% of each run, Pallas kernels for 0% -> 0%
where the time goes in v2:
time: 503 us; the launch traced here: 501 us
  waiting for transfers between devices  308 us (61%)
  local copies, waits for them, and re-layouts  54.9 us (11%)
  matrix products  45.8 us (9%)
  blocking collectives  45.4 us (9%)
  other arithmetic  27.8 us (6%)
  between operations  15.5 us (3%)
    psum x1, waiting for transfers between devices, on_device(): packed = lax.psum(packed, 'context')  95.4 us
    reduce_scatter x1, waiting for transfers between devices, on_device(): lax.psum_scatter(jnp.concatenate([back_result[1], back_result[2]], axis=1...  72 us
    reduce_scatter x1, waiting for transfers between devices, on_device(): packed = lax.psum_scatter(packed, 'fsdp', scatter_dimension=0, tiled=True)  59.7 us
    all_gather x1, waiting for transfers between devices, on_device(): lax.all_gather(jnp.concatenate([key_flat, value_flat], axis=1), 'context'...  50 us
    ppermute x4, waiting for transfers between devices, pair_sum(): other = lax.ppermute(values, axis_name, perm=[(0, 1), (1, 0)])  24 us
    all_gather x1, blocking collectives, on_device(): lax.all_gather(down_weight, 'fsdp', axis=1, tiled=True)  17 us
    unnamed x1, blocking collectives  15.3 us
    all_gather x1, blocking collectives, on_device(): lax.all_gather(proj_weight, 'fsdp', axis=1, tiled=True)  13.2 us
  transfers between devices with their start and end apart: 10, of which 8 were waited for; matrix products, arithmetic and copies ran while one was open for 8% of the time, Pallas kernels for 0%

profile of v2, /device:TPU:0, one launch (start us, length us, event | category | flops | bytes accessed | tf_op | source)
XLA Modules:
  0.0 501.4 jit_solution(11851167980308831654)
XLA Ops:
  11.6 15.3 %all-reduce.2 = (bf16[768]{0:T(1024)(128)(2,1)S(1)}, bf16[768]{0:T(1024)(128)(2,1)}) all-reduce(bf16[768]{0:T(1024)(128)(2,1)S(1)} %dynamic-update-slice, bf16[768]{0:T(1024)(128)(2,1)S(1)} %dynamic-update-slice.1), channel_id=1, replica_groups=mesh['fsdp'=8,'tensor'=2,'context'=8] {'fsdp'}, use_global_device_ids=true, to_apply=%add | all-reduce | flops 1536 | bytes 6144
  31.1 5.8 %all-gather.4.cloned.1.call-done = bf16[768,3,384]{2,0,1:T(8,128)(2,1)} async-done(((bf16[96,3,384]{2,0,1:T(8,128)(2,1)}), bf16[768,3,384]{2,0,1:T(8,128)(2,1)}) %all-gather.4.cloned.1.call-update) | async-done | bytes 1769488 | tf_op jit(solution)/shard_map/all_gather | solution.py:127
  36.9 2.6 copy.52
  42.9 13.2 %all_gather.24 = bf16[384,768]{0,1:T(8,128)(2,1)S(1)} all-gather(bf16[384,96]{0,1:T(8,128)(2,1)S(1)} %copy-done.53), channel_id=1, replica_groups=mesh['fsdp'=8,'tensor'=2,'context'=8] {'fsdp'}, dimensions={1}, use_global_device_ids=true | all-gather | bytes 663552 | tf_op jit(solution)/shard_map/all_gather | solution.py:128
  56.1 50.0 %all-gather.6.cloned.1.call-done = bf16[2048,768]{0,1:T(8,128)(2,1)} async-done(((bf16[256,768]{0,1:T(8,128)(2,1)}), bf16[2048,768]{0,1:T(8,128)(2,1)}) %all-gather.6.cloned.1.call-update) | async-done | bytes 3145744 | tf_op jit(solution)/shard_map/all_gather | solution.py:152
  106.1 2.2 fusion.52
  108.3 2.5 select_reduce_fusion.1
  110.7 4.0 select_reduce_fusion
  114.8 3.0 fusion.13
  118.9 17.0 %all_gather.27 = bf16[576,768]{0,1:T(8,128)(2,1)} all-gather(bf16[576,96]{0,1:T(8,128)(2,1)S(1)} %copy-done.52), channel_id=1, replica_groups=mesh['fsdp'=8,'tensor'=2,'context'=8] {'fsdp'}, dimensions={1}, use_global_device_ids=true | all-gather | bytes 995328 | tf_op jit(solution)/shard_map/all_gather | solution.py:130
  135.9 4.0 copy.54
  139.9 1.5 fusion.51
  143.3 1.6 convolution_bitcast_fusion.1
  144.9 1.5 collective-permute-start.2
  147.1 1.4 multiply_convert_fusion.1
  148.6 1.8 convolution_convert_fusion.1
  151.1 14.6 %collective-permute-done.2 = f32[256,768]{1,0:T(8,128)} collective-permute-done((f32[256,768]{1,0:T(8,128)}, f32[256,768]{1,0:T(8,128)}, u32[]{:S(2)}, u32[]{:S(2)}) %collective-permute-start.2) | collective-permute-done | bytes 786464 | tf_op jit(solution)/shard_map/ppermute | solution.py:72
  165.7 2.4 multiply_reduce_fusion
  168.0 5.4 %collective-permute-done.1 = bf16[256,768]{1,0:T(8,128)(2,1)S(1)} collective-permute-done((bf16[256,768]{1,0:T(8,128)(2,1)S(1)}, bf16[256,768]{1,0:T(8,128)(2,1)S(1)}, u32[]{:S(2)}, u32[]{:S(2)}) %collective-permute-start.1) | collective-permute-done | bytes 393248 | tf_op jit(solution)/shard_map/ppermute | solution.py:72
  173.4 1.7 multiply_add_fusion
  176.4 2.1 broadcast.211
  178.5 2.1 broadcast.211.clone
  180.5 38.6 %while.20 = (s32[]{:T(128)}, f32[256,6,64]{0,2,1:T(8,128)}, f32[2048,384]{0,1:T(8,128)}, f32[2048,384]{0,1:T(8,128)}, bf16[2048,384]{0,1:T(8,128)(2,1)S(1)}, /*i...) while((s32[]{:T(128)}, f32[256,6,64]{0,2,1:T(8,128)}, ...), condition=%wide.region_16.17_spmd.clone, body=%wide.region_14.16_spmd.clone.sunk | while | flops 1024107520 | bytes 143765232 | solution.py:93
  182.3 1.8 constant_dynamic-slice_fusion.5
  184.1 3.3 fusion.108
  187.5 2.6 fusion.109
  190.1 4.3 fusion.110
  197.2 1.7 copy-done.3
  201.6 1.8 constant_dynamic-slice_fusion.5
  203.4 3.3 fusion.108
  206.8 2.7 fusion.109
  209.4 4.3 fusion.110
  216.5 1.7 copy-done.3
  219.2 2.3 convert.27
  222.2 2.0 pad_maximum_fusion
  225.5 1.8 convolution_bitcast_fusion
  227.3 2.7 fusion.50
  230.0 72.0 %reduce-scatter.3.cloned.1.call-done = bf16[256,768]{0,1:T(8,128)(2,1)} async-done(((bf16[2048,768]{0,1:T(8,128)(2,1)}), bf16[256,768]{0,1:T(8,128)(2,1)}) %reduce-scatter.3.cloned.1.call-update) | async-done | bytes 393232 | tf_op jit(solution)/shard_map/reduce_scatter | solution.py:283
  305.9 1.5 fusion.40
  308.3 2.6 fusion.47
  310.9 4.1 collective-permute-done.3
  316.7 13.1 %concatenate.30 = f32[768,3266]{1,0:T(8,128)} concatenate(f32[768,1]{1,0:T(8,128)} %broadcast_in_dim.141, f32[768,1]{1,0:T(8,128)} %broadcast_in_dim.142, f32[768,1152]{1,0:T(8,128)} %fusion.47, f32[768,1152]{1,0:T(8,128)} %fusion.50, f32[768,384]{1,0:T(8,128)} %fusion.40, f32[768,576]{1,0:T(8,128)S(1)} %copy-done.19), dimensions={1} | concatenate | bytes 20066304 | tf_op jit(solution)/shard_map/concatenate | solution.py:322
  329.8 59.7 %reduce-scatter.5.cloned.1.call-done = f32[96,3266]{1,0:T(8,128)} async-done(((f32[768,3266]{1,0:T(8,128)}), f32[96,3266]{1,0:T(8,128)}) %reduce-scatter.5.cloned.1.call-update) | async-done | bytes 1254160 | tf_op jit(solution)/shard_map/reduce_scatter | solution.py:323
  390.8 95.4 %all-reduce.5.cloned.1.call-done = f32[96,3266]{1,0:T(8,128)} async-done(((f32[96,3266]{1,0:T(8,128)}), f32[96,3266]{1,0:T(8,128)}) %all-reduce.5.cloned.1.call-update) | async-done | bytes 1254160 | tf_op jit(solution)/shard_map/psum | solution.py:324
  486.1 1.5 fusion.53
  489.5 1.6 slice_reduce_fusion
  491.1 1.7 slice_bitcast_fusion.5
  492.8 1.8 slice_bitcast_fusion.4
  (259 shorter events, 39.1 us)
Async XLA Ops:
  7.2 32.4 %copy-start.12 = (bf16[256,768]{1,0:T(8,128)(2,1)S(1)}, bf16[256,768]{1,0:T(8,128)(2,1)}, u32[]{:S(2)}) copy-start(bf16[256,768]{1,0:T(8,128)(2,1)} %param.11) | copy-start | bytes 1179652
  7.2 29.7 %all-gather.4.cloned.1.call-start = ((), (), s32[]{:S(2)}) async-start(), calls=%async_computation.2 | async-start | bytes 1990656 | tf_op jit(solution)/shard_map/all_gather | solution.py:127
  7.9 98.1 %all-gather.6.cloned.1.call-start = ((), (), s32[]{:S(2)}) async-start(), calls=%async_computation.3 | async-start | bytes 3538944 | tf_op jit(solution)/shard_map/all_gather | solution.py:152
  30.9 9.4 %copy-start.56 = (f32[256]{0:T(256)}, f32[256]{0:T(256)S(1)}, u32[]{:S(2)}) copy-start(f32[256]{0:T(256)S(1)} %add_rsqrt_fusion.1) | copy-start | bytes 3076
  31.1 9.3 %copy-start.45 = (f32[256,32]{0,1:T(8,128)}, f32[256,32]{0,1:T(8,128)S(1)}, u32[]{:S(2)}) copy-start(f32[256,32]{0,1:T(8,128)S(1)} %get-tuple-element.420) | copy-start | bytes 98308
  31.1 9.3 %copy-start.46 = (f32[256,32]{0,1:T(8,128)}, f32[256,32]{0,1:T(8,128)S(1)}, u32[]{:S(2)}) copy-start(f32[256,32]{0,1:T(8,128)S(1)} %get-tuple-element.421) | copy-start | bytes 98308
  40.7 67.5 %copy-start.39 = (bf16[256,6,32]{0,2,1:T(8,128)(2,1)}, bf16[256,6,32]{0,2,1:T(8,128)(2,1)S(1)}, u32[]{:S(2)}) copy-start(bf16[256,6,32]{0,2,1:T(8,128)(2,1)S(1)} %get-tuple-element.412) | copy-start | bytes 294916
  40.7 67.5 %copy-start.41 = (bf16[256,6,32]{0,2,1:T(8,128)(2,1)}, bf16[256,6,32]{0,2,1:T(8,128)(2,1)S(1)}, u32[]{:S(2)}) copy-start(bf16[256,6,32]{0,2,1:T(8,128)(2,1)S(1)} %get-tuple-element.413) | copy-start | bytes 294916
  41.6 94.3 %all-gather.8.cloned.1.call-start = ((), (), s32[]{:S(2)}) async-start(), calls=%async_computation.4 | async-start | bytes 2211840 | tf_op jit(solution)/shard_map/all_gather | solution.py:129
  42.4 259.7 %reduce-scatter.3.cloned.1.call-start = ((), (), s32[]{:S(2)}) async-start(), calls=%async_computation.5 | async-start | bytes 3538944 | tf_op jit(solution)/shard_map/reduce_scatter | solution.py:283
  56.1 61.7 %copy-start.23 = (bf16[384,768]{0,1:T(8,128)(2,1)}, bf16[384,768]{0,1:T(8,128)(2,1)S(1)}, u32[]{:S(2)}) copy-start(bf16[384,768]{0,1:T(8,128)(2,1)S(1)} %all_gather.24) | copy-start | bytes 1769476
  108.2 6.5 %copy-start.11 = (bf16[2048,384]{0,1:T(8,128)(2,1)}, bf16[2048,384]{0,1:T(8,128)(2,1)S(1)}, u32[]{:S(2)}) copy-start(bf16[2048,384]{0,1:T(8,128)(2,1)S(1)} %get-tuple-element.512) | copy-start | bytes 4718596
  114.7 4.2 copy-start.67
  114.7 4.1 copy-start.52
  117.8 22.1 %copy-start.32 = (bf16[6,64,256]{2,1,0:T(8,128)(2,1)}, bf16[6,64,256]{2,1,0:T(8,128)(2,1)S(1)}, u32[]{:S(2)}) copy-start(bf16[6,64,256]{2,1,0:T(8,128)(2,1)S(1)} %fusion.13) | copy-start | bytes 589828
  118.2 21.7 %collective-permute-start = (f32[256,768]{1,0:T(8,128)S(1)}, f32[256,768]{1,0:T(8,128)}, u32[]{:S(2)}, u32[]{:S(2)}) collective-permute-start(f32[256,768]{1,0:T(8,128)S(1)} %fusion.55), channel_id=1, source_target_pairs={{0,8},{8,0},{1,9},{9,1},{2,10},{10,2},{3,11},{11,3},{4,12},{12,4},... | collective-permute-start | bytes 2359304 | tf_op jit(solution)/shard_map/ppermute | solution.py:72
  141.3 32.1 %copy-start.9 = (f32[256,768]{1,0:T(8,128)}, f32[256,768]{1,0:T(8,128)S(1)}, u32[]{:S(2)}) copy-start(f32[256,768]{1,0:T(8,128)S(1)} %get-tuple-element.395) | copy-start | bytes 2359300
  141.4 24.3 %copy-start.54 = (f32[256]{0:T(256)}, f32[256]{0:T(256)S(1)}, u32[]{:S(2)}) copy-start(f32[256]{0:T(256)S(1)} %broadcast_multiply_fusion.4) | copy-start | bytes 3076
  141.6 24.0 %copy-start.58 = (f32[256]{0:T(256)}, f32[256]{0:T(256)S(1)}, u32[]{:S(2)}) copy-start(f32[256]{0:T(256)S(1)} %add_rsqrt_fusion) | copy-start | bytes 3076
  142.4 4.0 copy-start.68
  142.4 4.7 copy-start.40
  142.4 4.6 copy-start.42
  144.9 20.7 %collective-permute-start.2 = (f32[256,768]{1,0:T(8,128)}, f32[256,768]{1,0:T(8,128)}, u32[]{:S(2)}, u32[]{:S(2)}) collective-permute-start(f32[256,768]{1,0:T(8,128)} %convolution_bitcast_fusion.1), channel_id=1, source_target_pairs={{0,8},{8,0},{1,9},{9,1},{2,10},{10,2},{3,11},{11,3},{4,12},{12,4},... | collective-permute-start | bytes 2359304 | tf_op jit(solution)/shard_map/ppermute | solution.py:72
  147.1 26.3 %copy-start.37 = (bf16[256,768]{1,0:T(8,128)(2,1)S(1)}, bf16[256,768]{1,0:T(8,128)(2,1)}, u32[]{:S(2)}) copy-start(bf16[256,768]{1,0:T(8,128)(2,1)} %param.19) | copy-start | bytes 1179652
  148.5 24.9 %copy-start.29 = (bf16[256,576]{0,1:T(8,128)(2,1)}, bf16[256,576]{0,1:T(8,128)(2,1)S(1)}, u32[]{:S(2)}) copy-start(bf16[256,576]{0,1:T(8,128)(2,1)S(1)} %multiply_convert_fusion.1) | copy-start | bytes 884740
  150.4 24.8 %copy-start.24 = (bf16[384,768]{0,1:T(8,128)(2,1)S(1)}, bf16[384,768]{0,1:T(8,128)(2,1)}, u32[]{:S(2)}) copy-start(bf16[384,768]{0,1:T(8,128)(2,1)} %copy-done.23) | copy-start | bytes 1769476
  150.4 23.0 %collective-permute-start.1 = (bf16[256,768]{1,0:T(8,128)(2,1)S(1)}, bf16[256,768]{1,0:T(8,128)(2,1)S(1)}, u32[]{:S(2)}, u32[]{:S(2)}) collective-permute-start(bf16[256,768]{1,0:T(8,128)(2,1)S(1)} %convolution_convert_fusion.1), channel_id=1, source_target_pairs={{0,8},{8,0},{1,9},{9,1},{2,10},{10,2},{3,11},{11,3},{4,12},{12,4},... | collective-permute-start | bytes 1179656 | tf_op jit(solution)/shard_map/ppermute | solution.py:72
  168.0 7.7 %copy-start.33 = (bf16[6,64,256]{2,1,0:T(8,128)(2,1)S(1)}, bf16[6,64,256]{2,1,0:T(8,128)(2,1)}, u32[]{:S(2)}) copy-start(bf16[6,64,256]{2,1,0:T(8,128)(2,1)} %copy-done.32) | copy-start | bytes 589828
  175.2 5.4 %copy-start.17 = (f32[256,768]{1,0:T(8,128)}, f32[256,768]{1,0:T(8,128)S(1)}, u32[]{:S(2)}) copy-start(f32[256,768]{1,0:T(8,128)S(1)} %get-tuple-element.406) | copy-start | bytes 2359300
  176.4 4.2 copy-start.61
  182.0 5.5 %copy-start.1 = (f32[6,1024,256]{2,1,0:T(8,128)}, f32[6,1024,256]{2,1,0:T(8,128)S(1)}, u32[]{:S(2)}) copy-start(f32[6,1024,256]{2,1,0:T(8,128)S(1)} %fusion.107) | copy-start | bytes 18874372 | tf_op jit(solution)/shard_map/while
  182.3 5.2 %copy-start.21 = (pred[256,1024]{0,1:T(8,128)(4,1)}, pred[256,1024]{0,1:T(8,128)(4,1)S(1)}, u32[]{:S(2)}) copy-start(pred[256,1024]{0,1:T(8,128)(4,1)S(1)} %broadcast_compare_fusion.3) | copy-start | bytes 786436 | tf_op jit(solution)/shard_map/while
  190.1 5.4 %copy-start.5 = (f32[2048,384]{0,1:T(8,128)S(1)}, f32[2048,384]{0,1:T(8,128)}, u32[]{:S(2)}) copy-start(f32[2048,384]{0,1:T(8,128)} %get-tuple-element.522) | copy-start | bytes 9437188 | tf_op jit(solution)/shard_map/while
  196.3 3.5 copy-start.62
  201.3 5.5 %copy-start.1 = (f32[6,1024,256]{2,1,0:T(8,128)}, f32[6,1024,256]{2,1,0:T(8,128)S(1)}, u32[]{:S(2)}) copy-start(f32[6,1024,256]{2,1,0:T(8,128)S(1)} %fusion.107) | copy-start | bytes 18874372 | tf_op jit(solution)/shard_map/while
  201.6 5.2 %copy-start.21 = (pred[256,1024]{0,1:T(8,128)(4,1)}, pred[256,1024]{0,1:T(8,128)(4,1)S(1)}, u32[]{:S(2)}) copy-start(pred[256,1024]{0,1:T(8,128)(4,1)S(1)} %broadcast_compare_fusion.3) | copy-start | bytes 786436 | tf_op jit(solution)/shard_map/while
  209.4 5.4 %copy-start.5 = (f32[2048,384]{0,1:T(8,128)S(1)}, f32[2048,384]{0,1:T(8,128)}, u32[]{:S(2)}) copy-start(f32[2048,384]{0,1:T(8,128)} %get-tuple-element.522) | copy-start | bytes 9437188 | tf_op jit(solution)/shard_map/while
  224.3 165.2 %reduce-scatter.5.cloned.1.call-start = ((), (), s32[]{:S(2)}) async-start(), calls=%async_computation.6 | async-start | bytes 11501568 | tf_op jit(solution)/shard_map/reduce_scatter | solution.py:323
  227.3 75.7 %copy-start.16 = (f32[256,6,64]{0,2,1:T(8,128)S(1)}, f32[256,6,64]{0,2,1:T(8,128)}, u32[]{:S(2)}) copy-start(f32[256,6,64]{0,2,1:T(8,128)} %get-tuple-element.581) | copy-start | bytes 1179652
  230.0 74.2 %copy-start.15 = (bf16[768,3,384]{0,2,1:T(8,128)(2,1)S(1)}, bf16[768,3,384]{0,2,1:T(8,128)(2,1)}, u32[]{:S(2)}) copy-start(bf16[768,3,384]{0,2,1:T(8,128)(2,1)} %copy-done.14) | copy-start | bytes 5308420
  304.1 4.2 copy-start.13
  304.1 4.1 copy-start.57
  304.9 10.1 %copy-start.27 = (bf16[256,768]{1,0:T(8,128)(2,1)}, bf16[256,768]{1,0:T(8,128)(2,1)S(1)}, u32[]{:S(2)}) copy-start(bf16[256,768]{1,0:T(8,128)(2,1)S(1)} %convolution_convert_fusion) | copy-start | bytes 1179652
  305.0 10.0 %collective-permute-start.3 = (bf16[256,768]{1,0:T(8,128)(2,1)S(1)}, bf16[256,768]{1,0:T(8,128)(2,1)S(1)}, u32[]{:S(2)}, u32[]{:S(2)}) collective-permute-start(bf16[256,768]{1,0:T(8,128)(2,1)S(1)} %convolution_convert_fusion), channel_id=1, source_target_pairs={{0,8},{8,0},{1,9},{9,1},{2,10},{10,2},{3,11},{11,3},{4,12},{12,4},... | collective-permute-start | bytes 1179656 | tf_op jit(solution)/shard_map/ppermute | solution.py:72
  308.3 8.4 %copy-start.19 = (f32[768,576]{1,0:T(8,128)S(1)}, f32[768,576]{1,0:T(8,128)}, u32[]{:S(2)}) copy-start(f32[768,576]{1,0:T(8,128)} %convolution_bitcast_fusion) | copy-start | bytes 5308420
  329.7 59.8 %copy-start.28 = (bf16[256,768]{1,0:T(8,128)(2,1)S(1)}, bf16[256,768]{1,0:T(8,128)(2,1)}, u32[]{:S(2)}) copy-start(bf16[256,768]{1,0:T(8,128)(2,1)} %copy-done.27) | copy-start | bytes 1179652
  329.8 59.8 %copy-start.35 = (bf16[256,768]{1,0:T(8,128)(2,1)S(1)}, bf16[256,768]{1,0:T(8,128)(2,1)}, u32[]{:S(2)}) copy-start(bf16[256,768]{1,0:T(8,128)(2,1)} %copy-done.34) | copy-start | bytes 1179652
  329.8 156.4 %all-reduce.5.cloned.1.call-start = ((), (), s32[]{:S(2)}) async-start(), calls=%async_computation.7 | async-start | bytes 2555904 | tf_op jit(solution)/shard_map/psum | solution.py:324
  (48 other events, 110.1 us)
Sparse Core Ops, SparseCore 0:
  9.7 27.1 all-gather.3
  41.7 64.3 all-gather.5
  108.3 23.7 all-gather.7
  224.4 77.5 reduce-scatter.2
  329.9 59.5 reduce-scatter.4
  391.9 94.2 all-reduce.4

commit v3 on v2

--- a/solution.py
+++ b/solution.py
@@ -319,9 +319,9 @@
         down_grad_t,
     )
     widths = [g.shape[1] for g in grads]
-    packed = jnp.concatenate(grads, axis=1)
+    packed = jnp.concatenate(grads, axis=1).astype(jnp.bfloat16)
     packed = lax.psum_scatter(packed, "fsdp", scatter_dimension=0, tiled=True)
-    packed = lax.psum(packed, "context")
+    packed = lax.psum(packed, "context").astype(jnp.float32)
     pieces = []
     start = 0
     for width in widths:

time: 503 us -> 467 us (0.928)
  waiting for transfers between devices: 308 us -> 281 us
  local copies, waits for them, and re-layouts: 54.9 us -> 48.9 us
    reduce_scatter x1, waiting for transfers between devices: 59.7 us -> 38.2 us  [on_device(): packed = lax.psum_scatter(packed, 'fsdp', scatter_dimension=0, tiled=True)]
    psum x1, waiting for transfers between devices: 95.4 us -> 88.1 us  [on_device(): packed = lax.psum(packed, 'context').astype(jnp.float32)]
where the time goes in v3:
time: 467 us; the launch traced here: 466 us
  waiting for transfers between devices  281 us (60%)
  local copies, waits for them, and re-layouts  48.9 us (10%)
  blocking collectives  45.4 us (10%)
  matrix products  41.8 us (9%)
  other arithmetic  29.7 us (6%)
  between operations  15.6 us (3%)
    psum x1, waiting for transfers between devices, on_device(): packed = lax.psum(packed, 'context').astype(jnp.float32)  88.1 us
    reduce_scatter x1, waiting for transfers between devices, on_device(): lax.psum_scatter(jnp.concatenate([back_result[1], back_result[2]], axis=1...  71.9 us
    all_gather x1, waiting for transfers between devices, on_device(): lax.all_gather(jnp.concatenate([key_flat, value_flat], axis=1), 'context'...  50 us
    reduce_scatter x1, waiting for transfers between devices, on_device(): packed = lax.psum_scatter(packed, 'fsdp', scatter_dimension=0, tiled=True)  38.2 us
    ppermute x4, waiting for transfers between devices, pair_sum(): other = lax.ppermute(values, axis_name, perm=[(0, 1), (1, 0)])  26.1 us
    all_gather x1, blocking collectives, on_device(): lax.all_gather(down_weight, 'fsdp', axis=1, tiled=True)  17 us
    unnamed x1, blocking collectives  15.3 us
    all_gather x1, blocking collectives, on_device(): lax.all_gather(proj_weight, 'fsdp', axis=1, tiled=True)  13.2 us
  transfers between devices with their start and end apart: 10, of which 8 were waited for; matrix products, arithmetic and copies ran while one was open for 8% of the time, Pallas kernels for 0%

profile of v3, /device:TPU:0, one launch (start us, length us, event | category | flops | bytes accessed | tf_op | source)
XLA Modules:
  0.0 466.3 jit_solution(8159661553496569473)
XLA Ops:
  8.0 1.2 dynamic-slice
  11.6 15.3 %all-reduce.2 = (bf16[768]{0:T(1024)(128)(2,1)S(1)}, bf16[768]{0:T(1024)(128)(2,1)}) all-reduce(bf16[768]{0:T(1024)(128)(2,1)S(1)} %dynamic-update-slice, bf16[768]{0:T(1024)(128)(2,1)S(1)} %dynamic-update-slice.1), channel_id=1, replica_groups=mesh['fsdp'=8,'tensor'=2,'context'=8] {'fsdp'}, use_global_device_ids=true, to_apply=%add | all-reduce | flops 1536 | bytes 6144
  29.7 1.2 fusion.28
  31.1 5.8 %all-gather.4.cloned.1.call-done = bf16[768,3,384]{2,0,1:T(8,128)(2,1)} async-done(((bf16[96,3,384]{2,0,1:T(8,128)(2,1)}), bf16[768,3,384]{2,0,1:T(8,128)(2,1)}) %all-gather.4.cloned.1.call-update) | async-done | bytes 1769488 | tf_op jit(solution)/shard_map/all_gather | solution.py:127
  36.9 2.6 copy.64
  42.9 13.2 %all_gather.24 = bf16[384,768]{0,1:T(8,128)(2,1)S(1)} all-gather(bf16[384,96]{0,1:T(8,128)(2,1)S(1)} %copy-done.55), channel_id=1, replica_groups=mesh['fsdp'=8,'tensor'=2,'context'=8] {'fsdp'}, dimensions={1}, use_global_device_ids=true | all-gather | bytes 663552 | tf_op jit(solution)/shard_map/all_gather | solution.py:128
  56.1 50.0 %all-gather.6.cloned.1.call-done = bf16[2048,768]{0,1:T(8,128)(2,1)} async-done(((bf16[256,768]{0,1:T(8,128)(2,1)}), bf16[2048,768]{0,1:T(8,128)(2,1)}) %all-gather.6.cloned.1.call-update) | async-done | bytes 3145744 | tf_op jit(solution)/shard_map/all_gather | solution.py:152
  106.0 2.2 fusion.50
  108.2 2.5 select_reduce_fusion.1
  110.7 4.0 select_reduce_fusion
  114.7 3.0 fusion.14
  118.9 17.0 %all_gather.27 = bf16[576,768]{0,1:T(8,128)(2,1)} all-gather(bf16[576,96]{0,1:T(8,128)(2,1)S(1)} %copy-done.54), channel_id=1, replica_groups=mesh['fsdp'=8,'tensor'=2,'context'=8] {'fsdp'}, dimensions={1}, use_global_device_ids=true | all-gather | bytes 995328 | tf_op jit(solution)/shard_map/all_gather | solution.py:130
  135.8 3.9 copy.66
  139.8 1.5 fusion.49
  143.2 1.6 convolution_bitcast_fusion
  144.8 1.5 collective-permute-start.2
  147.0 1.4 multiply_convert_fusion.1
  148.5 1.8 convolution_convert_fusion.5
  151.0 14.6 %collective-permute-done.2 = f32[256,768]{1,0:T(8,128)} collective-permute-done((f32[256,768]{1,0:T(8,128)}, f32[256,768]{1,0:T(8,128)}, u32[]{:S(2)}, u32[]{:S(2)}) %collective-permute-start.2) | collective-permute-done | bytes 786464 | tf_op jit(solution)/shard_map/ppermute | solution.py:72
  165.6 2.4 multiply_reduce_fusion
  167.9 5.4 %collective-permute-done.1 = bf16[256,768]{1,0:T(8,128)(2,1)S(1)} collective-permute-done((bf16[256,768]{1,0:T(8,128)(2,1)S(1)}, bf16[256,768]{1,0:T(8,128)(2,1)S(1)}, u32[]{:S(2)}, u32[]{:S(2)}) %collective-permute-start.1) | collective-permute-done | bytes 393248 | tf_op jit(solution)/shard_map/ppermute | solution.py:72
  173.3 1.7 multiply_add_fusion
  176.3 2.1 broadcast.211
  178.4 2.1 broadcast.211.clone
  180.4 38.6 %while.20 = (s32[]{:T(128)}, f32[256,6,64]{0,2,1:T(8,128)}, f32[2048,384]{0,1:T(8,128)}, f32[2048,384]{0,1:T(8,128)}, bf16[2048,384]{0,1:T(8,128)(2,1)S(1)}, /*i...) while((s32[]{:T(128)}, f32[256,6,64]{0,2,1:T(8,128)}, ...), condition=%wide.region_16.17_spmd.clone, body=%wide.region_14.16_spmd.clone.sunk | while | flops 1024107520 | bytes 143691344 | solution.py:93
  182.3 1.8 constant_dynamic-slice_fusion.5
  184.1 3.3 fusion.106
  187.4 2.6 fusion.107
  190.0 4.3 fusion.108
  197.1 1.7 copy-done.3
  201.5 1.8 constant_dynamic-slice_fusion.5
  203.3 3.3 fusion.106
  206.7 2.7 fusion.107
  209.3 4.3 fusion.108
  216.4 1.7 copy-done.3
  219.0 2.3 convert.48
  222.1 2.0 pad_maximum_fusion
  225.6 1.3 copy.71
  228.0 2.1 convolution_convert_fusion
  230.1 71.9 %reduce-scatter.3.cloned.1.call-done = bf16[256,768]{0,1:T(8,128)(2,1)} async-done(((bf16[2048,768]{0,1:T(8,128)(2,1)}), bf16[256,768]{0,1:T(8,128)(2,1)}) %reduce-scatter.3.cloned.1.call-update) | async-done | bytes 393232 | tf_op jit(solution)/shard_map/reduce_scatter | solution.py:283
  304.9 1.2 convolution_convert_fusion.3
  307.9 6.1 %collective-permute-done.3 = bf16[256,768]{1,0:T(8,128)(2,1)S(1)} collective-permute-done((bf16[256,768]{1,0:T(8,128)(2,1)S(1)}, bf16[256,768]{1,0:T(8,128)(2,1)S(1)}, u32[]{:S(2)}, u32[]{:S(2)}) %collective-permute-start.3) | collective-permute-done | bytes 393248 | tf_op jit(solution)/shard_map/ppermute | solution.py:72
  316.6 9.5 %concatenate.31 = bf16[768,3266]{1,0:T(8,128)(2,1)} concatenate(bf16[768,1]{1,0:T(8,128)(2,1)} %broadcast_in_dim.143, bf16[768,1]{1,0:T(8,128)(2,1)} %broadcast_in_dim.144, bf16[768,1152]{1,0:T(8,128)(2,1)S(1)} %convolution_convert_fusion.1, bf16[768,1152]{1,0:T(8,128)(2,1)} %convolution_convert_fusion, bf16[768,384]{1,0:T(8,128)(2,1)} %convolution_convert_fusion.3, ...), dimensions={1} | concatenate | bytes 10033152 | tf_op jit(solution)/shard_map/concatenate | solution.py:322
  326.3 38.2 %reduce-scatter.5.cloned.1.call-done = bf16[96,3266]{1,0:T(8,128)(2,1)} async-done(((bf16[768,3266]{1,0:T(8,128)(2,1)}), bf16[96,3266]{1,0:T(8,128)(2,1)}) %reduce-scatter.5.cloned.1.call-update) | async-done | bytes 627088 | tf_op jit(solution)/shard_map/reduce_scatter | solution.py:323
  364.5 1.2 fusion.26
  365.8 88.1 %all-reduce.5.cloned.1.call-done = bf16[96,3266]{1,0:T(8,128)(2,1)} async-done(((bf16[96,3266]{1,0:T(8,128)(2,1)}), bf16[96,3266]{1,0:T(8,128)(2,1)}) %all-reduce.5.cloned.1.call-update) | async-done | bytes 627088 | tf_op jit(solution)/shard_map/psum | solution.py:324
  453.8 1.2 convert_element_type.174
  458.3 1.1 reshape.302
  (257 shorter events, 38.9 us)
Async XLA Ops:
  7.2 32.4 %copy-start.12 = (bf16[256,768]{1,0:T(8,128)(2,1)S(1)}, bf16[256,768]{1,0:T(8,128)(2,1)}, u32[]{:S(2)}) copy-start(bf16[256,768]{1,0:T(8,128)(2,1)} %param.11) | copy-start | bytes 1179652
  7.2 29.7 %all-gather.4.cloned.1.call-start = ((), (), s32[]{:S(2)}) async-start(), calls=%async_computation.2 | async-start | bytes 1990656 | tf_op jit(solution)/shard_map/all_gather | solution.py:127
  7.9 98.1 %all-gather.6.cloned.1.call-start = ((), (), s32[]{:S(2)}) async-start(), calls=%async_computation.3 | async-start | bytes 3538944 | tf_op jit(solution)/shard_map/all_gather | solution.py:152
  30.9 9.4 %copy-start.58 = (f32[256]{0:T(256)}, f32[256]{0:T(256)S(1)}, u32[]{:S(2)}) copy-start(f32[256]{0:T(256)S(1)} %add_rsqrt_fusion.1) | copy-start | bytes 3076
  31.1 9.3 %copy-start.46 = (f32[256,32]{0,1:T(8,128)}, f32[256,32]{0,1:T(8,128)S(1)}, u32[]{:S(2)}) copy-start(f32[256,32]{0,1:T(8,128)S(1)} %get-tuple-element.428) | copy-start | bytes 98308
  31.1 9.3 %copy-start.48 = (f32[256,32]{0,1:T(8,128)}, f32[256,32]{0,1:T(8,128)S(1)}, u32[]{:S(2)}) copy-start(f32[256,32]{0,1:T(8,128)S(1)} %get-tuple-element.429) | copy-start | bytes 98308
  40.7 67.5 %copy-start.40 = (bf16[256,6,32]{0,2,1:T(8,128)(2,1)}, bf16[256,6,32]{0,2,1:T(8,128)(2,1)S(1)}, u32[]{:S(2)}) copy-start(bf16[256,6,32]{0,2,1:T(8,128)(2,1)S(1)} %get-tuple-element.420) | copy-start | bytes 294916
  40.7 67.5 %copy-start.42 = (bf16[256,6,32]{0,2,1:T(8,128)(2,1)}, bf16[256,6,32]{0,2,1:T(8,128)(2,1)S(1)}, u32[]{:S(2)}) copy-start(bf16[256,6,32]{0,2,1:T(8,128)(2,1)S(1)} %get-tuple-element.421) | copy-start | bytes 294916
  41.6 94.3 %all-gather.8.cloned.1.call-start = ((), (), s32[]{:S(2)}) async-start(), calls=%async_computation.4 | async-start | bytes 2211840 | tf_op jit(solution)/shard_map/all_gather | solution.py:129
  42.4 259.6 %reduce-scatter.3.cloned.1.call-start = ((), (), s32[]{:S(2)}) async-start(), calls=%async_computation.5 | async-start | bytes 3538944 | tf_op jit(solution)/shard_map/reduce_scatter | solution.py:283
  56.1 61.7 %copy-start.23 = (bf16[384,768]{0,1:T(8,128)(2,1)}, bf16[384,768]{0,1:T(8,128)(2,1)S(1)}, u32[]{:S(2)}) copy-start(bf16[384,768]{0,1:T(8,128)(2,1)S(1)} %all_gather.24) | copy-start | bytes 1769476
  108.2 6.5 %copy-start.11 = (bf16[2048,384]{0,1:T(8,128)(2,1)}, bf16[2048,384]{0,1:T(8,128)(2,1)S(1)}, u32[]{:S(2)}) copy-start(bf16[2048,384]{0,1:T(8,128)(2,1)S(1)} %get-tuple-element.520) | copy-start | bytes 4718596
  114.7 4.2 copy-start.69
  117.8 22.0 %copy-start.32 = (bf16[6,64,256]{2,1,0:T(8,128)(2,1)}, bf16[6,64,256]{2,1,0:T(8,128)(2,1)S(1)}, u32[]{:S(2)}) copy-start(bf16[6,64,256]{2,1,0:T(8,128)(2,1)S(1)} %fusion.14) | copy-start | bytes 589828
  118.2 21.6 %collective-permute-start = (f32[256,768]{1,0:T(8,128)S(1)}, f32[256,768]{1,0:T(8,128)}, u32[]{:S(2)}, u32[]{:S(2)}) collective-permute-start(f32[256,768]{1,0:T(8,128)S(1)} %fusion.53), channel_id=1, source_target_pairs={{0,8},{8,0},{1,9},{9,1},{2,10},{10,2},{3,11},{11,3},{4,12},{12,4},... | collective-permute-start | bytes 2359304 | tf_op jit(solution)/shard_map/ppermute | solution.py:72
  141.3 32.1 %copy-start.9 = (f32[256,768]{1,0:T(8,128)}, f32[256,768]{1,0:T(8,128)S(1)}, u32[]{:S(2)}) copy-start(f32[256,768]{1,0:T(8,128)S(1)} %get-tuple-element.403) | copy-start | bytes 2359300
  141.3 24.3 %copy-start.56 = (f32[256]{0:T(256)}, f32[256]{0:T(256)S(1)}, u32[]{:S(2)}) copy-start(f32[256]{0:T(256)S(1)} %broadcast_multiply_fusion.4) | copy-start | bytes 3076
  141.5 24.0 %copy-start.60 = (f32[256]{0:T(256)}, f32[256]{0:T(256)S(1)}, u32[]{:S(2)}) copy-start(f32[256]{0:T(256)S(1)} %add_rsqrt_fusion) | copy-start | bytes 3076
  142.3 4.7 copy-start.41
  142.3 4.6 copy-start.43
  144.8 20.7 %collective-permute-start.2 = (f32[256,768]{1,0:T(8,128)}, f32[256,768]{1,0:T(8,128)}, u32[]{:S(2)}, u32[]{:S(2)}) collective-permute-start(f32[256,768]{1,0:T(8,128)} %convolution_bitcast_fusion), channel_id=1, source_target_pairs={{0,8},{8,0},{1,9},{9,1},{2,10},{10,2},{3,11},{11,3},{4,12},{12,4},... | collective-permute-start | bytes 2359304 | tf_op jit(solution)/shard_map/ppermute | solution.py:72
  147.0 26.3 %copy-start.38 = (bf16[256,768]{1,0:T(8,128)(2,1)S(1)}, bf16[256,768]{1,0:T(8,128)(2,1)}, u32[]{:S(2)}) copy-start(bf16[256,768]{1,0:T(8,128)(2,1)} %param.19) | copy-start | bytes 1179652
  148.5 24.9 %copy-start.29 = (bf16[256,576]{0,1:T(8,128)(2,1)}, bf16[256,576]{0,1:T(8,128)(2,1)S(1)}, u32[]{:S(2)}) copy-start(bf16[256,576]{0,1:T(8,128)(2,1)S(1)} %multiply_convert_fusion.1) | copy-start | bytes 884740
  150.3 24.8 %copy-start.24 = (bf16[384,768]{0,1:T(8,128)(2,1)S(1)}, bf16[384,768]{0,1:T(8,128)(2,1)}, u32[]{:S(2)}) copy-start(bf16[384,768]{0,1:T(8,128)(2,1)} %copy-done.23) | copy-start | bytes 1769476
  150.3 23.0 %collective-permute-start.1 = (bf16[256,768]{1,0:T(8,128)(2,1)S(1)}, bf16[256,768]{1,0:T(8,128)(2,1)S(1)}, u32[]{:S(2)}, u32[]{:S(2)}) collective-permute-start(bf16[256,768]{1,0:T(8,128)(2,1)S(1)} %convolution_convert_fusion.5), channel_id=1, source_target_pairs={{0,8},{8,0},{1,9},{9,1},{2,10},{10,2},{3,11},{11,3},{4,12},{12,4},... | collective-permute-start | bytes 1179656 | tf_op jit(solution)/shard_map/ppermute | solution.py:72
  167.9 7.7 %copy-start.33 = (bf16[6,64,256]{2,1,0:T(8,128)(2,1)S(1)}, bf16[6,64,256]{2,1,0:T(8,128)(2,1)}, u32[]{:S(2)}) copy-start(bf16[6,64,256]{2,1,0:T(8,128)(2,1)} %copy-done.32) | copy-start | bytes 589828
  175.1 5.4 %copy-start.17 = (f32[256,768]{1,0:T(8,128)}, f32[256,768]{1,0:T(8,128)S(1)}, u32[]{:S(2)}) copy-start(f32[256,768]{1,0:T(8,128)S(1)} %get-tuple-element.412) | copy-start | bytes 2359300
  176.3 4.2 copy-start.62
  176.3 4.2 copy-start.64
  176.3 4.2 copy-start.65
  182.0 5.4 %copy-start.1 = (f32[6,1024,256]{2,1,0:T(8,128)}, f32[6,1024,256]{2,1,0:T(8,128)S(1)}, u32[]{:S(2)}) copy-start(f32[6,1024,256]{2,1,0:T(8,128)S(1)} %fusion.105) | copy-start | bytes 18874372 | tf_op jit(solution)/shard_map/while
  182.3 5.1 %copy-start.21 = (pred[256,1024]{0,1:T(8,128)(4,1)}, pred[256,1024]{0,1:T(8,128)(4,1)S(1)}, u32[]{:S(2)}) copy-start(pred[256,1024]{0,1:T(8,128)(4,1)S(1)} %broadcast_compare_fusion.3) | copy-start | bytes 786436 | tf_op jit(solution)/shard_map/while
  190.0 5.4 %copy-start.5 = (f32[2048,384]{0,1:T(8,128)S(1)}, f32[2048,384]{0,1:T(8,128)}, u32[]{:S(2)}) copy-start(f32[2048,384]{0,1:T(8,128)} %get-tuple-element.530) | copy-start | bytes 9437188 | tf_op jit(solution)/shard_map/while
  201.2 5.4 %copy-start.1 = (f32[6,1024,256]{2,1,0:T(8,128)}, f32[6,1024,256]{2,1,0:T(8,128)S(1)}, u32[]{:S(2)}) copy-start(f32[6,1024,256]{2,1,0:T(8,128)S(1)} %fusion.105) | copy-start | bytes 18874372 | tf_op jit(solution)/shard_map/while
  201.5 5.1 %copy-start.21 = (pred[256,1024]{0,1:T(8,128)(4,1)}, pred[256,1024]{0,1:T(8,128)(4,1)S(1)}, u32[]{:S(2)}) copy-start(pred[256,1024]{0,1:T(8,128)(4,1)S(1)} %broadcast_compare_fusion.3) | copy-start | bytes 786436 | tf_op jit(solution)/shard_map/while
  209.3 5.4 %copy-start.5 = (f32[2048,384]{0,1:T(8,128)S(1)}, f32[2048,384]{0,1:T(8,128)}, u32[]{:S(2)}) copy-start(f32[2048,384]{0,1:T(8,128)} %get-tuple-element.530) | copy-start | bytes 9437188 | tf_op jit(solution)/shard_map/while
  224.2 140.3 %reduce-scatter.5.cloned.1.call-start = ((), (), s32[]{:S(2)}) async-start(), calls=%async_computation.6 | async-start | bytes 5750784 | tf_op jit(solution)/shard_map/reduce_scatter | solution.py:323
  225.6 77.4 %copy-start.16 = (f32[256,6,64]{0,2,1:T(8,128)S(1)}, f32[256,6,64]{0,2,1:T(8,128)}, u32[]{:S(2)}) copy-start(f32[256,6,64]{0,2,1:T(8,128)} %get-tuple-element.285) | copy-start | bytes 1179652
  225.6 77.4 %copy-start.47 = (f32[256,32]{0,1:T(8,128)S(1)}, f32[256,32]{0,1:T(8,128)}, u32[]{:S(2)}) copy-start(f32[256,32]{0,1:T(8,128)} %copy-done.46) | copy-start | bytes 98308
  225.6 77.4 %copy-start.49 = (f32[256,32]{0,1:T(8,128)S(1)}, f32[256,32]{0,1:T(8,128)}, u32[]{:S(2)}) copy-start(f32[256,32]{0,1:T(8,128)} %copy-done.48) | copy-start | bytes 98308
  228.0 75.3 %copy-start.15 = (bf16[768,3,384]{0,2,1:T(8,128)(2,1)S(1)}, bf16[768,3,384]{0,2,1:T(8,128)(2,1)}, u32[]{:S(2)}) copy-start(bf16[768,3,384]{0,2,1:T(8,128)(2,1)} %copy-done.14) | copy-start | bytes 5308420
  304.0 12.6 %copy-start.27 = (bf16[768,576]{1,0:T(8,128)(2,1)S(1)}, bf16[768,576]{1,0:T(8,128)(2,1)}, u32[]{:S(2)}) copy-start(bf16[768,576]{1,0:T(8,128)(2,1)} %copy.71) | copy-start | bytes 2654212
  304.0 10.0 %collective-permute-start.3 = (bf16[256,768]{1,0:T(8,128)(2,1)S(1)}, bf16[256,768]{1,0:T(8,128)(2,1)S(1)}, u32[]{:S(2)}, u32[]{:S(2)}) collective-permute-start(bf16[256,768]{1,0:T(8,128)(2,1)S(1)} %convolution_convert_fusion.4), channel_id=1, source_target_pairs={{0,8},{8,0},{1,9},{9,1},{2,10},{10,2},{3,11},{11,3},{4,12},{12,4},... | collective-permute-start | bytes 1179656 | tf_op jit(solution)/shard_map/ppermute | solution.py:72
  326.2 38.3 %copy-start.68 = (f32[256]{0:T(256)S(1)}, f32[256]{0:T(256)}, u32[]{:S(2)}) copy-start(f32[256]{0:T(256)} %get-tuple-element.372) | copy-start | bytes 3076
  326.2 38.3 %copy-start.67 = (f32[256]{0:T(256)S(1)}, f32[256]{0:T(256)}, u32[]{:S(2)}) copy-start(f32[256]{0:T(256)} %get-tuple-element.373) | copy-start | bytes 3076
  326.2 38.3 %copy-start.19 = (f32[256,768]{1,0:T(8,128)S(1)}, f32[256,768]{1,0:T(8,128)}, u32[]{:S(2)}) copy-start(f32[256,768]{1,0:T(8,128)} %copy-done.17) | copy-start | bytes 2359300
  326.2 38.3 %copy-start.36 = (bf16[256,768]{1,0:T(8,128)(2,1)S(1)}, bf16[256,768]{1,0:T(8,128)(2,1)}, u32[]{:S(2)}) copy-start(bf16[256,768]{1,0:T(8,128)(2,1)} %copy-done.35) | copy-start | bytes 1179652
  326.2 127.6 %all-reduce.5.cloned.1.call-start = ((), (), s32[]{:S(2)}) async-start(), calls=%async_computation.7 | async-start | bytes 1277952 | tf_op jit(solution)/shard_map/psum | solution.py:324
  (46 other events, 109.5 us)
Sparse Core Ops, SparseCore 0:
  9.7 27.1 all-gather.3
  41.7 64.3 all-gather.5
  108.3 23.7 all-gather.7
  224.3 77.6 reduce-scatter.2
  326.3 38.0 reduce-scatter.4
  367.0 86.8 all-reduce.4

commit v4 on v3

--- a/solution.py
+++ b/solution.py
@@ -71,6 +71,22 @@
         return lax.psum(values, axis_name)
     other = lax.ppermute(values, axis_name, perm=[(0, 1), (1, 0)])
     return values.astype(jnp.float32) + other.astype(jnp.float32)
+
+
+def context_gather(values, axis_name):
+    count = lax.axis_size(axis_name)
+    spread = jnp.broadcast_to(values[None], (count,) + values.shape)
+    gathered = lax.all_to_all(spread, axis_name, 0, 0, tiled=True)
+    return gathered.reshape((count * values.shape[0],) + values.shape[1:])
+
+
+def context_scatter_sum(values, axis_name):
+    count = lax.axis_size(axis_name)
+    rows = values.shape[0] // count
+    parts = lax.all_to_all(
+        values.reshape((count, rows) + values.shape[1:]), axis_name, 0, 0, tiled=True
+    )
+    return jnp.sum(parts.astype(jnp.float32), axis=0)
 
 
 def split_count(row_count):
@@ -149,9 +165,7 @@
     value_bf = projected[:, 2].astype(jnp.bfloat16)
     key_flat = key_bf.reshape(row_count, local_width)
     value_flat = value_bf.reshape(row_count, local_width)
-    kv_group = lax.all_gather(
-        jnp.concatenate([key_flat, value_flat], axis=1), "context", axis=0, tiled=True
-    )
+    kv_group = context_gather(jnp.concatenate([key_flat, value_flat], axis=1), "context")
     keys_group, values_group = (kv_group[:, :local_width], kv_group[:, local_width:])
     keys_heads = keys_group.reshape(group_rows, head_count, HD)
     values_heads = values_group.reshape(group_rows, head_count, HD)
@@ -280,12 +294,9 @@
         jnp.int32(0),
     )
     query_grad = back_result[0]
-    kv_grad = lax.psum_scatter(
-        jnp.concatenate([back_result[1], back_result[2]], axis=1).astype(jnp.bfloat16),
-        "context",
-        scatter_dimension=0,
-        tiled=True,
-    ).astype(jnp.float32)
+    kv_grad = context_scatter_sum(
+        jnp.concatenate([back_result[1], back_result[2]], axis=1).astype(jnp.bfloat16), "context"
+    )
     key_grad, value_grad = (kv_grad[:, :local_width], kv_grad[:, local_width:])
     key_grad = key_grad.reshape(row_count, head_count, HD)
     value_grad = value_grad.reshape(row_count, head_count, HD)
@@ -321,7 +332,9 @@
     widths = [g.shape[1] for g in grads]
     packed = jnp.concatenate(grads, axis=1).astype(jnp.bfloat16)
     packed = lax.psum_scatter(packed, "fsdp", scatter_dimension=0, tiled=True)
-    packed = lax.psum(packed, "context").astype(jnp.float32)
+    packed = context_gather(
+        context_scatter_sum(packed, "context").astype(jnp.bfloat16), "context"
+    ).astype(jnp.float32)
     pieces = []
     start = 0
     for width in widths:

time: 467 us -> 415 us (0.89); the launches traced: 466 us -> 409 us
  waiting for transfers between devices: 281 us -> 139 us
  local copies, waits for them, and re-layouts: 48.9 us -> 93.9 us
  starting transfers between devices: 4 us -> 20.9 us
  blocking collectives: 45.4 us -> 61.8 us
  other arithmetic: 29.7 us -> 34.9 us
    psum x1 -> x0, waiting for transfers between devices: 88.1 us -> none  [on_device(): packed = lax.psum(packed, 'context').astype(jnp.float32)]
    reduce_scatter x1 -> x0, waiting for transfers between devices: 71.9 us -> none  [on_device(): lax.psum_scatter(jnp.concatenate([back_result[1], back_result[2]], axis=1...]
    all_to_all x0 -> x3, waiting for transfers between devices: none -> 69.1 us  [the longest x2 34.6 us: context_gather(): gathered = lax.all_to_all(spread, axis_name, 0, 0, tiled=True)]
    all_gather x1 -> x0, waiting for transfers between devices: 50 us -> none  [on_device(): lax.all_gather(jnp.concatenate([key_flat, value_flat], axis=1), 'context'...]
    dynamic_slice x0 -> x8, local copies, waits for them, and re-layouts: none -> 19.9 us  [the longest x4 11.3 us: owner_step(): lax.dynamic_slice_in_dim(key_all, first_row, key_count, 0) + key_piece]
    all_to_all x0 -> x1, blocking collectives: none -> 19.2 us  [context_scatter_sum(): lax.all_to_all(values.reshape((count, rows) + values.shape[1:]), axis_nam...]
    all_to_all x0 -> x3, starting transfers between devices: none -> 15.2 us  [the longest x2 10.6 us: context_gather(): gathered = lax.all_to_all(spread, axis_name, 0, 0, tiled=True)]
    dynamic_update_slice x0 -> x6, local copies, waits for them, and re-layouts: none -> 13.6 us  [the longest x4 9.88 us: owner_step(): lax.dynamic_update_slice_in_dim(value_all, lax.dynamic_slice_in_dim(value...]
  transfers between devices with their start and end apart: 10 -> 10, of which waited for: 8 -> 9; matrix products, arithmetic and copies ran while one was open for 8% -> 12% of each run, Pallas kernels for 0% -> 0%
where the time goes in v4:
time: 415 us; the launch traced here: 409 us
  waiting for transfers between devices  139 us (33%)
  local copies, waits for them, and re-layouts  93.9 us (23%)
  blocking collectives  61.8 us (15%)
  matrix products  43 us (10%)
  other arithmetic  34.9 us (8%)
  starting transfers between devices  20.9 us (5%)
  between operations  15.2 us (4%)
    reduce_scatter x1, waiting for transfers between devices, on_device(): packed = lax.psum_scatter(packed, 'fsdp', scatter_dimension=0, tiled=True)  37.4 us
    all_to_all x2, waiting for transfers between devices, context_gather(): gathered = lax.all_to_all(spread, axis_name, 0, 0, tiled=True)  34.6 us
    all_to_all x1, waiting for transfers between devices, context_scatter_sum(): lax.all_to_all(values.reshape((count, rows) + values.shape[1:]), axis_nam...  34.5 us
    ppermute x4, waiting for transfers between devices, pair_sum(): other = lax.ppermute(values, axis_name, perm=[(0, 1), (1, 0)])  25.8 us
    all_to_all x1, blocking collectives, context_scatter_sum(): lax.all_to_all(values.reshape((count, rows) + values.shape[1:]), axis_nam...  19.2 us
    unnamed x1, blocking collectives  14.7 us
    all_gather x1, blocking collectives, on_device(): lax.all_gather(down_weight, 'fsdp', axis=1, tiled=True)  14.7 us
    all_gather x1, blocking collectives, on_device(): lax.all_gather(proj_weight, 'fsdp', axis=1, tiled=True)  13.2 us
  transfers between devices with their start and end apart: 10, of which 9 were waited for; matrix products, arithmetic and copies ran while one was open for 12% of the time, Pallas kernels for 0%

profile of v4, /device:TPU:0, one launch (start us, length us, event | category | flops | bytes accessed | tf_op | source)
XLA Modules:
  0.0 409.4 jit_solution(8884322977822190658)
XLA Ops:
  11.5 14.7 %all-reduce.2 = (bf16[768]{0:T(1024)(128)(2,1)S(1)}, bf16[768]{0:T(1024)(128)(2,1)S(1)}) all-reduce(bf16[768]{0:T(1024)(128)(2,1)S(1)} %dynamic-update-slice, bf16[768]{0:T(1024)(128)(2,1)S(1)} %dynamic-update-slice.1), channel_id=1, replica_groups=mesh['fsdp'=8,'tensor'=2,'context'=8] {'fsdp'}, use_global_device_ids=true, to_apply=%add | all-reduce | flops 1536 | bytes 6144
  30.5 6.3 %all-gather.3.cloned.1.call-done = bf16[768,3,384]{2,0,1:T(8,128)(2,1)} async-done(((bf16[96,3,384]{2,0,1:T(8,128)(2,1)}), bf16[768,3,384]{2,0,1:T(8,128)(2,1)}) %all-gather.3.cloned.1.call-update) | async-done | bytes 1769488 | tf_op jit(solution)/shard_map/all_gather | solution.py:143
  36.8 2.6 copy.91
  42.7 7.0 %all-to-all-start = ((bf16[8,256,768]{1,2,0:T(8,128)(2,1)}), bf16[8,256,768]{1,2,0:T(8,128)(2,1)}, u32[]{:S(2)}, u32[]{:S(2)}) async-start(bf16[8,256,768]{1,2,0:T(8,128)(2,1)} %broadcast_in_dim.146), calls=%async_computation | async-start | bytes 6291456 | tf_op jit(solution)/shard_map/all_to_all | solution.py:79
  50.6 13.2 %all_gather.20 = bf16[384,768]{0,1:T(8,128)(2,1)S(1)} all-gather(bf16[384,96]{0,1:T(8,128)(2,1)S(1)} %copy-done.43), channel_id=1, replica_groups=mesh['fsdp'=8,'tensor'=2,'context'=8] {'fsdp'}, dimensions={1}, use_global_device_ids=true | all-gather | bytes 663552 | tf_op jit(solution)/shard_map/all_gather | solution.py:144
  65.0 25.0 %all-to-all-done = bf16[8,256,768]{1,2,0:T(8,128)(2,1)} async-done(((bf16[8,256,768]{1,2,0:T(8,128)(2,1)}), bf16[8,256,768]{1,2,0:T(8,128)(2,1)}, u32[]{:S(2)}, u32[]{:S(2)}) %all-to-all-start) | async-done | bytes 3145760 | tf_op jit(solution)/shard_map/all_to_all | solution.py:79
  90.0 4.7 %copy.92 = bf16[8,256,768]{2,1,0:T(8,128)(2,1)} copy(bf16[8,256,768]{1,2,0:T(8,128)(2,1)} %all-to-all-done) | data formatting | bytes 6291456 | tf_op jit(solution)/shard_map/all_to_all | solution.py:79
  94.6 3.4 fusion.50
  98.0 2.6 copy.93
  102.3 4.0 select_reduce_fusion.1
  106.3 4.0 select_reduce_fusion
  110.3 4.2 %fusion.14 = bf16[6,64,256]{2,1,0:T(8,128)(2,1)S(1)} fusion(bf16[2048,6,64]{0,2,1:T(8,128)(2,1)} %bitcast.14, f32[6,256,2048]{2,1,0:T(8,128)S(1)} %get-tuple-element.467, f32[6,256]{1,0:T(8,128)S(1)} %log_add_fusion, pred[256,2048]{1,0:T(8,128)(4,1)S(1)} %copy-done.19), kind=kOutput, calls=%fused_computation.45 | convolution fusion | flops 415334400 | bytes 14882816 | tf_op jit(solution)/shard_map/hqk,khd->qhd/dot_general | solution.py:185
  116.4 14.7 %all_gather.23 = bf16[576,768]{0,1:T(8,128)(2,1)} all-gather(bf16[576,96]{0,1:T(8,128)(2,1)S(1)} %copy-done.40), channel_id=1, replica_groups=mesh['fsdp'=8,'tensor'=2,'context'=8] {'fsdp'}, dimensions={1}, use_global_device_ids=true | all-gather | bytes 995328 | tf_op jit(solution)/shard_map/all_gather | solution.py:146
  131.0 2.7 copy.96
  144.6 14.9 %collective-permute-done.2 = f32[256,768]{1,0:T(8,128)} collective-permute-done((f32[256,768]{1,0:T(8,128)S(1)}, f32[256,768]{1,0:T(8,128)}, u32[]{:S(2)}, u32[]{:S(2)}) %collective-permute-start.2) | collective-permute-done | bytes 786464 | tf_op jit(solution)/shard_map/ppermute | solution.py:72
  159.5 2.3 multiply_reduce_fusion
  161.8 4.5 %collective-permute-done.1 = bf16[256,768]{1,0:T(8,128)(2,1)S(1)} collective-permute-done((bf16[256,768]{1,0:T(8,128)(2,1)S(1)}, bf16[256,768]{1,0:T(8,128)(2,1)S(1)}, u32[]{:S(2)}, u32[]{:S(2)}) %collective-permute-start.1) | collective-permute-done | bytes 393248 | tf_op jit(solution)/shard_map/ppermute | solution.py:72
  170.2 1.9 broadcast.213.clone
  174.0 72.6 %while.20 = (s32[]{:T(128)}, f32[256,6,64]{0,2,1:T(8,128)}, f32[2048,384]{1,0:T(8,128)}, f32[2048,384]{1,0:T(8,128)}, bf16[2048,384]{0,1:T(8,128)(2,1)}, /*index...) while((s32[]{:T(128)}, f32[256,6,64]{0,2,1:T(8,128)}, ...), condition=%wide.region_16.17_spmd.clone, body=%wide.region_14.16_spmd.clone.sunk | while | flops 1024107520 | bytes 134827520 | solution.py:109
  179.1 3.1 fusion.106
  182.2 2.7 fusion.107
  186.1 3.0 copy.139
  189.2 4.3 %fusion.108 = f32[6,1024,64]{1,2,0:T(8,128)S(1)} fusion(bf16[256,6,64]{0,2,1:T(8,128)(2,1)} %get-tuple-element.589, f32[6,1024,256]{2,1,0:T(8,128)} %copy-done.1, f32[6,256]{1,0:T(8,128)} %get-tuple-element.587, pred[256,1024]{0,1:T(8,128)(4,1)} %copy-done.16), kind=kOutput, calls=%fused_computation.4.clone.1 | convolution fusion | flops 207618048 | bytes 8329216 | tf_op jit(solution)/shard_map/while/body/eval_jaxpr/hqk,qhd->khd/dot_general | solution.py:265
  194.9 3.0 copy.140
  198.0 2.6 constant_dynamic-slice_fusion.11
  200.6 3.0 copy.141
  215.3 3.1 fusion.106
  218.5 2.8 fusion.107
  222.5 3.0 copy.139
  225.5 4.3 %fusion.108 = f32[6,1024,64]{1,2,0:T(8,128)S(1)} fusion(bf16[256,6,64]{0,2,1:T(8,128)(2,1)} %get-tuple-element.589, f32[6,1024,256]{2,1,0:T(8,128)} %copy-done.1, f32[6,256]{1,0:T(8,128)} %get-tuple-element.587, pred[256,1024]{0,1:T(8,128)(4,1)} %copy-done.16), kind=kOutput, calls=%fused_computation.4.clone.1 | convolution fusion | flops 207618048 | bytes 8329216 | tf_op jit(solution)/shard_map/while/body/eval_jaxpr/hqk,qhd->khd/dot_general | solution.py:265
  231.3 3.0 copy.140
  234.3 2.6 constant_dynamic-slice_fusion.11
  237.0 3.0 copy.141
  244.7 1.9 constant_dynamic-update-slice_fusion.3
  246.6 2.2 convert.52
  249.9 2.8 copy.102
  252.7 4.6 %all-to-all-start.1 = ((bf16[8,256,768]{1,2,0:T(8,128)(2,1)}), bf16[8,256,768]{1,2,0:T(8,128)(2,1)}, u32[]{:S(2)}, u32[]{:S(2)}) async-start(bf16[8,256,768]{1,2,0:T(8,128)(2,1)} %copy.102), calls=%async_computation.1 | async-start | bytes 6291456 | tf_op jit(solution)/shard_map/all_to_all | solution.py:86
  259.5 2.1 convolution_convert_fusion
  261.6 34.5 %all-to-all-done.1 = bf16[8,256,768]{1,2,0:T(8,128)(2,1)} async-done(((bf16[8,256,768]{1,2,0:T(8,128)(2,1)}), bf16[8,256,768]{1,2,0:T(8,128)(2,1)}, u32[]{:S(2)}, u32[]{:S(2)}) %all-to-all-start.1) | async-done | bytes 3145760 | tf_op jit(solution)/shard_map/all_to_all | solution.py:86
  296.1 2.4 convert_reduce_fusion.1
  300.7 2.4 collective-permute-start.3
  305.5 5.5 %collective-permute-done.3 = bf16[256,768]{1,0:T(8,128)(2,1)S(1)} collective-permute-done((bf16[256,768]{1,0:T(8,128)(2,1)S(1)}, bf16[256,768]{1,0:T(8,128)(2,1)S(1)}, u32[]{:S(2)}, u32[]{:S(2)}) %collective-permute-start.3) | collective-permute-done | bytes 393248 | tf_op jit(solution)/shard_map/ppermute | solution.py:72
  313.6 9.9 %concatenate.38 = bf16[768,3266]{1,0:T(8,128)(2,1)} concatenate(bf16[768,1]{1,0:T(8,128)(2,1)} %broadcast_in_dim.157, bf16[768,1]{1,0:T(8,128)(2,1)S(1)} %broadcast_in_dim.158, bf16[768,1152]{1,0:T(8,128)(2,1)S(1)} %convolution_convert_fusion.1, bf16[768,1152]{1,0:T(8,128)(2,1)} %convolution_convert_fusion, bf16[768,384]{1,0:T(8,128)(2,1)} %convolution_convert_fusion.3, ...), dimensions={1} | concatenate | bytes 10033152 | tf_op jit(solution)/shard_map/concatenate | solution.py:333
  323.5 37.4 %reduce-scatter.2.cloned.1.call-done = bf16[96,3266]{1,0:T(8,128)(2,1)} async-done(((bf16[768,3266]{1,0:T(8,128)(2,1)}), bf16[96,3266]{1,0:T(8,128)(2,1)}) %reduce-scatter.2.cloned.1.call-update) | async-done | bytes 627088 | tf_op jit(solution)/shard_map/reduce_scatter | solution.py:334
  362.3 19.2 %all_to_all.20 = bf16[8,12,3266]{2,1,0:T(8,128)(2,1)S(1)} all-to-all(bf16[8,12,3266]{2,1,0:T(8,128)(2,1)S(1)} %reshape.318), channel_id=1, replica_groups=mesh['fsdp'=8,'tensor'=2,'context'=8] {'context'}, dimensions={0} | all-to-all | bytes 1254144 | tf_op jit(solution)/shard_map/all_to_all | solution.py:86
  382.6 3.5 all-to-all-start.3
  386.2 2.2 fusion.26
  388.4 9.6 %all-to-all-done.3 = bf16[8,12,3266]{2,1,0:T(8,128)(2,1)S(1)} async-done(((bf16[8,12,3266]{2,1,0:T(8,128)(2,1)}), bf16[8,12,3266]{2,1,0:T(8,128)(2,1)S(1)}, u32[]{:S(2)}, u32[]{:S(2)}) %all-to-all-start.3) | async-done | bytes 627104 | tf_op jit(solution)/shard_map/all_to_all | solution.py:79
  (239 shorter events, 77.1 us)
Async XLA Ops:
  7.2 32.3 %copy-start.9 = (bf16[256,768]{1,0:T(8,128)(2,1)S(1)}, bf16[256,768]{1,0:T(8,128)(2,1)}, u32[]{:S(2)}) copy-start(bf16[256,768]{1,0:T(8,128)(2,1)} %param.11) | copy-start | bytes 1179652
  7.2 29.7 %all-gather.3.cloned.1.call-start = ((), (), s32[]{:S(2)}) async-start(), calls=%async_computation.5 | async-start | bytes 1990656 | tf_op jit(solution)/shard_map/all_gather | solution.py:143
  26.2 14.1 %copy-start.41 = (f32[768]{0:T(1024)}, f32[768]{0:T(1024)S(1)}, u32[]{:S(2)}) copy-start(f32[768]{0:T(1024)S(1)} %convert_element_type.150) | copy-start | bytes 9220
  29.0 10.4 %copy-start.44 = (f32[256]{0:T(256)}, f32[256]{0:T(256)S(1)}, u32[]{:S(2)}) copy-start(f32[256]{0:T(256)S(1)} %broadcast_multiply_fusion.5) | copy-start | bytes 3076
  30.3 9.2 %copy-start.46 = (f32[256]{0:T(256)}, f32[256]{0:T(256)S(1)}, u32[]{:S(2)}) copy-start(f32[256]{0:T(256)S(1)} %add_rsqrt_fusion.1) | copy-start | bytes 3076
  30.5 9.9 %copy-start.31 = (f32[256,32]{0,1:T(8,128)}, f32[256,32]{0,1:T(8,128)S(1)}, u32[]{:S(2)}) copy-start(f32[256,32]{0,1:T(8,128)S(1)} %get-tuple-element.464) | copy-start | bytes 98308
  30.5 9.9 %copy-start.33 = (f32[256,32]{0,1:T(8,128)}, f32[256,32]{0,1:T(8,128)S(1)}, u32[]{:S(2)}) copy-start(f32[256,32]{0,1:T(8,128)S(1)} %get-tuple-element.465) | copy-start | bytes 98308
  42.7 7.1 %copy-start.39 = (bf16[96,2,576]{2,1,0:T(2,128)(2,1)S(1)}, bf16[96,2,576]{2,1,0:T(2,128)(2,1)}, u32[]{:S(2)}) copy-start(bf16[96,2,576]{2,1,0:T(2,128)(2,1)} %param.17) | copy-start | bytes 663556
  42.7 8.0 %copy-start.43 = (bf16[384,96]{0,1:T(8,128)(2,1)S(1)}, bf16[384,96]{0,1:T(8,128)(2,1)}, u32[]{:S(2)}) copy-start(bf16[384,96]{0,1:T(8,128)(2,1)} %param.15) | copy-start | bytes 221188
  42.7 47.3 %all-to-all-start = ((bf16[8,256,768]{1,2,0:T(8,128)(2,1)}), bf16[8,256,768]{1,2,0:T(8,128)(2,1)}, u32[]{:S(2)}, u32[]{:S(2)}) async-start(bf16[8,256,768]{1,2,0:T(8,128)(2,1)} %broadcast_in_dim.146), calls=%async_computation | async-start | bytes 6291456 | tf_op jit(solution)/shard_map/all_to_all | solution.py:79
  49.7 81.3 %all-gather.5.cloned.1.call-start = ((), (), s32[]{:S(2)}) async-start(), calls=%async_computation.6 | async-start | bytes 2211840 | tf_op jit(solution)/shard_map/all_gather | solution.py:145
  63.8 50.7 %copy-start.17 = (bf16[384,768]{0,1:T(8,128)(2,1)}, bf16[384,768]{0,1:T(8,128)(2,1)S(1)}, u32[]{:S(2)}) copy-start(bf16[384,768]{0,1:T(8,128)(2,1)S(1)} %all_gather.20) | copy-start | bytes 1769476
  102.3 4.0 copy-start.19
  110.3 4.2 %copy-start.48 = (f32[6,256]{1,0:T(8,128)}, f32[6,256]{1,0:T(8,128)S(1)}, u32[]{:S(2)}) copy-start(f32[6,256]{1,0:T(8,128)S(1)} %log_add_fusion) | copy-start | bytes 18436
  110.3 6.1 %copy-start.40 = (bf16[576,96]{0,1:T(8,128)(2,1)S(1)}, bf16[576,96]{0,1:T(8,128)(2,1)}, u32[]{:S(2)}) copy-start(bf16[576,96]{0,1:T(8,128)(2,1)} %param.18) | copy-start | bytes 331780
  115.8 18.8 %collective-permute-start = (f32[256,768]{1,0:T(8,128)}, f32[256,768]{1,0:T(8,128)}, u32[]{:S(2)}, u32[]{:S(2)}) collective-permute-start(f32[256,768]{1,0:T(8,128)} %fusion.53), channel_id=1, source_target_pairs={{0,8},{8,0},{1,9},{9,1},{2,10},{10,2},{3,11},{11,3},{4,12},{12,4},... | collective-permute-start | bytes 2359304 | tf_op jit(solution)/shard_map/ppermute | solution.py:72
  136.2 30.2 %copy-start.7 = (f32[256,768]{1,0:T(8,128)}, f32[256,768]{1,0:T(8,128)S(1)}, u32[]{:S(2)}) copy-start(f32[256,768]{1,0:T(8,128)S(1)} %get-tuple-element.439) | copy-start | bytes 2359300
  137.9 4.5 %copy-start.22 = (bf16[576,768]{0,1:T(8,128)(2,1)S(1)}, bf16[576,768]{0,1:T(8,128)(2,1)}, u32[]{:S(2)}) copy-start(bf16[576,768]{0,1:T(8,128)(2,1)} %all_gather.23) | copy-start | bytes 2654212
  138.8 5.8 %copy-start.30 = (f32[256,768]{1,0:T(8,128)}, f32[256,768]{1,0:T(8,128)S(1)}, u32[]{:S(2)}) copy-start(f32[256,768]{1,0:T(8,128)S(1)} %convolution_bitcast_fusion) | copy-start | bytes 2359300
  138.8 20.7 %collective-permute-start.2 = (f32[256,768]{1,0:T(8,128)S(1)}, f32[256,768]{1,0:T(8,128)}, u32[]{:S(2)}, u32[]{:S(2)}) collective-permute-start(f32[256,768]{1,0:T(8,128)S(1)} %convolution_bitcast_fusion), channel_id=1, source_target_pairs={{0,8},{8,0},{1,9},{9,1},{2,10},{10,2},{3,11},{11,3},{4,12},{12,4},... | collective-permute-start | bytes 2359304 | tf_op jit(solution)/shard_map/ppermute | solution.py:72
  140.3 26.1 %copy-start.28 = (bf16[256,768]{1,0:T(8,128)(2,1)S(1)}, bf16[256,768]{1,0:T(8,128)(2,1)}, u32[]{:S(2)}) copy-start(bf16[256,768]{1,0:T(8,128)(2,1)} %param.19) | copy-start | bytes 1179652
  142.9 24.5 %copy-start.18 = (bf16[384,768]{0,1:T(8,128)(2,1)S(1)}, bf16[384,768]{0,1:T(8,128)(2,1)}, u32[]{:S(2)}) copy-start(bf16[384,768]{0,1:T(8,128)(2,1)} %copy-done.17) | copy-start | bytes 1769476
  143.0 23.4 %collective-permute-start.1 = (bf16[256,768]{1,0:T(8,128)(2,1)S(1)}, bf16[256,768]{1,0:T(8,128)(2,1)S(1)}, u32[]{:S(2)}, u32[]{:S(2)}) collective-permute-start(bf16[256,768]{1,0:T(8,128)(2,1)S(1)} %convolution_convert_fusion.5), channel_id=1, source_target_pairs={{0,8},{8,0},{1,9},{9,1},{2,10},{10,2},{3,11},{11,3},{4,12},{12,4},... | collective-permute-start | bytes 1179656 | tf_op jit(solution)/shard_map/ppermute | solution.py:72
  167.4 6.6 %copy-start.14 = (f32[256,768]{1,0:T(8,128)}, f32[256,768]{1,0:T(8,128)S(1)}, u32[]{:S(2)}) copy-start(f32[256,768]{1,0:T(8,128)S(1)} %get-tuple-element.450) | copy-start | bytes 2359300
  175.2 3.9 copy-start.49
  175.2 3.9 copy-start.50
  176.3 5.9 %copy-start.1 = (f32[6,1024,256]{2,1,0:T(8,128)}, f32[6,1024,256]{2,1,0:T(8,128)S(1)}, u32[]{:S(2)}) copy-start(f32[6,1024,256]{2,1,0:T(8,128)S(1)} %fusion.105) | copy-start | bytes 18874372 | tf_op jit(solution)/shard_map/while
  177.3 4.9 %copy-start.16 = (pred[256,1024]{0,1:T(8,128)(4,1)}, pred[256,1024]{0,1:T(8,128)(4,1)S(1)}, u32[]{:S(2)}) copy-start(pred[256,1024]{0,1:T(8,128)(4,1)S(1)} %broadcast_compare_fusion.3) | copy-start | bytes 786436 | tf_op jit(solution)/shard_map/while
  189.2 4.3 %copy-start.3 = (f32[1024,384]{0,1:T(8,128)S(1)}, f32[1024,384]{0,1:T(8,128)}, u32[]{:S(2)}) copy-start(f32[1024,384]{0,1:T(8,128)} %copy.139) | copy-start | bytes 4718596 | tf_op jit(solution)/shard_map/while
  212.5 5.9 %copy-start.1 = (f32[6,1024,256]{2,1,0:T(8,128)}, f32[6,1024,256]{2,1,0:T(8,128)S(1)}, u32[]{:S(2)}) copy-start(f32[6,1024,256]{2,1,0:T(8,128)S(1)} %fusion.105) | copy-start | bytes 18874372 | tf_op jit(solution)/shard_map/while
  213.5 4.9 %copy-start.16 = (pred[256,1024]{0,1:T(8,128)(4,1)}, pred[256,1024]{0,1:T(8,128)(4,1)S(1)}, u32[]{:S(2)}) copy-start(pred[256,1024]{0,1:T(8,128)(4,1)S(1)} %broadcast_compare_fusion.3) | copy-start | bytes 786436 | tf_op jit(solution)/shard_map/while
  225.5 4.3 %copy-start.3 = (f32[1024,384]{0,1:T(8,128)S(1)}, f32[1024,384]{0,1:T(8,128)}, u32[]{:S(2)}) copy-start(f32[1024,384]{0,1:T(8,128)} %copy.139) | copy-start | bytes 4718596 | tf_op jit(solution)/shard_map/while
  252.7 4.9 %copy-start.24 = (bf16[256,576]{0,1:T(8,128)(2,1)S(1)}, bf16[256,576]{0,1:T(8,128)(2,1)}, u32[]{:S(2)}) copy-start(bf16[256,576]{0,1:T(8,128)(2,1)} %copy-done.23) | copy-start | bytes 884740
  252.7 4.9 %copy-start.29 = (bf16[256,768]{1,0:T(8,128)(2,1)S(1)}, bf16[256,768]{1,0:T(8,128)(2,1)}, u32[]{:S(2)}) copy-start(bf16[256,768]{1,0:T(8,128)(2,1)} %param.19) | copy-start | bytes 1179652
  252.7 43.4 %all-to-all-start.1 = ((bf16[8,256,768]{1,2,0:T(8,128)(2,1)}), bf16[8,256,768]{1,2,0:T(8,128)(2,1)}, u32[]{:S(2)}, u32[]{:S(2)}) async-start(bf16[8,256,768]{1,2,0:T(8,128)(2,1)} %copy.102), calls=%async_computation.1 | async-start | bytes 6291456 | tf_op jit(solution)/shard_map/all_to_all | solution.py:86
  257.3 103.5 %reduce-scatter.2.cloned.1.call-start = ((), (), s32[]{:S(2)}) async-start(), calls=%async_computation.7 | async-start | bytes 5750784 | tf_op jit(solution)/shard_map/reduce_scatter | solution.py:334
  261.6 37.0 %copy-start.13 = (f32[256,6,64]{0,2,1:T(8,128)S(1)}, f32[256,6,64]{0,2,1:T(8,128)}, u32[]{:S(2)}) copy-start(f32[256,6,64]{0,2,1:T(8,128)} %get-tuple-element.285) | copy-start | bytes 1179652
  261.6 37.0 %copy-start.32 = (f32[256,32]{0,1:T(8,128)S(1)}, f32[256,32]{0,1:T(8,128)}, u32[]{:S(2)}) copy-start(f32[256,32]{0,1:T(8,128)} %copy-done.31) | copy-start | bytes 98308
  261.6 37.0 %copy-start.34 = (f32[256,32]{0,1:T(8,128)S(1)}, f32[256,32]{0,1:T(8,128)}, u32[]{:S(2)}) copy-start(f32[256,32]{0,1:T(8,128)} %copy-done.33) | copy-start | bytes 98308
  298.6 4.5 %copy-start.15 = (f32[256,768]{1,0:T(8,128)S(1)}, f32[256,768]{1,0:T(8,128)}, u32[]{:S(2)}) copy-start(f32[256,768]{1,0:T(8,128)} %copy-done.14) | copy-start | bytes 2359300
  298.8 5.6 %copy-start.51 = (bf16[768]{0:T(1024)(128)(2,1)S(1)}, bf16[768]{0:T(1024)(128)(2,1)}, u32[]{:S(2)}) copy-start(bf16[768]{0:T(1024)(128)(2,1)} %get-tuple-element.403) | copy-start | bytes 4612
  298.8 5.7 %copy-start.10 = (bf16[256,768]{1,0:T(8,128)(2,1)S(1)}, bf16[256,768]{1,0:T(8,128)(2,1)}, u32[]{:S(2)}) copy-start(bf16[256,768]{1,0:T(8,128)(2,1)} %param.11) | copy-start | bytes 1179652
  298.8 5.7 %copy-start.42 = (f32[768]{0:T(1024)S(1)}, f32[768]{0:T(1024)}, u32[]{:S(2)}) copy-start(f32[768]{0:T(1024)} %copy-done.41) | copy-start | bytes 9220
  298.8 5.7 %copy-start.45 = (f32[256]{0:T(256)S(1)}, f32[256]{0:T(256)}, u32[]{:S(2)}) copy-start(f32[256]{0:T(256)} %copy-done.44) | copy-start | bytes 3076
  298.9 5.7 %copy-start.47 = (f32[256]{0:T(256)S(1)}, f32[256]{0:T(256)}, u32[]{:S(2)}) copy-start(f32[256]{0:T(256)} %copy-done.46) | copy-start | bytes 3076
  300.7 10.3 %collective-permute-start.3 = (bf16[256,768]{1,0:T(8,128)(2,1)S(1)}, bf16[256,768]{1,0:T(8,128)(2,1)S(1)}, u32[]{:S(2)}, u32[]{:S(2)}) collective-permute-start(bf16[256,768]{1,0:T(8,128)(2,1)S(1)} %convolution_convert_fusion.4), channel_id=1, source_target_pairs={{0,8},{8,0},{1,9},{9,1},{2,10},{10,2},{3,11},{11,3},{4,12},{12,4},... | collective-permute-start | bytes 1179656 | tf_op jit(solution)/shard_map/ppermute | solution.py:72
  323.5 62.7 %copy-start.52 = (f32[256]{0:T(256)S(1)}, f32[256]{0:T(256)}, u32[]{:S(2)}) copy-start(f32[256]{0:T(256)} %get-tuple-element.408) | copy-start | bytes 3076
  382.6 15.4 %all-to-all-start.3 = ((bf16[8,12,3266]{2,1,0:T(8,128)(2,1)}), bf16[8,12,3266]{2,1,0:T(8,128)(2,1)S(1)}, u32[]{:S(2)}, u32[]{:S(2)}) async-start(bf16[8,12,3266]{2,1,0:T(8,128)(2,1)} %broadcast_in_dim.154), calls=%async_computation.4 | async-start | bytes 1703936 | tf_op jit(solution)/shard_map/all_to_all | solution.py:79
  (25 other events, 53.4 us)
Sparse Core Ops, SparseCore 0:
  9.7 27.0 all-gather.2
  52.8 25.5 all-gather.4
  323.6 37.2 reduce-scatter.1

commit v5 on v4

--- a/solution.py
+++ b/solution.py
@@ -87,37 +87,6 @@
         values.reshape((count, rows) + values.shape[1:]), axis_name, 0, 0, tiled=True
     )
     return jnp.sum(parts.astype(jnp.float32), axis=0)
-
-
-def split_count(row_count):
-    pieces = 1
-    while row_count // pieces > 1024 and row_count % (2 * pieces) == 0:
-        pieces = pieces * 2
-    return pieces
-
-
-def over_blocks(step, running, members):
-    row_count = members[0].shape[0]
-    pieces = split_count(row_count)
-    stride = row_count // pieces
-
-    def one_block(counter, current):
-        offset = counter * stride
-        sliced = tuple((lax.dynamic_slice_in_dim(member, offset, stride, 0) for member in members))
-        return step(current, sliced, offset)
-
-    return lax.fori_loop(0, pieces, one_block, running)
-
-
-def guarded(step):
-
-    def wrapped(running, members, first_row):
-        return step(running, members, first_row)
-
-    def folded(running, members, first_row):
-        return over_blocks(wrapped, running, members)
-
-    return folded
 
 
 def on_device(
@@ -139,24 +108,42 @@
     own_rows = own_first + jnp.arange(row_count, dtype=jnp.int32)
     own_segment, positions = segments_of(own_rows, lengths)
     cosine, sine_tab = rope_tables(positions, HD)
-    gathered = (
-        lax.all_gather(qkv_weight, "fsdp", axis=0, tiled=True),
-        lax.all_gather(proj_weight, "fsdp", axis=1, tiled=True),
-        lax.all_gather(gelu_weight, "fsdp", axis=0, tiled=True),
-        lax.all_gather(down_weight, "fsdp", axis=1, tiled=True),
-        lax.all_gather(attn_gain, "fsdp", axis=0, tiled=True),
-        lax.all_gather(mlp_gain, "fsdp", axis=0, tiled=True),
-    )
-    qkv_full, proj_full, gelu_full, down_full, attn_full, mlp_full = gathered
-    local_width = qkv_full.shape[2]
+    shard_rows = qkv_weight.shape[0]
+    local_width = qkv_weight.shape[2]
     head_count = local_width // HD
-    hidden = gelu_full.shape[2]
+    hidden = gelu_weight.shape[2]
+    first_pack = lax.all_gather(
+        jnp.concatenate(
+            [
+                qkv_weight.reshape(shard_rows, 3 * local_width),
+                attn_gain[:, None],
+                mlp_gain[:, None],
+            ],
+            axis=1,
+        ),
+        "fsdp",
+        axis=0,
+        tiled=True,
+    )
+    second_pack = lax.all_gather(
+        jnp.concatenate(
+            [proj_weight.T, gelu_weight.reshape(shard_rows, 2 * hidden), down_weight.T], axis=1
+        ),
+        "fsdp",
+        axis=0,
+        tiled=True,
+    )
+    qkv_flat = first_pack[:, : 3 * local_width]
+    attn_full = first_pack[:, 3 * local_width]
+    mlp_full = first_pack[:, 3 * local_width + 1]
+    proj_t = second_pack[:, :local_width]
+    gelu_flat = second_pack[:, local_width : local_width + 2 * hidden]
+    down_t = second_pack[:, local_width + 2 * hidden :]
     attn_scale = attn_full.astype(jnp.float32)
     mlp_scale = mlp_full.astype(jnp.float32)
     inputs = block_input.astype(jnp.float32)
     normed_attn, spread_attn = layer_norm(inputs)
     hidden_attn = (normed_attn * attn_scale).astype(jnp.bfloat16)
-    qkv_flat = qkv_full.reshape(feature_count, 3 * local_width)
     projected = jnp.dot(hidden_attn, qkv_flat, preferred_element_type=jnp.float32).reshape(
         row_count, 3, head_count, HD
     )
@@ -179,29 +166,27 @@
         jnp.where(same_group, jnp.exp(fwd_scores - row_max[:, :, None]), 0.0), axis=2
     )
     log_total = row_max + jnp.log(denom_sum)
-    fwd_weights = jnp.where(same_group, jnp.exp(fwd_scores - log_total[:, :, None]), 0.0).astype(
-        jnp.bfloat16
-    )
+    fwd_probs = jnp.where(same_group, jnp.exp(fwd_scores - log_total[:, :, None]), 0.0)
+    fwd_weights = fwd_probs.astype(jnp.bfloat16)
     mixed = jnp.einsum(
         "hqk,khd->qhd", fwd_weights, values_heads, preferred_element_type=jnp.float32
     ).astype(jnp.bfloat16)
     mixed_flat = mixed.reshape(row_count, local_width)
-    attn_part = jnp.dot(mixed_flat, proj_full, preferred_element_type=jnp.float32)
+    attn_part = jnp.dot(mixed_flat, proj_t.T, preferred_element_type=jnp.float32)
     residual = inputs + pair_sum(attn_part, "tensor")
     normed_mlp, spread_mlp = layer_norm(residual)
     hidden_mlp = (normed_mlp * mlp_scale).astype(jnp.bfloat16)
-    gelu_flat = gelu_full.reshape(feature_count, 2 * hidden)
     gate_up = jnp.dot(hidden_mlp, gelu_flat, preferred_element_type=jnp.float32).reshape(
         row_count, 2, hidden
     )
     gate_pre, up_pre = (gate_up[:, 0], gate_up[:, 1])
     gelu_val, gelu_slope = gelu_parts(gate_pre)
     activ = (gelu_val * up_pre).astype(jnp.bfloat16)
-    mlp_part = jnp.dot(activ, down_full, preferred_element_type=jnp.float32)
+    mlp_part = jnp.dot(activ, down_t.T, preferred_element_type=jnp.float32)
     block_output = (
         residual + pair_sum(mlp_part.astype(jnp.bfloat16), "tensor")
     ).astype(jnp.bfloat16)
-    act_grad = jnp.dot(out_cotangent, down_full.T, preferred_element_type=jnp.float32)
+    act_grad = jnp.dot(out_cotangent, down_t, preferred_element_type=jnp.float32)
     down_grad_t = jnp.dot(out_cotangent.T, activ, preferred_element_type=jnp.float32)
     gate_up_grad = (
         jnp.stack([act_grad * up_pre * gelu_slope, act_grad * gelu_val], axis=1)
@@ -219,7 +204,7 @@
         mlp_in_grad, normed_mlp, spread_mlp, mlp_scale
     )
     resid_bf = resid_grad.astype(jnp.bfloat16)
-    out_grad = jnp.dot(resid_bf, proj_full.T, preferred_element_type=jnp.float32).astype(
+    out_grad = jnp.dot(resid_bf, proj_t, preferred_element_type=jnp.float32).astype(
         jnp.bfloat16
     )
     proj_grad_t = jnp.dot(resid_bf.T, mixed_flat, preferred_element_type=jnp.float32)
@@ -228,74 +213,23 @@
         jnp.sum(out_heads.astype(jnp.float32) * mixed.astype(jnp.float32), axis=2)
     )
 
-    def key_terms(members, first_row):
-        key_count = members[0].shape[0]
-        key_part = members[0].reshape(key_count, head_count, HD)
-        value_part = members[1].reshape(key_count, head_count, HD)
-        key_segment, unused = segments_of(
-            first_row + jnp.arange(key_count, dtype=jnp.int32), lengths
-        )
-        same_doc = (own_segment[:, None] == key_segment[None, :])[None]
-        scores = (
-            jnp.einsum("qhd,khd->hqk", query_bf, key_part, preferred_element_type=jnp.float32)
-            * 0.125
-        )
-        weights = jnp.where(same_doc, jnp.exp(scores - log_total[:, :, None]), 0.0)
-        prob_grad = jnp.einsum(
-            "qhd,khd->hqk", out_heads, value_part, preferred_element_type=jnp.float32
-        )
-        score_grad = (weights * (prob_grad - delta[:, :, None])).astype(jnp.bfloat16)
-        return (key_part, weights, score_grad)
-
-    def owner_step(running, members, first_row):
-        query_grad, key_all, value_all = running
-        key_part, weights, score_grad = key_terms(members, first_row)
-        key_count = key_part.shape[0]
-        query_grad = (
-            query_grad
-            + jnp.einsum("hqk,khd->qhd", score_grad, key_part, preferred_element_type=jnp.float32)
-            * 0.125
-        )
-        key_piece = (
-            jnp.einsum(
-                "hqk,qhd->khd", score_grad, query_bf, preferred_element_type=jnp.float32
-            ).reshape(key_count, local_width)
-            * 0.125
-        )
-        value_piece = jnp.einsum(
-            "hqk,qhd->khd",
-            weights.astype(jnp.bfloat16),
-            out_heads,
-            preferred_element_type=jnp.float32,
-        ).reshape(key_count, local_width)
-        key_all = lax.dynamic_update_slice_in_dim(
-            key_all,
-            lax.dynamic_slice_in_dim(key_all, first_row, key_count, 0) + key_piece,
-            first_row,
-            0,
-        )
-        value_all = lax.dynamic_update_slice_in_dim(
-            value_all,
-            lax.dynamic_slice_in_dim(value_all, first_row, key_count, 0) + value_piece,
-            first_row,
-            0,
-        )
-        return (query_grad, key_all, value_all)
-
-    grad_start = jnp.zeros((row_count, head_count, HD), jnp.float32)
-    back_state = (
-        grad_start,
-        jnp.zeros((group_rows, local_width), jnp.float32),
-        jnp.zeros((group_rows, local_width), jnp.float32),
-    )
-    back_result = guarded(owner_step)(
-        back_state,
-        (keys_group, values_group),
-        jnp.int32(0),
-    )
-    query_grad = back_result[0]
+    prob_grad = jnp.einsum(
+        "qhd,khd->hqk", out_heads, values_heads, preferred_element_type=jnp.float32
+    )
+    score_grad = (fwd_probs * (prob_grad - delta[:, :, None])).astype(jnp.bfloat16)
+    query_grad = (
+        jnp.einsum("hqk,khd->qhd", score_grad, keys_heads, preferred_element_type=jnp.float32)
+        * 0.125
+    )
+    key_all = (
+        jnp.einsum("hqk,qhd->khd", score_grad, query_bf, preferred_element_type=jnp.float32)
+        * 0.125
+    ).reshape(group_rows, local_width)
+    value_all = jnp.einsum(
+        "hqk,qhd->khd", fwd_weights, out_heads, preferred_element_type=jnp.float32
+    ).reshape(group_rows, local_width)
     kv_grad = context_scatter_sum(
-        jnp.concatenate([back_result[1], back_result[2]], axis=1).astype(jnp.bfloat16), "context"
+        jnp.concatenate([key_all, value_all], axis=1).astype(jnp.bfloat16), "context"
     )
     key_grad, value_grad = (kv_grad[:, :local_width], kv_grad[:, local_width:])
     key_grad = key_grad.reshape(row_count, head_count, HD)

time: 415 us -> 347 us (0.84)
  local copies, waits for them, and re-layouts: 93.9 us -> 43.5 us
  blocking collectives: 61.8 us -> 19.2 us
  waiting for transfers between devices: 139 us -> 178 us
  other arithmetic: 34.9 us -> 24.1 us
    all_gather x2 -> x0, blocking collectives: 27.8 us -> none  [the longest x1 14.7 us: on_device(): lax.all_gather(down_weight, 'fsdp', axis=1, tiled=True)]
    dynamic_slice x12 -> x0, local copies, waits for them, and re-layouts: 25.8 us -> none  [the longest x4 11.3 us: owner_step(): lax.dynamic_slice_in_dim(key_all, first_row, key_count, 0) + key_piece]
    ppermute x4, waiting for transfers between devices: 25.8 us -> 44.9 us  [pair_sum(): other = lax.ppermute(values, axis_name, perm=[(0, 1), (1, 0)])]
    all_gather x2, waiting for transfers between devices: 6.31 us -> 23.2 us  [the longest x1 23.2 us: on_device(): lax.all_gather(jnp.concatenate([qkv_weight.reshape(shard_rows, 3 * local_...]
    unnamed x1 -> x0, blocking collectives: 14.7 us -> none
    dynamic_update_slice x6 -> x0, local copies, waits for them, and re-layouts: 13.6 us -> none  [the longest x4 9.88 us: owner_step(): lax.dynamic_update_slice_in_dim(value_all, lax.dynamic_slice_in_dim(value...]
    all_to_all x2, waiting for transfers between devices: 34.6 us -> 45.6 us  [context_gather(): gathered = lax.all_to_all(spread, axis_name, 0, 0, tiled=True)]
    all_to_all x1, waiting for transfers between devices: 34.5 us -> 25.3 us  [context_scatter_sum(): lax.all_to_all(values.reshape((count, rows) + values.shape[1:]), axis_nam...]
  transfers between devices with their start and end apart: 10 -> 10, of which waited for: 9 -> 9; matrix products, arithmetic and copies ran while one was open for 12% -> 14% of each run, Pallas kernels for 0% -> 0%
where the time goes in v5:
time: 347 us; the launch traced here: 343 us
  waiting for transfers between devices  178 us (51%)
  matrix products  44.2 us (13%)
  local copies, waits for them, and re-layouts  43.5 us (13%)
  other arithmetic  24.1 us (7%)
  starting transfers between devices  19.2 us (6%)
  blocking collectives  19.2 us (6%)
  between operations  14.4 us (4%)
    all_to_all x2, waiting for transfers between devices, context_gather(): gathered = lax.all_to_all(spread, axis_name, 0, 0, tiled=True)  45.6 us
    ppermute x4, waiting for transfers between devices, pair_sum(): other = lax.ppermute(values, axis_name, perm=[(0, 1), (1, 0)])  44.9 us
    reduce_scatter x1, waiting for transfers between devices, on_device(): packed = lax.psum_scatter(packed, 'fsdp', scatter_dimension=0, tiled=True)  38.8 us
    all_to_all x1, waiting for transfers between devices, context_scatter_sum(): lax.all_to_all(values.reshape((count, rows) + values.shape[1:]), axis_nam...  25.3 us
    all_gather x1, waiting for transfers between devices, on_device(): lax.all_gather(jnp.concatenate([qkv_weight.reshape(shard_rows, 3 * local_...  23.2 us
    all_to_all x1, blocking collectives, context_scatter_sum(): lax.all_to_all(values.reshape((count, rows) + values.shape[1:]), axis_nam...  19.2 us
    all_to_all x2, starting transfers between devices, context_gather(): gathered = lax.all_to_all(spread, axis_name, 0, 0, tiled=True)  10.6 us
    concatenate x1, local copies, waits for them, and re-layouts, on_device(): packed = jnp.concatenate(grads, axis=1).astype(jnp.bfloat16)  9.96 us
  transfers between devices with their start and end apart: 10, of which 9 were waited for; matrix products, arithmetic and copies ran while one was open for 14% of the time, Pallas kernels for 0%

profile of v5, /device:TPU:0, one launch (start us, length us, event | category | flops | bytes accessed | tf_op | source)
XLA Modules:
  0.0 342.6 jit_solution(11885147907502237978)
XLA Ops:
  12.2 1.1 convert_reduce_fusion.1
  13.4 1.2 fusion.29
  14.9 23.2 %all-gather.3.cloned.1.call-done = bf16[768,1154]{1,0:T(8,128)(2,1)} async-done(((bf16[96,1154]{1,0:T(8,128)(2,1)}), bf16[768,1154]{1,0:T(8,128)(2,1)}) %all-gather.3.cloned.1.call-update) | async-done | bytes 1772560 | tf_op jit(solution)/shard_map/all_gather | solution.py:115
  38.1 1.3 convert_reduce_fusion.2
  39.4 2.5 fusion.7
  42.9 1.9 broadcast_in_dim.55
  44.8 7.0 %all-to-all-start = ((bf16[8,256,768]{1,2,0:T(8,128)(2,1)}), bf16[8,256,768]{1,2,0:T(8,128)(2,1)S(1)}, u32[]{:S(2)}, u32[]{:S(2)}) async-start(bf16[8,256,768]{1,2,0:T(8,128)(2,1)} %broadcast_in_dim.55), calls=%async_computation | async-start | bytes 6291456 | tf_op jit(solution)/shard_map/all_to_all | solution.py:79
  51.8 1.1 reshape.249
  53.0 1.7 pad_maximum_fusion.3
  54.8 1.2 broadcast_compare_fusion
  56.0 36.0 %all-to-all-done = bf16[8,256,768]{1,2,0:T(8,128)(2,1)S(1)} async-done(((bf16[8,256,768]{1,2,0:T(8,128)(2,1)}), bf16[8,256,768]{1,2,0:T(8,128)(2,1)S(1)}, u32[]{:S(2)}, u32[]{:S(2)}) %all-to-all-start) | async-done | bytes 3145760 | tf_op jit(solution)/shard_map/all_to_all | solution.py:79
  91.9 2.8 copy.87
  94.7 3.3 fusion.55
  98.1 1.7 copy.89
  99.8 1.7 copy.88
  101.5 3.6 %select_reduce_fusion.1 = (f32[6,256]{1,0:T(8,128)S(1)}, f32[6,256,2048]{2,1,0:T(8,128)S(1)}) fusion(pred[256,2048]{1,0:T(8,128)(4,1)} %broadcast_compare_fusion, bf16[2048,6,64]{0,2,1:T(8,128)(2,1)S(1)} %bitcast.117, bf16[256,6,32]{0,2,1:T(8,128)(2,1)S(1)} %copy-done.17, bf16[256,6,32]{0,2,1:T(8,128)(2,1)S(1)} %copy-done.15), kind=kOutput, calls=%fused_computation.3 | convolution fusion | flops 412482048 | bytes 14882816 | tf_op jit(solution)/shard_map/qhd,khd->hqk/dot_general | solution.py:162
  105.1 4.0 %select_reduce_fusion = f32[6,256]{1,0:T(8,128)S(1)} fusion(f32[6,256,2048]{2,1,0:T(8,128)S(1)} %get-tuple-element.87, f32[6,256]{1,0:T(8,128)S(1)} %get-tuple-element.86, pred[256,2048]{1,0:T(8,128)(4,1)S(1)} %copy-done.3), kind=kLoop, calls=%fused_computation.2 | loop fusion | flops 12581376 | bytes 13119488 | tf_op jit(solution)/shard_map/reduce_sum | solution.py:165
  109.8 3.0 convolution_convert_fusion.6
  112.9 1.6 fusion.40
  115.3 17.9 %collective-permute-done = f32[256,768]{1,0:T(8,128)S(1)} collective-permute-done((f32[256,768]{1,0:T(8,128)S(1)}, f32[256,768]{1,0:T(8,128)S(1)}, u32[]{:S(2)}, u32[]{:S(2)}) %collective-permute-start) | collective-permute-done | bytes 786464 | tf_op jit(solution)/shard_map/ppermute | solution.py:72
  137.3 1.5 collective-permute-start.1
  138.8 17.8 %collective-permute-done.2 = f32[256,768]{1,0:T(8,128)S(1)} collective-permute-done((f32[256,768]{1,0:T(8,128)S(1)}, f32[256,768]{1,0:T(8,128)S(1)}, u32[]{:S(2)}, u32[]{:S(2)}) %collective-permute-start.2) | collective-permute-done | bytes 786464 | tf_op jit(solution)/shard_map/ppermute | solution.py:72
  157.5 4.7 %collective-permute-done.1 = bf16[256,768]{1,0:T(8,128)(2,1)S(1)} collective-permute-done((bf16[256,768]{1,0:T(8,128)(2,1)S(1)}, bf16[256,768]{1,0:T(8,128)(2,1)S(1)}, u32[]{:S(2)}, u32[]{:S(2)}) %collective-permute-start.1) | collective-permute-done | bytes 393248 | tf_op jit(solution)/shard_map/ppermute | solution.py:72
  164.3 1.7 copy.91
  166.1 1.1 multiply_reduce_fusion.4
  167.2 7.5 %convolution_convert_fusion.2 = bf16[6,64,2048]{2,1,0:T(8,128)(2,1)S(1)} fusion(bf16[256,6,64]{0,2,1:T(8,128)(2,1)} %bitcast.140, f32[6,256,2048]{2,1,0:T(8,128)} %copy-done, f32[6,256]{1,0:T(8,128)} %copy-done.30, pred[256,2048]{1,0:T(8,128)(4,1)} %broadcast_compare_fusion), kind=kOutput, calls=%fused_computation.10 | convolution fusion | flops 416022528 | bytes 14882816 | tf_op jit(solution)/shard_map/hqk,qhd->khd/dot_general | solution.py:228
  174.8 7.7 %multiply_convert_fusion = bf16[6,256,2048]{2,1,0:T(8,128)(2,1)S(1)} fusion(f32[6,256,2048]{2,1,0:T(8,128)} %copy-done, f32[6,256]{1,0:T(8,128)S(1)} %bitcast.148, f32[6,256]{1,0:T(8,128)S(1)} %copy-done.31, pred[256,2048]{1,0:T(8,128)(4,1)S(1)} %copy-done.4, bf16[256,6,64]{0,2,1:T(8,128)(2,1)S(1)} %bitcast.141, bf16[2048,6,64]{0,2,1:T(8,128)(2,1)S(1)} %bitcast.131), kind=kOutput, calls=%fused_computation | convolution fusion | flops 421527552 | bytes 21180416 | tf_op jit(solution)/shard_map/qhd,khd->hqk/dot_general | solution.py:216
  182.6 1.2 multiply_convert_fusion.1
  183.8 1.4 copy-done.1
  186.9 1.9 pad_maximum_fusion
  188.7 4.7 %all-to-all-start.1 = ((bf16[8,256,768]{1,2,0:T(8,128)(2,1)}), bf16[8,256,768]{1,2,0:T(8,128)(2,1)}, u32[]{:S(2)}, u32[]{:S(2)}) async-start(bf16[8,256,768]{1,2,0:T(8,128)(2,1)} %pad_maximum_fusion), calls=%async_computation.1 | async-start | bytes 6291456 | tf_op jit(solution)/shard_map/all_to_all | solution.py:86
  193.7 2.5 fusion.9
  196.1 2.2 copy.97
  198.3 3.1 convolution_convert_fusion
  201.5 4.8 %fusion.13 = f32[256,6,64]{0,2,1:T(8,128)S(1)} fusion(bf16[2048,6,64]{0,2,1:T(8,128)(2,1)S(1)} %bitcast.118, bf16[6,256,2048]{2,1,0:T(8,128)(2,1)} %copy-done.1), kind=kOutput, calls=%fused_computation.26 | convolution fusion | flops 402751488 | bytes 8257536 | tf_op jit(solution)/shard_map/hqk,khd->qhd/dot_general | solution.py:221
  206.3 25.3 %all-to-all-done.1 = bf16[8,256,768]{1,2,0:T(8,128)(2,1)} async-done(((bf16[8,256,768]{1,2,0:T(8,128)(2,1)}), bf16[8,256,768]{1,2,0:T(8,128)(2,1)}, u32[]{:S(2)}, u32[]{:S(2)}) %all-to-all-start.1) | async-done | bytes 3145760 | tf_op jit(solution)/shard_map/all_to_all | solution.py:86
  231.6 2.4 convert_reduce_fusion
  234.4 1.2 copy-done.26
  237.0 1.2 convolution_convert_fusion.4
  239.9 4.5 %collective-permute-done.3 = bf16[256,768]{1,0:T(8,128)(2,1)S(1)} collective-permute-done((bf16[256,768]{1,0:T(8,128)(2,1)S(1)}, bf16[256,768]{1,0:T(8,128)(2,1)S(1)}, u32[]{:S(2)}, u32[]{:S(2)}) %collective-permute-start.3) | collective-permute-done | bytes 393248 | tf_op jit(solution)/shard_map/ppermute | solution.py:72
  245.3 10.0 %concatenate.48 = bf16[768,3266]{1,0:T(8,128)(2,1)} concatenate(bf16[768,1]{1,0:T(8,128)(2,1)S(1)} %broadcast_in_dim.103, bf16[768,1]{1,0:T(8,128)(2,1)} %broadcast_in_dim.104, bf16[768,1152]{1,0:T(8,128)(2,1)S(1)} %convolution_convert_fusion.1, bf16[768,1152]{1,0:T(8,128)(2,1)} %convolution_convert_fusion, bf16[768,384]{1,0:T(8,128)(2,1)} %convolution_convert_fusion.4, ...), dimensions={1} | concatenate | bytes 10033152 | tf_op jit(solution)/shard_map/concatenate | solution.py:267
  255.3 38.8 %reduce-scatter.2.cloned.1.call-done = bf16[96,3266]{1,0:T(8,128)(2,1)} async-done(((bf16[768,3266]{1,0:T(8,128)(2,1)}), bf16[96,3266]{1,0:T(8,128)(2,1)}) %reduce-scatter.2.cloned.1.call-update) | async-done | bytes 627088 | tf_op jit(solution)/shard_map/reduce_scatter | solution.py:268
  294.1 1.4 reshape.253
  295.5 19.2 %all_to_all.20 = bf16[8,12,3266]{2,1,0:T(8,128)(2,1)S(1)} all-to-all(bf16[8,12,3266]{2,1,0:T(8,128)(2,1)S(1)} %reshape.253), channel_id=1, replica_groups=mesh['fsdp'=8,'tensor'=2,'context'=8] {'context'}, dimensions={0} | all-to-all | bytes 1254144 | tf_op jit(solution)/shard_map/all_to_all | solution.py:86
  315.9 3.5 %all-to-all-start.3 = ((bf16[8,12,3266]{2,1,0:T(8,128)(2,1)}), bf16[8,12,3266]{2,1,0:T(8,128)(2,1)S(1)}, u32[]{:S(2)}, u32[]{:S(2)}) async-start(bf16[8,12,3266]{2,1,0:T(8,128)(2,1)} %broadcast_in_dim.102), calls=%async_computation.4 | async-start | bytes 1703936 | tf_op jit(solution)/shard_map/all_to_all | solution.py:79
  319.4 2.2 fusion.27
  321.7 9.6 %all-to-all-done.3 = bf16[8,12,3266]{2,1,0:T(8,128)(2,1)S(1)} async-done(((bf16[8,12,3266]{2,1,0:T(8,128)(2,1)}), bf16[8,12,3266]{2,1,0:T(8,128)(2,1)S(1)}, u32[]{:S(2)}, u32[]{:S(2)}) %all-to-all-start.3) | async-done | bytes 627104 | tf_op jit(solution)/shard_map/all_to_all | solution.py:79
  334.1 1.1 reshape.255
  (133 shorter events, 25.9 us)
Async XLA Ops:
  7.2 30.9 %all-gather.3.cloned.1.call-start = ((), (), s32[]{:S(2)}) async-start(), calls=%async_computation.5 | async-start | bytes 2211840 | tf_op jit(solution)/shard_map/all_gather | solution.py:115
  14.6 27.5 %copy-start.28 = (f32[256]{0:T(256)}, f32[256]{0:T(256)S(1)}, u32[]{:S(2)}) copy-start(f32[256]{0:T(256)S(1)} %add_rsqrt_fusion.1) | copy-start | bytes 3076
  14.8 28.0 %copy-start.20 = (f32[256,32]{0,1:T(8,128)}, f32[256,32]{0,1:T(8,128)S(1)}, u32[]{:S(2)}) copy-start(f32[256,32]{0,1:T(8,128)S(1)} %get-tuple-element.84) | copy-start | bytes 98308
  14.8 28.0 %copy-start.22 = (f32[256,32]{0,1:T(8,128)}, f32[256,32]{0,1:T(8,128)S(1)}, u32[]{:S(2)}) copy-start(f32[256,32]{0,1:T(8,128)S(1)} %get-tuple-element.85) | copy-start | bytes 98308
  44.8 8.2 %copy-start.25 = (bf16[576,96]{0,1:T(8,128)(2,1)S(1)}, bf16[576,96]{0,1:T(8,128)(2,1)}, u32[]{:S(2)}) copy-start(bf16[576,96]{0,1:T(8,128)(2,1)} %param.16) | copy-start | bytes 331780
  44.8 47.1 %all-to-all-start = ((bf16[8,256,768]{1,2,0:T(8,128)(2,1)}), bf16[8,256,768]{1,2,0:T(8,128)(2,1)S(1)}, u32[]{:S(2)}, u32[]{:S(2)}) async-start(bf16[8,256,768]{1,2,0:T(8,128)(2,1)} %broadcast_in_dim.55), calls=%async_computation | async-start | bytes 6291456 | tf_op jit(solution)/shard_map/all_to_all | solution.py:79
  51.8 61.1 %all-gather.5.cloned.1.call-start = ((), (), s32[]{:S(2)}) async-start(), calls=%async_computation.6 | async-start | bytes 3760128 | tf_op jit(solution)/shard_map/all_gather | solution.py:128
  98.1 3.4 %copy-start.15 = (bf16[256,6,32]{0,2,1:T(8,128)(2,1)S(1)}, bf16[256,6,32]{0,2,1:T(8,128)(2,1)}, u32[]{:S(2)}) copy-start(bf16[256,6,32]{0,2,1:T(8,128)(2,1)} %get-tuple-element.76) | copy-start | bytes 294916
  98.1 3.4 %copy-start.17 = (bf16[256,6,32]{0,2,1:T(8,128)(2,1)S(1)}, bf16[256,6,32]{0,2,1:T(8,128)(2,1)}, u32[]{:S(2)}) copy-start(bf16[256,6,32]{0,2,1:T(8,128)(2,1)} %get-tuple-element.77) | copy-start | bytes 294916
  101.5 3.6 %copy-start.3 = (pred[256,2048]{1,0:T(8,128)(4,1)S(1)}, pred[256,2048]{1,0:T(8,128)(4,1)}, u32[]{:S(2)}) copy-start(pred[256,2048]{1,0:T(8,128)(4,1)} %broadcast_compare_fusion) | copy-start | bytes 1572868
  105.1 4.7 %copy-start = (f32[6,256,2048]{2,1,0:T(8,128)}, f32[6,256,2048]{2,1,0:T(8,128)S(1)}, u32[]{:S(2)}) copy-start(f32[6,256,2048]{2,1,0:T(8,128)S(1)} %get-tuple-element.87) | copy-start | bytes 37748740
  105.1 4.7 %copy-start.9 = (bf16[2048,384]{0,1:T(8,128)(2,1)S(1)}, bf16[2048,384]{0,1:T(8,128)(2,1)}, u32[]{:S(2)}) copy-start(bf16[2048,384]{0,1:T(8,128)(2,1)} %copy.88) | copy-start | bytes 4718596
  109.1 3.7 %copy-start.30 = (f32[6,256]{1,0:T(8,128)}, f32[6,256]{1,0:T(8,128)S(1)}, u32[]{:S(2)}) copy-start(f32[6,256]{1,0:T(8,128)S(1)} %log_add_fusion) | copy-start | bytes 18436
  109.8 23.5 %copy-start.2 = (bf16[256,768]{1,0:T(8,128)(2,1)S(1)}, bf16[256,768]{1,0:T(8,128)(2,1)}, u32[]{:S(2)}) copy-start(bf16[256,768]{1,0:T(8,128)(2,1)} %param.9) | copy-start | bytes 1179652
  112.8 2.5 copy-start.7
  112.9 20.9 %copy-start.5 = (bf16[768,2112]{1,0:T(8,128)(2,1)S(1)}, bf16[768,2112]{1,0:T(8,128)(2,1)}, u32[]{:S(2)}) copy-start(bf16[768,2112]{1,0:T(8,128)(2,1)} %all-gather.5.cloned.1.call-done) | copy-start | bytes 9732100
  114.5 20.2 %copy-start.14 = (bf16[256,768]{1,0:T(8,128)(2,1)S(1)}, bf16[256,768]{1,0:T(8,128)(2,1)}, u32[]{:S(2)}) copy-start(bf16[256,768]{1,0:T(8,128)(2,1)} %param.17) | copy-start | bytes 1179652
  114.5 18.8 %collective-permute-start = (f32[256,768]{1,0:T(8,128)S(1)}, f32[256,768]{1,0:T(8,128)S(1)}, u32[]{:S(2)}, u32[]{:S(2)}) collective-permute-start(f32[256,768]{1,0:T(8,128)S(1)} %fusion.40), channel_id=1, source_target_pairs={{0,8},{8,0},{1,9},{9,1},{2,10},{10,2},{3,11},{11,3},{4,12},{12,4},... | collective-permute-start | bytes 2359304 | tf_op jit(solution)/shard_map/ppermute | solution.py:72
  133.7 28.5 %copy-start.27 = (f32[256]{0:T(256)}, f32[256]{0:T(256)S(1)}, u32[]{:S(2)}) copy-start(f32[256]{0:T(256)S(1)} %add_rsqrt_fusion) | copy-start | bytes 3076
  135.3 2.0 copy-start.24
  135.4 22.2 %copy-start.6 = (bf16[256,2,576]{0,2,1:T(8,128)(2,1)}, bf16[256,2,576]{0,2,1:T(8,128)(2,1)S(1)}, u32[]{:S(2)}) copy-start(bf16[256,2,576]{0,2,1:T(8,128)(2,1)S(1)} %pad_maximum_fusion.1) | copy-start | bytes 1769476
  136.1 20.6 %collective-permute-start.2 = (f32[256,768]{1,0:T(8,128)S(1)}, f32[256,768]{1,0:T(8,128)S(1)}, u32[]{:S(2)}, u32[]{:S(2)}) collective-permute-start(f32[256,768]{1,0:T(8,128)S(1)} %fusion.1), channel_id=1, source_target_pairs={{0,8},{8,0},{1,9},{9,1},{2,10},{10,2},{3,11},{11,3},{4,12},{12,4},... | collective-permute-start | bytes 2359304 | tf_op jit(solution)/shard_map/ppermute | solution.py:72
  137.3 24.9 %collective-permute-start.1 = (bf16[256,768]{1,0:T(8,128)(2,1)S(1)}, bf16[256,768]{1,0:T(8,128)(2,1)S(1)}, u32[]{:S(2)}, u32[]{:S(2)}) collective-permute-start(bf16[256,768]{1,0:T(8,128)(2,1)S(1)} %convolution_convert_fusion.5), channel_id=1, source_target_pairs={{0,8},{8,0},{1,9},{9,1},{2,10},{10,2},{3,11},{11,3},{4,12},{12,4},... | collective-permute-start | bytes 1179656 | tf_op jit(solution)/shard_map/ppermute | solution.py:72
  167.2 7.6 %copy-start.4 = (pred[256,2048]{1,0:T(8,128)(4,1)S(1)}, pred[256,2048]{1,0:T(8,128)(4,1)}, u32[]{:S(2)}) copy-start(pred[256,2048]{1,0:T(8,128)(4,1)} %broadcast_compare_fusion) | copy-start | bytes 1572868
  167.2 7.6 %copy-start.10 = (bf16[2048,384]{0,1:T(8,128)(2,1)S(1)}, bf16[2048,384]{0,1:T(8,128)(2,1)}, u32[]{:S(2)}) copy-start(bf16[2048,384]{0,1:T(8,128)(2,1)} %copy.88) | copy-start | bytes 4718596
  167.2 7.6 %copy-start.19 = (bf16[256,384]{0,1:T(8,128)(2,1)S(1)}, bf16[256,384]{0,1:T(8,128)(2,1)}, u32[]{:S(2)}) copy-start(bf16[256,384]{0,1:T(8,128)(2,1)} %copy.91) | copy-start | bytes 589828
  167.2 7.6 %copy-start.31 = (f32[6,256]{1,0:T(8,128)S(1)}, f32[6,256]{1,0:T(8,128)}, u32[]{:S(2)}) copy-start(f32[6,256]{1,0:T(8,128)} %copy-done.30) | copy-start | bytes 18436
  174.8 7.8 %copy-start.16 = (bf16[256,6,32]{0,2,1:T(8,128)(2,1)S(1)}, bf16[256,6,32]{0,2,1:T(8,128)(2,1)}, u32[]{:S(2)}) copy-start(bf16[256,6,32]{0,2,1:T(8,128)(2,1)} %get-tuple-element.76) | copy-start | bytes 294916
  174.8 7.8 %copy-start.18 = (bf16[256,6,32]{0,2,1:T(8,128)(2,1)S(1)}, bf16[256,6,32]{0,2,1:T(8,128)(2,1)}, u32[]{:S(2)}) copy-start(bf16[256,6,32]{0,2,1:T(8,128)(2,1)} %get-tuple-element.77) | copy-start | bytes 294916
  182.6 2.7 copy-start.1
  188.7 42.9 %all-to-all-start.1 = ((bf16[8,256,768]{1,2,0:T(8,128)(2,1)}), bf16[8,256,768]{1,2,0:T(8,128)(2,1)}, u32[]{:S(2)}, u32[]{:S(2)}) async-start(bf16[8,256,768]{1,2,0:T(8,128)(2,1)} %pad_maximum_fusion), calls=%async_computation.1 | async-start | bytes 6291456 | tf_op jit(solution)/shard_map/all_to_all | solution.py:86
  193.4 100.7 %reduce-scatter.2.cloned.1.call-start = ((), (), s32[]{:S(2)}) async-start(), calls=%async_computation.7 | async-start | bytes 5750784 | tf_op jit(solution)/shard_map/reduce_scatter | solution.py:268
  206.3 27.8 %copy-start.21 = (f32[256,32]{0,1:T(8,128)S(1)}, f32[256,32]{0,1:T(8,128)}, u32[]{:S(2)}) copy-start(f32[256,32]{0,1:T(8,128)} %copy-done.20) | copy-start | bytes 98308
  206.3 27.8 %copy-start.23 = (f32[256,32]{0,1:T(8,128)S(1)}, f32[256,32]{0,1:T(8,128)}, u32[]{:S(2)}) copy-start(f32[256,32]{0,1:T(8,128)} %copy-done.22) | copy-start | bytes 98308
  234.0 1.5 copy-start.26
  234.1 2.9 copy-start.8
  234.3 3.9 %copy-start.32 = (bf16[768]{0:T(1024)(128)(2,1)S(1)}, bf16[768]{0:T(1024)(128)(2,1)}, u32[]{:S(2)}) copy-start(bf16[768]{0:T(1024)(128)(2,1)} %get-tuple-element.50) | copy-start | bytes 4612
  234.3 4.8 %copy-start.29 = (f32[256]{0:T(256)S(1)}, f32[256]{0:T(256)}, u32[]{:S(2)}) copy-start(f32[256]{0:T(256)} %copy-done.28) | copy-start | bytes 3076
  236.3 8.1 %copy-start.11 = (bf16[256,768]{1,0:T(8,128)(2,1)}, bf16[256,768]{1,0:T(8,128)(2,1)S(1)}, u32[]{:S(2)}) copy-start(bf16[256,768]{1,0:T(8,128)(2,1)S(1)} %fusion.10) | copy-start | bytes 1179652
  236.3 8.1 %collective-permute-start.3 = (bf16[256,768]{1,0:T(8,128)(2,1)S(1)}, bf16[256,768]{1,0:T(8,128)(2,1)S(1)}, u32[]{:S(2)}, u32[]{:S(2)}) collective-permute-start(bf16[256,768]{1,0:T(8,128)(2,1)S(1)} %fusion.10), channel_id=1, source_target_pairs={{0,8},{8,0},{1,9},{9,1},{2,10},{10,2},{3,11},{11,3},{4,12},{12,4},... | collective-permute-start | bytes 1179656 | tf_op jit(solution)/shard_map/ppermute | solution.py:72
  244.4 0.7 copy-start.13
  255.3 64.1 %copy-start.12 = (bf16[256,768]{1,0:T(8,128)(2,1)S(1)}, bf16[256,768]{1,0:T(8,128)(2,1)}, u32[]{:S(2)}) copy-start(bf16[256,768]{1,0:T(8,128)(2,1)} %copy-done.11) | copy-start | bytes 1179652
  315.9 15.4 %all-to-all-start.3 = ((bf16[8,12,3266]{2,1,0:T(8,128)(2,1)}), bf16[8,12,3266]{2,1,0:T(8,128)(2,1)S(1)}, u32[]{:S(2)}, u32[]{:S(2)}) async-start(bf16[8,12,3266]{2,1,0:T(8,128)(2,1)} %broadcast_in_dim.102), calls=%async_computation.4 | async-start | bytes 1703936 | tf_op jit(solution)/shard_map/all_to_all | solution.py:79
Sparse Core Ops, SparseCore 0:
  10.7 27.3 all-gather.2
  54.9 29.0 all-gather.4
  255.4 38.6 reduce-scatter.1

commit v6 on v5

--- a/solution.py
+++ b/solution.py
@@ -255,33 +255,32 @@
     )
     attngain_grad = jnp.sum(attn_in_grad * normed_attn, axis=0)
     input_grad = resid_grad + norm_back(attn_in_grad, normed_attn, spread_attn, attn_scale)
-    grads = (
-        attngain_grad[:, None],
-        mlpgain_grad[:, None],
-        qkv_grad.reshape(feature_count, 3 * local_width),
-        gelu_grad.reshape(feature_count, 2 * hidden),
-        proj_grad_t,
-        down_grad_t,
-    )
-    widths = [g.shape[1] for g in grads]
-    packed = jnp.concatenate(grads, axis=1).astype(jnp.bfloat16)
-    packed = lax.psum_scatter(packed, "fsdp", scatter_dimension=0, tiled=True)
-    packed = context_gather(
-        context_scatter_sum(packed, "context").astype(jnp.bfloat16), "context"
-    ).astype(jnp.float32)
-    pieces = []
-    start = 0
-    for width in widths:
-        pieces.append(packed[:, start : start + width])
-        start += width
-    shard_rows = packed.shape[0]
+    def reduce_pack(members):
+        packed = jnp.concatenate(members, axis=1).astype(jnp.bfloat16)
+        packed = lax.psum_scatter(packed, "fsdp", scatter_dimension=0, tiled=True)
+        packed = context_gather(
+            context_scatter_sum(packed, "context").astype(jnp.bfloat16), "context"
+        ).astype(jnp.float32)
+        pieces = []
+        start = 0
+        for member in members:
+            pieces.append(packed[:, start : start + member.shape[1]])
+            start += member.shape[1]
+        return pieces
+
+    mlp_pieces = reduce_pack(
+        [mlpgain_grad[:, None], gelu_grad.reshape(feature_count, 2 * hidden), down_grad_t]
+    )
+    attn_pieces = reduce_pack(
+        [attngain_grad[:, None], qkv_grad.reshape(feature_count, 3 * local_width), proj_grad_t]
+    )
     shares = (
-        pieces[0][:, 0],
-        pieces[2].reshape(shard_rows, 3, local_width),
-        pieces[4].T,
-        pieces[1][:, 0],
-        pieces[3].reshape(shard_rows, 2, hidden),
-        pieces[5].T,
+        attn_pieces[0][:, 0],
+        attn_pieces[1].reshape(shard_rows, 3, local_width),
+        attn_pieces[2].T,
+        mlp_pieces[0][:, 0],
+        mlp_pieces[1].reshape(shard_rows, 2, hidden),
+        mlp_pieces[2].T,
     )
     return (
         block_output,

time: 347 us -> 337 us (0.971)
  waiting for transfers between devices: 178 us -> 159 us
  starting transfers between devices: 19.2 us -> 29 us
    reduce_scatter x1 -> x2, waiting for transfers between devices: 38.8 us -> 12.8 us  [reduce_pack(): packed = lax.psum_scatter(packed, 'fsdp', scatter_dimension=0, tiled=True)]
    all_to_all x1 -> x2, waiting for transfers between devices: 25.3 us -> 41.3 us  [context_scatter_sum(): lax.all_to_all(values.reshape((count, rows) + values.shape[1:]), axis_nam...]
    all_to_all x1 -> x2, starting transfers between devices: 4.65 us -> 11.1 us  [context_scatter_sum(): lax.all_to_all(values.reshape((count, rows) + values.shape[1:]), axis_nam...]
    ppermute x4, waiting for transfers between devices: 44.9 us -> 39 us  [pair_sum(): other = lax.ppermute(values, axis_name, perm=[(0, 1), (1, 0)])]
    all_to_all x2 -> x3, starting transfers between devices: 10.6 us -> 13.9 us  [context_gather(): gathered = lax.all_to_all(spread, axis_name, 0, 0, tiled=True)]
    all_to_all x2 -> x3, waiting for transfers between devices: 45.6 us -> 42.7 us  [context_gather(): gathered = lax.all_to_all(spread, axis_name, 0, 0, tiled=True)]
    concatenate x1 -> x2, local copies, waits for them, and re-layouts: 9.96 us -> 10.8 us  [reduce_pack(): packed = jnp.concatenate(members, axis=1).astype(jnp.bfloat16)]
  transfers between devices with their start and end apart: 10 -> 13, of which waited for: 9 -> 10; matrix products, arithmetic and copies ran while one was open for 14% -> 25% of each run, Pallas kernels for 0% -> 0%
where the time goes in v6:
time: 337 us; the launch traced here: 335 us
  waiting for transfers between devices  159 us (47%)
  matrix products  46 us (14%)
  local copies, waits for them, and re-layouts  44.5 us (13%)
  starting transfers between devices  29 us (9%)
  other arithmetic  26.3 us (8%)
  blocking collectives  15.8 us (5%)
  between operations  14.5 us (4%)
    all_to_all x3, waiting for transfers between devices, context_gather(): gathered = lax.all_to_all(spread, axis_name, 0, 0, tiled=True)  42.7 us
    all_to_all x2, waiting for transfers between devices, context_scatter_sum(): lax.all_to_all(values.reshape((count, rows) + values.shape[1:]), axis_nam...  41.3 us
    ppermute x4, waiting for transfers between devices, pair_sum(): other = lax.ppermute(values, axis_name, perm=[(0, 1), (1, 0)])  39 us
    all_gather x1, waiting for transfers between devices, on_device(): lax.all_gather(jnp.concatenate([qkv_weight.reshape(shard_rows, 3 * local_...  23.2 us
    all_to_all x1, blocking collectives, context_scatter_sum(): lax.all_to_all(values.reshape((count, rows) + values.shape[1:]), axis_nam...  15.8 us
    all_to_all x3, starting transfers between devices, context_gather(): gathered = lax.all_to_all(spread, axis_name, 0, 0, tiled=True)  13.9 us
    reduce_scatter x2, waiting for transfers between devices, reduce_pack(): packed = lax.psum_scatter(packed, 'fsdp', scatter_dimension=0, tiled=True)  12.8 us
    all_to_all x2, starting transfers between devices, context_scatter_sum(): lax.all_to_all(values.reshape((count, rows) + values.shape[1:]), axis_nam...  11.1 us
  transfers between devices with their start and end apart: 13, of which 10 were waited for; matrix products, arithmetic and copies ran while one was open for 25% of the time, Pallas kernels for 0%

profile of v6, /device:TPU:0, one launch (start us, length us, event | category | flops | bytes accessed | tf_op | source)
XLA Modules:
  0.0 335.3 jit_solution(4427643873821780797)
XLA Ops:
  13.4 1.2 fusion.29
  14.9 23.2 %all-gather.3.cloned.1.call-done = bf16[768,1154]{1,0:T(8,128)(2,1)} async-done(((bf16[96,1154]{1,0:T(8,128)(2,1)}), bf16[768,1154]{1,0:T(8,128)(2,1)}) %all-gather.3.cloned.1.call-update) | async-done | bytes 1772560 | tf_op jit(solution)/shard_map/all_gather | solution.py:115
  38.1 1.3 convert_reduce_fusion.2
  39.4 2.5 fusion.7
  42.8 1.9 broadcast_in_dim.57
  44.7 7.0 %all-to-all-start = ((bf16[8,256,768]{1,2,0:T(8,128)(2,1)}), bf16[8,256,768]{1,2,0:T(8,128)(2,1)S(1)}, u32[]{:S(2)}, u32[]{:S(2)}) async-start(bf16[8,256,768]{1,2,0:T(8,128)(2,1)} %broadcast_in_dim.57), calls=%async_computation | async-start | bytes 6291456 | tf_op jit(solution)/shard_map/all_to_all | solution.py:79
  52.9 1.7 pad_maximum_fusion.3
  56.0 35.9 %all-to-all-done = bf16[8,256,768]{1,2,0:T(8,128)(2,1)S(1)} async-done(((bf16[8,256,768]{1,2,0:T(8,128)(2,1)}), bf16[8,256,768]{1,2,0:T(8,128)(2,1)S(1)}, u32[]{:S(2)}, u32[]{:S(2)}) %all-to-all-start) | async-done | bytes 3145760 | tf_op jit(solution)/shard_map/all_to_all | solution.py:79
  91.9 2.9 copy.87
  94.7 3.3 fusion.55
  98.1 1.7 copy.89
  99.8 1.7 copy.88
  101.5 3.6 %select_reduce_fusion.1 = (f32[6,256]{1,0:T(8,128)S(1)}, f32[6,256,2048]{2,1,0:T(8,128)S(1)}) fusion(pred[256,2048]{1,0:T(8,128)(4,1)} %broadcast_compare_fusion, bf16[2048,6,64]{0,2,1:T(8,128)(2,1)S(1)} %bitcast.117, bf16[256,6,32]{0,2,1:T(8,128)(2,1)S(1)} %copy-done.17, bf16[256,6,32]{0,2,1:T(8,128)(2,1)S(1)} %copy-done.15), kind=kOutput, calls=%fused_computation.3 | convolution fusion | flops 412482048 | bytes 14882816 | tf_op jit(solution)/shard_map/qhd,khd->hqk/dot_general | solution.py:162
  105.1 4.0 %select_reduce_fusion = f32[6,256]{1,0:T(8,128)S(1)} fusion(f32[6,256,2048]{2,1,0:T(8,128)S(1)} %get-tuple-element.83, f32[6,256]{1,0:T(8,128)S(1)} %get-tuple-element.82, pred[256,2048]{1,0:T(8,128)(4,1)S(1)} %copy-done.3), kind=kLoop, calls=%fused_computation.2 | loop fusion | flops 12581376 | bytes 13119488 | tf_op jit(solution)/shard_map/reduce_sum | solution.py:165
  109.8 3.0 convolution_convert_fusion.6
  112.9 1.6 fusion.40
  115.3 17.9 %collective-permute-done = f32[256,768]{1,0:T(8,128)S(1)} collective-permute-done((f32[256,768]{1,0:T(8,128)S(1)}, f32[256,768]{1,0:T(8,128)S(1)}, u32[]{:S(2)}, u32[]{:S(2)}) %collective-permute-start) | collective-permute-done | bytes 786464 | tf_op jit(solution)/shard_map/ppermute | solution.py:72
  135.3 1.6 fusion.1
  137.6 1.3 convolution_convert_fusion.5
  138.8 1.4 collective-permute-start.1
  140.3 1.3 fusion.9
  141.6 2.2 copy.97
  143.8 2.1 convolution_convert_fusion
  146.0 11.8 %collective-permute-done.2 = f32[256,768]{1,0:T(8,128)} collective-permute-done((f32[256,768]{1,0:T(8,128)}, f32[256,768]{1,0:T(8,128)}, u32[]{:S(2)}, u32[]{:S(2)}) %collective-permute-start.2) | collective-permute-done | bytes 786464 | tf_op jit(solution)/shard_map/ppermute | solution.py:72
  157.8 2.4 multiply_reduce_fusion
  160.1 3.2 collective-permute-done.1
  163.3 2.2 multiply_add_fusion
  165.5 1.4 convolution_convert_fusion.7
  169.1 5.9 %concatenate.53 = bf16[768,1729]{1,0:T(8,128)(2,1)} concatenate(bf16[768,1]{1,0:T(8,128)(2,1)S(1)} %broadcast_in_dim.111, bf16[768,1152]{1,0:T(8,128)(2,1)} %convolution_convert_fusion, bf16[768,576]{1,0:T(8,128)(2,1)} %copy.97), dimensions={1} | concatenate | bytes 5311488 | tf_op jit(solution)/shard_map/concatenate | solution.py:259
  175.0 8.2 %multiply_convert_fusion = bf16[6,256,2048]{2,1,0:T(8,128)(2,1)S(1)} fusion(f32[6,256,2048]{2,1,0:T(8,128)} %copy-done, f32[6,256]{1,0:T(8,128)S(1)} %bitcast.148, f32[6,256]{1,0:T(8,128)S(1)} %copy-done.33, pred[256,2048]{1,0:T(8,128)(4,1)S(1)} %copy-done.4, bf16[256,6,64]{0,2,1:T(8,128)(2,1)} %bitcast.140, bf16[2048,6,64]{0,2,1:T(8,128)(2,1)} %bitcast.130), kind=kOutput, calls=%fused_computation | convolution fusion | flops 421527552 | bytes 21180416 | tf_op jit(solution)/shard_map/qhd,khd->hqk/dot_general | solution.py:216
  183.3 9.8 %convolution_convert_fusion.2 = bf16[6,64,2048]{2,1,0:T(8,128)(2,1)S(1)} fusion(bf16[256,6,64]{0,2,1:T(8,128)(2,1)S(1)} %bitcast.141, f32[6,256,2048]{2,1,0:T(8,128)} %copy-done, f32[6,256]{1,0:T(8,128)S(1)} %copy-done.33, pred[256,2048]{1,0:T(8,128)(4,1)S(1)} %copy-done.4), kind=kOutput, calls=%fused_computation.10 | convolution fusion | flops 416022528 | bytes 14882816 | tf_op jit(solution)/shard_map/hqk,qhd->khd/dot_general | solution.py:228
  193.1 1.2 multiply_convert_fusion.1
  196.0 1.9 pad_maximum_fusion
  197.9 4.6 %all-to-all-start.1 = ((bf16[8,256,768]{1,2,0:T(8,128)(2,1)}), bf16[8,256,768]{1,2,0:T(8,128)(2,1)}, u32[]{:S(2)}, u32[]{:S(2)}) async-start(bf16[8,256,768]{1,2,0:T(8,128)(2,1)} %pad_maximum_fusion), calls=%async_computation.1 | async-start | bytes 6291456 | tf_op jit(solution)/shard_map/all_to_all | solution.py:86
  202.7 4.8 %fusion.13 = f32[256,6,64]{0,2,1:T(8,128)S(1)} fusion(bf16[2048,6,64]{0,2,1:T(8,128)(2,1)S(1)} %bitcast.118, bf16[6,256,2048]{2,1,0:T(8,128)(2,1)} %copy-done.1), kind=kOutput, calls=%fused_computation.26 | convolution fusion | flops 402751488 | bytes 8257536 | tf_op jit(solution)/shard_map/hqk,khd->qhd/dot_general | solution.py:221
  207.5 33.0 %all-to-all-done.1 = bf16[8,256,768]{1,2,0:T(8,128)(2,1)} async-done(((bf16[8,256,768]{1,2,0:T(8,128)(2,1)}), bf16[8,256,768]{1,2,0:T(8,128)(2,1)}, u32[]{:S(2)}, u32[]{:S(2)}) %all-to-all-start.1) | async-done | bytes 3145760 | tf_op jit(solution)/shard_map/all_to_all | solution.py:86
  240.6 2.4 convert_reduce_fusion
  247.3 6.1 %collective-permute-done.3 = bf16[256,768]{1,0:T(8,128)(2,1)S(1)} collective-permute-done((bf16[256,768]{1,0:T(8,128)(2,1)S(1)}, bf16[256,768]{1,0:T(8,128)(2,1)S(1)}, u32[]{:S(2)}, u32[]{:S(2)}) %collective-permute-start.3) | collective-permute-done | bytes 393248 | tf_op jit(solution)/shard_map/ppermute | solution.py:72
  255.2 4.9 %concatenate.52 = bf16[768,1537]{1,0:T(8,128)(2,1)} concatenate(bf16[768,1]{1,0:T(8,128)(2,1)} %broadcast_in_dim.110, bf16[768,1152]{1,0:T(8,128)(2,1)S(1)} %convolution_convert_fusion.1, bf16[768,384]{1,0:T(8,128)(2,1)S(1)} %convolution_convert_fusion.4), dimensions={1} | concatenate | bytes 4721664 | tf_op jit(solution)/shard_map/concatenate | solution.py:259
  261.3 15.8 %all_to_all.30 = bf16[8,12,1729]{2,1,0:T(8,128)(2,1)S(1)} all-to-all(bf16[8,12,1729]{2,1,0:T(8,128)(2,1)S(1)} %reshape.262), channel_id=1, replica_groups=mesh['fsdp'=8,'tensor'=2,'context'=8] {'context'}, dimensions={0} | all-to-all | bytes 663936 | tf_op jit(solution)/shard_map/all_to_all | solution.py:86
  278.0 3.5 %all-to-all-start.5 = ((bf16[8,12,1729]{2,1,0:T(8,128)(2,1)}), bf16[8,12,1729]{2,1,0:T(8,128)(2,1)S(1)}, u32[]{:S(2)}, u32[]{:S(2)}) async-start(bf16[8,12,1729]{2,1,0:T(8,128)(2,1)} %broadcast_in_dim.109), calls=%async_computation.7 | async-start | bytes 917504 | tf_op jit(solution)/shard_map/all_to_all | solution.py:79
  281.5 12.8 %reduce-scatter.3.cloned.1.call-done = bf16[96,1537]{1,0:T(8,128)(2,1)} async-done(((bf16[768,1537]{1,0:T(8,128)(2,1)}), bf16[96,1537]{1,0:T(8,128)(2,1)}) %reduce-scatter.3.cloned.1.call-update) | async-done | bytes 295120 | tf_op jit(solution)/shard_map/reduce_scatter | solution.py:260
  294.3 1.8 reshape.260
  296.1 6.5 %all-to-all-start.2 = ((bf16[8,12,1537]{2,1,0:T(8,128)(2,1)}), bf16[8,12,1537]{2,1,0:T(8,128)(2,1)S(1)}, u32[]{:S(2)}, u32[]{:S(2)}) async-start(bf16[8,12,1537]{2,1,0:T(8,128)(2,1)} %reshape.260), calls=%async_computation.3 | async-start | bytes 851968 | tf_op jit(solution)/shard_map/all_to_all | solution.py:86
  302.7 1.2 fusion.27
  304.0 8.3 %all-to-all-done.2 = bf16[8,12,1537]{2,1,0:T(8,128)(2,1)S(1)} async-done(((bf16[8,12,1537]{2,1,0:T(8,128)(2,1)}), bf16[8,12,1537]{2,1,0:T(8,128)(2,1)S(1)}, u32[]{:S(2)}, u32[]{:S(2)}) %all-to-all-start.2) | async-done | bytes 295136 | tf_op jit(solution)/shard_map/all_to_all | solution.py:86
  313.2 3.5 %all-to-all-start.3 = ((bf16[8,12,1537]{2,1,0:T(8,128)(2,1)}), bf16[8,12,1537]{2,1,0:T(8,128)(2,1)S(1)}, u32[]{:S(2)}, u32[]{:S(2)}) async-start(bf16[8,12,1537]{2,1,0:T(8,128)(2,1)} %broadcast_in_dim.107), calls=%async_computation.4 | async-start | bytes 851968 | tf_op jit(solution)/shard_map/all_to_all | solution.py:79
  319.4 6.8 %all-to-all-done.3 = bf16[8,12,1537]{2,1,0:T(8,128)(2,1)S(1)} async-done(((bf16[8,12,1537]{2,1,0:T(8,128)(2,1)}), bf16[8,12,1537]{2,1,0:T(8,128)(2,1)S(1)}, u32[]{:S(2)}, u32[]{:S(2)}) %all-to-all-start.3) | async-done | bytes 295136 | tf_op jit(solution)/shard_map/all_to_all | solution.py:79
  (157 shorter events, 32.4 us)
Async XLA Ops:
  7.2 30.9 %all-gather.3.cloned.1.call-start = ((), (), s32[]{:S(2)}) async-start(), calls=%async_computation.8 | async-start | bytes 2211840 | tf_op jit(solution)/shard_map/all_gather | solution.py:115
  11.5 30.4 %copy-start.30 = (s32[256]{0:T(256)}, s32[256]{0:T(256)S(1)}, u32[]{:S(2)}) copy-start(s32[256]{0:T(256)S(1)} %convert_reduce_fusion.5) | copy-start | bytes 3076
  14.6 27.4 %copy-start.28 = (f32[256]{0:T(256)}, f32[256]{0:T(256)S(1)}, u32[]{:S(2)}) copy-start(f32[256]{0:T(256)S(1)} %add_rsqrt_fusion.1) | copy-start | bytes 3076
  14.8 28.0 %copy-start.21 = (f32[256,32]{0,1:T(8,128)}, f32[256,32]{0,1:T(8,128)S(1)}, u32[]{:S(2)}) copy-start(f32[256,32]{0,1:T(8,128)S(1)} %get-tuple-element.80) | copy-start | bytes 98308
  14.8 27.9 %copy-start.23 = (f32[256,32]{0,1:T(8,128)}, f32[256,32]{0,1:T(8,128)S(1)}, u32[]{:S(2)}) copy-start(f32[256,32]{0,1:T(8,128)S(1)} %get-tuple-element.81) | copy-start | bytes 98308
  44.7 8.2 %copy-start.25 = (bf16[576,96]{0,1:T(8,128)(2,1)S(1)}, bf16[576,96]{0,1:T(8,128)(2,1)}, u32[]{:S(2)}) copy-start(bf16[576,96]{0,1:T(8,128)(2,1)} %param.16) | copy-start | bytes 331780
  44.7 10.0 %copy-start.37 = (s32[3,1]{0,1:T(1,128)S(1)}, s32[3,1]{0,1:T(1,128)}, u32[]{:S(2)}) copy-start(s32[3,1]{0,1:T(1,128)} %copy-done.36) | copy-start | bytes 40
  44.7 10.1 %copy-start.31 = (s32[256]{0:T(256)S(1)}, s32[256]{0:T(256)}, u32[]{:S(2)}) copy-start(s32[256]{0:T(256)} %copy-done.30) | copy-start | bytes 3076
  44.7 47.1 %all-to-all-start = ((bf16[8,256,768]{1,2,0:T(8,128)(2,1)}), bf16[8,256,768]{1,2,0:T(8,128)(2,1)S(1)}, u32[]{:S(2)}, u32[]{:S(2)}) async-start(bf16[8,256,768]{1,2,0:T(8,128)(2,1)} %broadcast_in_dim.57), calls=%async_computation | async-start | bytes 6291456 | tf_op jit(solution)/shard_map/all_to_all | solution.py:79
  51.7 61.1 %all-gather.5.cloned.1.call-start = ((), (), s32[]{:S(2)}) async-start(), calls=%async_computation.9 | async-start | bytes 3760128 | tf_op jit(solution)/shard_map/all_gather | solution.py:128
  54.6 205.5 %reduce-scatter.5.cloned.1.call-start = ((), (), s32[]{:S(2)}) async-start(), calls=%async_computation.11 | async-start | bytes 3096576 | tf_op jit(solution)/shard_map/reduce_scatter | solution.py:260
  98.1 3.4 %copy-start.15 = (bf16[256,6,32]{0,2,1:T(8,128)(2,1)S(1)}, bf16[256,6,32]{0,2,1:T(8,128)(2,1)}, u32[]{:S(2)}) copy-start(bf16[256,6,32]{0,2,1:T(8,128)(2,1)} %get-tuple-element.72) | copy-start | bytes 294916
  98.1 3.4 %copy-start.17 = (bf16[256,6,32]{0,2,1:T(8,128)(2,1)S(1)}, bf16[256,6,32]{0,2,1:T(8,128)(2,1)}, u32[]{:S(2)}) copy-start(bf16[256,6,32]{0,2,1:T(8,128)(2,1)} %get-tuple-element.73) | copy-start | bytes 294916
  101.5 3.6 %copy-start.3 = (pred[256,2048]{1,0:T(8,128)(4,1)S(1)}, pred[256,2048]{1,0:T(8,128)(4,1)}, u32[]{:S(2)}) copy-start(pred[256,2048]{1,0:T(8,128)(4,1)} %broadcast_compare_fusion) | copy-start | bytes 1572868
  105.1 4.7 %copy-start = (f32[6,256,2048]{2,1,0:T(8,128)}, f32[6,256,2048]{2,1,0:T(8,128)S(1)}, u32[]{:S(2)}) copy-start(f32[6,256,2048]{2,1,0:T(8,128)S(1)} %get-tuple-element.83) | copy-start | bytes 37748740
  105.1 4.7 %copy-start.8 = (bf16[2048,384]{0,1:T(8,128)(2,1)S(1)}, bf16[2048,384]{0,1:T(8,128)(2,1)}, u32[]{:S(2)}) copy-start(bf16[2048,384]{0,1:T(8,128)(2,1)} %copy.88) | copy-start | bytes 4718596
  109.1 3.7 %copy-start.32 = (f32[6,256]{1,0:T(8,128)}, f32[6,256]{1,0:T(8,128)S(1)}, u32[]{:S(2)}) copy-start(f32[6,256]{1,0:T(8,128)S(1)} %log_add_fusion) | copy-start | bytes 18436
  109.8 23.5 %copy-start.2 = (bf16[256,768]{1,0:T(8,128)(2,1)S(1)}, bf16[256,768]{1,0:T(8,128)(2,1)}, u32[]{:S(2)}) copy-start(bf16[256,768]{1,0:T(8,128)(2,1)} %param.9) | copy-start | bytes 1179652
  112.8 2.5 copy-start.6
  112.9 20.9 %copy-start.5 = (bf16[768,2112]{1,0:T(8,128)(2,1)S(1)}, bf16[768,2112]{1,0:T(8,128)(2,1)}, u32[]{:S(2)}) copy-start(bf16[768,2112]{1,0:T(8,128)(2,1)} %all-gather.5.cloned.1.call-done) | copy-start | bytes 9732100
  114.5 20.2 %copy-start.13 = (bf16[256,768]{1,0:T(8,128)(2,1)S(1)}, bf16[256,768]{1,0:T(8,128)(2,1)}, u32[]{:S(2)}) copy-start(bf16[256,768]{1,0:T(8,128)(2,1)} %param.17) | copy-start | bytes 1179652
  114.5 18.8 %collective-permute-start = (f32[256,768]{1,0:T(8,128)S(1)}, f32[256,768]{1,0:T(8,128)S(1)}, u32[]{:S(2)}, u32[]{:S(2)}) collective-permute-start(f32[256,768]{1,0:T(8,128)S(1)} %fusion.40), channel_id=1, source_target_pairs={{0,8},{8,0},{1,9},{9,1},{2,10},{10,2},{3,11},{11,3},{4,12},{12,4},... | collective-permute-start | bytes 2359304 | tf_op jit(solution)/shard_map/ppermute | solution.py:72
  133.7 24.1 %copy-start.27 = (f32[256]{0:T(256)}, f32[256]{0:T(256)S(1)}, u32[]{:S(2)}) copy-start(f32[256]{0:T(256)S(1)} %add_rsqrt_fusion) | copy-start | bytes 3076
  137.0 20.8 %collective-permute-start.2 = (f32[256,768]{1,0:T(8,128)}, f32[256,768]{1,0:T(8,128)}, u32[]{:S(2)}, u32[]{:S(2)}) collective-permute-start(f32[256,768]{1,0:T(8,128)} %fusion.1), channel_id=1, source_target_pairs={{0,8},{8,0},{1,9},{9,1},{2,10},{10,2},{3,11},{11,3},{4,12},{12,4},... | collective-permute-start | bytes 2359304 | tf_op jit(solution)/shard_map/ppermute | solution.py:72
  138.8 24.5 %collective-permute-start.1 = (bf16[256,768]{1,0:T(8,128)(2,1)}, bf16[256,768]{1,0:T(8,128)(2,1)}, u32[]{:S(2)}, u32[]{:S(2)}) collective-permute-start(bf16[256,768]{1,0:T(8,128)(2,1)} %convolution_convert_fusion.5), channel_id=1, source_target_pairs={{0,8},{8,0},{1,9},{9,1},{2,10},{10,2},{3,11},{11,3},{4,12},{12,4},... | collective-permute-start | bytes 1179656 | tf_op jit(solution)/shard_map/ppermute | solution.py:72
  143.8 19.5 %copy-start.14 = (bf16[256,768]{1,0:T(8,128)(2,1)S(1)}, bf16[256,768]{1,0:T(8,128)(2,1)}, u32[]{:S(2)}) copy-start(bf16[256,768]{1,0:T(8,128)(2,1)} %param.17) | copy-start | bytes 1179652
  169.1 6.0 %copy-start.4 = (pred[256,2048]{1,0:T(8,128)(4,1)S(1)}, pred[256,2048]{1,0:T(8,128)(4,1)}, u32[]{:S(2)}) copy-start(pred[256,2048]{1,0:T(8,128)(4,1)} %broadcast_compare_fusion) | copy-start | bytes 1572868
  169.1 6.0 %copy-start.33 = (f32[6,256]{1,0:T(8,128)S(1)}, f32[6,256]{1,0:T(8,128)}, u32[]{:S(2)}) copy-start(f32[6,256]{1,0:T(8,128)} %copy-done.32) | copy-start | bytes 18436
  175.0 8.2 %copy-start.20 = (bf16[256,384]{0,1:T(8,128)(2,1)S(1)}, bf16[256,384]{0,1:T(8,128)(2,1)}, u32[]{:S(2)}) copy-start(bf16[256,384]{0,1:T(8,128)(2,1)} %copy-done.19) | copy-start | bytes 589828
  183.3 9.8 %copy-start.1 = (bf16[6,256,2048]{2,1,0:T(8,128)(2,1)}, bf16[6,256,2048]{2,1,0:T(8,128)(2,1)S(1)}, u32[]{:S(2)}) copy-start(bf16[6,256,2048]{2,1,0:T(8,128)(2,1)S(1)} %multiply_convert_fusion) | copy-start | bytes 18874372
  183.3 9.8 %copy-start.16 = (bf16[256,6,32]{0,2,1:T(8,128)(2,1)S(1)}, bf16[256,6,32]{0,2,1:T(8,128)(2,1)}, u32[]{:S(2)}) copy-start(bf16[256,6,32]{0,2,1:T(8,128)(2,1)} %get-tuple-element.72) | copy-start | bytes 294916
  183.3 9.8 %copy-start.18 = (bf16[256,6,32]{0,2,1:T(8,128)(2,1)S(1)}, bf16[256,6,32]{0,2,1:T(8,128)(2,1)}, u32[]{:S(2)}) copy-start(bf16[256,6,32]{0,2,1:T(8,128)(2,1)} %get-tuple-element.73) | copy-start | bytes 294916
  197.9 42.7 %all-to-all-start.1 = ((bf16[8,256,768]{1,2,0:T(8,128)(2,1)}), bf16[8,256,768]{1,2,0:T(8,128)(2,1)}, u32[]{:S(2)}, u32[]{:S(2)}) async-start(bf16[8,256,768]{1,2,0:T(8,128)(2,1)} %pad_maximum_fusion), calls=%async_computation.1 | async-start | bytes 6291456 | tf_op jit(solution)/shard_map/all_to_all | solution.py:86
  202.4 91.9 %reduce-scatter.3.cloned.1.call-start = ((), (), s32[]{:S(2)}) async-start(), calls=%async_computation.10 | async-start | bytes 2875392 | tf_op jit(solution)/shard_map/reduce_scatter | solution.py:260
  207.5 35.5 %copy-start.22 = (f32[256,32]{0,1:T(8,128)S(1)}, f32[256,32]{0,1:T(8,128)}, u32[]{:S(2)}) copy-start(f32[256,32]{0,1:T(8,128)} %copy-done.21) | copy-start | bytes 98308
  207.5 35.6 %copy-start.24 = (f32[256,32]{0,1:T(8,128)S(1)}, f32[256,32]{0,1:T(8,128)}, u32[]{:S(2)}) copy-start(f32[256,32]{0,1:T(8,128)} %copy-done.23) | copy-start | bytes 98308
  243.0 1.5 copy-start.26
  243.1 2.9 copy-start.7
  243.3 3.1 copy-start.29
  245.3 8.1 %copy-start.9 = (bf16[256,768]{1,0:T(8,128)(2,1)}, bf16[256,768]{1,0:T(8,128)(2,1)S(1)}, u32[]{:S(2)}) copy-start(bf16[256,768]{1,0:T(8,128)(2,1)S(1)} %fusion.10) | copy-start | bytes 1179652
  245.3 8.0 %collective-permute-start.3 = (bf16[256,768]{1,0:T(8,128)(2,1)S(1)}, bf16[256,768]{1,0:T(8,128)(2,1)S(1)}, u32[]{:S(2)}, u32[]{:S(2)}) collective-permute-start(bf16[256,768]{1,0:T(8,128)(2,1)S(1)} %fusion.10), channel_id=1, source_target_pairs={{0,8},{8,0},{1,9},{9,1},{2,10},{10,2},{3,11},{11,3},{4,12},{12,4},... | collective-permute-start | bytes 1179656 | tf_op jit(solution)/shard_map/ppermute | solution.py:72
  260.1 21.4 %copy-start.35 = (f32[256]{0:T(256)S(1)}, f32[256]{0:T(256)}, u32[]{:S(2)}) copy-start(f32[256]{0:T(256)} %get-tuple-element.53) | copy-start | bytes 3076
  260.1 21.4 %copy-start.34 = (f32[256]{0:T(256)S(1)}, f32[256]{0:T(256)}, u32[]{:S(2)}) copy-start(f32[256]{0:T(256)} %get-tuple-element.54) | copy-start | bytes 3076
  260.1 42.5 %copy-start.10 = (bf16[256,768]{1,0:T(8,128)(2,1)S(1)}, bf16[256,768]{1,0:T(8,128)(2,1)}, u32[]{:S(2)}) copy-start(bf16[256,768]{1,0:T(8,128)(2,1)} %copy-done.9) | copy-start | bytes 1179652
  260.1 42.5 %copy-start.12 = (bf16[256,768]{1,0:T(8,128)(2,1)S(1)}, bf16[256,768]{1,0:T(8,128)(2,1)}, u32[]{:S(2)}) copy-start(bf16[256,768]{1,0:T(8,128)(2,1)} %copy-done.11) | copy-start | bytes 1179652
  278.0 18.1 %all-to-all-start.5 = ((bf16[8,12,1729]{2,1,0:T(8,128)(2,1)}), bf16[8,12,1729]{2,1,0:T(8,128)(2,1)S(1)}, u32[]{:S(2)}, u32[]{:S(2)}) async-start(bf16[8,12,1729]{2,1,0:T(8,128)(2,1)} %broadcast_in_dim.109), calls=%async_computation.7 | async-start | bytes 917504 | tf_op jit(solution)/shard_map/all_to_all | solution.py:79
  296.1 16.2 %all-to-all-start.2 = ((bf16[8,12,1537]{2,1,0:T(8,128)(2,1)}), bf16[8,12,1537]{2,1,0:T(8,128)(2,1)S(1)}, u32[]{:S(2)}, u32[]{:S(2)}) async-start(bf16[8,12,1537]{2,1,0:T(8,128)(2,1)} %reshape.260), calls=%async_computation.3 | async-start | bytes 851968 | tf_op jit(solution)/shard_map/all_to_all | solution.py:86
  313.2 13.1 %all-to-all-start.3 = ((bf16[8,12,1537]{2,1,0:T(8,128)(2,1)}), bf16[8,12,1537]{2,1,0:T(8,128)(2,1)S(1)}, u32[]{:S(2)}, u32[]{:S(2)}) async-start(bf16[8,12,1537]{2,1,0:T(8,128)(2,1)} %broadcast_in_dim.107), calls=%async_computation.4 | async-start | bytes 851968 | tf_op jit(solution)/shard_map/all_to_all | solution.py:79
  (3 other events, 2.9 us)
Sparse Core Ops, SparseCore 0:
  10.7 27.3 all-gather.2
  54.8 29.0 all-gather.4
  175.1 32.8 reduce-scatter.4
  260.2 34.0 reduce-scatter.2

commit v7 on v6

--- a/solution.py
+++ b/solution.py
@@ -1,6 +1,10 @@
+import functools
+
 import jax
 import jax.numpy as jnp
 from jax import lax
+from jax.experimental import pallas as pl
+from jax.experimental.pallas import tpu as pltpu
 from jax.sharding import PartitionSpec as P
 
 HD = 64
@@ -73,19 +77,70 @@
     return values.astype(jnp.float32) + other.astype(jnp.float32)
 
 
+def exchange_kernel(same, axis_name, count, source, landed, send_sem, recv_sem):
+    me = lax.axis_index(axis_name)
+    barrier = pltpu.get_barrier_semaphore()
+    for step in range(1, count):
+        peer = lax.rem(me + step, count)
+        pl.semaphore_signal(
+            barrier, inc=1, device_id={axis_name: peer}, device_id_type=pl.DeviceIdType.MESH
+        )
+    pl.semaphore_wait(barrier, count - 1)
+    copies = []
+    for step in range(1, count):
+        peer = lax.rem(me + step, count)
+        copy = pltpu.make_async_remote_copy(
+            src_ref=source if same else source.at[peer],
+            dst_ref=landed.at[me],
+            send_sem=send_sem.at[step],
+            recv_sem=recv_sem.at[step],
+            device_id={axis_name: peer},
+            device_id_type=pl.DeviceIdType.MESH,
+        )
+        copy.start()
+        copies.append(copy)
+    landed[me] = source[...] if same else source[me]
+    for copy in copies:
+        copy.wait()
+
+
+EXCHANGE_IDS = {}
+
+
+def exchange(values, axis_name, same):
+    count = lax.axis_size(axis_name)
+    slot_shape = values.shape if same else values.shape[1:]
+    key = (axis_name, same, values.shape, str(values.dtype))
+    if key not in EXCHANGE_IDS:
+        EXCHANGE_IDS[key] = len(EXCHANGE_IDS)
+    slot_bytes = values.dtype.itemsize
+    for size in slot_shape:
+        slot_bytes *= size
+    return pl.pallas_call(
+        functools.partial(exchange_kernel, same, axis_name, count),
+        out_shape=jax.ShapeDtypeStruct((count,) + slot_shape, values.dtype),
+        in_specs=[pl.BlockSpec(memory_space=pltpu.VMEM)],
+        out_specs=pl.BlockSpec(memory_space=pltpu.VMEM),
+        scratch_shapes=[pltpu.SemaphoreType.DMA((count,)), pltpu.SemaphoreType.DMA((count,))],
+        compiler_params=pltpu.CompilerParams(
+            collective_id=EXCHANGE_IDS[key], has_side_effects=True
+        ),
+        cost_estimate=pl.CostEstimate(
+            flops=0, bytes_accessed=2 * count * slot_bytes, transcendentals=0
+        ),
+    )(values)
+
+
 def context_gather(values, axis_name):
     count = lax.axis_size(axis_name)
-    spread = jnp.broadcast_to(values[None], (count,) + values.shape)
-    gathered = lax.all_to_all(spread, axis_name, 0, 0, tiled=True)
+    gathered = exchange(values, axis_name, True)
     return gathered.reshape((count * values.shape[0],) + values.shape[1:])
 
 
 def context_scatter_sum(values, axis_name):
     count = lax.axis_size(axis_name)
     rows = values.shape[0] // count
-    parts = lax.all_to_all(
-        values.reshape((count, rows) + values.shape[1:]), axis_name, 0, 0, tiled=True
-    )
+    parts = exchange(values.reshape((count, rows) + values.shape[1:]), axis_name, False)
     return jnp.sum(parts.astype(jnp.float32), axis=0)
 
 

time: 337 us -> 365 us (1.083)
  Pallas kernels: 0 us -> 134 us
  waiting for transfers between devices: 159 us -> 90.7 us
  starting transfers between devices: 29 us -> 4.01 us
  blocking collectives: 15.8 us -> 0 us
    pallas_call x0 -> x6, Pallas kernels: none -> 134 us  [exchange(): pl.pallas_call(functools.partial(exchange_kernel, same, axis_name, count)...]
    all_to_all x5 -> x0, waiting for transfers between devices: 84.1 us -> none  [the longest x3 42.7 us: context_gather(): gathered = lax.all_to_all(spread, axis_name, 0, 0, tiled=True)]
    all_to_all x5 -> x0, starting transfers between devices: 25 us -> none  [the longest x3 13.9 us: context_gather(): gathered = lax.all_to_all(spread, axis_name, 0, 0, tiled=True)]
    all_to_all x1 -> x0, blocking collectives: 15.8 us -> none  [context_scatter_sum(): lax.all_to_all(values.reshape((count, rows) + values.shape[1:]), axis_nam...]
    reduce_scatter x2, waiting for transfers between devices: 12.8 us -> 22.8 us  [reduce_pack(): packed = lax.psum_scatter(packed, 'fsdp', scatter_dimension=0, tiled=True)]
    ppermute x4, waiting for transfers between devices: 39 us -> 47.9 us  [pair_sum(): other = lax.ppermute(values, axis_name, perm=[(0, 1), (1, 0)])]
  transfers between devices with their start and end apart: 13 -> 8, of which waited for: 10 -> 7; matrix products, arithmetic and copies ran while one was open for 25% -> 15% of each run, Pallas kernels for 0% -> 19%
where the time goes in v7:
time: 365 us; the launch traced here: 363 us
  Pallas kernels  134 us (37%)
  waiting for transfers between devices  90.7 us (25%)
  local copies, waits for them, and re-layouts  46 us (13%)
  matrix products  44.9 us (12%)
  other arithmetic  28.9 us (8%)
  between operations  14.6 us (4%)
  starting transfers between devices  4.01 us (1%)
    pallas_call x6, Pallas kernels, exchange(): pl.pallas_call(functools.partial(exchange_kernel, same, axis_name, count)...  134 us
    ppermute x4, waiting for transfers between devices, pair_sum(): other = lax.ppermute(values, axis_name, perm=[(0, 1), (1, 0)])  47.9 us
    reduce_scatter x2, waiting for transfers between devices, reduce_pack(): packed = lax.psum_scatter(packed, 'fsdp', scatter_dimension=0, tiled=True)  22.8 us
    all_gather x1, waiting for transfers between devices, on_device(): lax.all_gather(jnp.concatenate([qkv_weight.reshape(shard_rows, 3 * local_...  19.9 us
    concatenate x2, local copies, waits for them, and re-layouts, reduce_pack(): packed = jnp.concatenate(members, axis=1).astype(jnp.bfloat16)  11.5 us
    dot_general x1, matrix products, on_device(): jnp.einsum('hqk,qhd->khd', fwd_weights, out_heads, preferred_element_type...  8.75 us
    dot_general x1, matrix products, on_device(): jnp.einsum('qhd,khd->hqk', out_heads, values_heads, preferred_element_typ...  7.89 us
  transfers between devices with their start and end apart: 8, of which 7 were waited for; matrix products, arithmetic and copies ran while one was open for 15% of the time, Pallas kernels for 19%

profile of v7, /device:TPU:0, one launch (start us, length us, event | category | flops | bytes accessed | tf_op | source)
XLA Modules:
  0.0 363.3 jit_solution(12837875458329664296)
XLA Ops:
  11.8 1.7 pad_maximum_fusion.3
  17.0 1.2 broadcast_compare_fusion
  18.2 19.9 %all-gather.3.cloned.1.call-done = bf16[768,1154]{1,0:T(8,128)(2,1)} async-done(((bf16[96,1154]{1,0:T(8,128)(2,1)}), bf16[768,1154]{1,0:T(8,128)(2,1)}) %all-gather.3.cloned.1.call-update) | async-done | bytes 1772560 | tf_op jit(solution)/shard_map/all_gather | solution.py:170
  38.1 1.3 convert_reduce_fusion.2
  39.5 2.4 fusion.7
  43.9 44.2 %shard_map.152 = bf16[8,256,768]{2,1,0:T(8,128)(2,1)} custom-call(bf16[256,768]{1,0:T(8,128)(2,1)} %pad_maximum_fusion.4.source), custom_call_target="tpu_custom_call" | custom-call | bytes 6291456 | tf_op jit(solution)/shard_map/pallas_call | solution.py:119
  88.1 3.3 fusion.55
  91.5 1.7 copy.94
  93.2 1.7 copy.93
  94.9 3.7 %select_reduce_fusion.1 = (f32[6,256]{1,0:T(8,128)S(1)}, f32[6,256,2048]{2,1,0:T(8,128)S(1)}) fusion(pred[256,2048]{1,0:T(8,128)(4,1)} %broadcast_compare_fusion, bf16[2048,6,64]{0,2,1:T(8,128)(2,1)S(1)} %bitcast.117, bf16[256,6,32]{0,2,1:T(8,128)(2,1)} %get-tuple-element.65, bf16[256,6,32]{0,2,1:T(8,128)(2,1)} %get-tuple-element.64), kind=kOutput, calls=%fused_computation.3 | convolution fusion | flops 412482048 | bytes 14882816 | tf_op jit(solution)/shard_map/qhd,khd->hqk/dot_general | solution.py:217
  98.5 4.0 %select_reduce_fusion = f32[6,256]{1,0:T(8,128)S(1)} fusion(f32[6,256,2048]{2,1,0:T(8,128)S(1)} %get-tuple-element.75, f32[6,256]{1,0:T(8,128)S(1)} %get-tuple-element.74, pred[256,2048]{1,0:T(8,128)(4,1)S(1)} %copy-done.2), kind=kLoop, calls=%fused_computation.2 | loop fusion | flops 12581376 | bytes 13119488 | tf_op jit(solution)/shard_map/reduce_sum | solution.py:220
  103.3 3.0 convolution_convert_fusion.6
  106.3 1.6 fusion.40
  107.9 1.2 collective-permute-start
  109.2 18.5 %collective-permute-done = f32[256,768]{1,0:T(8,128)S(1)} collective-permute-done((f32[256,768]{1,0:T(8,128)S(1)}, f32[256,768]{1,0:T(8,128)S(1)}, u32[]{:S(2)}, u32[]{:S(2)}) %collective-permute-start) | collective-permute-done | bytes 786464 | tf_op jit(solution)/shard_map/ppermute | solution.py:76
  131.4 1.8 collective-permute-start.1
  133.2 17.8 %collective-permute-done.2 = f32[256,768]{1,0:T(8,128)S(1)} collective-permute-done((f32[256,768]{1,0:T(8,128)S(1)}, f32[256,768]{1,0:T(8,128)S(1)}, u32[]{:S(2)}, u32[]{:S(2)}) %collective-permute-start.2) | collective-permute-done | bytes 786464 | tf_op jit(solution)/shard_map/ppermute | solution.py:76
  152.0 5.7 %collective-permute-done.1 = bf16[256,768]{1,0:T(8,128)(2,1)S(1)} collective-permute-done((bf16[256,768]{1,0:T(8,128)(2,1)S(1)}, bf16[256,768]{1,0:T(8,128)(2,1)S(1)}, u32[]{:S(2)}, u32[]{:S(2)}) %collective-permute-start.1) | collective-permute-done | bytes 393248 | tf_op jit(solution)/shard_map/ppermute | solution.py:76
  159.8 1.7 copy.96
  162.7 8.7 %convolution_convert_fusion.2 = bf16[6,64,2048]{2,1,0:T(8,128)(2,1)} fusion(bf16[256,6,64]{0,2,1:T(8,128)(2,1)} %bitcast.141, f32[6,256,2048]{2,1,0:T(8,128)} %copy-done, f32[6,256]{1,0:T(8,128)} %copy-done.30, pred[256,2048]{1,0:T(8,128)(4,1)} %broadcast_compare_fusion), kind=kOutput, calls=%fused_computation.10 | convolution fusion | flops 416022528 | bytes 14882816 | tf_op jit(solution)/shard_map/hqk,qhd->khd/dot_general | solution.py:283
  171.4 7.9 %multiply_convert_fusion = bf16[6,256,2048]{2,1,0:T(8,128)(2,1)S(1)} fusion(f32[6,256,2048]{2,1,0:T(8,128)} %copy-done, f32[6,256]{1,0:T(8,128)S(1)} %bitcast.148, f32[6,256]{1,0:T(8,128)S(1)} %copy-done.31, pred[256,2048]{1,0:T(8,128)(4,1)S(1)} %copy-done.3, bf16[256,6,64]{0,2,1:T(8,128)(2,1)S(1)} %bitcast.142, bf16[2048,6,64]{0,2,1:T(8,128)(2,1)S(1)} %bitcast.131), kind=kOutput, calls=%fused_computation | convolution fusion | flops 421527552 | bytes 21180416 | tf_op jit(solution)/shard_map/qhd,khd->hqk/dot_general | solution.py:271
  179.4 2.8 fusion.13
  182.1 1.2 multiply_convert_fusion.1
  183.9 2.0 copy.97
  185.9 1.9 copy.112
  187.8 2.0 copy.98
  189.8 3.8 %pad_maximum_fusion.source = bf16[8,256,768]{2,1,0:T(8,128)(2,1)} fusion(bf16[8,256,384]{2,1,0:T(8,128)(2,1)} %copy.98, bf16[8,256,384]{2,1,0:T(8,128)(2,1)} %copy.97), kind=kLoop, calls=%fused_computation.8 | loop fusion | flops 6291456 | bytes 6291456 | tf_op jit(solution)/shard_map/concatenate | solution.py:287
  193.6 41.6 %shard_map.153 = bf16[8,256,768]{2,1,0:T(8,128)(2,1)} custom-call(bf16[8,256,768]{2,1,0:T(8,128)(2,1)} %pad_maximum_fusion.source), custom_call_target="tpu_custom_call" | custom-call | bytes 6291456 | tf_op jit(solution)/shard_map/pallas_call | solution.py:119
  235.2 2.4 convert_reduce_fusion
  238.3 2.2 fusion.10
  241.4 2.1 convolution_convert_fusion.1
  243.5 5.9 %collective-permute-done.3 = bf16[256,768]{1,0:T(8,128)(2,1)S(1)} collective-permute-done((bf16[256,768]{1,0:T(8,128)(2,1)S(1)}, bf16[256,768]{1,0:T(8,128)(2,1)S(1)}, u32[]{:S(2)}, u32[]{:S(2)}) %collective-permute-start.3) | collective-permute-done | bytes 393248 | tf_op jit(solution)/shard_map/ppermute | solution.py:76
  250.6 5.7 %concatenate.52 = bf16[768,1537]{1,0:T(8,128)(2,1)} concatenate(bf16[768,1]{1,0:T(8,128)(2,1)S(1)} %broadcast_in_dim.89, bf16[768,1152]{1,0:T(8,128)(2,1)} %convolution_convert_fusion.1, bf16[768,384]{1,0:T(8,128)(2,1)S(1)} %convolution_convert_fusion.4), dimensions={1} | concatenate | bytes 4721664 | tf_op jit(solution)/shard_map/concatenate | solution.py:314
  256.4 2.3 fusion.9
  258.7 1.5 copy.104
  260.3 2.7 convolution_convert_fusion
  263.9 5.8 %concatenate.53 = bf16[768,1729]{1,0:T(8,128)(2,1)} concatenate(bf16[768,1]{1,0:T(8,128)(2,1)S(1)} %broadcast_in_dim.90, bf16[768,1152]{1,0:T(8,128)(2,1)} %convolution_convert_fusion, bf16[768,576]{1,0:T(8,128)(2,1)S(1)} %copy.104), dimensions={1} | concatenate | bytes 5311488 | tf_op jit(solution)/shard_map/concatenate | solution.py:314
  269.7 1.2 fusion.27
  271.0 17.5 %reduce-scatter.3.cloned.1.call-done = bf16[96,1537]{1,0:T(8,128)(2,1)} async-done(((bf16[768,1537]{1,0:T(8,128)(2,1)}), bf16[96,1537]{1,0:T(8,128)(2,1)}) %reduce-scatter.3.cloned.1.call-update) | async-done | bytes 295120 | tf_op jit(solution)/shard_map/reduce_scatter | solution.py:315
  288.5 1.8 reshape.257.source
  290.3 12.6 %shard_map.154 = bf16[8,12,1537]{2,1,0:T(8,128)(2,1)} custom-call(bf16[8,12,1537]{2,1,0:T(8,128)(2,1)} %reshape.257.source), custom_call_target="tpu_custom_call" | custom-call | bytes 590208 | tf_op jit(solution)/shard_map/pallas_call | solution.py:119
  302.8 1.7 reduce_sum.183.source
  304.6 11.5 %shard_map.155 = bf16[8,12,1537]{2,1,0:T(8,128)(2,1)} custom-call(bf16[12,1537]{1,0:T(8,128)(2,1)} %reduce_sum.183.source), custom_call_target="tpu_custom_call" | custom-call | bytes 590208 | tf_op jit(solution)/shard_map/pallas_call | solution.py:119
  319.5 5.3 %reduce-scatter.5.cloned.1.call-done = bf16[96,1729]{1,0:T(8,128)(2,1)} async-done(((bf16[768,1729]{1,0:T(8,128)(2,1)}), bf16[96,1729]{1,0:T(8,128)(2,1)}) %reduce-scatter.5.cloned.1.call-update) | async-done | bytes 331984 | tf_op jit(solution)/shard_map/reduce_scatter | solution.py:315
  324.9 1.8 reshape.259.source
  326.7 12.7 %shard_map.156 = bf16[8,12,1729]{2,1,0:T(8,128)(2,1)} custom-call(bf16[8,12,1729]{2,1,0:T(8,128)(2,1)} %reshape.259.source), custom_call_target="tpu_custom_call" | custom-call | bytes 663936 | tf_op jit(solution)/shard_map/pallas_call | solution.py:119
  339.4 1.7 reduce_sum.185.source
  341.2 11.7 %shard_map.157 = bf16[8,12,1729]{2,1,0:T(8,128)(2,1)} custom-call(bf16[12,1729]{1,0:T(8,128)(2,1)} %reduce_sum.185.source), custom_call_target="tpu_custom_call" | custom-call | bytes 663936 | tf_op jit(solution)/shard_map/pallas_call | solution.py:119
  (144 shorter events, 30.1 us)
Async XLA Ops:
  7.2 9.1 %copy-start.1 = (bf16[256,768]{1,0:T(8,128)(2,1)S(1)}, bf16[256,768]{1,0:T(8,128)(2,1)}, u32[]{:S(2)}) copy-start(bf16[256,768]{1,0:T(8,128)(2,1)} %param.9) | copy-start | bytes 1179652
  7.2 30.9 %all-gather.3.cloned.1.call-start = ((), (), s32[]{:S(2)}) async-start(), calls=%async_computation.2 | async-start | bytes 2211840 | tf_op jit(solution)/shard_map/all_gather | solution.py:170
  10.6 95.7 %all-gather.5.cloned.1.call-start = ((), (), s32[]{:S(2)}) async-start(), calls=%async_computation.3 | async-start | bytes 3760128 | tf_op jit(solution)/shard_map/all_gather | solution.py:183
  13.5 274.9 %reduce-scatter.3.cloned.1.call-start = ((), (), s32[]{:S(2)}) async-start(), calls=%async_computation.4 | async-start | bytes 2875392 | tf_op jit(solution)/shard_map/reduce_scatter | solution.py:315
  16.8 25.2 %copy-start.27 = (f32[256]{0:T(256)}, f32[256]{0:T(256)S(1)}, u32[]{:S(2)}) copy-start(f32[256]{0:T(256)S(1)} %add_rsqrt_fusion.1) | copy-start | bytes 3076
  17.0 25.0 %copy-start.21 = (f32[256,32]{0,1:T(8,128)}, f32[256,32]{0,1:T(8,128)S(1)}, u32[]{:S(2)}) copy-start(f32[256,32]{0,1:T(8,128)S(1)} %get-tuple-element.72) | copy-start | bytes 98308
  17.0 25.0 %copy-start.23 = (f32[256,32]{0,1:T(8,128)}, f32[256,32]{0,1:T(8,128)S(1)}, u32[]{:S(2)}) copy-start(f32[256,32]{0,1:T(8,128)S(1)} %get-tuple-element.73) | copy-start | bytes 98308
  94.9 3.7 %copy-start.2 = (pred[256,2048]{1,0:T(8,128)(4,1)S(1)}, pred[256,2048]{1,0:T(8,128)(4,1)}, u32[]{:S(2)}) copy-start(pred[256,2048]{1,0:T(8,128)(4,1)} %broadcast_compare_fusion) | copy-start | bytes 1572868
  98.5 4.7 %copy-start = (f32[6,256,2048]{2,1,0:T(8,128)}, f32[6,256,2048]{2,1,0:T(8,128)S(1)}, u32[]{:S(2)}) copy-start(f32[6,256,2048]{2,1,0:T(8,128)S(1)} %get-tuple-element.75) | copy-start | bytes 37748740
  98.5 4.7 %copy-start.10 = (bf16[2048,384]{0,1:T(8,128)(2,1)S(1)}, bf16[2048,384]{0,1:T(8,128)(2,1)}, u32[]{:S(2)}) copy-start(bf16[2048,384]{0,1:T(8,128)(2,1)} %copy.93) | copy-start | bytes 4718596
  102.5 3.7 %copy-start.30 = (f32[6,256]{1,0:T(8,128)}, f32[6,256]{1,0:T(8,128)S(1)}, u32[]{:S(2)}) copy-start(f32[6,256]{1,0:T(8,128)S(1)} %log_add_fusion) | copy-start | bytes 18436
  106.3 2.9 copy-start.7
  106.3 21.8 %copy-start.4 = (bf16[768,2112]{1,0:T(8,128)(2,1)S(1)}, bf16[768,2112]{1,0:T(8,128)(2,1)}, u32[]{:S(2)}) copy-start(bf16[768,2112]{1,0:T(8,128)(2,1)} %all-gather.5.cloned.1.call-done) | copy-start | bytes 9732100
  107.9 21.1 %copy-start.16 = (bf16[256,768]{1,0:T(8,128)(2,1)S(1)}, bf16[256,768]{1,0:T(8,128)(2,1)}, u32[]{:S(2)}) copy-start(bf16[256,768]{1,0:T(8,128)(2,1)} %param.17) | copy-start | bytes 1179652
  107.9 19.7 %collective-permute-start = (f32[256,768]{1,0:T(8,128)S(1)}, f32[256,768]{1,0:T(8,128)S(1)}, u32[]{:S(2)}, u32[]{:S(2)}) collective-permute-start(f32[256,768]{1,0:T(8,128)S(1)} %fusion.40), channel_id=1, source_target_pairs={{0,8},{8,0},{1,9},{9,1},{2,10},{10,2},{3,11},{11,3},{4,12},{12,4},... | collective-permute-start | bytes 2359304 | tf_op jit(solution)/shard_map/ppermute | solution.py:76
  128.1 29.6 %copy-start.26 = (f32[256]{0:T(256)}, f32[256]{0:T(256)S(1)}, u32[]{:S(2)}) copy-start(f32[256]{0:T(256)S(1)} %add_rsqrt_fusion) | copy-start | bytes 3076
  129.7 1.8 copy-start.25
  129.8 22.2 %copy-start.5 = (bf16[256,2,576]{0,2,1:T(8,128)(2,1)}, bf16[256,2,576]{0,2,1:T(8,128)(2,1)S(1)}, u32[]{:S(2)}) copy-start(bf16[256,2,576]{0,2,1:T(8,128)(2,1)S(1)} %pad_maximum_fusion.1) | copy-start | bytes 1769476
  130.5 20.6 %collective-permute-start.2 = (f32[256,768]{1,0:T(8,128)S(1)}, f32[256,768]{1,0:T(8,128)S(1)}, u32[]{:S(2)}, u32[]{:S(2)}) collective-permute-start(f32[256,768]{1,0:T(8,128)S(1)} %fusion.1), channel_id=1, source_target_pairs={{0,8},{8,0},{1,9},{9,1},{2,10},{10,2},{3,11},{11,3},{4,12},{12,4},... | collective-permute-start | bytes 2359304 | tf_op jit(solution)/shard_map/ppermute | solution.py:76
  131.4 26.2 %collective-permute-start.1 = (bf16[256,768]{1,0:T(8,128)(2,1)S(1)}, bf16[256,768]{1,0:T(8,128)(2,1)S(1)}, u32[]{:S(2)}, u32[]{:S(2)}) collective-permute-start(bf16[256,768]{1,0:T(8,128)(2,1)S(1)} %convolution_convert_fusion.5), channel_id=1, source_target_pairs={{0,8},{8,0},{1,9},{9,1},{2,10},{10,2},{3,11},{11,3},{4,12},{12,4},... | collective-permute-start | bytes 1179656 | tf_op jit(solution)/shard_map/ppermute | solution.py:76
  162.6 8.8 %copy-start.3 = (pred[256,2048]{1,0:T(8,128)(4,1)S(1)}, pred[256,2048]{1,0:T(8,128)(4,1)}, u32[]{:S(2)}) copy-start(pred[256,2048]{1,0:T(8,128)(4,1)} %broadcast_compare_fusion) | copy-start | bytes 1572868
  162.6 8.8 %copy-start.11 = (bf16[2048,384]{0,1:T(8,128)(2,1)S(1)}, bf16[2048,384]{0,1:T(8,128)(2,1)}, u32[]{:S(2)}) copy-start(bf16[2048,384]{0,1:T(8,128)(2,1)} %copy.93) | copy-start | bytes 4718596
  162.6 8.8 %copy-start.20 = (bf16[256,384]{0,1:T(8,128)(2,1)S(1)}, bf16[256,384]{0,1:T(8,128)(2,1)}, u32[]{:S(2)}) copy-start(bf16[256,384]{0,1:T(8,128)(2,1)} %copy.96) | copy-start | bytes 589828
  162.7 8.8 %copy-start.31 = (f32[6,256]{1,0:T(8,128)S(1)}, f32[6,256]{1,0:T(8,128)}, u32[]{:S(2)}) copy-start(f32[6,256]{1,0:T(8,128)} %copy-done.30) | copy-start | bytes 18436
  179.3 2.8 copy-start.18
  179.3 2.8 copy-start.19
  235.2 2.9 copy-start.9
  235.2 2.9 copy-start.22
  235.2 2.9 copy-start.24
  238.1 2.9 copy-start.8
  238.2 3.2 copy-start.28
  240.6 8.8 %copy-start.12 = (bf16[256,768]{1,0:T(8,128)(2,1)}, bf16[256,768]{1,0:T(8,128)(2,1)S(1)}, u32[]{:S(2)}) copy-start(bf16[256,768]{1,0:T(8,128)(2,1)S(1)} %fusion.10) | copy-start | bytes 1179652
  240.6 8.8 %collective-permute-start.3 = (bf16[256,768]{1,0:T(8,128)(2,1)S(1)}, bf16[256,768]{1,0:T(8,128)(2,1)S(1)}, u32[]{:S(2)}, u32[]{:S(2)}) collective-permute-start(bf16[256,768]{1,0:T(8,128)(2,1)S(1)} %fusion.10), channel_id=1, source_target_pairs={{0,8},{8,0},{1,9},{9,1},{2,10},{10,2},{3,11},{11,3},{4,12},{12,4},... | collective-permute-start | bytes 1179656 | tf_op jit(solution)/shard_map/ppermute | solution.py:76
  249.4 1.0 copy-start.14
  250.6 5.8 %copy-start.17 = (bf16[256,768]{1,0:T(8,128)(2,1)S(1)}, bf16[256,768]{1,0:T(8,128)(2,1)}, u32[]{:S(2)}) copy-start(bf16[256,768]{1,0:T(8,128)(2,1)} %param.17) | copy-start | bytes 1179652
  256.3 4.0 %copy-start.6 = (bf16[256,2,576]{0,2,1:T(8,128)(2,1)S(1)}, bf16[256,2,576]{0,2,1:T(8,128)(2,1)}, u32[]{:S(2)}) copy-start(bf16[256,2,576]{0,2,1:T(8,128)(2,1)} %copy-done.5) | copy-start | bytes 1769476
  256.4 68.5 %reduce-scatter.5.cloned.1.call-start = ((), (), s32[]{:S(2)}) async-start(), calls=%async_computation.5 | async-start | bytes 3096576 | tf_op jit(solution)/shard_map/reduce_scatter | solution.py:315
  263.8 5.8 %copy-start.33 = (f32[256]{0:T(256)S(1)}, f32[256]{0:T(256)}, u32[]{:S(2)}) copy-start(f32[256]{0:T(256)} %get-tuple-element.45) | copy-start | bytes 3076
  263.8 5.9 %copy-start.32 = (f32[256]{0:T(256)S(1)}, f32[256]{0:T(256)}, u32[]{:S(2)}) copy-start(f32[256]{0:T(256)} %get-tuple-element.46) | copy-start | bytes 3076
  263.9 5.9 %copy-start.13 = (bf16[256,768]{1,0:T(8,128)(2,1)S(1)}, bf16[256,768]{1,0:T(8,128)(2,1)}, u32[]{:S(2)}) copy-start(bf16[256,768]{1,0:T(8,128)(2,1)} %copy-done.12) | copy-start | bytes 1179652
  263.9 5.9 %copy-start.15 = (bf16[256,768]{1,0:T(8,128)(2,1)S(1)}, bf16[256,768]{1,0:T(8,128)(2,1)}, u32[]{:S(2)}) copy-start(bf16[256,768]{1,0:T(8,128)(2,1)} %copy-done.14) | copy-start | bytes 1179652
  263.9 5.9 %copy-start.29 = (f32[256]{0:T(256)S(1)}, f32[256]{0:T(256)}, u32[]{:S(2)}) copy-start(f32[256]{0:T(256)} %copy-done.27) | copy-start | bytes 3076
Sparse Core Ops, SparseCore 0:
  10.7 27.3 all-gather.2
  40.4 28.7 all-gather.4
  256.5 31.9 reduce-scatter.2
  290.9 33.9 reduce-scatter.4

commit v8 on v6

--- a/solution.py
+++ b/solution.py
@@ -1,6 +1,10 @@
+import functools
+
 import jax
 import jax.numpy as jnp
 from jax import lax
+from jax.experimental import pallas as pl
+from jax.experimental.pallas import tpu as pltpu
 from jax.sharding import PartitionSpec as P
 
 HD = 64
@@ -66,11 +70,47 @@
     return (gate_pre * normal_cdf, normal_cdf + gate_pre * density)
 
 
-def pair_sum(values, axis_name):
+def pair_kernel(axis_name, source, total, landed, send_sem, recv_sem):
+    partner = 1 - lax.axis_index(axis_name)
+    barrier = pltpu.get_barrier_semaphore()
+    pl.semaphore_signal(
+        barrier, inc=1, device_id={axis_name: partner}, device_id_type=pl.DeviceIdType.MESH
+    )
+    pl.semaphore_wait(barrier, 1)
+    copy = pltpu.make_async_remote_copy(
+        src_ref=source,
+        dst_ref=landed,
+        send_sem=send_sem,
+        recv_sem=recv_sem,
+        device_id={axis_name: partner},
+        device_id_type=pl.DeviceIdType.MESH,
+    )
+    copy.start()
+    copy.wait()
+    total[...] = source[...].astype(jnp.float32) + landed[...].astype(jnp.float32)
+
+
+def pair_sum(values, axis_name, call_id):
     if lax.axis_size(axis_name) != 2:
-        return lax.psum(values, axis_name)
-    other = lax.ppermute(values, axis_name, perm=[(0, 1), (1, 0)])
-    return values.astype(jnp.float32) + other.astype(jnp.float32)
+        return lax.psum(values.astype(jnp.float32), axis_name)
+    value_bytes = values.dtype.itemsize * values.size
+    return pl.pallas_call(
+        functools.partial(pair_kernel, axis_name),
+        out_shape=jax.ShapeDtypeStruct(values.shape, jnp.float32),
+        in_specs=[pl.BlockSpec(memory_space=pltpu.VMEM)],
+        out_specs=pl.BlockSpec(memory_space=pltpu.VMEM),
+        scratch_shapes=[
+            pltpu.VMEM(values.shape, values.dtype),
+            pltpu.SemaphoreType.DMA(()),
+            pltpu.SemaphoreType.DMA(()),
+        ],
+        compiler_params=pltpu.CompilerParams(
+            collective_id=call_id, has_side_effects=True
+        ),
+        cost_estimate=pl.CostEstimate(
+            flops=values.size, bytes_accessed=3 * value_bytes + 4 * values.size, transcendentals=0
+        ),
+    )(values)
 
 
 def context_gather(values, axis_name):
@@ -173,7 +213,7 @@
     ).astype(jnp.bfloat16)
     mixed_flat = mixed.reshape(row_count, local_width)
     attn_part = jnp.dot(mixed_flat, proj_t.T, preferred_element_type=jnp.float32)
-    residual = inputs + pair_sum(attn_part, "tensor")
+    residual = inputs + pair_sum(attn_part, "tensor", 0)
     normed_mlp, spread_mlp = layer_norm(residual)
     hidden_mlp = (normed_mlp * mlp_scale).astype(jnp.bfloat16)
     gate_up = jnp.dot(hidden_mlp, gelu_flat, preferred_element_type=jnp.float32).reshape(
@@ -184,7 +224,7 @@
     activ = (gelu_val * up_pre).astype(jnp.bfloat16)
     mlp_part = jnp.dot(activ, down_t.T, preferred_element_type=jnp.float32)
     block_output = (
-        residual + pair_sum(mlp_part.astype(jnp.bfloat16), "tensor")
+        residual + pair_sum(mlp_part.astype(jnp.bfloat16), "tensor", 1)
     ).astype(jnp.bfloat16)
     act_grad = jnp.dot(out_cotangent, down_t, preferred_element_type=jnp.float32)
     down_grad_t = jnp.dot(out_cotangent.T, activ, preferred_element_type=jnp.float32)
@@ -197,7 +237,7 @@
         feature_count, 2, hidden
     )
     mlp_in_grad = pair_sum(
-        jnp.dot(gate_up_grad, gelu_flat.T, preferred_element_type=jnp.float32), "tensor"
+        jnp.dot(gate_up_grad, gelu_flat.T, preferred_element_type=jnp.float32), "tensor", 2
     )
     mlpgain_grad = jnp.sum(mlp_in_grad * normed_mlp, axis=0)
     resid_grad = out_cotangent.astype(jnp.float32) + norm_back(
@@ -252,6 +292,7 @@
     attn_in_grad = pair_sum(
         jnp.dot(qkv_rows, qkv_flat.T, preferred_element_type=jnp.float32).astype(jnp.bfloat16),
         "tensor",
+        3,
     )
     attngain_grad = jnp.sum(attn_in_grad * normed_attn, axis=0)
     input_grad = resid_grad + norm_back(attn_in_grad, normed_attn, spread_attn, attn_scale)

time: 337 us -> 358 us (1.062)
  Pallas kernels: 0 us -> 60.5 us
  waiting for transfers between devices: 159 us -> 118 us
  local copies, waits for them, and re-layouts: 44.5 us -> 49.5 us
    pallas_call x0 -> x4, Pallas kernels: none -> 60.5 us  [pair_sum(): pl.pallas_call(functools.partial(pair_kernel, axis_name), out_shape=jax.S...]
    ppermute x4 -> x0, waiting for transfers between devices: 39 us -> none  [pair_sum(): other = lax.ppermute(values, axis_name, perm=[(0, 1), (1, 0)])]
    dot_general x1, matrix products: 9.77 us -> 3.21 us  [on_device(): jnp.einsum('hqk,qhd->khd', fwd_weights, out_heads, preferred_element_type...]
  transfers between devices with their start and end apart: 13 -> 9, of which waited for: 10 -> 6; matrix products, arithmetic and copies ran while one was open for 25% -> 21% of each run, Pallas kernels for 0% -> 3%
where the time goes in v8:
time: 358 us; the launch traced here: 356 us
  waiting for transfers between devices  118 us (33%)
  Pallas kernels  60.5 us (17%)
  local copies, waits for them, and re-layouts  49.5 us (14%)
  matrix products  42.8 us (12%)
  other arithmetic  28.1 us (8%)
  starting transfers between devices  26.7 us (7%)
  blocking collectives  16 us (4%)
  between operations  14.5 us (4%)
    pallas_call x4, Pallas kernels, pair_sum(): pl.pallas_call(functools.partial(pair_kernel, axis_name), out_shape=jax.S...  60.5 us
    all_to_all x3, waiting for transfers between devices, context_gather(): gathered = lax.all_to_all(spread, axis_name, 0, 0, tiled=True)  41.2 us
    all_to_all x2, waiting for transfers between devices, context_scatter_sum(): lax.all_to_all(values.reshape((count, rows) + values.shape[1:]), axis_nam...  40.5 us
    all_gather x1, waiting for transfers between devices, on_device(): lax.all_gather(jnp.concatenate([qkv_weight.reshape(shard_rows, 3 * local_...  23.2 us
    all_to_all x1, blocking collectives, context_scatter_sum(): lax.all_to_all(values.reshape((count, rows) + values.shape[1:]), axis_nam...  16 us
    all_to_all x3, starting transfers between devices, context_gather(): gathered = lax.all_to_all(spread, axis_name, 0, 0, tiled=True)  13.9 us
    reduce_scatter x2, waiting for transfers between devices, reduce_pack(): packed = lax.psum_scatter(packed, 'fsdp', scatter_dimension=0, tiled=True)  12.7 us
    all_to_all x2, starting transfers between devices, context_scatter_sum(): lax.all_to_all(values.reshape((count, rows) + values.shape[1:]), axis_nam...  12.1 us
  transfers between devices with their start and end apart: 9, of which 6 were waited for; matrix products, arithmetic and copies ran while one was open for 21% of the time, Pallas kernels for 3%

profile of v8, /device:TPU:0, one launch (start us, length us, event | category | flops | bytes accessed | tf_op | source)
XLA Modules:
  0.0 355.8 jit_solution(1213209695151618665)
XLA Ops:
  14.9 23.2 %all-gather.3.cloned.1.call-done = bf16[768,1154]{1,0:T(8,128)(2,1)} async-done(((bf16[96,1154]{1,0:T(8,128)(2,1)}), bf16[768,1154]{1,0:T(8,128)(2,1)}) %all-gather.3.cloned.1.call-update) | async-done | bytes 1772560 | tf_op jit(solution)/shard_map/all_gather | solution.py:155
  39.4 2.5 fusion.7
  42.2 1.9 broadcast_in_dim.57
  44.2 7.0 %all-to-all-start = ((bf16[8,256,768]{1,2,0:T(8,128)(2,1)}), bf16[8,256,768]{1,2,0:T(8,128)(2,1)S(1)}, u32[]{:S(2)}, u32[]{:S(2)}) async-start(bf16[8,256,768]{1,2,0:T(8,128)(2,1)} %broadcast_in_dim.57), calls=%async_computation | async-start | bytes 6291456 | tf_op jit(solution)/shard_map/all_to_all | solution.py:119
  51.2 1.8 reshape.256
  53.1 1.7 pad_maximum_fusion.3
  57.0 34.4 %all-to-all-done = bf16[8,256,768]{1,2,0:T(8,128)(2,1)S(1)} async-done(((bf16[8,256,768]{1,2,0:T(8,128)(2,1)}), bf16[8,256,768]{1,2,0:T(8,128)(2,1)S(1)}, u32[]{:S(2)}, u32[]{:S(2)}) %all-to-all-start) | async-done | bytes 3145760 | tf_op jit(solution)/shard_map/all_to_all | solution.py:119
  91.3 2.8 copy.87
  94.1 3.9 %fusion.53 = (bf16[2048,384]{1,0:T(8,128)(2,1)}, bf16[2048,384]{1,0:T(8,128)(2,1)}) fusion(bf16[2048,768]{1,0:T(8,128)(2,1)} %bitcast.121), kind=kLoop, calls=%fused_computation.131 | loop fusion | bytes 6291456 | tf_op jit(solution)/shard_map/slice | solution.py:196
  98.0 1.8 copy.89
  99.8 2.6 copy.88
  102.5 2.5 select_reduce_fusion.1
  104.9 4.0 %select_reduce_fusion = f32[6,256]{1,0:T(8,128)S(1)} fusion(f32[6,256,2048]{2,1,0:T(8,128)S(1)} %get-tuple-element.82, f32[6,256]{1,0:T(8,128)S(1)} %get-tuple-element.81, pred[256,2048]{1,0:T(8,128)(4,1)S(1)} %copy-done.4), kind=kLoop, calls=%fused_computation.2 | loop fusion | flops 12581376 | bytes 13119488 | tf_op jit(solution)/shard_map/reduce_sum | solution.py:205
  109.7 3.0 convolution_convert_fusion.6
  112.7 2.4 fusion.38.source
  115.2 20.6 %shard_map.152 = f32[256,768]{1,0:T(8,128)} custom-call(f32[256,768]{1,0:T(8,128)} %fusion.38.source), custom_call_target="tpu_custom_call" | custom-call | flops 196608 | bytes 3145728 | tf_op jit(solution)/shard_map/pallas_call | solution.py:97
  135.8 1.4 fusion.52
  137.5 2.4 fusion.3
  142.0 2.1 convolution_convert_fusion
  145.3 1.6 fusion.1.source
  146.9 2.3 copy.97
  149.2 11.1 %shard_map.153 = f32[256,768]{1,0:T(8,128)} custom-call(bf16[256,768]{1,0:T(8,128)(2,1)} %convolution_convert_fusion.5.source), custom_call_target="tpu_custom_call" | custom-call | flops 196608 | bytes 1966080 | tf_op jit(solution)/shard_map/pallas_call | solution.py:97
  160.3 18.9 %shard_map.154 = f32[256,768]{1,0:T(8,128)} custom-call(f32[256,768]{1,0:T(8,128)} %fusion.1.source), custom_call_target="tpu_custom_call" | custom-call | flops 196608 | bytes 3145728 | tf_op jit(solution)/shard_map/pallas_call | solution.py:97
  179.2 2.1 multiply_reduce_fusion
  181.3 2.5 multiply_add_fusion
  183.8 1.4 convolution_convert_fusion.7
  187.3 5.9 %concatenate.53 = bf16[768,1729]{1,0:T(8,128)(2,1)} concatenate(bf16[768,1]{1,0:T(8,128)(2,1)S(1)} %broadcast_in_dim.111, bf16[768,1152]{1,0:T(8,128)(2,1)} %convolution_convert_fusion, bf16[768,576]{1,0:T(8,128)(2,1)} %copy.97), dimensions={1} | concatenate | bytes 5311488 | tf_op jit(solution)/shard_map/concatenate | solution.py:300
  193.3 8.3 %multiply_convert_fusion = bf16[6,256,2048]{2,1,0:T(8,128)(2,1)S(1)} fusion(f32[6,256,2048]{2,1,0:T(8,128)} %copy-done, f32[6,256]{1,0:T(8,128)S(1)} %bitcast.150, f32[6,256]{1,0:T(8,128)S(1)} %copy-done.30, pred[256,2048]{1,0:T(8,128)(4,1)S(1)} %copy-done.5, bf16[256,6,64]{0,2,1:T(8,128)(2,1)} %bitcast.142, bf16[2048,6,64]{0,2,1:T(8,128)(2,1)} %bitcast.132), kind=kOutput, calls=%fused_computation | convolution fusion | flops 421527552 | bytes 21180416 | tf_op jit(solution)/shard_map/qhd,khd->hqk/dot_general | solution.py:256
  202.9 2.0 copy-done.1
  206.4 3.2 convolution_convert_fusion.2
  210.4 1.9 pad_maximum_fusion
  212.4 5.7 %all-to-all-start.1 = ((bf16[8,256,768]{1,2,0:T(8,128)(2,1)}), bf16[8,256,768]{1,2,0:T(8,128)(2,1)}, u32[]{:S(2)}, u32[]{:S(2)}) async-start(bf16[8,256,768]{1,2,0:T(8,128)(2,1)} %pad_maximum_fusion), calls=%async_computation.1 | async-start | bytes 6291456 | tf_op jit(solution)/shard_map/all_to_all | solution.py:126
  218.3 4.9 %fusion.13 = f32[256,6,64]{0,2,1:T(8,128)S(1)} fusion(bf16[2048,6,64]{0,2,1:T(8,128)(2,1)S(1)} %bitcast.120, bf16[6,256,2048]{2,1,0:T(8,128)(2,1)} %copy-done.1), kind=kOutput, calls=%fused_computation.26 | convolution fusion | flops 402751488 | bytes 8257536 | tf_op jit(solution)/shard_map/hqk,khd->qhd/dot_general | solution.py:261
  223.3 32.1 %all-to-all-done.1 = bf16[8,256,768]{1,2,0:T(8,128)(2,1)} async-done(((bf16[8,256,768]{1,2,0:T(8,128)(2,1)}), bf16[8,256,768]{1,2,0:T(8,128)(2,1)}, u32[]{:S(2)}, u32[]{:S(2)}) %all-to-all-start.1) | async-done | bytes 3145760 | tf_op jit(solution)/shard_map/all_to_all | solution.py:126
  255.4 2.4 convert_reduce_fusion
  259.3 1.5 fusion.10.source
  261.2 9.8 %shard_map.155 = f32[256,768]{1,0:T(8,128)} custom-call(bf16[256,768]{1,0:T(8,128)(2,1)} %fusion.10.source), custom_call_target="tpu_custom_call" | custom-call | flops 196608 | bytes 1966080 | tf_op jit(solution)/shard_map/pallas_call | solution.py:97
  271.1 1.5 fusion.28
  272.8 2.1 convolution_convert_fusion.1
  274.9 5.7 %concatenate.52 = bf16[768,1537]{1,0:T(8,128)(2,1)} concatenate(bf16[768,1]{1,0:T(8,128)(2,1)S(1)} %broadcast_in_dim.110, bf16[768,1152]{1,0:T(8,128)(2,1)} %convolution_convert_fusion.1, bf16[768,384]{1,0:T(8,128)(2,1)S(1)} %convolution_convert_fusion.4), dimensions={1} | concatenate | bytes 4721664 | tf_op jit(solution)/shard_map/concatenate | solution.py:300
  281.8 16.0 %all_to_all.30 = bf16[8,12,1729]{2,1,0:T(8,128)(2,1)S(1)} all-to-all(bf16[8,12,1729]{2,1,0:T(8,128)(2,1)S(1)} %reshape.262), channel_id=1, replica_groups=mesh['fsdp'=8,'tensor'=2,'context'=8] {'context'}, dimensions={0} | all-to-all | bytes 663936 | tf_op jit(solution)/shard_map/all_to_all | solution.py:126
  298.6 3.5 all-to-all-start.5
  302.2 12.7 %reduce-scatter.3.cloned.1.call-done = bf16[96,1537]{1,0:T(8,128)(2,1)} async-done(((bf16[768,1537]{1,0:T(8,128)(2,1)}), bf16[96,1537]{1,0:T(8,128)(2,1)}) %reduce-scatter.3.cloned.1.call-update) | async-done | bytes 295120 | tf_op jit(solution)/shard_map/reduce_scatter | solution.py:301
  314.9 1.8 reshape.260
  316.7 6.5 %all-to-all-start.2 = ((bf16[8,12,1537]{2,1,0:T(8,128)(2,1)}), bf16[8,12,1537]{2,1,0:T(8,128)(2,1)S(1)}, u32[]{:S(2)}, u32[]{:S(2)}) async-start(bf16[8,12,1537]{2,1,0:T(8,128)(2,1)} %reshape.260), calls=%async_computation.3 | async-start | bytes 851968 | tf_op jit(solution)/shard_map/all_to_all | solution.py:126
  324.5 8.3 %all-to-all-done.2 = bf16[8,12,1537]{2,1,0:T(8,128)(2,1)S(1)} async-done(((bf16[8,12,1537]{2,1,0:T(8,128)(2,1)}), bf16[8,12,1537]{2,1,0:T(8,128)(2,1)S(1)}, u32[]{:S(2)}, u32[]{:S(2)}) %all-to-all-start.2) | async-done | bytes 295136 | tf_op jit(solution)/shard_map/all_to_all | solution.py:126
  333.7 3.5 all-to-all-start.3
  339.9 6.8 %all-to-all-done.3 = bf16[8,12,1537]{2,1,0:T(8,128)(2,1)S(1)} async-done(((bf16[8,12,1537]{2,1,0:T(8,128)(2,1)}), bf16[8,12,1537]{2,1,0:T(8,128)(2,1)S(1)}, u32[]{:S(2)}, u32[]{:S(2)}) %all-to-all-start.3) | async-done | bytes 295136 | tf_op jit(solution)/shard_map/all_to_all | solution.py:119
  (148 shorter events, 33.1 us)
Async XLA Ops:
  7.2 30.9 %all-gather.3.cloned.1.call-start = ((), (), s32[]{:S(2)}) async-start(), calls=%async_computation.8 | async-start | bytes 2211840 | tf_op jit(solution)/shard_map/all_gather | solution.py:155
  11.4 3.3 copy-start.31
  11.5 0.7 copy-start.27
  14.6 27.4 %copy-start.25 = (f32[256]{0:T(256)}, f32[256]{0:T(256)S(1)}, u32[]{:S(2)}) copy-start(f32[256]{0:T(256)S(1)} %add_rsqrt_fusion.1) | copy-start | bytes 3076
  14.8 27.3 %copy-start.17 = (f32[256,32]{0,1:T(8,128)}, f32[256,32]{0,1:T(8,128)S(1)}, u32[]{:S(2)}) copy-start(f32[256,32]{0,1:T(8,128)S(1)} %get-tuple-element.79) | copy-start | bytes 98308
  14.9 27.3 %copy-start.19 = (f32[256,32]{0,1:T(8,128)}, f32[256,32]{0,1:T(8,128)S(1)}, u32[]{:S(2)}) copy-start(f32[256,32]{0,1:T(8,128)S(1)} %get-tuple-element.80) | copy-start | bytes 98308
  42.2 60.3 %copy-start.11 = (bf16[256,6,32]{0,2,1:T(8,128)(2,1)}, bf16[256,6,32]{0,2,1:T(8,128)(2,1)S(1)}, u32[]{:S(2)}) copy-start(bf16[256,6,32]{0,2,1:T(8,128)(2,1)S(1)} %get-tuple-element.71) | copy-start | bytes 294916
  42.2 60.3 %copy-start.13 = (bf16[256,6,32]{0,2,1:T(8,128)(2,1)}, bf16[256,6,32]{0,2,1:T(8,128)(2,1)S(1)}, u32[]{:S(2)}) copy-start(bf16[256,6,32]{0,2,1:T(8,128)(2,1)S(1)} %get-tuple-element.72) | copy-start | bytes 294916
  44.2 8.9 %copy-start.21 = (bf16[576,96]{0,1:T(8,128)(2,1)S(1)}, bf16[576,96]{0,1:T(8,128)(2,1)}, u32[]{:S(2)}) copy-start(bf16[576,96]{0,1:T(8,128)(2,1)} %param.16) | copy-start | bytes 331780
  44.2 8.9 %copy-start.23 = (bf16[384,96]{0,1:T(8,128)(2,1)S(1)}, bf16[384,96]{0,1:T(8,128)(2,1)}, u32[]{:S(2)}) copy-start(bf16[384,96]{0,1:T(8,128)(2,1)} %param.13) | copy-start | bytes 221188
  44.2 11.6 %copy-start.28 = (s32[256]{0:T(256)S(1)}, s32[256]{0:T(256)}, u32[]{:S(2)}) copy-start(s32[256]{0:T(256)} %copy-done.27) | copy-start | bytes 3076
  44.2 47.1 %all-to-all-start = ((bf16[8,256,768]{1,2,0:T(8,128)(2,1)}), bf16[8,256,768]{1,2,0:T(8,128)(2,1)S(1)}, u32[]{:S(2)}, u32[]{:S(2)}) async-start(bf16[8,256,768]{1,2,0:T(8,128)(2,1)} %broadcast_in_dim.57), calls=%async_computation | async-start | bytes 6291456 | tf_op jit(solution)/shard_map/all_to_all | solution.py:119
  51.2 61.5 %all-gather.5.cloned.1.call-start = ((), (), s32[]{:S(2)}) async-start(), calls=%async_computation.9 | async-start | bytes 3760128 | tf_op jit(solution)/shard_map/all_gather | solution.py:168
  54.8 225.8 %reduce-scatter.5.cloned.1.call-start = ((), (), s32[]{:S(2)}) async-start(), calls=%async_computation.11 | async-start | bytes 3096576 | tf_op jit(solution)/shard_map/reduce_scatter | solution.py:301
  98.0 4.4 %copy-start.4 = (pred[256,2048]{1,0:T(8,128)(4,1)S(1)}, pred[256,2048]{1,0:T(8,128)(4,1)}, u32[]{:S(2)}) copy-start(pred[256,2048]{1,0:T(8,128)(4,1)} %broadcast_compare_fusion) | copy-start | bytes 1572868
  104.9 4.7 %copy-start = (f32[6,256,2048]{2,1,0:T(8,128)}, f32[6,256,2048]{2,1,0:T(8,128)S(1)}, u32[]{:S(2)}) copy-start(f32[6,256,2048]{2,1,0:T(8,128)S(1)} %get-tuple-element.82) | copy-start | bytes 37748740
  104.9 4.7 %copy-start.9 = (bf16[2048,384]{0,1:T(8,128)(2,1)S(1)}, bf16[2048,384]{0,1:T(8,128)(2,1)}, u32[]{:S(2)}) copy-start(bf16[2048,384]{0,1:T(8,128)(2,1)} %copy.88) | copy-start | bytes 4718596
  108.9 3.7 %copy-start.29 = (f32[6,256]{1,0:T(8,128)}, f32[6,256]{1,0:T(8,128)S(1)}, u32[]{:S(2)}) copy-start(f32[6,256]{1,0:T(8,128)S(1)} %log_add_fusion) | copy-start | bytes 18436
  112.7 2.5 copy-start.7
  112.7 23.1 %copy-start.2 = (bf16[256,768]{1,0:T(8,128)(2,1)S(1)}, bf16[256,768]{1,0:T(8,128)(2,1)}, u32[]{:S(2)}) copy-start(bf16[256,768]{1,0:T(8,128)(2,1)} %param.9) | copy-start | bytes 1179652
  135.8 4.1 %copy-start.6 = (bf16[768,2112]{1,0:T(8,128)(2,1)S(1)}, bf16[768,2112]{1,0:T(8,128)(2,1)}, u32[]{:S(2)}) copy-start(bf16[768,2112]{1,0:T(8,128)(2,1)} %all-gather.5.cloned.1.call-done) | copy-start | bytes 9732100
  135.8 4.1 %copy-start.10 = (bf16[256,768]{1,0:T(8,128)(2,1)S(1)}, bf16[256,768]{1,0:T(8,128)(2,1)}, u32[]{:S(2)}) copy-start(bf16[256,768]{1,0:T(8,128)(2,1)} %param.17) | copy-start | bytes 1179652
  137.5 41.7 %copy-start.24 = (f32[256]{0:T(256)}, f32[256]{0:T(256)S(1)}, u32[]{:S(2)}) copy-start(f32[256]{0:T(256)S(1)} %add_rsqrt_fusion) | copy-start | bytes 3076
  185.4 1.1 copy-start.15
  187.3 6.0 %copy-start.5 = (pred[256,2048]{1,0:T(8,128)(4,1)S(1)}, pred[256,2048]{1,0:T(8,128)(4,1)}, u32[]{:S(2)}) copy-start(pred[256,2048]{1,0:T(8,128)(4,1)} %broadcast_compare_fusion) | copy-start | bytes 1572868
  187.3 6.0 %copy-start.30 = (f32[6,256]{1,0:T(8,128)S(1)}, f32[6,256]{1,0:T(8,128)}, u32[]{:S(2)}) copy-start(f32[6,256]{1,0:T(8,128)} %copy-done.29) | copy-start | bytes 18436
  193.3 8.4 %copy-start.12 = (bf16[256,6,32]{0,2,1:T(8,128)(2,1)S(1)}, bf16[256,6,32]{0,2,1:T(8,128)(2,1)}, u32[]{:S(2)}) copy-start(bf16[256,6,32]{0,2,1:T(8,128)(2,1)} %copy-done.11) | copy-start | bytes 294916
  193.3 8.4 %copy-start.14 = (bf16[256,6,32]{0,2,1:T(8,128)(2,1)S(1)}, bf16[256,6,32]{0,2,1:T(8,128)(2,1)}, u32[]{:S(2)}) copy-start(bf16[256,6,32]{0,2,1:T(8,128)(2,1)} %copy-done.13) | copy-start | bytes 294916
  193.3 12.4 %slice-start = ((s8[12582912]{0:T(1024)(128)(4,1)}), s8[4194304]{0:T(1024)(128)(4,1)S(1)}, s32[]{:S(2)}) async-start(s8[12582912]{0:T(1024)(128)(4,1)} %bitcast.117), calls=%async_computation.12 | async-start | bytes 8388608
  193.3 12.4 %slice-start.1 = ((s8[12582912]{0:T(1024)(128)(4,1)}), s8[4194304]{0:T(1024)(128)(4,1)S(1)}, s32[]{:S(2)}) async-start(s8[12582912]{0:T(1024)(128)(4,1)} %bitcast.117), calls=%async_computation.13 | async-start | bytes 8388608
  201.7 3.2 copy-start.1
  201.7 4.5 %slice-start.2 = ((s8[12582912]{0:T(1024)(128)(4,1)}), s8[4194304]{0:T(1024)(128)(4,1)S(1)}, s32[]{:S(2)}) async-start(s8[12582912]{0:T(1024)(128)(4,1)} %bitcast.117), calls=%async_computation.14 | async-start | bytes 8388608
  204.9 1.5 copy-start.16
  212.4 43.0 %all-to-all-start.1 = ((bf16[8,256,768]{1,2,0:T(8,128)(2,1)}), bf16[8,256,768]{1,2,0:T(8,128)(2,1)}, u32[]{:S(2)}, u32[]{:S(2)}) async-start(bf16[8,256,768]{1,2,0:T(8,128)(2,1)} %pad_maximum_fusion), calls=%async_computation.1 | async-start | bytes 6291456 | tf_op jit(solution)/shard_map/all_to_all | solution.py:126
  218.0 96.8 %reduce-scatter.3.cloned.1.call-start = ((), (), s32[]{:S(2)}) async-start(), calls=%async_computation.10 | async-start | bytes 2875392 | tf_op jit(solution)/shard_map/reduce_scatter | solution.py:301
  255.4 2.5 copy-start.18
  255.4 2.5 copy-start.20
  257.8 1.5 copy-start.22
  257.9 2.9 copy-start.8
  259.3 11.7 %copy-start.26 = (f32[256]{0:T(256)S(1)}, f32[256]{0:T(256)}, u32[]{:S(2)}) copy-start(f32[256]{0:T(256)} %copy-done.25) | copy-start | bytes 3076
  280.6 42.6 %copy-start.3 = (f32[256,768]{1,0:T(8,128)S(1)}, f32[256,768]{1,0:T(8,128)}, u32[]{:S(2)}) copy-start(f32[256,768]{1,0:T(8,128)} %shard_map.155) | copy-start | bytes 2359300
  298.6 18.0 %all-to-all-start.5 = ((bf16[8,12,1729]{2,1,0:T(8,128)(2,1)}), bf16[8,12,1729]{2,1,0:T(8,128)(2,1)S(1)}, u32[]{:S(2)}, u32[]{:S(2)}) async-start(bf16[8,12,1729]{2,1,0:T(8,128)(2,1)} %broadcast_in_dim.109), calls=%async_computation.7 | async-start | bytes 917504 | tf_op jit(solution)/shard_map/all_to_all | solution.py:119
  316.7 16.1 %all-to-all-start.2 = ((bf16[8,12,1537]{2,1,0:T(8,128)(2,1)}), bf16[8,12,1537]{2,1,0:T(8,128)(2,1)S(1)}, u32[]{:S(2)}, u32[]{:S(2)}) async-start(bf16[8,12,1537]{2,1,0:T(8,128)(2,1)} %reshape.260), calls=%async_computation.3 | async-start | bytes 851968 | tf_op jit(solution)/shard_map/all_to_all | solution.py:126
  333.7 13.1 %all-to-all-start.3 = ((bf16[8,12,1537]{2,1,0:T(8,128)(2,1)}), bf16[8,12,1537]{2,1,0:T(8,128)(2,1)S(1)}, u32[]{:S(2)}, u32[]{:S(2)}) async-start(bf16[8,12,1537]{2,1,0:T(8,128)(2,1)} %broadcast_in_dim.107), calls=%async_computation.4 | async-start | bytes 851968 | tf_op jit(solution)/shard_map/all_to_all | solution.py:119
Sparse Core Ops, SparseCore 0:
  10.7 27.3 all-gather.2
  54.9 29.0 all-gather.4
  193.4 34.1 reduce-scatter.4
  280.7 34.1 reduce-scatter.2

commit v9 on v6

--- a/solution.py
+++ b/solution.py
@@ -173,7 +173,7 @@
     ).astype(jnp.bfloat16)
     mixed_flat = mixed.reshape(row_count, local_width)
     attn_part = jnp.dot(mixed_flat, proj_t.T, preferred_element_type=jnp.float32)
-    residual = inputs + pair_sum(attn_part, "tensor")
+    residual = inputs + pair_sum(attn_part.astype(jnp.bfloat16), "tensor")
     normed_mlp, spread_mlp = layer_norm(residual)
     hidden_mlp = (normed_mlp * mlp_scale).astype(jnp.bfloat16)
     gate_up = jnp.dot(hidden_mlp, gelu_flat, preferred_element_type=jnp.float32).reshape(
@@ -197,7 +197,10 @@
         feature_count, 2, hidden
     )
     mlp_in_grad = pair_sum(
-        jnp.dot(gate_up_grad, gelu_flat.T, preferred_element_type=jnp.float32), "tensor"
+        jnp.dot(gate_up_grad, gelu_flat.T, preferred_element_type=jnp.float32).astype(
+            jnp.bfloat16
+        ),
+        "tensor",
     )
     mlpgain_grad = jnp.sum(mlp_in_grad * normed_mlp, axis=0)
     resid_grad = out_cotangent.astype(jnp.float32) + norm_back(
@@ -269,15 +272,20 @@
         return pieces
 
     mlp_pieces = reduce_pack(
-        [mlpgain_grad[:, None], gelu_grad.reshape(feature_count, 2 * hidden), down_grad_t]
+        [
+            mlpgain_grad[:, None],
+            gelu_grad.reshape(feature_count, 2 * hidden),
+            down_grad_t,
+            proj_grad_t,
+        ]
     )
     attn_pieces = reduce_pack(
-        [attngain_grad[:, None], qkv_grad.reshape(feature_count, 3 * local_width), proj_grad_t]
+        [attngain_grad[:, None], qkv_grad.reshape(feature_count, 3 * local_width)]
     )
     shares = (
         attn_pieces[0][:, 0],
         attn_pieces[1].reshape(shard_rows, 3, local_width),
-        attn_pieces[2].T,
+        mlp_pieces[3].T,
         mlp_pieces[0][:, 0],
         mlp_pieces[1].reshape(shard_rows, 2, hidden),
         mlp_pieces[2].T,

time: 337 us -> 361 us (1.071)
  waiting for transfers between devices: 159 us -> 193 us
  blocking collectives: 15.8 us -> 0 us
  starting transfers between devices: 29 us -> 36.6 us
    reduce_scatter x2, waiting for transfers between devices: 12.8 us -> 46.3 us  [reduce_pack(): packed = lax.psum_scatter(packed, 'fsdp', scatter_dimension=0, tiled=True)]
    all_to_all x1 -> x0, blocking collectives: 15.8 us -> none  [context_scatter_sum(): lax.all_to_all(values.reshape((count, rows) + values.shape[1:]), axis_nam...]
    ppermute x4, waiting for transfers between devices: 39 us -> 30.1 us  [pair_sum(): other = lax.ppermute(values, axis_name, perm=[(0, 1), (1, 0)])]
    all_to_all x3, waiting for transfers between devices: 42.7 us -> 50.9 us  [context_gather(): gathered = lax.all_to_all(spread, axis_name, 0, 0, tiled=True)]
    all_to_all x2 -> x3, starting transfers between devices: 11.1 us -> 18.5 us  [context_scatter_sum(): lax.all_to_all(values.reshape((count, rows) + values.shape[1:]), axis_nam...]
    concatenate x2 -> x1, local copies, waits for them, and re-layouts: 10.8 us -> 6.78 us  [reduce_pack(): packed = jnp.concatenate(members, axis=1).astype(jnp.bfloat16)]
    all_to_all x2 -> x3, waiting for transfers between devices: 41.3 us -> 42.7 us  [context_scatter_sum(): lax.all_to_all(values.reshape((count, rows) + values.shape[1:]), axis_nam...]
  transfers between devices with their start and end apart: 13 -> 14, of which waited for: 10 -> 12; matrix products, arithmetic and copies ran while one was open for 25% -> 17% of each run, Pallas kernels for 0% -> 0%
where the time goes in v9:
time: 361 us; the launch traced here: 358 us
  waiting for transfers between devices  193 us (53%)
  local copies, waits for them, and re-layouts  45 us (12%)
  matrix products  42.6 us (12%)
  starting transfers between devices  36.6 us (10%)
  other arithmetic  26.1 us (7%)
  between operations  14.6 us (4%)
    all_to_all x3, waiting for transfers between devices, context_gather(): gathered = lax.all_to_all(spread, axis_name, 0, 0, tiled=True)  50.9 us
    reduce_scatter x2, waiting for transfers between devices, reduce_pack(): packed = lax.psum_scatter(packed, 'fsdp', scatter_dimension=0, tiled=True)  46.3 us
    all_to_all x3, waiting for transfers between devices, context_scatter_sum(): lax.all_to_all(values.reshape((count, rows) + values.shape[1:]), axis_nam...  42.7 us
    ppermute x4, waiting for transfers between devices, pair_sum(): other = lax.ppermute(values, axis_name, perm=[(0, 1), (1, 0)])  30.1 us
    all_gather x1, waiting for transfers between devices, on_device(): lax.all_gather(jnp.concatenate([qkv_weight.reshape(shard_rows, 3 * local_...  23.2 us
    all_to_all x3, starting transfers between devices, context_scatter_sum(): lax.all_to_all(values.reshape((count, rows) + values.shape[1:]), axis_nam...  18.5 us
    all_to_all x3, starting transfers between devices, context_gather(): gathered = lax.all_to_all(spread, axis_name, 0, 0, tiled=True)  14 us
    dot_general x1, matrix products, on_device(): jnp.einsum('qhd,khd->hqk', out_heads, values_heads, preferred_element_typ...  7.73 us
  transfers between devices with their start and end apart: 14, of which 12 were waited for; matrix products, arithmetic and copies ran while one was open for 17% of the time, Pallas kernels for 0%

profile of v9, /device:TPU:0, one launch (start us, length us, event | category | flops | bytes accessed | tf_op | source)
XLA Modules:
  0.0 358.2 jit_solution(12075825974921851474)
XLA Ops:
  13.4 1.2 fusion.32
  14.9 23.2 %all-gather.3.cloned.1.call-done = bf16[768,1154]{1,0:T(8,128)(2,1)} async-done(((bf16[96,1154]{1,0:T(8,128)(2,1)}), bf16[768,1154]{1,0:T(8,128)(2,1)}) %all-gather.3.cloned.1.call-update) | async-done | bytes 1772560 | tf_op jit(solution)/shard_map/all_gather | solution.py:115
  38.1 1.3 convert_reduce_fusion.2
  39.4 2.5 fusion.7
  42.2 1.9 broadcast_in_dim.57
  44.1 7.0 %all-to-all-start = ((bf16[8,256,768]{1,2,0:T(8,128)(2,1)}), bf16[8,256,768]{1,2,0:T(8,128)(2,1)S(1)}, u32[]{:S(2)}, u32[]{:S(2)}) async-start(bf16[8,256,768]{1,2,0:T(8,128)(2,1)} %broadcast_in_dim.57), calls=%async_computation | async-start | bytes 6291456 | tf_op jit(solution)/shard_map/all_to_all | solution.py:79
  51.2 1.8 reshape.256
  53.0 1.7 pad_maximum_fusion.4
  56.7 34.6 %all-to-all-done = bf16[8,256,768]{1,2,0:T(8,128)(2,1)S(1)} async-done(((bf16[8,256,768]{1,2,0:T(8,128)(2,1)}), bf16[8,256,768]{1,2,0:T(8,128)(2,1)S(1)}, u32[]{:S(2)}, u32[]{:S(2)}) %all-to-all-start) | async-done | bytes 3145760 | tf_op jit(solution)/shard_map/all_to_all | solution.py:79
  91.2 2.8 copy.98
  94.0 3.9 %fusion.59 = (bf16[2048,384]{1,0:T(8,128)(2,1)}, bf16[2048,384]{1,0:T(8,128)(2,1)}) fusion(bf16[2048,768]{1,0:T(8,128)(2,1)} %bitcast.119), kind=kLoop, calls=%fused_computation.137 | loop fusion | bytes 6291456 | tf_op jit(solution)/shard_map/slice | solution.py:156
  97.9 1.8 copy.100
  99.7 2.6 copy.99
  102.3 2.5 select_reduce_fusion.1
  104.8 4.0 %select_reduce_fusion = f32[6,256]{1,0:T(8,128)S(1)} fusion(f32[6,256,2048]{2,1,0:T(8,128)S(1)} %get-tuple-element.90, f32[6,256]{1,0:T(8,128)S(1)} %get-tuple-element.89, pred[256,2048]{1,0:T(8,128)(4,1)S(1)} %copy-done.3), kind=kLoop, calls=%fused_computation.2 | loop fusion | flops 12581376 | bytes 13119488 | tf_op jit(solution)/shard_map/reduce_sum | solution.py:165
  109.5 3.0 convolution_convert_fusion.7
  112.6 1.6 convolution_convert_fusion.6
  115.1 9.5 %collective-permute-done = bf16[256,768]{1,0:T(8,128)(2,1)S(1)} collective-permute-done((bf16[256,768]{1,0:T(8,128)(2,1)S(1)}, bf16[256,768]{1,0:T(8,128)(2,1)S(1)}, u32[]{:S(2)}, u32[]{:S(2)}) %collective-permute-start) | collective-permute-done | bytes 393248 | tf_op jit(solution)/shard_map/ppermute | solution.py:72
  128.6 1.5 collective-permute-start.1
  130.2 9.4 %collective-permute-done.2 = bf16[256,768]{1,0:T(8,128)(2,1)S(1)} collective-permute-done((bf16[256,768]{1,0:T(8,128)(2,1)S(1)}, bf16[256,768]{1,0:T(8,128)(2,1)S(1)}, u32[]{:S(2)}, u32[]{:S(2)}) %collective-permute-start.2) | collective-permute-done | bytes 393248 | tf_op jit(solution)/shard_map/ppermute | solution.py:72
  140.5 4.6 %collective-permute-done.1 = bf16[256,768]{1,0:T(8,128)(2,1)S(1)} collective-permute-done((bf16[256,768]{1,0:T(8,128)(2,1)S(1)}, bf16[256,768]{1,0:T(8,128)(2,1)S(1)}, u32[]{:S(2)}, u32[]{:S(2)}) %collective-permute-start.1) | collective-permute-done | bytes 393248 | tf_op jit(solution)/shard_map/ppermute | solution.py:72
  147.3 1.7 copy.102
  150.2 7.5 %convolution_convert_fusion.2 = bf16[6,64,2048]{2,1,0:T(8,128)(2,1)S(1)} fusion(bf16[256,6,64]{0,2,1:T(8,128)(2,1)} %bitcast.140, f32[6,256,2048]{2,1,0:T(8,128)} %copy-done, f32[6,256]{1,0:T(8,128)} %copy-done.38, pred[256,2048]{1,0:T(8,128)(4,1)} %broadcast_compare_fusion), kind=kOutput, calls=%fused_computation.10 | convolution fusion | flops 416022528 | bytes 14882816 | tf_op jit(solution)/shard_map/hqk,qhd->khd/dot_general | solution.py:231
  157.8 7.7 %multiply_convert_fusion = bf16[6,256,2048]{2,1,0:T(8,128)(2,1)S(1)} fusion(f32[6,256,2048]{2,1,0:T(8,128)} %copy-done, f32[6,256]{1,0:T(8,128)S(1)} %bitcast.148, f32[6,256]{1,0:T(8,128)S(1)} %copy-done.39, pred[256,2048]{1,0:T(8,128)(4,1)S(1)} %copy-done.4, bf16[256,6,64]{0,2,1:T(8,128)(2,1)S(1)} %bitcast.141, bf16[2048,6,64]{0,2,1:T(8,128)(2,1)S(1)} %bitcast.131), kind=kOutput, calls=%fused_computation | convolution fusion | flops 421527552 | bytes 21180416 | tf_op jit(solution)/shard_map/qhd,khd->hqk/dot_general | solution.py:219
  166.8 1.4 copy-done.1
  169.8 1.9 pad_maximum_fusion
  171.7 4.6 %all-to-all-start.1 = ((bf16[8,256,768]{1,2,0:T(8,128)(2,1)}), bf16[8,256,768]{1,2,0:T(8,128)(2,1)}, u32[]{:S(2)}, u32[]{:S(2)}) async-start(bf16[8,256,768]{1,2,0:T(8,128)(2,1)} %pad_maximum_fusion), calls=%async_computation.1 | async-start | bytes 6291456 | tf_op jit(solution)/shard_map/all_to_all | solution.py:86
  176.6 5.6 %fusion.16 = f32[256,6,64]{0,2,1:T(8,128)} fusion(bf16[2048,6,64]{0,2,1:T(8,128)(2,1)S(1)} %bitcast.118, bf16[6,256,2048]{2,1,0:T(8,128)(2,1)} %copy-done.1), kind=kOutput, calls=%fused_computation.29 | convolution fusion | flops 402751488 | bytes 8257536 | tf_op jit(solution)/shard_map/hqk,khd->qhd/dot_general | solution.py:224
  182.2 32.4 %all-to-all-done.1 = bf16[8,256,768]{1,2,0:T(8,128)(2,1)} async-done(((bf16[8,256,768]{1,2,0:T(8,128)(2,1)}), bf16[8,256,768]{1,2,0:T(8,128)(2,1)}, u32[]{:S(2)}, u32[]{:S(2)}) %all-to-all-start.1) | async-done | bytes 3145760 | tf_op jit(solution)/shard_map/all_to_all | solution.py:86
  214.6 2.4 convert_reduce_fusion
  220.8 6.5 %collective-permute-done.3 = bf16[256,768]{1,0:T(8,128)(2,1)S(1)} collective-permute-done((bf16[256,768]{1,0:T(8,128)(2,1)S(1)}, bf16[256,768]{1,0:T(8,128)(2,1)S(1)}, u32[]{:S(2)}, u32[]{:S(2)}) %collective-permute-start.3) | collective-permute-done | bytes 393248 | tf_op jit(solution)/shard_map/ppermute | solution.py:72
  228.6 2.2 pad_maximum_fusion.1
  230.9 2.3 fusion.9
  233.2 1.5 copy.108
  234.8 2.8 convolution_convert_fusion
  238.9 6.8 %concatenate.53 = bf16[768,2113]{1,0:T(8,128)(2,1)} concatenate(bf16[768,1]{1,0:T(8,128)(2,1)S(1)} %broadcast_in_dim.111, bf16[768,1152]{1,0:T(8,128)(2,1)} %convolution_convert_fusion, bf16[768,576]{1,0:T(8,128)(2,1)S(1)} %copy.108, bf16[768,384]{1,0:T(8,128)(2,1)S(1)} %convolution_convert_fusion.4), dimensions={1} | concatenate | bytes 6491136 | tf_op jit(solution)/shard_map/concatenate | solution.py:262
  245.7 17.7 %reduce-scatter.3.cloned.1.call-done = bf16[96,1153]{1,0:T(8,128)(2,1)} async-done(((bf16[768,1153]{1,0:T(8,128)(2,1)}), bf16[96,1153]{1,0:T(8,128)(2,1)}) %reduce-scatter.3.cloned.1.call-update) | async-done | bytes 221392 | tf_op jit(solution)/shard_map/reduce_scatter | solution.py:263
  263.4 1.7 reshape.260
  265.2 7.0 %all-to-all-start.2 = ((bf16[8,12,1153]{2,1,0:T(8,128)(2,1)}), bf16[8,12,1153]{2,1,0:T(8,128)(2,1)S(1)}, u32[]{:S(2)}, u32[]{:S(2)}) async-start(bf16[8,12,1153]{2,1,0:T(8,128)(2,1)} %reshape.260), calls=%async_computation.3 | async-start | bytes 655360 | tf_op jit(solution)/shard_map/all_to_all | solution.py:86
  272.2 28.6 %reduce-scatter.5.cloned.1.call-done = bf16[96,2113]{1,0:T(8,128)(2,1)} async-done(((bf16[768,2113]{1,0:T(8,128)(2,1)}), bf16[96,2113]{1,0:T(8,128)(2,1)}) %reduce-scatter.5.cloned.1.call-update) | async-done | bytes 405712 | tf_op jit(solution)/shard_map/reduce_scatter | solution.py:263
  300.8 1.9 reshape.262
  302.7 6.9 %all-to-all-start.4 = ((bf16[8,12,2113]{2,1,0:T(8,128)(2,1)}), bf16[8,12,2113]{2,1,0:T(8,128)(2,1)S(1)}, u32[]{:S(2)}, u32[]{:S(2)}) async-start(bf16[8,12,2113]{2,1,0:T(8,128)(2,1)} %reshape.262), calls=%async_computation.6 | async-start | bytes 1114112 | tf_op jit(solution)/shard_map/all_to_all | solution.py:86
  309.7 10.3 %all-to-all-done.4 = bf16[8,12,2113]{2,1,0:T(8,128)(2,1)S(1)} async-done(((bf16[8,12,2113]{2,1,0:T(8,128)(2,1)}), bf16[8,12,2113]{2,1,0:T(8,128)(2,1)S(1)}, u32[]{:S(2)}, u32[]{:S(2)}) %all-to-all-start.4) | async-done | bytes 405728 | tf_op jit(solution)/shard_map/all_to_all | solution.py:86
  320.7 3.4 all-to-all-start.3
  324.3 8.9 %all-to-all-done.3 = bf16[8,12,1153]{2,1,0:T(8,128)(2,1)S(1)} async-done(((bf16[8,12,1153]{2,1,0:T(8,128)(2,1)}), bf16[8,12,1153]{2,1,0:T(8,128)(2,1)S(1)}, u32[]{:S(2)}, u32[]{:S(2)}) %all-to-all-start.3) | async-done | bytes 221408 | tf_op jit(solution)/shard_map/all_to_all | solution.py:79
  334.1 3.5 all-to-all-start.5
  337.7 1.2 fusion.30
  340.6 7.4 %all-to-all-done.5 = bf16[8,12,2113]{2,1,0:T(8,128)(2,1)S(1)} async-done(((bf16[8,12,2113]{2,1,0:T(8,128)(2,1)}), bf16[8,12,2113]{2,1,0:T(8,128)(2,1)S(1)}, u32[]{:S(2)}, u32[]{:S(2)}) %all-to-all-start.5) | async-done | bytes 405728 | tf_op jit(solution)/shard_map/all_to_all | solution.py:79
  (168 shorter events, 35.0 us)
Async XLA Ops:
  7.2 30.9 %all-gather.3.cloned.1.call-start = ((), (), s32[]{:S(2)}) async-start(), calls=%async_computation.8 | async-start | bytes 2211840 | tf_op jit(solution)/shard_map/all_gather | solution.py:115
  11.4 3.3 copy-start.42
  14.6 27.4 %copy-start.33 = (f32[256]{0:T(256)}, f32[256]{0:T(256)S(1)}, u32[]{:S(2)}) copy-start(f32[256]{0:T(256)S(1)} %add_rsqrt_fusion.1) | copy-start | bytes 3076
  14.8 27.3 %copy-start.24 = (f32[256,32]{0,1:T(8,128)}, f32[256,32]{0,1:T(8,128)S(1)}, u32[]{:S(2)}) copy-start(f32[256,32]{0,1:T(8,128)S(1)} %get-tuple-element.87) | copy-start | bytes 98308
  14.9 27.3 %copy-start.26 = (f32[256,32]{0,1:T(8,128)}, f32[256,32]{0,1:T(8,128)S(1)}, u32[]{:S(2)}) copy-start(f32[256,32]{0,1:T(8,128)S(1)} %get-tuple-element.88) | copy-start | bytes 98308
  42.2 60.2 %copy-start.19 = (bf16[256,6,32]{0,2,1:T(8,128)(2,1)}, bf16[256,6,32]{0,2,1:T(8,128)(2,1)S(1)}, u32[]{:S(2)}) copy-start(bf16[256,6,32]{0,2,1:T(8,128)(2,1)S(1)} %get-tuple-element.79) | copy-start | bytes 294916
  42.2 60.1 %copy-start.21 = (bf16[256,6,32]{0,2,1:T(8,128)(2,1)}, bf16[256,6,32]{0,2,1:T(8,128)(2,1)S(1)}, u32[]{:S(2)}) copy-start(bf16[256,6,32]{0,2,1:T(8,128)(2,1)S(1)} %get-tuple-element.80) | copy-start | bytes 294916
  44.1 8.9 %copy-start.29 = (bf16[576,96]{0,1:T(8,128)(2,1)S(1)}, bf16[576,96]{0,1:T(8,128)(2,1)}, u32[]{:S(2)}) copy-start(bf16[576,96]{0,1:T(8,128)(2,1)} %param.16) | copy-start | bytes 331780
  44.1 8.9 %copy-start.31 = (bf16[384,96]{0,1:T(8,128)(2,1)S(1)}, bf16[384,96]{0,1:T(8,128)(2,1)}, u32[]{:S(2)}) copy-start(bf16[384,96]{0,1:T(8,128)(2,1)} %param.13) | copy-start | bytes 221188
  44.1 11.4 %copy-start.37 = (s32[256]{0:T(256)S(1)}, s32[256]{0:T(256)}, u32[]{:S(2)}) copy-start(s32[256]{0:T(256)} %copy-done.36) | copy-start | bytes 3076
  44.1 47.1 %all-to-all-start = ((bf16[8,256,768]{1,2,0:T(8,128)(2,1)}), bf16[8,256,768]{1,2,0:T(8,128)(2,1)S(1)}, u32[]{:S(2)}, u32[]{:S(2)}) async-start(bf16[8,256,768]{1,2,0:T(8,128)(2,1)} %broadcast_in_dim.57), calls=%async_computation | async-start | bytes 6291456 | tf_op jit(solution)/shard_map/all_to_all | solution.py:79
  51.1 61.5 %all-gather.5.cloned.1.call-start = ((), (), s32[]{:S(2)}) async-start(), calls=%async_computation.9 | async-start | bytes 3760128 | tf_op jit(solution)/shard_map/all_gather | solution.py:128
  97.9 4.4 %copy-start.3 = (pred[256,2048]{1,0:T(8,128)(4,1)S(1)}, pred[256,2048]{1,0:T(8,128)(4,1)}, u32[]{:S(2)}) copy-start(pred[256,2048]{1,0:T(8,128)(4,1)} %broadcast_compare_fusion) | copy-start | bytes 1572868
  104.8 4.7 %copy-start = (f32[6,256,2048]{2,1,0:T(8,128)}, f32[6,256,2048]{2,1,0:T(8,128)S(1)}, u32[]{:S(2)}) copy-start(f32[6,256,2048]{2,1,0:T(8,128)S(1)} %get-tuple-element.90) | copy-start | bytes 37748740
  104.8 4.7 %copy-start.11 = (bf16[2048,384]{0,1:T(8,128)(2,1)S(1)}, bf16[2048,384]{0,1:T(8,128)(2,1)}, u32[]{:S(2)}) copy-start(bf16[2048,384]{0,1:T(8,128)(2,1)} %copy.99) | copy-start | bytes 4718596
  108.8 3.7 %copy-start.38 = (f32[6,256]{1,0:T(8,128)}, f32[6,256]{1,0:T(8,128)S(1)}, u32[]{:S(2)}) copy-start(f32[6,256]{1,0:T(8,128)S(1)} %log_add_fusion) | copy-start | bytes 18436
  109.5 15.1 %copy-start.2 = (bf16[256,768]{1,0:T(8,128)(2,1)S(1)}, bf16[256,768]{1,0:T(8,128)(2,1)}, u32[]{:S(2)}) copy-start(bf16[256,768]{1,0:T(8,128)(2,1)} %param.9) | copy-start | bytes 1179652
  112.6 12.5 %copy-start.5 = (bf16[768,2112]{1,0:T(8,128)(2,1)S(1)}, bf16[768,2112]{1,0:T(8,128)(2,1)}, u32[]{:S(2)}) copy-start(bf16[768,2112]{1,0:T(8,128)(2,1)} %all-gather.5.cloned.1.call-done) | copy-start | bytes 9732100
  114.2 11.8 %copy-start.17 = (bf16[256,768]{1,0:T(8,128)(2,1)S(1)}, bf16[256,768]{1,0:T(8,128)(2,1)}, u32[]{:S(2)}) copy-start(bf16[256,768]{1,0:T(8,128)(2,1)} %param.17) | copy-start | bytes 1179652
  114.2 10.4 %collective-permute-start = (bf16[256,768]{1,0:T(8,128)(2,1)S(1)}, bf16[256,768]{1,0:T(8,128)(2,1)S(1)}, u32[]{:S(2)}, u32[]{:S(2)}) collective-permute-start(bf16[256,768]{1,0:T(8,128)(2,1)S(1)} %convolution_convert_fusion.6), channel_id=1, source_target_pairs={{0,8},{8,0},{1,9},{9,1},{2,10},{10,2},{3,11},{11,3},{4,12},{12,4},... | collective-permute-start | bytes 1179656 | tf_op jit(solution)/shard_map/ppermute | solution.py:72
  125.1 20.1 %copy-start.32 = (f32[256]{0:T(256)}, f32[256]{0:T(256)S(1)}, u32[]{:S(2)}) copy-start(f32[256]{0:T(256)S(1)} %add_rsqrt_fusion) | copy-start | bytes 3076
  126.7 13.8 %copy-start.6 = (bf16[256,2,576]{0,2,1:T(8,128)(2,1)}, bf16[256,2,576]{0,2,1:T(8,128)(2,1)S(1)}, u32[]{:S(2)}) copy-start(bf16[256,2,576]{0,2,1:T(8,128)(2,1)S(1)} %pad_maximum_fusion.2) | copy-start | bytes 1769476
  127.4 12.1 %collective-permute-start.2 = (bf16[256,768]{1,0:T(8,128)(2,1)S(1)}, bf16[256,768]{1,0:T(8,128)(2,1)S(1)}, u32[]{:S(2)}, u32[]{:S(2)}) collective-permute-start(bf16[256,768]{1,0:T(8,128)(2,1)S(1)} %fusion.13), channel_id=1, source_target_pairs={{0,8},{8,0},{1,9},{9,1},{2,10},{10,2},{3,11},{11,3},{4,12},{12,4},... | collective-permute-start | bytes 1179656 | tf_op jit(solution)/shard_map/ppermute | solution.py:72
  128.6 16.5 %collective-permute-start.1 = (bf16[256,768]{1,0:T(8,128)(2,1)S(1)}, bf16[256,768]{1,0:T(8,128)(2,1)S(1)}, u32[]{:S(2)}, u32[]{:S(2)}) collective-permute-start(bf16[256,768]{1,0:T(8,128)(2,1)S(1)} %convolution_convert_fusion.5), channel_id=1, source_target_pairs={{0,8},{8,0},{1,9},{9,1},{2,10},{10,2},{3,11},{11,3},{4,12},{12,4},... | collective-permute-start | bytes 1179656 | tf_op jit(solution)/shard_map/ppermute | solution.py:72
  150.1 7.6 %copy-start.4 = (pred[256,2048]{1,0:T(8,128)(4,1)S(1)}, pred[256,2048]{1,0:T(8,128)(4,1)}, u32[]{:S(2)}) copy-start(pred[256,2048]{1,0:T(8,128)(4,1)} %broadcast_compare_fusion) | copy-start | bytes 1572868
  150.1 7.6 %copy-start.12 = (bf16[2048,384]{0,1:T(8,128)(2,1)S(1)}, bf16[2048,384]{0,1:T(8,128)(2,1)}, u32[]{:S(2)}) copy-start(bf16[2048,384]{0,1:T(8,128)(2,1)} %copy.99) | copy-start | bytes 4718596
  150.1 7.6 %copy-start.23 = (bf16[256,384]{0,1:T(8,128)(2,1)S(1)}, bf16[256,384]{0,1:T(8,128)(2,1)}, u32[]{:S(2)}) copy-start(bf16[256,384]{0,1:T(8,128)(2,1)} %copy.102) | copy-start | bytes 589828
  150.2 7.6 %copy-start.39 = (f32[6,256]{1,0:T(8,128)S(1)}, f32[6,256]{1,0:T(8,128)}, u32[]{:S(2)}) copy-start(f32[6,256]{1,0:T(8,128)} %copy-done.38) | copy-start | bytes 18436
  157.8 7.8 %copy-start.20 = (bf16[256,6,32]{0,2,1:T(8,128)(2,1)S(1)}, bf16[256,6,32]{0,2,1:T(8,128)(2,1)}, u32[]{:S(2)}) copy-start(bf16[256,6,32]{0,2,1:T(8,128)(2,1)} %copy-done.19) | copy-start | bytes 294916
  157.8 7.8 %copy-start.22 = (bf16[256,6,32]{0,2,1:T(8,128)(2,1)S(1)}, bf16[256,6,32]{0,2,1:T(8,128)(2,1)}, u32[]{:S(2)}) copy-start(bf16[256,6,32]{0,2,1:T(8,128)(2,1)} %copy-done.21) | copy-start | bytes 294916
  171.7 42.9 %all-to-all-start.1 = ((bf16[8,256,768]{1,2,0:T(8,128)(2,1)}), bf16[8,256,768]{1,2,0:T(8,128)(2,1)}, u32[]{:S(2)}, u32[]{:S(2)}) async-start(bf16[8,256,768]{1,2,0:T(8,128)(2,1)} %pad_maximum_fusion), calls=%async_computation.1 | async-start | bytes 6291456 | tf_op jit(solution)/shard_map/all_to_all | solution.py:86
  176.4 87.1 %reduce-scatter.3.cloned.1.call-start = ((), (), s32[]{:S(2)}) async-start(), calls=%async_computation.10 | async-start | bytes 2211840 | tf_op jit(solution)/shard_map/reduce_scatter | solution.py:263
  182.2 34.9 %copy-start.10 = (f32[256,6,64]{0,2,1:T(8,128)S(1)}, f32[256,6,64]{0,2,1:T(8,128)}, u32[]{:S(2)}) copy-start(f32[256,6,64]{0,2,1:T(8,128)} %fusion.16) | copy-start | bytes 1179652
  217.1 2.9 copy-start.34
  219.3 11.6 %copy-start.13 = (bf16[256,768]{1,0:T(8,128)(2,1)}, bf16[256,768]{1,0:T(8,128)(2,1)S(1)}, u32[]{:S(2)}) copy-start(bf16[256,768]{1,0:T(8,128)(2,1)S(1)} %fusion.10) | copy-start | bytes 1179652
  219.3 8.1 %collective-permute-start.3 = (bf16[256,768]{1,0:T(8,128)(2,1)S(1)}, bf16[256,768]{1,0:T(8,128)(2,1)S(1)}, u32[]{:S(2)}, u32[]{:S(2)}) collective-permute-start(bf16[256,768]{1,0:T(8,128)(2,1)S(1)} %fusion.10), channel_id=1, source_target_pairs={{0,8},{8,0},{1,9},{9,1},{2,10},{10,2},{3,11},{11,3},{4,12},{12,4},... | collective-permute-start | bytes 1179656 | tf_op jit(solution)/shard_map/ppermute | solution.py:72
  230.8 3.9 %copy-start.7 = (bf16[256,2,576]{0,2,1:T(8,128)(2,1)S(1)}, bf16[256,2,576]{0,2,1:T(8,128)(2,1)}, u32[]{:S(2)}) copy-start(bf16[256,2,576]{0,2,1:T(8,128)(2,1)} %copy-done.6) | copy-start | bytes 1769476
  230.9 69.9 %reduce-scatter.5.cloned.1.call-start = ((), (), s32[]{:S(2)}) async-start(), calls=%async_computation.11 | async-start | bytes 3760128 | tf_op jit(solution)/shard_map/reduce_scatter | solution.py:263
  234.8 3.6 %copy-start.9 = (bf16[6,64,256]{2,1,0:T(8,128)(2,1)S(1)}, bf16[6,64,256]{2,1,0:T(8,128)(2,1)}, u32[]{:S(2)}) copy-start(bf16[6,64,256]{2,1,0:T(8,128)(2,1)} %copy-done.8) | copy-start | bytes 589828
  245.7 63.9 %copy-start.41 = (f32[256]{0:T(256)S(1)}, f32[256]{0:T(256)}, u32[]{:S(2)}) copy-start(f32[256]{0:T(256)} %get-tuple-element.61) | copy-start | bytes 3076
  245.7 78.5 %copy-start.40 = (f32[256]{0:T(256)S(1)}, f32[256]{0:T(256)}, u32[]{:S(2)}) copy-start(f32[256]{0:T(256)} %get-tuple-element.62) | copy-start | bytes 3076
  265.2 72.5 %copy-start.14 = (bf16[256,768]{1,0:T(8,128)(2,1)S(1)}, bf16[256,768]{1,0:T(8,128)(2,1)}, u32[]{:S(2)}) copy-start(bf16[256,768]{1,0:T(8,128)(2,1)} %copy-done.13) | copy-start | bytes 1179652
  265.2 72.5 %copy-start.16 = (bf16[256,768]{1,0:T(8,128)(2,1)S(1)}, bf16[256,768]{1,0:T(8,128)(2,1)}, u32[]{:S(2)}) copy-start(bf16[256,768]{1,0:T(8,128)(2,1)} %copy-done.15) | copy-start | bytes 1179652
  265.2 72.5 %copy-start.35 = (f32[256]{0:T(256)S(1)}, f32[256]{0:T(256)}, u32[]{:S(2)}) copy-start(f32[256]{0:T(256)} %copy-done.33) | copy-start | bytes 3076
  265.2 37.5 %all-to-all-start.2 = ((bf16[8,12,1153]{2,1,0:T(8,128)(2,1)}), bf16[8,12,1153]{2,1,0:T(8,128)(2,1)S(1)}, u32[]{:S(2)}, u32[]{:S(2)}) async-start(bf16[8,12,1153]{2,1,0:T(8,128)(2,1)} %reshape.260), calls=%async_computation.3 | async-start | bytes 655360 | tf_op jit(solution)/shard_map/all_to_all | solution.py:86
  302.7 17.3 %all-to-all-start.4 = ((bf16[8,12,2113]{2,1,0:T(8,128)(2,1)}), bf16[8,12,2113]{2,1,0:T(8,128)(2,1)S(1)}, u32[]{:S(2)}, u32[]{:S(2)}) async-start(bf16[8,12,2113]{2,1,0:T(8,128)(2,1)} %reshape.262), calls=%async_computation.6 | async-start | bytes 1114112 | tf_op jit(solution)/shard_map/all_to_all | solution.py:86
  320.7 12.5 %all-to-all-start.3 = ((bf16[8,12,1153]{2,1,0:T(8,128)(2,1)}), bf16[8,12,1153]{2,1,0:T(8,128)(2,1)S(1)}, u32[]{:S(2)}, u32[]{:S(2)}) async-start(bf16[8,12,1153]{2,1,0:T(8,128)(2,1)} %broadcast_in_dim.107), calls=%async_computation.4 | async-start | bytes 655360 | tf_op jit(solution)/shard_map/all_to_all | solution.py:79
  334.1 13.8 %all-to-all-start.5 = ((bf16[8,12,2113]{2,1,0:T(8,128)(2,1)}), bf16[8,12,2113]{2,1,0:T(8,128)(2,1)S(1)}, u32[]{:S(2)}, u32[]{:S(2)}) async-start(bf16[8,12,2113]{2,1,0:T(8,128)(2,1)} %broadcast_in_dim.109), calls=%async_computation.7 | async-start | bytes 1114112 | tf_op jit(solution)/shard_map/all_to_all | solution.py:79
  (9 other events, 18.1 us)
Sparse Core Ops, SparseCore 0:
  10.7 27.3 all-gather.2
  54.9 29.0 all-gather.4
  231.0 32.3 reduce-scatter.2
  265.8 34.8 reduce-scatter.4

commit v10 on v9

--- a/solution.py
+++ b/solution.py
@@ -211,6 +211,28 @@
         jnp.bfloat16
     )
     proj_grad_t = jnp.dot(resid_bf.T, mixed_flat, preferred_element_type=jnp.float32)
+
+    def reduce_pack(packed, members):
+        packed = context_gather(
+            context_scatter_sum(packed, "context").astype(jnp.bfloat16), "context"
+        ).astype(jnp.float32)
+        pieces = []
+        start = 0
+        for member in members:
+            pieces.append(packed[:, start : start + member.shape[1]])
+            start += member.shape[1]
+        return pieces
+
+    mlp_members = [
+        mlpgain_grad[:, None],
+        gelu_grad.reshape(feature_count, 2 * hidden),
+        down_grad_t,
+        proj_grad_t,
+    ]
+    mlp_packed, out_grad = lax.optimization_barrier(
+        (jnp.concatenate(mlp_members, axis=1).astype(jnp.bfloat16), out_grad)
+    )
+    mlp_shard = lax.psum_scatter(mlp_packed, "fsdp", scatter_dimension=0, tiled=True)
     out_heads = out_grad.reshape(row_count, head_count, HD)
     delta = jnp.transpose(
         jnp.sum(out_heads.astype(jnp.float32) * mixed.astype(jnp.float32), axis=2)
@@ -231,9 +253,11 @@
     value_all = jnp.einsum(
         "hqk,qhd->khd", fwd_weights, out_heads, preferred_element_type=jnp.float32
     ).reshape(group_rows, local_width)
-    kv_grad = context_scatter_sum(
-        jnp.concatenate([key_all, value_all], axis=1).astype(jnp.bfloat16), "context"
-    )
+    kv_partial, mlp_shard = lax.optimization_barrier(
+        (jnp.concatenate([key_all, value_all], axis=1).astype(jnp.bfloat16), mlp_shard)
+    )
+    kv_grad = context_scatter_sum(kv_partial, "context")
+    mlp_pieces = reduce_pack(mlp_shard, mlp_members)
     key_grad, value_grad = (kv_grad[:, :local_width], kv_grad[:, local_width:])
     key_grad = key_grad.reshape(row_count, head_count, HD)
     value_grad = value_grad.reshape(row_count, head_count, HD)
@@ -258,29 +282,15 @@
     )
     attngain_grad = jnp.sum(attn_in_grad * normed_attn, axis=0)
     input_grad = resid_grad + norm_back(attn_in_grad, normed_attn, spread_attn, attn_scale)
-    def reduce_pack(members):
-        packed = jnp.concatenate(members, axis=1).astype(jnp.bfloat16)
-        packed = lax.psum_scatter(packed, "fsdp", scatter_dimension=0, tiled=True)
-        packed = context_gather(
-            context_scatter_sum(packed, "context").astype(jnp.bfloat16), "context"
-        ).astype(jnp.float32)
-        pieces = []
-        start = 0
-        for member in members:
-            pieces.append(packed[:, start : start + member.shape[1]])
-            start += member.shape[1]
-        return pieces
-
-    mlp_pieces = reduce_pack(
-        [
-            mlpgain_grad[:, None],
-            gelu_grad.reshape(feature_count, 2 * hidden),
-            down_grad_t,
-            proj_grad_t,
-        ]
-    )
+    attn_members = [attngain_grad[:, None], qkv_grad.reshape(feature_count, 3 * local_width)]
     attn_pieces = reduce_pack(
-        [attngain_grad[:, None], qkv_grad.reshape(feature_count, 3 * local_width)]
+        lax.psum_scatter(
+            jnp.concatenate(attn_members, axis=1).astype(jnp.bfloat16),
+            "fsdp",
+            scatter_dimension=0,
+            tiled=True,
+        ),
+        attn_members,
     )
     shares = (
         attn_pieces[0][:, 0],

time: 361 us -> 331 us (0.917)
  waiting for transfers between devices: 193 us -> 133 us
  blocking collectives: 0 us -> 30 us
  starting transfers between devices: 36.6 us -> 27.8 us
  matrix products: 42.6 us -> 47.2 us
    reduce_scatter x2, waiting for transfers between devices: 46.3 us -> 2.27 us  [the longest x1 2.23 us: on_device(): lax.psum_scatter(mlp_packed, 'fsdp', scatter_dimension=0, tiled=True)]
    all_to_all x0 -> x2, blocking collectives: none -> 30 us  [the longest x1 17 us: context_scatter_sum(): lax.all_to_all(values.reshape((count, rows) + values.shape[1:]), axis_nam...]
    ppermute x4, waiting for transfers between devices: 30.1 us -> 22.5 us  [pair_sum(): other = lax.ppermute(values, axis_name, perm=[(0, 1), (1, 0)])]
    all_to_all x3 -> x2, waiting for transfers between devices: 50.9 us -> 43.8 us  [context_gather(): gathered = lax.all_to_all(spread, axis_name, 0, 0, tiled=True)]
    reshape x0 -> x2, local copies, waits for them, and re-layouts: none -> 5.25 us  [the longest x1 2.67 us: on_device(): key_all = (jnp.einsum('hqk,qhd->khd', score_grad, query_bf, preferred_ele...]
    all_to_all x3 -> x2, starting transfers between devices: 18.5 us -> 13.4 us  [context_scatter_sum(): lax.all_to_all(values.reshape((count, rows) + values.shape[1:]), axis_nam...]
    reshape x2 -> x3, local copies, waits for them, and re-layouts: 3.64 us -> 7.5 us  [context_scatter_sum(): values.reshape((count, rows) + values.shape[1:])]
    all_to_all x3 -> x2, starting transfers between devices: 14 us -> 10.4 us  [context_gather(): gathered = lax.all_to_all(spread, axis_name, 0, 0, tiled=True)]
  transfers between devices with their start and end apart: 14 -> 12, of which waited for: 12 -> 10; matrix products, arithmetic and copies ran while one was open for 17% -> 25% of each run, Pallas kernels for 0% -> 0%
where the time goes in v10:
time: 331 us; the launch traced here: 330 us
  waiting for transfers between devices  133 us (40%)
  local copies, waits for them, and re-layouts  48.5 us (15%)
  matrix products  47.2 us (14%)
  blocking collectives  30 us (9%)
  other arithmetic  29.4 us (9%)
  starting transfers between devices  27.8 us (8%)
  between operations  14.3 us (4%)
    all_to_all x2, waiting for transfers between devices, context_gather(): gathered = lax.all_to_all(spread, axis_name, 0, 0, tiled=True)  43.8 us
    all_to_all x2, waiting for transfers between devices, context_scatter_sum(): lax.all_to_all(values.reshape((count, rows) + values.shape[1:]), axis_nam...  40.8 us
    all_gather x1, waiting for transfers between devices, on_device(): lax.all_gather(jnp.concatenate([qkv_weight.reshape(shard_rows, 3 * local_...  23.2 us
    ppermute x4, waiting for transfers between devices, pair_sum(): other = lax.ppermute(values, axis_name, perm=[(0, 1), (1, 0)])  22.5 us
    all_to_all x1, blocking collectives, context_scatter_sum(): lax.all_to_all(values.reshape((count, rows) + values.shape[1:]), axis_nam...  17 us
    all_to_all x2, starting transfers between devices, context_scatter_sum(): lax.all_to_all(values.reshape((count, rows) + values.shape[1:]), axis_nam...  13.4 us
    all_to_all x1, blocking collectives, context_gather(): gathered = lax.all_to_all(spread, axis_name, 0, 0, tiled=True)  12.9 us
    all_to_all x2, starting transfers between devices, context_gather(): gathered = lax.all_to_all(spread, axis_name, 0, 0, tiled=True)  10.4 us
  transfers between devices with their start and end apart: 12, of which 10 were waited for; matrix products, arithmetic and copies ran while one was open for 25% of the time, Pallas kernels for 0%

profile of v10, /device:TPU:0, one launch (start us, length us, event | category | flops | bytes accessed | tf_op | source)
XLA Modules:
  0.0 329.8 jit_solution(15689237860721782842)
XLA Ops:
  14.9 23.2 %all-gather.3.cloned.1.call-done = bf16[768,1154]{1,0:T(8,128)(2,1)} async-done(((bf16[96,1154]{1,0:T(8,128)(2,1)}), bf16[768,1154]{1,0:T(8,128)(2,1)}) %all-gather.3.cloned.1.call-update) | async-done | bytes 1772560 | tf_op jit(solution)/shard_map/all_gather | solution.py:115
  39.4 2.5 fusion.7
  42.9 1.9 broadcast_in_dim.57
  44.7 7.0 %all-to-all-start = ((bf16[8,256,768]{1,2,0:T(8,128)(2,1)}), bf16[8,256,768]{1,2,0:T(8,128)(2,1)S(1)}, u32[]{:S(2)}, u32[]{:S(2)}) async-start(bf16[8,256,768]{1,2,0:T(8,128)(2,1)} %broadcast_in_dim.57), calls=%async_computation | async-start | bytes 6291456 | tf_op jit(solution)/shard_map/all_to_all | solution.py:79
  52.9 1.7 pad_maximum_fusion.4
  56.0 35.9 %all-to-all-done = bf16[8,256,768]{1,2,0:T(8,128)(2,1)S(1)} async-done(((bf16[8,256,768]{1,2,0:T(8,128)(2,1)}), bf16[8,256,768]{1,2,0:T(8,128)(2,1)S(1)}, u32[]{:S(2)}, u32[]{:S(2)}) %all-to-all-start) | async-done | bytes 3145760 | tf_op jit(solution)/shard_map/all_to_all | solution.py:79
  91.9 2.8 copy.98
  94.7 3.3 %fusion.59 = (bf16[2048,384]{1,0:T(8,128)(2,1)}, bf16[2048,384]{1,0:T(8,128)(2,1)S(1)}) fusion(bf16[2048,768]{1,0:T(8,128)(2,1)} %bitcast.115), kind=kLoop, calls=%fused_computation.137 | loop fusion | bytes 6291456 | tf_op jit(solution)/shard_map/slice | solution.py:156
  98.0 1.7 copy.100
  99.8 1.7 copy.99
  101.5 3.6 %select_reduce_fusion.1 = (f32[6,256]{1,0:T(8,128)S(1)}, f32[6,256,2048]{2,1,0:T(8,128)S(1)}) fusion(pred[256,2048]{1,0:T(8,128)(4,1)} %broadcast_compare_fusion, bf16[2048,6,64]{0,2,1:T(8,128)(2,1)S(1)} %bitcast.112, bf16[256,6,32]{0,2,1:T(8,128)(2,1)S(1)} %copy-done.18, bf16[256,6,32]{0,2,1:T(8,128)(2,1)S(1)} %copy-done.16), kind=kOutput, calls=%fused_computation.3 | convolution fusion | flops 412482048 | bytes 14882816 | tf_op jit(solution)/shard_map/qhd,khd->hqk/dot_general | solution.py:162
  105.1 4.0 %select_reduce_fusion = f32[6,256]{1,0:T(8,128)S(1)} fusion(f32[6,256,2048]{2,1,0:T(8,128)S(1)} %get-tuple-element.98, f32[6,256]{1,0:T(8,128)S(1)} %get-tuple-element.97, pred[256,2048]{1,0:T(8,128)(4,1)S(1)} %copy-done.3), kind=kLoop, calls=%fused_computation.2 | loop fusion | flops 12581376 | bytes 13119488 | tf_op jit(solution)/shard_map/reduce_sum | solution.py:165
  109.8 3.0 convolution_convert_fusion.7
  112.9 1.6 convolution_convert_fusion.6
  115.4 9.5 %collective-permute-done = bf16[256,768]{1,0:T(8,128)(2,1)S(1)} collective-permute-done((bf16[256,768]{1,0:T(8,128)(2,1)S(1)}, bf16[256,768]{1,0:T(8,128)(2,1)S(1)}, u32[]{:S(2)}, u32[]{:S(2)}) %collective-permute-start) | collective-permute-done | bytes 393248 | tf_op jit(solution)/shard_map/ppermute | solution.py:72
  127.0 1.5 fusion.13
  130.3 1.3 fusion.9
  131.7 1.4 collective-permute-start.1
  133.1 2.2 copy.104
  135.3 2.1 convolution_convert_fusion.1
  137.4 3.4 %collective-permute-done.2 = bf16[256,768]{1,0:T(8,128)(2,1)} collective-permute-done((bf16[256,768]{1,0:T(8,128)(2,1)}, bf16[256,768]{1,0:T(8,128)(2,1)}, u32[]{:S(2)}, u32[]{:S(2)}) %collective-permute-start.2) | collective-permute-done | bytes 393248 | tf_op jit(solution)/shard_map/ppermute | solution.py:72
  140.8 1.5 multiply_reduce_fusion
  143.2 3.2 collective-permute-done.1
  146.4 2.5 multiply_add_fusion
  149.3 7.1 %concatenate.42 = bf16[768,2113]{1,0:T(8,128)(2,1)} concatenate(bf16[768,1]{1,0:T(8,128)(2,1)} %broadcast_in_dim.110, bf16[768,1152]{1,0:T(8,128)(2,1)} %convolution_convert_fusion.1, bf16[768,576]{1,0:T(8,128)(2,1)} %copy.104, bf16[768,384]{1,0:T(8,128)(2,1)S(1)} %convolution_convert_fusion.4), dimensions={1} | concatenate | bytes 6491136 | tf_op jit(solution)/shard_map/concatenate | solution.py:233
  156.4 2.2 convolution_convert_fusion.8
  158.6 1.7 copy.105
  161.4 8.2 %multiply_convert_fusion = bf16[6,256,2048]{2,1,0:T(8,128)(2,1)S(1)} fusion(f32[6,256,2048]{2,1,0:T(8,128)} %copy-done, f32[6,256]{1,0:T(8,128)S(1)} %bitcast.142, f32[6,256]{1,0:T(8,128)S(1)} %copy-done.30, pred[256,2048]{1,0:T(8,128)(4,1)S(1)} %copy-done.4, bf16[256,6,64]{0,2,1:T(8,128)(2,1)} %bitcast.134, bf16[2048,6,64]{0,2,1:T(8,128)(2,1)} %bitcast.124), kind=kOutput, calls=%fused_computation | convolution fusion | flops 421527552 | bytes 21180416 | tf_op jit(solution)/shard_map/qhd,khd->hqk/dot_general | solution.py:241
  169.7 2.8 multiply_convert_fusion.1
  172.7 2.7 copy.106
  175.4 8.8 %convolution_convert_fusion.2 = bf16[6,64,2048]{2,1,0:T(8,128)(2,1)} fusion(bf16[256,6,64]{0,2,1:T(8,128)(2,1)} %bitcast.135, f32[6,256,2048]{2,1,0:T(8,128)} %copy-done, f32[6,256]{1,0:T(8,128)S(1)} %copy-done.30, pred[256,2048]{1,0:T(8,128)(4,1)S(1)} %copy-done.4), kind=kOutput, calls=%fused_computation.10 | convolution fusion | flops 416022528 | bytes 14882816 | tf_op jit(solution)/shard_map/hqk,qhd->khd/dot_general | solution.py:253
  184.2 2.6 copy.107
  186.7 3.9 %pad_maximum_fusion = bf16[2048,768]{1,0:T(8,128)(2,1)} fusion(bf16[2048,384]{1,0:T(8,128)(2,1)} %copy.107, bf16[2048,384]{1,0:T(8,128)(2,1)} %copy.106), kind=kLoop, calls=%fused_computation.8 | loop fusion | flops 6291456 | bytes 6291456 | tf_op jit(solution)/shard_map/concatenate | solution.py:257
  190.6 2.2 reduce-scatter.3.cloned.1.call-done
  192.8 4.7 %copy.108 = bf16[8,256,768]{1,2,0:T(8,128)(2,1)} copy(bf16[8,256,768]{2,1,0:T(8,128)(2,1)} %bitcast.114) | data formatting | bytes 6291456 | tf_op jit(solution)/shard_map/reshape | solution.py:87
  197.5 7.0 %all-to-all-start.1 = ((bf16[8,256,768]{1,2,0:T(8,128)(2,1)}), bf16[8,256,768]{1,2,0:T(8,128)(2,1)}, u32[]{:S(2)}, u32[]{:S(2)}) async-start(bf16[8,256,768]{1,2,0:T(8,128)(2,1)} %copy.108), calls=%async_computation.2 | async-start | bytes 6291456 | tf_op jit(solution)/shard_map/all_to_all | solution.py:86
  204.7 4.8 %fusion.16 = f32[256,6,64]{0,2,1:T(8,128)S(1)} fusion(bf16[2048,6,64]{0,2,1:T(8,128)(2,1)S(1)} %bitcast.113, bf16[6,256,2048]{2,1,0:T(8,128)(2,1)} %copy-done.1), kind=kOutput, calls=%fused_computation.29 | convolution fusion | flops 402751488 | bytes 8257536 | tf_op jit(solution)/shard_map/hqk,khd->qhd/dot_general | solution.py:246
  209.6 31.7 %all-to-all-done.1 = bf16[8,256,768]{1,2,0:T(8,128)(2,1)} async-done(((bf16[8,256,768]{1,2,0:T(8,128)(2,1)}), bf16[8,256,768]{1,2,0:T(8,128)(2,1)}, u32[]{:S(2)}, u32[]{:S(2)}) %all-to-all-start.1) | async-done | bytes 3145760 | tf_op jit(solution)/shard_map/all_to_all | solution.py:86
  241.2 2.5 convert_reduce_fusion
  246.4 6.3 %collective-permute-done.3 = bf16[256,768]{1,0:T(8,128)(2,1)S(1)} collective-permute-done((bf16[256,768]{1,0:T(8,128)(2,1)S(1)}, bf16[256,768]{1,0:T(8,128)(2,1)S(1)}, u32[]{:S(2)}, u32[]{:S(2)}) %collective-permute-start.3) | collective-permute-done | bytes 393248 | tf_op jit(solution)/shard_map/ppermute | solution.py:72
  253.7 2.2 pad_maximum_fusion.1
  257.0 17.0 %all_to_all.30 = bf16[8,12,2113]{2,1,0:T(8,128)(2,1)S(1)} all-to-all(bf16[8,12,2113]{2,1,0:T(8,128)(2,1)S(1)} %reshape.267), channel_id=1, replica_groups=mesh['fsdp'=8,'tensor'=2,'context'=8] {'context'}, dimensions={0} | all-to-all | bytes 811392 | tf_op jit(solution)/shard_map/all_to_all | solution.py:86
  274.2 12.9 %all_to_all.31 = bf16[8,12,2113]{2,1,0:T(8,128)(2,1)S(1)} all-to-all(bf16[8,12,2113]{2,1,0:T(8,128)(2,1)S(1)} %broadcast_in_dim.109), channel_id=1, replica_groups=mesh['fsdp'=8,'tensor'=2,'context'=8] {'context'}, dimensions={0} | all-to-all | bytes 811392 | tf_op jit(solution)/shard_map/all_to_all | solution.py:79
  290.9 1.7 reshape.265
  292.6 6.5 %all-to-all-start.2 = ((bf16[8,12,1153]{2,1,0:T(8,128)(2,1)}), bf16[8,12,1153]{2,1,0:T(8,128)(2,1)S(1)}, u32[]{:S(2)}, u32[]{:S(2)}) async-start(bf16[8,12,1153]{2,1,0:T(8,128)(2,1)} %reshape.265), calls=%async_computation.4 | async-start | bytes 655360 | tf_op jit(solution)/shard_map/all_to_all | solution.py:86
  299.1 9.1 %all-to-all-done.2 = bf16[8,12,1153]{2,1,0:T(8,128)(2,1)S(1)} async-done(((bf16[8,12,1153]{2,1,0:T(8,128)(2,1)}), bf16[8,12,1153]{2,1,0:T(8,128)(2,1)S(1)}, u32[]{:S(2)}, u32[]{:S(2)}) %all-to-all-start.2) | async-done | bytes 221408 | tf_op jit(solution)/shard_map/all_to_all | solution.py:86
  309.0 3.4 %all-to-all-start.3 = ((bf16[8,12,1153]{2,1,0:T(8,128)(2,1)}), bf16[8,12,1153]{2,1,0:T(8,128)(2,1)S(1)}, u32[]{:S(2)}, u32[]{:S(2)}) async-start(bf16[8,12,1153]{2,1,0:T(8,128)(2,1)} %broadcast_in_dim.108), calls=%async_computation.5 | async-start | bytes 655360 | tf_op jit(solution)/shard_map/all_to_all | solution.py:79
  313.7 7.8 %all-to-all-done.3 = bf16[8,12,1153]{2,1,0:T(8,128)(2,1)S(1)} async-done(((bf16[8,12,1153]{2,1,0:T(8,128)(2,1)}), bf16[8,12,1153]{2,1,0:T(8,128)(2,1)S(1)}, u32[]{:S(2)}, u32[]{:S(2)}) %all-to-all-start.3) | async-done | bytes 221408 | tf_op jit(solution)/shard_map/all_to_all | solution.py:79
  (141 shorter events, 32.9 us)
Async XLA Ops:
  7.2 30.9 %all-gather.3.cloned.1.call-start = ((), (), s32[]{:S(2)}) async-start(), calls=%async_computation.8 | async-start | bytes 2211840 | tf_op jit(solution)/shard_map/all_gather | solution.py:115
  14.6 28.2 %copy-start.27 = (f32[256]{0:T(256)}, f32[256]{0:T(256)S(1)}, u32[]{:S(2)}) copy-start(f32[256]{0:T(256)S(1)} %add_rsqrt_fusion.1) | copy-start | bytes 3076
  14.8 28.0 %copy-start.20 = (f32[256,32]{0,1:T(8,128)}, f32[256,32]{0,1:T(8,128)S(1)}, u32[]{:S(2)}) copy-start(f32[256,32]{0,1:T(8,128)S(1)} %get-tuple-element.95) | copy-start | bytes 98308
  14.8 28.0 %copy-start.22 = (f32[256,32]{0,1:T(8,128)}, f32[256,32]{0,1:T(8,128)S(1)}, u32[]{:S(2)}) copy-start(f32[256,32]{0,1:T(8,128)S(1)} %get-tuple-element.96) | copy-start | bytes 98308
  44.7 8.2 %copy-start.24 = (bf16[576,96]{0,1:T(8,128)(2,1)S(1)}, bf16[576,96]{0,1:T(8,128)(2,1)}, u32[]{:S(2)}) copy-start(bf16[576,96]{0,1:T(8,128)(2,1)} %param.16) | copy-start | bytes 331780
  44.7 47.1 %all-to-all-start = ((bf16[8,256,768]{1,2,0:T(8,128)(2,1)}), bf16[8,256,768]{1,2,0:T(8,128)(2,1)S(1)}, u32[]{:S(2)}, u32[]{:S(2)}) async-start(bf16[8,256,768]{1,2,0:T(8,128)(2,1)} %broadcast_in_dim.57), calls=%async_computation | async-start | bytes 6291456 | tf_op jit(solution)/shard_map/all_to_all | solution.py:79
  51.7 61.1 %all-gather.5.cloned.1.call-start = ((), (), s32[]{:S(2)}) async-start(), calls=%async_computation.9 | async-start | bytes 3760128 | tf_op jit(solution)/shard_map/all_gather | solution.py:128
  54.6 138.2 %reduce-scatter.3.cloned.1.call-start = ((), (), s32[]{:S(2)}) async-start(), calls=%async_computation.10 | async-start | bytes 3760128 | tf_op jit(solution)/shard_map/reduce_scatter | solution.py:235
  98.0 3.5 %copy-start.16 = (bf16[256,6,32]{0,2,1:T(8,128)(2,1)S(1)}, bf16[256,6,32]{0,2,1:T(8,128)(2,1)}, u32[]{:S(2)}) copy-start(bf16[256,6,32]{0,2,1:T(8,128)(2,1)} %get-tuple-element.87) | copy-start | bytes 294916
  98.0 3.5 %copy-start.18 = (bf16[256,6,32]{0,2,1:T(8,128)(2,1)S(1)}, bf16[256,6,32]{0,2,1:T(8,128)(2,1)}, u32[]{:S(2)}) copy-start(bf16[256,6,32]{0,2,1:T(8,128)(2,1)} %get-tuple-element.88) | copy-start | bytes 294916
  101.5 3.6 %copy-start.3 = (pred[256,2048]{1,0:T(8,128)(4,1)S(1)}, pred[256,2048]{1,0:T(8,128)(4,1)}, u32[]{:S(2)}) copy-start(pred[256,2048]{1,0:T(8,128)(4,1)} %broadcast_compare_fusion) | copy-start | bytes 1572868
  105.1 4.7 %copy-start = (f32[6,256,2048]{2,1,0:T(8,128)}, f32[6,256,2048]{2,1,0:T(8,128)S(1)}, u32[]{:S(2)}) copy-start(f32[6,256,2048]{2,1,0:T(8,128)S(1)} %get-tuple-element.98) | copy-start | bytes 37748740
  105.1 4.7 %copy-start.9 = (bf16[2048,384]{0,1:T(8,128)(2,1)S(1)}, bf16[2048,384]{0,1:T(8,128)(2,1)}, u32[]{:S(2)}) copy-start(bf16[2048,384]{0,1:T(8,128)(2,1)} %copy.99) | copy-start | bytes 4718596
  109.1 3.7 %copy-start.29 = (f32[6,256]{1,0:T(8,128)}, f32[6,256]{1,0:T(8,128)S(1)}, u32[]{:S(2)}) copy-start(f32[6,256]{1,0:T(8,128)S(1)} %log_add_fusion) | copy-start | bytes 18436
  109.8 15.1 %copy-start.2 = (bf16[256,768]{1,0:T(8,128)(2,1)S(1)}, bf16[256,768]{1,0:T(8,128)(2,1)}, u32[]{:S(2)}) copy-start(bf16[256,768]{1,0:T(8,128)(2,1)} %param.9) | copy-start | bytes 1179652
  112.8 2.5 copy-start.6
  112.9 12.5 %copy-start.5 = (bf16[768,2112]{1,0:T(8,128)(2,1)S(1)}, bf16[768,2112]{1,0:T(8,128)(2,1)}, u32[]{:S(2)}) copy-start(bf16[768,2112]{1,0:T(8,128)(2,1)} %all-gather.5.cloned.1.call-done) | copy-start | bytes 9732100
  114.5 11.8 %copy-start.14 = (bf16[256,768]{1,0:T(8,128)(2,1)S(1)}, bf16[256,768]{1,0:T(8,128)(2,1)}, u32[]{:S(2)}) copy-start(bf16[256,768]{1,0:T(8,128)(2,1)} %param.17) | copy-start | bytes 1179652
  114.5 10.4 %collective-permute-start = (bf16[256,768]{1,0:T(8,128)(2,1)S(1)}, bf16[256,768]{1,0:T(8,128)(2,1)S(1)}, u32[]{:S(2)}, u32[]{:S(2)}) collective-permute-start(bf16[256,768]{1,0:T(8,128)(2,1)S(1)} %convolution_convert_fusion.6), channel_id=1, source_target_pairs={{0,8},{8,0},{1,9},{9,1},{2,10},{10,2},{3,11},{11,3},{4,12},{12,4},... | collective-permute-start | bytes 1179656 | tf_op jit(solution)/shard_map/ppermute | solution.py:72
  125.3 15.5 %copy-start.26 = (f32[256]{0:T(256)}, f32[256]{0:T(256)S(1)}, u32[]{:S(2)}) copy-start(f32[256]{0:T(256)S(1)} %add_rsqrt_fusion) | copy-start | bytes 3076
  128.5 12.4 %collective-permute-start.2 = (bf16[256,768]{1,0:T(8,128)(2,1)}, bf16[256,768]{1,0:T(8,128)(2,1)}, u32[]{:S(2)}, u32[]{:S(2)}) collective-permute-start(bf16[256,768]{1,0:T(8,128)(2,1)} %fusion.13), channel_id=1, source_target_pairs={{0,8},{8,0},{1,9},{9,1},{2,10},{10,2},{3,11},{11,3},{4,12},{12,4},... | collective-permute-start | bytes 1179656 | tf_op jit(solution)/shard_map/ppermute | solution.py:72
  131.7 14.7 %collective-permute-start.1 = (bf16[256,768]{1,0:T(8,128)(2,1)}, bf16[256,768]{1,0:T(8,128)(2,1)}, u32[]{:S(2)}, u32[]{:S(2)}) collective-permute-start(bf16[256,768]{1,0:T(8,128)(2,1)} %convolution_convert_fusion.5), channel_id=1, source_target_pairs={{0,8},{8,0},{1,9},{9,1},{2,10},{10,2},{3,11},{11,3},{4,12},{12,4},... | collective-permute-start | bytes 1179656 | tf_op jit(solution)/shard_map/ppermute | solution.py:72
  135.3 11.1 %copy-start.15 = (bf16[256,768]{1,0:T(8,128)(2,1)S(1)}, bf16[256,768]{1,0:T(8,128)(2,1)}, u32[]{:S(2)}) copy-start(bf16[256,768]{1,0:T(8,128)(2,1)} %param.17) | copy-start | bytes 1179652
  137.4 11.5 %copy-start.7 = (bf16[6,64,256]{2,1,0:T(8,128)(2,1)S(1)}, bf16[6,64,256]{2,1,0:T(8,128)(2,1)}, u32[]{:S(2)}) copy-start(bf16[6,64,256]{2,1,0:T(8,128)(2,1)} %copy-done.6) | copy-start | bytes 589828
  156.4 4.0 %copy-start.8 = (bf16[6,64,256]{2,1,0:T(8,128)(2,1)S(1)}, bf16[6,64,256]{2,1,0:T(8,128)(2,1)}, u32[]{:S(2)}) copy-start(bf16[6,64,256]{2,1,0:T(8,128)(2,1)} %copy-done.6) | copy-start | bytes 589828
  156.4 5.0 %copy-start.4 = (pred[256,2048]{1,0:T(8,128)(4,1)S(1)}, pred[256,2048]{1,0:T(8,128)(4,1)}, u32[]{:S(2)}) copy-start(pred[256,2048]{1,0:T(8,128)(4,1)} %broadcast_compare_fusion) | copy-start | bytes 1572868
  156.4 5.0 %copy-start.30 = (f32[6,256]{1,0:T(8,128)S(1)}, f32[6,256]{1,0:T(8,128)}, u32[]{:S(2)}) copy-start(f32[6,256]{1,0:T(8,128)} %copy-done.29) | copy-start | bytes 18436
  161.4 8.3 %copy-start.17 = (bf16[256,6,32]{0,2,1:T(8,128)(2,1)S(1)}, bf16[256,6,32]{0,2,1:T(8,128)(2,1)}, u32[]{:S(2)}) copy-start(bf16[256,6,32]{0,2,1:T(8,128)(2,1)} %get-tuple-element.87) | copy-start | bytes 294916
  161.4 8.3 %copy-start.19 = (bf16[256,6,32]{0,2,1:T(8,128)(2,1)S(1)}, bf16[256,6,32]{0,2,1:T(8,128)(2,1)}, u32[]{:S(2)}) copy-start(bf16[256,6,32]{0,2,1:T(8,128)(2,1)} %get-tuple-element.88) | copy-start | bytes 294916
  169.7 3.1 copy-start.1
  197.5 43.7 %all-to-all-start.1 = ((bf16[8,256,768]{1,2,0:T(8,128)(2,1)}), bf16[8,256,768]{1,2,0:T(8,128)(2,1)}, u32[]{:S(2)}, u32[]{:S(2)}) async-start(bf16[8,256,768]{1,2,0:T(8,128)(2,1)} %copy.108), calls=%async_computation.2 | async-start | bytes 6291456 | tf_op jit(solution)/shard_map/all_to_all | solution.py:86
  204.5 86.4 %reduce-scatter.5.cloned.1.call-start = ((), (), s32[]{:S(2)}) async-start(), calls=%async_computation.11 | async-start | bytes 2211840 | tf_op jit(solution)/shard_map/reduce_scatter | solution.py:287
  209.5 34.3 %copy-start.21 = (f32[256,32]{0,1:T(8,128)S(1)}, f32[256,32]{0,1:T(8,128)}, u32[]{:S(2)}) copy-start(f32[256,32]{0,1:T(8,128)} %copy-done.20) | copy-start | bytes 98308
  209.6 34.3 %copy-start.23 = (f32[256,32]{0,1:T(8,128)S(1)}, f32[256,32]{0,1:T(8,128)}, u32[]{:S(2)}) copy-start(f32[256,32]{0,1:T(8,128)} %copy-done.22) | copy-start | bytes 98308
  241.2 2.9 copy-start.25
  243.9 1.7 copy-start.28
  244.9 7.9 %copy-start.10 = (bf16[256,768]{1,0:T(8,128)(2,1)}, bf16[256,768]{1,0:T(8,128)(2,1)S(1)}, u32[]{:S(2)}) copy-start(bf16[256,768]{1,0:T(8,128)(2,1)S(1)} %fusion.10) | copy-start | bytes 1179652
  244.9 7.9 %collective-permute-start.3 = (bf16[256,768]{1,0:T(8,128)(2,1)S(1)}, bf16[256,768]{1,0:T(8,128)(2,1)S(1)}, u32[]{:S(2)}, u32[]{:S(2)}) collective-permute-start(bf16[256,768]{1,0:T(8,128)(2,1)S(1)} %fusion.10), channel_id=1, source_target_pairs={{0,8},{8,0},{1,9},{9,1},{2,10},{10,2},{3,11},{11,3},{4,12},{12,4},... | collective-permute-start | bytes 1179656 | tf_op jit(solution)/shard_map/ppermute | solution.py:72
  252.7 0.7 copy-start.12
  287.1 25.3 %copy-start.11 = (bf16[256,768]{1,0:T(8,128)(2,1)S(1)}, bf16[256,768]{1,0:T(8,128)(2,1)}, u32[]{:S(2)}) copy-start(bf16[256,768]{1,0:T(8,128)(2,1)} %copy-done.10) | copy-start | bytes 1179652
  287.2 25.3 %copy-start.13 = (bf16[256,768]{1,0:T(8,128)(2,1)S(1)}, bf16[256,768]{1,0:T(8,128)(2,1)}, u32[]{:S(2)}) copy-start(bf16[256,768]{1,0:T(8,128)(2,1)} %copy-done.12) | copy-start | bytes 1179652
  292.6 15.6 %all-to-all-start.2 = ((bf16[8,12,1153]{2,1,0:T(8,128)(2,1)}), bf16[8,12,1153]{2,1,0:T(8,128)(2,1)S(1)}, u32[]{:S(2)}, u32[]{:S(2)}) async-start(bf16[8,12,1153]{2,1,0:T(8,128)(2,1)} %reshape.265), calls=%async_computation.4 | async-start | bytes 655360 | tf_op jit(solution)/shard_map/all_to_all | solution.py:86
  309.0 12.5 %all-to-all-start.3 = ((bf16[8,12,1153]{2,1,0:T(8,128)(2,1)}), bf16[8,12,1153]{2,1,0:T(8,128)(2,1)S(1)}, u32[]{:S(2)}, u32[]{:S(2)}) async-start(bf16[8,12,1153]{2,1,0:T(8,128)(2,1)} %broadcast_in_dim.108), calls=%async_computation.5 | async-start | bytes 655360 | tf_op jit(solution)/shard_map/all_to_all | solution.py:79
Sparse Core Ops, SparseCore 0:
  10.7 27.3 all-gather.2
  54.8 29.0 all-gather.4
  158.7 34.0 reduce-scatter.2
  256.0 34.8 reduce-scatter.4

commit v11 on v10

--- a/solution.py
+++ b/solution.py
@@ -152,8 +152,8 @@
     value_bf = projected[:, 2].astype(jnp.bfloat16)
     key_flat = key_bf.reshape(row_count, local_width)
     value_flat = value_bf.reshape(row_count, local_width)
-    kv_group = context_gather(jnp.concatenate([key_flat, value_flat], axis=1), "context")
-    keys_group, values_group = (kv_group[:, :local_width], kv_group[:, local_width:])
+    keys_group = context_gather(key_flat, "context")
+    values_group = context_gather(value_flat, "context")
     keys_heads = keys_group.reshape(group_rows, head_count, HD)
     values_heads = values_group.reshape(group_rows, head_count, HD)
     group_segment, unused_pos = segments_of(jnp.arange(group_rows, dtype=jnp.int32), lengths)
@@ -253,12 +253,12 @@
     value_all = jnp.einsum(
         "hqk,qhd->khd", fwd_weights, out_heads, preferred_element_type=jnp.float32
     ).reshape(group_rows, local_width)
-    kv_partial, mlp_shard = lax.optimization_barrier(
-        (jnp.concatenate([key_all, value_all], axis=1).astype(jnp.bfloat16), mlp_shard)
-    )
-    kv_grad = context_scatter_sum(kv_partial, "context")
+    value_partial, mlp_shard = lax.optimization_barrier(
+        (value_all.astype(jnp.bfloat16), mlp_shard)
+    )
+    value_grad = context_scatter_sum(value_partial, "context")
+    key_grad = context_scatter_sum(key_all.astype(jnp.bfloat16), "context")
     mlp_pieces = reduce_pack(mlp_shard, mlp_members)
-    key_grad, value_grad = (kv_grad[:, :local_width], kv_grad[:, local_width:])
     key_grad = key_grad.reshape(row_count, head_count, HD)
     value_grad = value_grad.reshape(row_count, head_count, HD)
     qkv_rows = (

time: 331 us -> 318 us (0.961)
  waiting for transfers between devices: 133 us -> 122 us
  starting transfers between devices: 27.8 us -> 35.6 us
  other arithmetic: 29.4 us -> 24.8 us
    all_to_all x2 -> x3, waiting for transfers between devices: 40.8 us -> 24.4 us  [context_scatter_sum(): lax.all_to_all(values.reshape((count, rows) + values.shape[1:]), axis_nam...]
    slice x5 -> x0, local copies, waits for them, and re-layouts: 6.85 us -> none  [the longest x2 5.08 us: on_device(): kv_group[:, :local_width]]
    another operation x0 -> x2, local copies, waits for them, and re-layouts: none -> 6.37 us  [the longest x1 3.78 us: on_device(): values_heads = values_group.reshape(group_rows, head_count, HD)]
    reshape x2 -> x0, local copies, waits for them, and re-layouts: 5.25 us -> none  [the longest x1 2.67 us: on_device(): key_all = (jnp.einsum('hqk,qhd->khd', score_grad, query_bf, preferred_ele...]
    all_to_all x2 -> x3, starting transfers between devices: 13.4 us -> 18 us  [context_scatter_sum(): lax.all_to_all(values.reshape((count, rows) + values.shape[1:]), axis_nam...]
    concatenate x2 -> x0, other arithmetic: 3.88 us -> none  [the longest x1 3.86 us: on_device(): jnp.concatenate([key_all, value_all], axis=1).astype(jnp.bfloat16)]
    reduce_scatter x1, waiting for transfers between devices: 0.04 us -> 3.74 us  [on_device(): lax.psum_scatter(jnp.concatenate(attn_members, axis=1).astype(jnp.bfloat1...]
    all_to_all x2 -> x3, starting transfers between devices: 10.4 us -> 13.9 us  [context_gather(): gathered = lax.all_to_all(spread, axis_name, 0, 0, tiled=True)]
  transfers between devices with their start and end apart: 12 -> 14, of which waited for: 10 -> 13; matrix products, arithmetic and copies ran while one was open for 25% -> 27% of each run, Pallas kernels for 0% -> 0%
where the time goes in v11:
time: 318 us; the launch traced here: 317 us
  waiting for transfers between devices  122 us (38%)
  local copies, waits for them, and re-layouts  47.9 us (15%)
  matrix products  45.6 us (14%)
  starting transfers between devices  35.6 us (11%)
  blocking collectives  26.8 us (8%)
  other arithmetic  24.8 us (8%)
  between operations  14.4 us (5%)
    all_to_all x3, waiting for transfers between devices, context_gather(): gathered = lax.all_to_all(spread, axis_name, 0, 0, tiled=True)  44.4 us
    all_to_all x3, waiting for transfers between devices, context_scatter_sum(): lax.all_to_all(values.reshape((count, rows) + values.shape[1:]), axis_nam...  24.4 us
    all_gather x1, waiting for transfers between devices, on_device(): lax.all_gather(jnp.concatenate([qkv_weight.reshape(shard_rows, 3 * local_...  22.8 us
    ppermute x4, waiting for transfers between devices, pair_sum(): other = lax.ppermute(values, axis_name, perm=[(0, 1), (1, 0)])  20.5 us
    all_to_all x3, starting transfers between devices, context_scatter_sum(): lax.all_to_all(values.reshape((count, rows) + values.shape[1:]), axis_nam...  18 us
    all_to_all x3, starting transfers between devices, context_gather(): gathered = lax.all_to_all(spread, axis_name, 0, 0, tiled=True)  13.9 us
    all_to_all x1, blocking collectives, context_scatter_sum(): lax.all_to_all(values.reshape((count, rows) + values.shape[1:]), axis_nam...  13.8 us
    all_to_all x1, blocking collectives, context_gather(): gathered = lax.all_to_all(spread, axis_name, 0, 0, tiled=True)  12.9 us
  transfers between devices with their start and end apart: 14, of which 13 were waited for; matrix products, arithmetic and copies ran while one was open for 27% of the time, Pallas kernels for 0%

profile of v11, /device:TPU:0, one launch (start us, length us, event | category | flops | bytes accessed | tf_op | source)
XLA Modules:
  0.0 316.7 jit_solution(14078650345513529136)
XLA Ops:
  11.8 1.7 pad_maximum_fusion.3
  15.3 22.8 %all-gather.3.cloned.1.call-done = bf16[768,1154]{1,0:T(8,128)(2,1)} async-done(((bf16[96,1154]{1,0:T(8,128)(2,1)}), bf16[768,1154]{1,0:T(8,128)(2,1)}) %all-gather.3.cloned.1.call-update) | async-done | bytes 1772560 | tf_op jit(solution)/shard_map/all_gather | solution.py:115
  39.4 2.4 fusion.7
  43.1 6.9 %all-to-all-start = ((bf16[8,256,384]{1,2,0:T(8,128)(2,1)}), bf16[8,256,384]{1,2,0:T(8,128)(2,1)S(1)}, u32[]{:S(2)}, u32[]{:S(2)}) async-start(bf16[8,256,384]{1,2,0:T(8,128)(2,1)} %broadcast_in_dim.56), calls=%async_computation | async-start | bytes 3145728 | tf_op jit(solution)/shard_map/all_to_all | solution.py:79
  51.2 22.0 %all-to-all-done = bf16[8,256,384]{1,2,0:T(8,128)(2,1)S(1)} async-done(((bf16[8,256,384]{1,2,0:T(8,128)(2,1)}), bf16[8,256,384]{1,2,0:T(8,128)(2,1)S(1)}, u32[]{:S(2)}, u32[]{:S(2)}) %all-to-all-start) | async-done | bytes 1572896 | tf_op jit(solution)/shard_map/all_to_all | solution.py:79
  74.5 3.6 %all-to-all-start.1 = ((bf16[8,256,384]{1,2,0:T(8,128)(2,1)}), bf16[8,256,384]{1,2,0:T(8,128)(2,1)S(1)}, u32[]{:S(2)}, u32[]{:S(2)}) async-start(bf16[8,256,384]{1,2,0:T(8,128)(2,1)} %broadcast_in_dim.61), calls=%async_computation.1 | async-start | bytes 3145728 | tf_op jit(solution)/shard_map/all_to_all | solution.py:79
  80.0 2.0 copy.99
  82.1 3.8 %reshape_reshape.6 = bf16[2048,6,64]{0,2,1:T(8,128)(2,1)} reshape(bf16[8,256,384]{1,0,2:T(8,128)(2,1)} %copy.99) | data formatting | bytes 3145728 | tf_op jit(solution)/shard_map/reshape;reshape | solution.py:158
  85.9 14.5 %all-to-all-done.1 = bf16[8,256,384]{1,2,0:T(8,128)(2,1)S(1)} async-done(((bf16[8,256,384]{1,2,0:T(8,128)(2,1)}), bf16[8,256,384]{1,2,0:T(8,128)(2,1)S(1)}, u32[]{:S(2)}, u32[]{:S(2)}) %all-to-all-start.1) | async-done | bytes 1572896 | tf_op jit(solution)/shard_map/all_to_all | solution.py:79
  100.4 2.0 copy.100
  102.4 2.6 reshape_reshape.7
  105.0 2.5 select_reduce_fusion.1
  107.5 4.0 %select_reduce_fusion = f32[6,256]{1,0:T(8,128)S(1)} fusion(f32[6,256,2048]{2,1,0:T(8,128)S(1)} %get-tuple-element.96, f32[6,256]{1,0:T(8,128)S(1)} %get-tuple-element.95, pred[256,2048]{1,0:T(8,128)(4,1)S(1)} %copy-done.3), kind=kLoop, calls=%fused_computation.2 | loop fusion | flops 12581376 | bytes 13119488 | tf_op jit(solution)/shard_map/reduce_sum | solution.py:165
  112.2 3.0 convolution_convert_fusion.7
  115.3 1.6 convolution_convert_fusion.6
  117.8 8.5 %collective-permute-done = bf16[256,768]{1,0:T(8,128)(2,1)S(1)} collective-permute-done((bf16[256,768]{1,0:T(8,128)(2,1)S(1)}, bf16[256,768]{1,0:T(8,128)(2,1)S(1)}, u32[]{:S(2)}, u32[]{:S(2)}) %collective-permute-start) | collective-permute-done | bytes 393248 | tf_op jit(solution)/shard_map/ppermute | solution.py:72
  134.6 2.2 copy.104
  136.8 2.1 convolution_convert_fusion.1
  138.9 3.4 %collective-permute-done.2 = bf16[256,768]{1,0:T(8,128)(2,1)} collective-permute-done((bf16[256,768]{1,0:T(8,128)(2,1)}, bf16[256,768]{1,0:T(8,128)(2,1)}, u32[]{:S(2)}, u32[]{:S(2)}) %collective-permute-start.2) | collective-permute-done | bytes 393248 | tf_op jit(solution)/shard_map/ppermute | solution.py:72
  142.3 1.5 multiply_reduce_fusion
  144.7 2.2 collective-permute-done.1
  146.9 2.5 multiply_add_fusion
  149.8 7.1 %concatenate.34 = bf16[768,2113]{1,0:T(8,128)(2,1)} concatenate(bf16[768,1]{1,0:T(8,128)(2,1)} %broadcast_in_dim.115, bf16[768,1152]{1,0:T(8,128)(2,1)} %convolution_convert_fusion.1, bf16[768,576]{1,0:T(8,128)(2,1)} %copy.104, bf16[768,384]{1,0:T(8,128)(2,1)S(1)} %convolution_convert_fusion.4), dimensions={1} | concatenate | bytes 6491136 | tf_op jit(solution)/shard_map/concatenate | solution.py:233
  156.9 2.2 convolution_convert_fusion.8
  159.1 1.7 copy.105
  161.9 8.2 %multiply_convert_fusion = bf16[6,256,2048]{2,1,0:T(8,128)(2,1)S(1)} fusion(f32[6,256,2048]{2,1,0:T(8,128)} %copy-done, f32[6,256]{1,0:T(8,128)S(1)} %bitcast.142, f32[6,256]{1,0:T(8,128)S(1)} %copy-done.27, pred[256,2048]{1,0:T(8,128)(4,1)S(1)} %copy-done.4, bf16[256,6,64]{0,2,1:T(8,128)(2,1)} %bitcast.135, bf16[2048,6,64]{0,2,1:T(8,128)(2,1)} %reshape_reshape.6), kind=kOutput, calls=%fused_computation | convolution fusion | flops 421527552 | bytes 21180416 | tf_op jit(solution)/shard_map/qhd,khd->hqk/dot_general | solution.py:241
  174.7 6.6 %all-to-all-start.2 = ((bf16[8,256,384]{1,2,0:T(8,128)(2,1)}), bf16[8,256,384]{1,2,0:T(8,128)(2,1)}, u32[]{:S(2)}, u32[]{:S(2)}) async-start(bf16[8,256,384]{1,2,0:T(8,128)(2,1)} %copy.106), calls=%async_computation.2 | async-start | bytes 3145728 | tf_op jit(solution)/shard_map/all_to_all | solution.py:86
  181.3 8.6 %convolution_convert_fusion.2 = bf16[6,64,2048]{2,1,0:T(8,128)(2,1)} fusion(bf16[256,6,64]{0,2,1:T(8,128)(2,1)S(1)} %bitcast.136, f32[6,256,2048]{2,1,0:T(8,128)} %copy-done, f32[6,256]{1,0:T(8,128)S(1)} %copy-done.27, pred[256,2048]{1,0:T(8,128)(4,1)S(1)} %copy-done.4), kind=kOutput, calls=%fused_computation.9 | convolution fusion | flops 416022528 | bytes 14882816 | tf_op jit(solution)/shard_map/hqk,qhd->khd/dot_general | solution.py:253
  189.9 5.6 %reduce-scatter.3.cloned.1.call-done = bf16[96,2113]{1,0:T(8,128)(2,1)} async-done(((bf16[768,2113]{1,0:T(8,128)(2,1)}), bf16[96,2113]{1,0:T(8,128)(2,1)}) %reduce-scatter.3.cloned.1.call-update) | async-done | bytes 405712 | tf_op jit(solution)/shard_map/reduce_scatter | solution.py:235
  195.4 2.6 copy.107
  198.0 2.6 copy.108
  200.6 2.0 all-to-all-done.2
  202.6 5.0 %all-to-all-start.3 = ((bf16[8,256,384]{1,2,0:T(8,128)(2,1)}), bf16[8,256,384]{1,2,0:T(8,128)(2,1)}, u32[]{:S(2)}, u32[]{:S(2)}) async-start(bf16[8,256,384]{1,2,0:T(8,128)(2,1)} %copy.108), calls=%async_computation.4 | async-start | bytes 3145728 | tf_op jit(solution)/shard_map/all_to_all | solution.py:86
  207.7 4.8 %fusion.16 = f32[256,6,64]{0,2,1:T(8,128)S(1)} fusion(bf16[2048,6,64]{0,2,1:T(8,128)(2,1)S(1)} %reshape_reshape.7, bf16[6,256,2048]{2,1,0:T(8,128)(2,1)} %copy-done.1), kind=kOutput, calls=%fused_computation.28 | convolution fusion | flops 402751488 | bytes 8257536 | tf_op jit(solution)/shard_map/hqk,khd->qhd/dot_general | solution.py:246
  212.5 1.7 convert_reduce_fusion
  214.4 13.3 %all-to-all-done.3 = bf16[8,256,384]{1,2,0:T(8,128)(2,1)} async-done(((bf16[8,256,384]{1,2,0:T(8,128)(2,1)}), bf16[8,256,384]{1,2,0:T(8,128)(2,1)}, u32[]{:S(2)}, u32[]{:S(2)}) %all-to-all-start.3) | async-done | bytes 1572896 | tf_op jit(solution)/shard_map/all_to_all | solution.py:86
  227.6 1.7 reduce.2
  229.4 2.2 fusion.10
  233.1 6.4 %collective-permute-done.3 = bf16[256,768]{1,0:T(8,128)(2,1)S(1)} collective-permute-done((bf16[256,768]{1,0:T(8,128)(2,1)S(1)}, bf16[256,768]{1,0:T(8,128)(2,1)S(1)}, u32[]{:S(2)}, u32[]{:S(2)}) %collective-permute-start.3) | collective-permute-done | bytes 393248 | tf_op jit(solution)/shard_map/ppermute | solution.py:72
  240.1 2.2 pad_maximum_fusion
  243.5 13.8 %all_to_all.40 = bf16[8,12,2113]{2,1,0:T(8,128)(2,1)S(1)} all-to-all(bf16[8,12,2113]{2,1,0:T(8,128)(2,1)S(1)} %reshape.257), channel_id=1, replica_groups=mesh['fsdp'=8,'tensor'=2,'context'=8] {'context'}, dimensions={0} | all-to-all | bytes 811392 | tf_op jit(solution)/shard_map/all_to_all | solution.py:86
  257.4 12.9 %all_to_all.41 = bf16[8,12,2113]{2,1,0:T(8,128)(2,1)S(1)} all-to-all(bf16[8,12,2113]{2,1,0:T(8,128)(2,1)S(1)} %broadcast_in_dim.114), channel_id=1, replica_groups=mesh['fsdp'=8,'tensor'=2,'context'=8] {'context'}, dimensions={0} | all-to-all | bytes 811392 | tf_op jit(solution)/shard_map/all_to_all | solution.py:79
  274.1 3.7 %reduce-scatter.5.cloned.1.call-done = bf16[96,1153]{1,0:T(8,128)(2,1)} async-done(((bf16[768,1153]{1,0:T(8,128)(2,1)}), bf16[96,1153]{1,0:T(8,128)(2,1)}) %reduce-scatter.5.cloned.1.call-update) | async-done | bytes 221392 | tf_op jit(solution)/shard_map/reduce_scatter | solution.py:287
  277.8 1.7 reshape.255
  279.5 6.5 %all-to-all-start.4 = ((bf16[8,12,1153]{2,1,0:T(8,128)(2,1)}), bf16[8,12,1153]{2,1,0:T(8,128)(2,1)S(1)}, u32[]{:S(2)}, u32[]{:S(2)}) async-start(bf16[8,12,1153]{2,1,0:T(8,128)(2,1)} %reshape.255), calls=%async_computation.6 | async-start | bytes 655360 | tf_op jit(solution)/shard_map/all_to_all | solution.py:86
  286.0 9.1 %all-to-all-done.4 = bf16[8,12,1153]{2,1,0:T(8,128)(2,1)S(1)} async-done(((bf16[8,12,1153]{2,1,0:T(8,128)(2,1)}), bf16[8,12,1153]{2,1,0:T(8,128)(2,1)S(1)}, u32[]{:S(2)}, u32[]{:S(2)}) %all-to-all-start.4) | async-done | bytes 221408 | tf_op jit(solution)/shard_map/all_to_all | solution.py:86
  296.0 3.4 %all-to-all-start.5 = ((bf16[8,12,1153]{2,1,0:T(8,128)(2,1)}), bf16[8,12,1153]{2,1,0:T(8,128)(2,1)S(1)}, u32[]{:S(2)}, u32[]{:S(2)}) async-start(bf16[8,12,1153]{2,1,0:T(8,128)(2,1)} %broadcast_in_dim.113), calls=%async_computation.7 | async-start | bytes 655360 | tf_op jit(solution)/shard_map/all_to_all | solution.py:79
  300.7 7.8 %all-to-all-done.5 = bf16[8,12,1153]{2,1,0:T(8,128)(2,1)S(1)} async-done(((bf16[8,12,1153]{2,1,0:T(8,128)(2,1)}), bf16[8,12,1153]{2,1,0:T(8,128)(2,1)S(1)}, u32[]{:S(2)}, u32[]{:S(2)}) %all-to-all-start.5) | async-done | bytes 221408 | tf_op jit(solution)/shard_map/all_to_all | solution.py:79
  (142 shorter events, 40.9 us)
Async XLA Ops:
  7.2 7.5 %copy-start.2 = (bf16[256,768]{1,0:T(8,128)(2,1)S(1)}, bf16[256,768]{1,0:T(8,128)(2,1)}, u32[]{:S(2)}) copy-start(bf16[256,768]{1,0:T(8,128)(2,1)} %param.9) | copy-start | bytes 1179652
  7.2 7.8 %copy-start.29 = (s32[1,3]{1,0:T(1,128)S(1)}, s32[1,3]{1,0:T(1,128)}, u32[]{:S(2)}) copy-start(s32[1,3]{1,0:T(1,128)} %param.10) | copy-start | bytes 40
  7.2 30.9 %all-gather.3.cloned.1.call-start = ((), (), s32[]{:S(2)}) async-start(), calls=%async_computation.10 | async-start | bytes 2211840 | tf_op jit(solution)/shard_map/all_gather | solution.py:115
  10.6 104.7 %all-gather.5.cloned.1.call-start = ((), (), s32[]{:S(2)}) async-start(), calls=%async_computation.11 | async-start | bytes 3760128 | tf_op jit(solution)/shard_map/all_gather | solution.py:128
  15.0 28.1 %copy-start.22 = (f32[256]{0:T(256)}, f32[256]{0:T(256)S(1)}, u32[]{:S(2)}) copy-start(f32[256]{0:T(256)S(1)} %add_rsqrt_fusion.1) | copy-start | bytes 3076
  15.2 34.8 %copy-start.28 = (s32[3,1]{0,1:T(1,128)}, s32[3,1]{0,1:T(1,128)S(1)}, u32[]{:S(2)}) copy-start(s32[3,1]{0,1:T(1,128)S(1)} %reduce-window.4) | copy-start | bytes 40
  15.3 34.7 %copy-start.24 = (s32[256]{0:T(256)}, s32[256]{0:T(256)S(1)}, u32[]{:S(2)}) copy-start(s32[256]{0:T(256)S(1)} %convert_reduce_fusion.5) | copy-start | bytes 3076
  43.1 30.2 %all-to-all-start = ((bf16[8,256,384]{1,2,0:T(8,128)(2,1)}), bf16[8,256,384]{1,2,0:T(8,128)(2,1)S(1)}, u32[]{:S(2)}, u32[]{:S(2)}) async-start(bf16[8,256,384]{1,2,0:T(8,128)(2,1)} %broadcast_in_dim.56), calls=%async_computation | async-start | bytes 3145728 | tf_op jit(solution)/shard_map/all_to_all | solution.py:79
  50.3 0.9 copy-start.17
  50.3 0.9 copy-start.19
  50.4 28.5 %copy-start.25 = (s32[256]{0:T(256)S(1)}, s32[256]{0:T(256)}, u32[]{:S(2)}) copy-start(s32[256]{0:T(256)} %copy-done.24) | copy-start | bytes 3076
  74.5 25.9 %all-to-all-start.1 = ((bf16[8,256,384]{1,2,0:T(8,128)(2,1)}), bf16[8,256,384]{1,2,0:T(8,128)(2,1)S(1)}, u32[]{:S(2)}, u32[]{:S(2)}) async-start(bf16[8,256,384]{1,2,0:T(8,128)(2,1)} %broadcast_in_dim.61), calls=%async_computation.1 | async-start | bytes 3145728 | tf_op jit(solution)/shard_map/all_to_all | solution.py:79
  78.1 117.4 %reduce-scatter.3.cloned.1.call-start = ((), (), s32[]{:S(2)}) async-start(), calls=%async_computation.12 | async-start | bytes 3760128 | tf_op jit(solution)/shard_map/reduce_scatter | solution.py:235
  85.9 19.1 %copy-start.3 = (pred[256,2048]{1,0:T(8,128)(4,1)S(1)}, pred[256,2048]{1,0:T(8,128)(4,1)}, u32[]{:S(2)}) copy-start(pred[256,2048]{1,0:T(8,128)(4,1)} %broadcast_compare_fusion) | copy-start | bytes 1572868
  85.9 19.1 %copy-start.12 = (bf16[256,6,32]{0,2,1:T(8,128)(2,1)S(1)}, bf16[256,6,32]{0,2,1:T(8,128)(2,1)}, u32[]{:S(2)}) copy-start(bf16[256,6,32]{0,2,1:T(8,128)(2,1)} %get-tuple-element.85) | copy-start | bytes 294916
  85.9 19.2 %copy-start.14 = (bf16[256,6,32]{0,2,1:T(8,128)(2,1)S(1)}, bf16[256,6,32]{0,2,1:T(8,128)(2,1)}, u32[]{:S(2)}) copy-start(bf16[256,6,32]{0,2,1:T(8,128)(2,1)} %get-tuple-element.86) | copy-start | bytes 294916
  107.5 4.7 %copy-start = (f32[6,256,2048]{2,1,0:T(8,128)}, f32[6,256,2048]{2,1,0:T(8,128)S(1)}, u32[]{:S(2)}) copy-start(f32[6,256,2048]{2,1,0:T(8,128)S(1)} %get-tuple-element.96) | copy-start | bytes 37748740
  107.5 4.7 %copy-start.9 = (bf16[2048,6,64]{0,2,1:T(8,128)(2,1)S(1)}, bf16[2048,6,64]{0,2,1:T(8,128)(2,1)}, u32[]{:S(2)}) copy-start(bf16[2048,6,64]{0,2,1:T(8,128)(2,1)} %reshape_reshape.6) | copy-start | bytes 4718596
  112.2 3.0 copy-start.26
  115.3 12.5 %copy-start.6 = (bf16[6,64,256]{2,1,0:T(8,128)(2,1)}, bf16[6,64,256]{2,1,0:T(8,128)(2,1)S(1)}, u32[]{:S(2)}) copy-start(bf16[6,64,256]{2,1,0:T(8,128)(2,1)S(1)} %convolution_convert_fusion.7) | copy-start | bytes 589828
  115.3 11.5 %copy-start.5 = (bf16[768,2112]{1,0:T(8,128)(2,1)S(1)}, bf16[768,2112]{1,0:T(8,128)(2,1)}, u32[]{:S(2)}) copy-start(bf16[768,2112]{1,0:T(8,128)(2,1)} %all-gather.5.cloned.1.call-done) | copy-start | bytes 9732100
  116.9 10.8 %copy-start.10 = (bf16[256,768]{1,0:T(8,128)(2,1)S(1)}, bf16[256,768]{1,0:T(8,128)(2,1)}, u32[]{:S(2)}) copy-start(bf16[256,768]{1,0:T(8,128)(2,1)} %param.17) | copy-start | bytes 1179652
  116.9 9.4 %collective-permute-start = (bf16[256,768]{1,0:T(8,128)(2,1)S(1)}, bf16[256,768]{1,0:T(8,128)(2,1)S(1)}, u32[]{:S(2)}, u32[]{:S(2)}) collective-permute-start(bf16[256,768]{1,0:T(8,128)(2,1)S(1)} %convolution_convert_fusion.6), channel_id=1, source_target_pairs={{0,8},{8,0},{1,9},{9,1},{2,10},{10,2},{3,11},{11,3},{4,12},{12,4},... | collective-permute-start | bytes 1179656 | tf_op jit(solution)/shard_map/ppermute | solution.py:72
  126.8 15.5 %copy-start.21 = (f32[256]{0:T(256)}, f32[256]{0:T(256)S(1)}, u32[]{:S(2)}) copy-start(f32[256]{0:T(256)S(1)} %add_rsqrt_fusion) | copy-start | bytes 3076
  129.9 12.4 %collective-permute-start.2 = (bf16[256,768]{1,0:T(8,128)(2,1)}, bf16[256,768]{1,0:T(8,128)(2,1)}, u32[]{:S(2)}, u32[]{:S(2)}) collective-permute-start(bf16[256,768]{1,0:T(8,128)(2,1)} %fusion.13), channel_id=1, source_target_pairs={{0,8},{8,0},{1,9},{9,1},{2,10},{10,2},{3,11},{11,3},{4,12},{12,4},... | collective-permute-start | bytes 1179656 | tf_op jit(solution)/shard_map/ppermute | solution.py:72
  133.1 13.8 %collective-permute-start.1 = (bf16[256,768]{1,0:T(8,128)(2,1)}, bf16[256,768]{1,0:T(8,128)(2,1)}, u32[]{:S(2)}, u32[]{:S(2)}) collective-permute-start(bf16[256,768]{1,0:T(8,128)(2,1)} %convolution_convert_fusion.5), channel_id=1, source_target_pairs={{0,8},{8,0},{1,9},{9,1},{2,10},{10,2},{3,11},{11,3},{4,12},{12,4},... | collective-permute-start | bytes 1179656 | tf_op jit(solution)/shard_map/ppermute | solution.py:72
  136.8 10.1 %copy-start.11 = (bf16[256,768]{1,0:T(8,128)(2,1)S(1)}, bf16[256,768]{1,0:T(8,128)(2,1)}, u32[]{:S(2)}) copy-start(bf16[256,768]{1,0:T(8,128)(2,1)} %param.17) | copy-start | bytes 1179652
  138.9 10.5 %copy-start.7 = (bf16[6,64,256]{2,1,0:T(8,128)(2,1)S(1)}, bf16[6,64,256]{2,1,0:T(8,128)(2,1)}, u32[]{:S(2)}) copy-start(bf16[6,64,256]{2,1,0:T(8,128)(2,1)} %copy-done.6) | copy-start | bytes 589828
  156.9 4.0 %copy-start.8 = (bf16[6,64,256]{2,1,0:T(8,128)(2,1)S(1)}, bf16[6,64,256]{2,1,0:T(8,128)(2,1)}, u32[]{:S(2)}) copy-start(bf16[6,64,256]{2,1,0:T(8,128)(2,1)} %copy-done.6) | copy-start | bytes 589828
  156.9 5.0 %copy-start.4 = (pred[256,2048]{1,0:T(8,128)(4,1)S(1)}, pred[256,2048]{1,0:T(8,128)(4,1)}, u32[]{:S(2)}) copy-start(pred[256,2048]{1,0:T(8,128)(4,1)} %broadcast_compare_fusion) | copy-start | bytes 1572868
  156.9 5.0 %copy-start.27 = (f32[6,256]{1,0:T(8,128)S(1)}, f32[6,256]{1,0:T(8,128)}, u32[]{:S(2)}) copy-start(f32[6,256]{1,0:T(8,128)} %copy-done.26) | copy-start | bytes 18436
  161.9 8.3 %copy-start.13 = (bf16[256,6,32]{0,2,1:T(8,128)(2,1)S(1)}, bf16[256,6,32]{0,2,1:T(8,128)(2,1)}, u32[]{:S(2)}) copy-start(bf16[256,6,32]{0,2,1:T(8,128)(2,1)} %get-tuple-element.85) | copy-start | bytes 294916
  161.9 8.3 %copy-start.15 = (bf16[256,6,32]{0,2,1:T(8,128)(2,1)S(1)}, bf16[256,6,32]{0,2,1:T(8,128)(2,1)}, u32[]{:S(2)}) copy-start(bf16[256,6,32]{0,2,1:T(8,128)(2,1)} %get-tuple-element.86) | copy-start | bytes 294916
  170.1 2.6 copy-start.1
  173.2 8.0 %copy-start.16 = (bf16[256,384]{0,1:T(8,128)(2,1)S(1)}, bf16[256,384]{0,1:T(8,128)(2,1)}, u32[]{:S(2)}) copy-start(bf16[256,384]{0,1:T(8,128)(2,1)} %copy.105) | copy-start | bytes 589828
  174.7 27.9 %all-to-all-start.2 = ((bf16[8,256,384]{1,2,0:T(8,128)(2,1)}), bf16[8,256,384]{1,2,0:T(8,128)(2,1)}, u32[]{:S(2)}, u32[]{:S(2)}) async-start(bf16[8,256,384]{1,2,0:T(8,128)(2,1)} %copy.106), calls=%async_computation.2 | async-start | bytes 3145728 | tf_op jit(solution)/shard_map/all_to_all | solution.py:86
  202.6 25.0 %all-to-all-start.3 = ((bf16[8,256,384]{1,2,0:T(8,128)(2,1)}), bf16[8,256,384]{1,2,0:T(8,128)(2,1)}, u32[]{:S(2)}, u32[]{:S(2)}) async-start(bf16[8,256,384]{1,2,0:T(8,128)(2,1)} %copy.108), calls=%async_computation.4 | async-start | bytes 3145728 | tf_op jit(solution)/shard_map/all_to_all | solution.py:86
  207.6 6.5 %copy-start.18 = (f32[256,32]{0,1:T(8,128)S(1)}, f32[256,32]{0,1:T(8,128)}, u32[]{:S(2)}) copy-start(f32[256,32]{0,1:T(8,128)} %copy-done.17) | copy-start | bytes 98308
  207.6 6.6 %copy-start.20 = (f32[256,32]{0,1:T(8,128)S(1)}, f32[256,32]{0,1:T(8,128)}, u32[]{:S(2)}) copy-start(f32[256,32]{0,1:T(8,128)} %copy-done.19) | copy-start | bytes 98308
  207.6 70.2 %reduce-scatter.5.cloned.1.call-start = ((), (), s32[]{:S(2)}) async-start(), calls=%async_computation.13 | async-start | bytes 2211840 | tf_op jit(solution)/shard_map/reduce_scatter | solution.py:287
  214.4 17.9 %copy-start.23 = (f32[256]{0:T(256)S(1)}, f32[256]{0:T(256)}, u32[]{:S(2)}) copy-start(f32[256]{0:T(256)} %copy-done.22) | copy-start | bytes 3076
  231.6 7.9 %collective-permute-start.3 = (bf16[256,768]{1,0:T(8,128)(2,1)S(1)}, bf16[256,768]{1,0:T(8,128)(2,1)S(1)}, u32[]{:S(2)}, u32[]{:S(2)}) collective-permute-start(bf16[256,768]{1,0:T(8,128)(2,1)S(1)} %fusion.10), channel_id=1, source_target_pairs={{0,8},{8,0},{1,9},{9,1},{2,10},{10,2},{3,11},{11,3},{4,12},{12,4},... | collective-permute-start | bytes 1179656 | tf_op jit(solution)/shard_map/ppermute | solution.py:72
  279.5 15.6 %all-to-all-start.4 = ((bf16[8,12,1153]{2,1,0:T(8,128)(2,1)}), bf16[8,12,1153]{2,1,0:T(8,128)(2,1)S(1)}, u32[]{:S(2)}, u32[]{:S(2)}) async-start(bf16[8,12,1153]{2,1,0:T(8,128)(2,1)} %reshape.255), calls=%async_computation.6 | async-start | bytes 655360 | tf_op jit(solution)/shard_map/all_to_all | solution.py:86
  296.0 12.5 %all-to-all-start.5 = ((bf16[8,12,1153]{2,1,0:T(8,128)(2,1)}), bf16[8,12,1153]{2,1,0:T(8,128)(2,1)S(1)}, u32[]{:S(2)}, u32[]{:S(2)}) async-start(bf16[8,12,1153]{2,1,0:T(8,128)(2,1)} %broadcast_in_dim.113), calls=%async_computation.7 | async-start | bytes 655360 | tf_op jit(solution)/shard_map/all_to_all | solution.py:79
Sparse Core Ops, SparseCore 0:
  10.7 27.3 all-gather.2
  40.4 28.7 all-gather.4
  159.2 36.1 reduce-scatter.2
  242.5 35.3 reduce-scatter.4

commit v12 on v11

--- a/solution.py
+++ b/solution.py
@@ -152,8 +152,8 @@
     value_bf = projected[:, 2].astype(jnp.bfloat16)
     key_flat = key_bf.reshape(row_count, local_width)
     value_flat = value_bf.reshape(row_count, local_width)
-    keys_group = context_gather(key_flat, "context")
-    values_group = context_gather(value_flat, "context")
+    kv_group = context_gather(jnp.concatenate([key_flat, value_flat], axis=1), "context")
+    keys_group, values_group = (kv_group[:, :local_width], kv_group[:, local_width:])
     keys_heads = keys_group.reshape(group_rows, head_count, HD)
     values_heads = values_group.reshape(group_rows, head_count, HD)
     group_segment, unused_pos = segments_of(jnp.arange(group_rows, dtype=jnp.int32), lengths)

time: 318 us -> 316 us (level)
  starting transfers between devices: 35.6 us -> 30.7 us
    slice x0 -> x3, local copies, waits for them, and re-layouts: none -> 8.25 us  [the longest x2 5.58 us: on_device(): kv_group[:, :local_width]]
    another operation x2 -> x0, local copies, waits for them, and re-layouts: 6.37 us -> none  [the longest x1 3.78 us: on_device(): values_heads = values_group.reshape(group_rows, head_count, HD)]
    all_to_all x3 -> x2, starting transfers between devices: 13.9 us -> 10.4 us  [context_gather(): gathered = lax.all_to_all(spread, axis_name, 0, 0, tiled=True)]
    all_to_all x3 -> x2, waiting for transfers between devices: 44.4 us -> 42.4 us  [context_gather(): gathered = lax.all_to_all(spread, axis_name, 0, 0, tiled=True)]
  transfers between devices with their start and end apart: 14 -> 13, of which waited for: 13 -> 12; matrix products, arithmetic and copies ran while one was open for 27% -> 25% of each run, Pallas kernels for 0% -> 0%
where the time goes in v12:
time: 316 us; the launch traced here: 315 us
  waiting for transfers between devices  122 us (39%)
  local copies, waits for them, and re-layouts  47.6 us (15%)
  matrix products  45.7 us (14%)
  starting transfers between devices  30.7 us (10%)
  other arithmetic  27 us (9%)
  blocking collectives  26.8 us (8%)
  between operations  14.4 us (5%)
    all_to_all x2, waiting for transfers between devices, context_gather(): gathered = lax.all_to_all(spread, axis_name, 0, 0, tiled=True)  42.4 us
    all_to_all x3, waiting for transfers between devices, context_scatter_sum(): lax.all_to_all(values.reshape((count, rows) + values.shape[1:]), axis_nam...  24 us
    all_gather x1, waiting for transfers between devices, on_device(): lax.all_gather(jnp.concatenate([qkv_weight.reshape(shard_rows, 3 * local_...  23.2 us
    ppermute x4, waiting for transfers between devices, pair_sum(): other = lax.ppermute(values, axis_name, perm=[(0, 1), (1, 0)])  22.4 us
    all_to_all x3, starting transfers between devices, context_scatter_sum(): lax.all_to_all(values.reshape((count, rows) + values.shape[1:]), axis_nam...  16.4 us
    all_to_all x1, blocking collectives, context_scatter_sum(): lax.all_to_all(values.reshape((count, rows) + values.shape[1:]), axis_nam...  13.8 us
    all_to_all x1, blocking collectives, context_gather(): gathered = lax.all_to_all(spread, axis_name, 0, 0, tiled=True)  12.9 us
    all_to_all x2, starting transfers between devices, context_gather(): gathered = lax.all_to_all(spread, axis_name, 0, 0, tiled=True)  10.4 us
  transfers between devices with their start and end apart: 13, of which 12 were waited for; matrix products, arithmetic and copies ran while one was open for 25% of the time, Pallas kernels for 0%

profile of v12, /device:TPU:0, one launch (start us, length us, event | category | flops | bytes accessed | tf_op | source)
XLA Modules:
  0.0 314.6 jit_solution(14577058990215839649)
XLA Ops:
  14.9 23.2 %all-gather.3.cloned.1.call-done = bf16[768,1154]{1,0:T(8,128)(2,1)} async-done(((bf16[96,1154]{1,0:T(8,128)(2,1)}), bf16[768,1154]{1,0:T(8,128)(2,1)}) %all-gather.3.cloned.1.call-update) | async-done | bytes 1772560 | tf_op jit(solution)/shard_map/all_gather | solution.py:115
  39.4 2.5 fusion.7
  42.2 1.9 broadcast_in_dim.57
  44.1 7.0 %all-to-all-start = ((bf16[8,256,768]{1,2,0:T(8,128)(2,1)}), bf16[8,256,768]{1,2,0:T(8,128)(2,1)S(1)}, u32[]{:S(2)}, u32[]{:S(2)}) async-start(bf16[8,256,768]{1,2,0:T(8,128)(2,1)} %broadcast_in_dim.57), calls=%async_computation | async-start | bytes 6291456 | tf_op jit(solution)/shard_map/all_to_all | solution.py:79
  51.2 1.8 reshape.256
  53.0 1.7 pad_maximum_fusion.3
  56.7 34.5 %all-to-all-done = bf16[8,256,768]{1,2,0:T(8,128)(2,1)S(1)} async-done(((bf16[8,256,768]{1,2,0:T(8,128)(2,1)}), bf16[8,256,768]{1,2,0:T(8,128)(2,1)S(1)}, u32[]{:S(2)}, u32[]{:S(2)}) %all-to-all-start) | async-done | bytes 3145760 | tf_op jit(solution)/shard_map/all_to_all | solution.py:79
  91.3 2.8 copy.99
  94.1 3.8 %fusion.59 = (bf16[2048,384]{1,0:T(8,128)(2,1)}, bf16[2048,384]{1,0:T(8,128)(2,1)}) fusion(bf16[2048,768]{1,0:T(8,128)(2,1)} %bitcast.117), kind=kLoop, calls=%fused_computation.135 | loop fusion | bytes 6291456 | tf_op jit(solution)/shard_map/slice | solution.py:156
  97.9 1.8 copy.101
  99.7 2.7 copy.100
  102.3 2.5 select_reduce_fusion.1
  104.8 4.0 %select_reduce_fusion = f32[6,256]{1,0:T(8,128)S(1)} fusion(f32[6,256,2048]{2,1,0:T(8,128)S(1)} %get-tuple-element.98, f32[6,256]{1,0:T(8,128)S(1)} %get-tuple-element.97, pred[256,2048]{1,0:T(8,128)(4,1)S(1)} %copy-done.3), kind=kLoop, calls=%fused_computation.2 | loop fusion | flops 12581376 | bytes 13119488 | tf_op jit(solution)/shard_map/reduce_sum | solution.py:165
  109.5 3.0 convolution_convert_fusion.7
  112.6 1.6 convolution_convert_fusion.6
  115.1 9.5 %collective-permute-done = bf16[256,768]{1,0:T(8,128)(2,1)S(1)} collective-permute-done((bf16[256,768]{1,0:T(8,128)(2,1)S(1)}, bf16[256,768]{1,0:T(8,128)(2,1)S(1)}, u32[]{:S(2)}, u32[]{:S(2)}) %collective-permute-start) | collective-permute-done | bytes 393248 | tf_op jit(solution)/shard_map/ppermute | solution.py:72
  132.8 2.2 copy.105
  135.1 2.1 convolution_convert_fusion.1
  137.1 3.4 %collective-permute-done.2 = bf16[256,768]{1,0:T(8,128)(2,1)} collective-permute-done((bf16[256,768]{1,0:T(8,128)(2,1)}, bf16[256,768]{1,0:T(8,128)(2,1)}, u32[]{:S(2)}, u32[]{:S(2)}) %collective-permute-start.2) | collective-permute-done | bytes 393248 | tf_op jit(solution)/shard_map/ppermute | solution.py:72
  140.6 1.5 multiply_reduce_fusion
  142.9 3.2 %collective-permute-done.1 = bf16[256,768]{1,0:T(8,128)(2,1)} collective-permute-done((bf16[256,768]{1,0:T(8,128)(2,1)}, bf16[256,768]{1,0:T(8,128)(2,1)}, u32[]{:S(2)}, u32[]{:S(2)}) %collective-permute-start.1) | collective-permute-done | bytes 393248 | tf_op jit(solution)/shard_map/ppermute | solution.py:72
  146.1 2.5 multiply_add_fusion
  149.0 7.1 %concatenate.38 = bf16[768,2113]{1,0:T(8,128)(2,1)} concatenate(bf16[768,1]{1,0:T(8,128)(2,1)} %broadcast_in_dim.110, bf16[768,1152]{1,0:T(8,128)(2,1)} %convolution_convert_fusion.1, bf16[768,576]{1,0:T(8,128)(2,1)} %copy.105, bf16[768,384]{1,0:T(8,128)(2,1)S(1)} %convolution_convert_fusion.4), dimensions={1} | concatenate | bytes 6491136 | tf_op jit(solution)/shard_map/concatenate | solution.py:233
  156.1 2.2 convolution_convert_fusion.8
  158.3 1.7 copy.106
  161.1 8.2 %multiply_convert_fusion = bf16[6,256,2048]{2,1,0:T(8,128)(2,1)S(1)} fusion(f32[6,256,2048]{2,1,0:T(8,128)} %copy-done, f32[6,256]{1,0:T(8,128)S(1)} %bitcast.146, f32[6,256]{1,0:T(8,128)S(1)} %copy-done.34, pred[256,2048]{1,0:T(8,128)(4,1)S(1)} %copy-done.4, bf16[256,6,64]{0,2,1:T(8,128)(2,1)} %bitcast.137, bf16[2048,6,64]{0,2,1:T(8,128)(2,1)} %bitcast.128), kind=kOutput, calls=%fused_computation | convolution fusion | flops 421527552 | bytes 21180416 | tf_op jit(solution)/shard_map/qhd,khd->hqk/dot_general | solution.py:241
  174.0 4.6 %all-to-all-start.1 = ((bf16[8,256,384]{1,2,0:T(8,128)(2,1)}), bf16[8,256,384]{1,2,0:T(8,128)(2,1)}, u32[]{:S(2)}, u32[]{:S(2)}) async-start(bf16[8,256,384]{1,2,0:T(8,128)(2,1)} %copy.107), calls=%async_computation.1 | async-start | bytes 3145728 | tf_op jit(solution)/shard_map/all_to_all | solution.py:86
  178.6 8.6 %convolution_convert_fusion.2 = bf16[6,64,2048]{2,1,0:T(8,128)(2,1)} fusion(bf16[256,6,64]{0,2,1:T(8,128)(2,1)S(1)} %bitcast.138, f32[6,256,2048]{2,1,0:T(8,128)} %copy-done, f32[6,256]{1,0:T(8,128)S(1)} %copy-done.34, pred[256,2048]{1,0:T(8,128)(4,1)S(1)} %copy-done.4), kind=kOutput, calls=%fused_computation.9 | convolution fusion | flops 416022528 | bytes 14882816 | tf_op jit(solution)/shard_map/hqk,qhd->khd/dot_general | solution.py:253
  187.2 5.6 %reduce-scatter.3.cloned.1.call-done = bf16[96,2113]{1,0:T(8,128)(2,1)} async-done(((bf16[768,2113]{1,0:T(8,128)(2,1)}), bf16[96,2113]{1,0:T(8,128)(2,1)}) %reduce-scatter.3.cloned.1.call-update) | async-done | bytes 405712 | tf_op jit(solution)/shard_map/reduce_scatter | solution.py:235
  192.8 2.6 copy.108
  195.4 2.6 copy.109
  198.0 2.0 all-to-all-done.1
  199.9 5.3 %all-to-all-start.2 = ((bf16[8,256,384]{1,2,0:T(8,128)(2,1)}), bf16[8,256,384]{1,2,0:T(8,128)(2,1)}, u32[]{:S(2)}, u32[]{:S(2)}) async-start(bf16[8,256,384]{1,2,0:T(8,128)(2,1)} %copy.109), calls=%async_computation.3 | async-start | bytes 3145728 | tf_op jit(solution)/shard_map/all_to_all | solution.py:86
  205.3 4.8 %fusion.16 = f32[256,6,64]{0,2,1:T(8,128)S(1)} fusion(bf16[2048,6,64]{0,2,1:T(8,128)(2,1)S(1)} %bitcast.116, bf16[6,256,2048]{2,1,0:T(8,128)(2,1)} %copy-done.1), kind=kOutput, calls=%fused_computation.28 | convolution fusion | flops 402751488 | bytes 8257536 | tf_op jit(solution)/shard_map/hqk,khd->qhd/dot_general | solution.py:246
  210.1 1.7 convert_reduce_fusion
  212.0 12.9 %all-to-all-done.2 = bf16[8,256,384]{1,2,0:T(8,128)(2,1)} async-done(((bf16[8,256,384]{1,2,0:T(8,128)(2,1)}), bf16[8,256,384]{1,2,0:T(8,128)(2,1)}, u32[]{:S(2)}, u32[]{:S(2)}) %all-to-all-start.2) | async-done | bytes 1572896 | tf_op jit(solution)/shard_map/all_to_all | solution.py:86
  224.9 1.7 reduce.2
  226.6 2.2 fusion.10
  230.5 6.2 %collective-permute-done.3 = bf16[256,768]{1,0:T(8,128)(2,1)S(1)} collective-permute-done((bf16[256,768]{1,0:T(8,128)(2,1)S(1)}, bf16[256,768]{1,0:T(8,128)(2,1)S(1)}, u32[]{:S(2)}, u32[]{:S(2)}) %collective-permute-start.3) | collective-permute-done | bytes 393248 | tf_op jit(solution)/shard_map/ppermute | solution.py:72
  237.9 2.2 pad_maximum_fusion
  240.3 13.8 %all_to_all.35 = bf16[8,12,2113]{2,1,0:T(8,128)(2,1)S(1)} all-to-all(bf16[8,12,2113]{2,1,0:T(8,128)(2,1)S(1)} %reshape.263), channel_id=1, replica_groups=mesh['fsdp'=8,'tensor'=2,'context'=8] {'context'}, dimensions={0} | all-to-all | bytes 811392 | tf_op jit(solution)/shard_map/all_to_all | solution.py:86
  254.3 12.9 %all_to_all.36 = bf16[8,12,2113]{2,1,0:T(8,128)(2,1)S(1)} all-to-all(bf16[8,12,2113]{2,1,0:T(8,128)(2,1)S(1)} %broadcast_in_dim.109), channel_id=1, replica_groups=mesh['fsdp'=8,'tensor'=2,'context'=8] {'context'}, dimensions={0} | all-to-all | bytes 811392 | tf_op jit(solution)/shard_map/all_to_all | solution.py:79
  271.0 4.8 %reduce-scatter.5.cloned.1.call-done = bf16[96,1153]{1,0:T(8,128)(2,1)} async-done(((bf16[768,1153]{1,0:T(8,128)(2,1)}), bf16[96,1153]{1,0:T(8,128)(2,1)}) %reduce-scatter.5.cloned.1.call-update) | async-done | bytes 221392 | tf_op jit(solution)/shard_map/reduce_scatter | solution.py:287
  275.8 1.7 reshape.261
  277.5 6.5 %all-to-all-start.3 = ((bf16[8,12,1153]{2,1,0:T(8,128)(2,1)}), bf16[8,12,1153]{2,1,0:T(8,128)(2,1)S(1)}, u32[]{:S(2)}, u32[]{:S(2)}) async-start(bf16[8,12,1153]{2,1,0:T(8,128)(2,1)} %reshape.261), calls=%async_computation.5 | async-start | bytes 655360 | tf_op jit(solution)/shard_map/all_to_all | solution.py:86
  284.0 9.1 %all-to-all-done.3 = bf16[8,12,1153]{2,1,0:T(8,128)(2,1)S(1)} async-done(((bf16[8,12,1153]{2,1,0:T(8,128)(2,1)}), bf16[8,12,1153]{2,1,0:T(8,128)(2,1)S(1)}, u32[]{:S(2)}, u32[]{:S(2)}) %all-to-all-start.3) | async-done | bytes 221408 | tf_op jit(solution)/shard_map/all_to_all | solution.py:86
  293.9 3.4 %all-to-all-start.4 = ((bf16[8,12,1153]{2,1,0:T(8,128)(2,1)}), bf16[8,12,1153]{2,1,0:T(8,128)(2,1)S(1)}, u32[]{:S(2)}, u32[]{:S(2)}) async-start(bf16[8,12,1153]{2,1,0:T(8,128)(2,1)} %broadcast_in_dim.108), calls=%async_computation.6 | async-start | bytes 655360 | tf_op jit(solution)/shard_map/all_to_all | solution.py:79
  298.6 7.8 %all-to-all-done.4 = bf16[8,12,1153]{2,1,0:T(8,128)(2,1)S(1)} async-done(((bf16[8,12,1153]{2,1,0:T(8,128)(2,1)}), bf16[8,12,1153]{2,1,0:T(8,128)(2,1)S(1)}, u32[]{:S(2)}, u32[]{:S(2)}) %all-to-all-start.4) | async-done | bytes 221408 | tf_op jit(solution)/shard_map/all_to_all | solution.py:79
  (156 shorter events, 38.7 us)
Async XLA Ops:
  7.2 30.9 %all-gather.3.cloned.1.call-start = ((), (), s32[]{:S(2)}) async-start(), calls=%async_computation.9 | async-start | bytes 2211840 | tf_op jit(solution)/shard_map/all_gather | solution.py:115
  11.4 3.3 %copy-start.37 = (s32[3,1]{0,1:T(1,128)}, s32[3,1]{0,1:T(1,128)S(1)}, u32[]{:S(2)}) copy-start(s32[3,1]{0,1:T(1,128)S(1)} %reduce-window.4) | copy-start | bytes 40
  14.6 27.4 %copy-start.29 = (f32[256]{0:T(256)}, f32[256]{0:T(256)S(1)}, u32[]{:S(2)}) copy-start(f32[256]{0:T(256)S(1)} %add_rsqrt_fusion.1) | copy-start | bytes 3076
  14.8 27.3 %copy-start.22 = (f32[256,32]{0,1:T(8,128)}, f32[256,32]{0,1:T(8,128)S(1)}, u32[]{:S(2)}) copy-start(f32[256,32]{0,1:T(8,128)S(1)} %get-tuple-element.95) | copy-start | bytes 98308
  14.9 27.3 %copy-start.24 = (f32[256,32]{0,1:T(8,128)}, f32[256,32]{0,1:T(8,128)S(1)}, u32[]{:S(2)}) copy-start(f32[256,32]{0,1:T(8,128)S(1)} %get-tuple-element.96) | copy-start | bytes 98308
  42.2 60.2 %copy-start.16 = (bf16[256,6,32]{0,2,1:T(8,128)(2,1)}, bf16[256,6,32]{0,2,1:T(8,128)(2,1)S(1)}, u32[]{:S(2)}) copy-start(bf16[256,6,32]{0,2,1:T(8,128)(2,1)S(1)} %get-tuple-element.87) | copy-start | bytes 294916
  42.2 60.2 %copy-start.18 = (bf16[256,6,32]{0,2,1:T(8,128)(2,1)}, bf16[256,6,32]{0,2,1:T(8,128)(2,1)S(1)}, u32[]{:S(2)}) copy-start(bf16[256,6,32]{0,2,1:T(8,128)(2,1)S(1)} %get-tuple-element.88) | copy-start | bytes 294916
  44.1 8.9 %copy-start.26 = (bf16[576,96]{0,1:T(8,128)(2,1)S(1)}, bf16[576,96]{0,1:T(8,128)(2,1)}, u32[]{:S(2)}) copy-start(bf16[576,96]{0,1:T(8,128)(2,1)} %param.16) | copy-start | bytes 331780
  44.1 8.9 %copy-start.27 = (bf16[384,96]{0,1:T(8,128)(2,1)S(1)}, bf16[384,96]{0,1:T(8,128)(2,1)}, u32[]{:S(2)}) copy-start(bf16[384,96]{0,1:T(8,128)(2,1)} %param.13) | copy-start | bytes 221188
  44.1 11.4 %copy-start.32 = (s32[256]{0:T(256)S(1)}, s32[256]{0:T(256)}, u32[]{:S(2)}) copy-start(s32[256]{0:T(256)} %copy-done.31) | copy-start | bytes 3076
  44.1 47.1 %all-to-all-start = ((bf16[8,256,768]{1,2,0:T(8,128)(2,1)}), bf16[8,256,768]{1,2,0:T(8,128)(2,1)S(1)}, u32[]{:S(2)}, u32[]{:S(2)}) async-start(bf16[8,256,768]{1,2,0:T(8,128)(2,1)} %broadcast_in_dim.57), calls=%async_computation | async-start | bytes 6291456 | tf_op jit(solution)/shard_map/all_to_all | solution.py:79
  51.1 61.5 %all-gather.5.cloned.1.call-start = ((), (), s32[]{:S(2)}) async-start(), calls=%async_computation.10 | async-start | bytes 3760128 | tf_op jit(solution)/shard_map/all_gather | solution.py:128
  54.8 138.1 %reduce-scatter.3.cloned.1.call-start = ((), (), s32[]{:S(2)}) async-start(), calls=%async_computation.11 | async-start | bytes 3760128 | tf_op jit(solution)/shard_map/reduce_scatter | solution.py:235
  97.9 4.5 %copy-start.3 = (pred[256,2048]{1,0:T(8,128)(4,1)S(1)}, pred[256,2048]{1,0:T(8,128)(4,1)}, u32[]{:S(2)}) copy-start(pred[256,2048]{1,0:T(8,128)(4,1)} %broadcast_compare_fusion) | copy-start | bytes 1572868
  104.8 4.7 %copy-start = (f32[6,256,2048]{2,1,0:T(8,128)}, f32[6,256,2048]{2,1,0:T(8,128)S(1)}, u32[]{:S(2)}) copy-start(f32[6,256,2048]{2,1,0:T(8,128)S(1)} %get-tuple-element.98) | copy-start | bytes 37748740
  104.8 4.7 %copy-start.9 = (bf16[2048,384]{0,1:T(8,128)(2,1)S(1)}, bf16[2048,384]{0,1:T(8,128)(2,1)}, u32[]{:S(2)}) copy-start(bf16[2048,384]{0,1:T(8,128)(2,1)} %copy.100) | copy-start | bytes 4718596
  108.8 3.7 %copy-start.33 = (f32[6,256]{1,0:T(8,128)}, f32[6,256]{1,0:T(8,128)S(1)}, u32[]{:S(2)}) copy-start(f32[6,256]{1,0:T(8,128)S(1)} %log_add_fusion) | copy-start | bytes 18436
  109.5 15.1 %copy-start.2 = (bf16[256,768]{1,0:T(8,128)(2,1)S(1)}, bf16[256,768]{1,0:T(8,128)(2,1)}, u32[]{:S(2)}) copy-start(bf16[256,768]{1,0:T(8,128)(2,1)} %param.9) | copy-start | bytes 1179652
  112.6 12.5 %copy-start.5 = (bf16[768,2112]{1,0:T(8,128)(2,1)S(1)}, bf16[768,2112]{1,0:T(8,128)(2,1)}, u32[]{:S(2)}) copy-start(bf16[768,2112]{1,0:T(8,128)(2,1)} %all-gather.5.cloned.1.call-done) | copy-start | bytes 9732100
  114.2 11.8 %copy-start.14 = (bf16[256,768]{1,0:T(8,128)(2,1)S(1)}, bf16[256,768]{1,0:T(8,128)(2,1)}, u32[]{:S(2)}) copy-start(bf16[256,768]{1,0:T(8,128)(2,1)} %param.17) | copy-start | bytes 1179652
  114.2 10.4 %collective-permute-start = (bf16[256,768]{1,0:T(8,128)(2,1)S(1)}, bf16[256,768]{1,0:T(8,128)(2,1)S(1)}, u32[]{:S(2)}, u32[]{:S(2)}) collective-permute-start(bf16[256,768]{1,0:T(8,128)(2,1)S(1)} %convolution_convert_fusion.6), channel_id=1, source_target_pairs={{0,8},{8,0},{1,9},{9,1},{2,10},{10,2},{3,11},{11,3},{4,12},{12,4},... | collective-permute-start | bytes 1179656 | tf_op jit(solution)/shard_map/ppermute | solution.py:72
  125.1 15.5 %copy-start.28 = (f32[256]{0:T(256)}, f32[256]{0:T(256)S(1)}, u32[]{:S(2)}) copy-start(f32[256]{0:T(256)S(1)} %add_rsqrt_fusion) | copy-start | bytes 3076
  128.2 12.4 %collective-permute-start.2 = (bf16[256,768]{1,0:T(8,128)(2,1)}, bf16[256,768]{1,0:T(8,128)(2,1)}, u32[]{:S(2)}, u32[]{:S(2)}) collective-permute-start(bf16[256,768]{1,0:T(8,128)(2,1)} %fusion.13), channel_id=1, source_target_pairs={{0,8},{8,0},{1,9},{9,1},{2,10},{10,2},{3,11},{11,3},{4,12},{12,4},... | collective-permute-start | bytes 1179656 | tf_op jit(solution)/shard_map/ppermute | solution.py:72
  131.4 14.7 %collective-permute-start.1 = (bf16[256,768]{1,0:T(8,128)(2,1)}, bf16[256,768]{1,0:T(8,128)(2,1)}, u32[]{:S(2)}, u32[]{:S(2)}) collective-permute-start(bf16[256,768]{1,0:T(8,128)(2,1)} %convolution_convert_fusion.5), channel_id=1, source_target_pairs={{0,8},{8,0},{1,9},{9,1},{2,10},{10,2},{3,11},{11,3},{4,12},{12,4},... | collective-permute-start | bytes 1179656 | tf_op jit(solution)/shard_map/ppermute | solution.py:72
  135.1 11.1 %copy-start.15 = (bf16[256,768]{1,0:T(8,128)(2,1)S(1)}, bf16[256,768]{1,0:T(8,128)(2,1)}, u32[]{:S(2)}) copy-start(bf16[256,768]{1,0:T(8,128)(2,1)} %param.17) | copy-start | bytes 1179652
  137.1 11.5 %copy-start.7 = (bf16[6,64,256]{2,1,0:T(8,128)(2,1)S(1)}, bf16[6,64,256]{2,1,0:T(8,128)(2,1)}, u32[]{:S(2)}) copy-start(bf16[6,64,256]{2,1,0:T(8,128)(2,1)} %copy-done.6) | copy-start | bytes 589828
  156.1 4.0 %copy-start.8 = (bf16[6,64,256]{2,1,0:T(8,128)(2,1)S(1)}, bf16[6,64,256]{2,1,0:T(8,128)(2,1)}, u32[]{:S(2)}) copy-start(bf16[6,64,256]{2,1,0:T(8,128)(2,1)} %copy-done.6) | copy-start | bytes 589828
  156.1 5.0 %copy-start.4 = (pred[256,2048]{1,0:T(8,128)(4,1)S(1)}, pred[256,2048]{1,0:T(8,128)(4,1)}, u32[]{:S(2)}) copy-start(pred[256,2048]{1,0:T(8,128)(4,1)} %broadcast_compare_fusion) | copy-start | bytes 1572868
  156.1 5.0 %copy-start.34 = (f32[6,256]{1,0:T(8,128)S(1)}, f32[6,256]{1,0:T(8,128)}, u32[]{:S(2)}) copy-start(f32[6,256]{1,0:T(8,128)} %copy-done.33) | copy-start | bytes 18436
  161.1 8.3 %copy-start.17 = (bf16[256,6,32]{0,2,1:T(8,128)(2,1)S(1)}, bf16[256,6,32]{0,2,1:T(8,128)(2,1)}, u32[]{:S(2)}) copy-start(bf16[256,6,32]{0,2,1:T(8,128)(2,1)} %copy-done.16) | copy-start | bytes 294916
  161.1 8.3 %copy-start.19 = (bf16[256,6,32]{0,2,1:T(8,128)(2,1)S(1)}, bf16[256,6,32]{0,2,1:T(8,128)(2,1)}, u32[]{:S(2)}) copy-start(bf16[256,6,32]{0,2,1:T(8,128)(2,1)} %copy-done.18) | copy-start | bytes 294916
  169.4 2.6 copy-start.1
  172.5 6.1 %copy-start.20 = (bf16[256,384]{0,1:T(8,128)(2,1)S(1)}, bf16[256,384]{0,1:T(8,128)(2,1)}, u32[]{:S(2)}) copy-start(bf16[256,384]{0,1:T(8,128)(2,1)} %copy.106) | copy-start | bytes 589828
  174.0 26.0 %all-to-all-start.1 = ((bf16[8,256,384]{1,2,0:T(8,128)(2,1)}), bf16[8,256,384]{1,2,0:T(8,128)(2,1)}, u32[]{:S(2)}, u32[]{:S(2)}) async-start(bf16[8,256,384]{1,2,0:T(8,128)(2,1)} %copy.107), calls=%async_computation.1 | async-start | bytes 3145728 | tf_op jit(solution)/shard_map/all_to_all | solution.py:86
  199.9 25.0 %all-to-all-start.2 = ((bf16[8,256,384]{1,2,0:T(8,128)(2,1)}), bf16[8,256,384]{1,2,0:T(8,128)(2,1)}, u32[]{:S(2)}, u32[]{:S(2)}) async-start(bf16[8,256,384]{1,2,0:T(8,128)(2,1)} %copy.109), calls=%async_computation.3 | async-start | bytes 3145728 | tf_op jit(solution)/shard_map/all_to_all | solution.py:86
  205.2 6.5 %copy-start.23 = (f32[256,32]{0,1:T(8,128)S(1)}, f32[256,32]{0,1:T(8,128)}, u32[]{:S(2)}) copy-start(f32[256,32]{0,1:T(8,128)} %copy-done.22) | copy-start | bytes 98308
  205.2 6.5 %copy-start.25 = (f32[256,32]{0,1:T(8,128)S(1)}, f32[256,32]{0,1:T(8,128)}, u32[]{:S(2)}) copy-start(f32[256,32]{0,1:T(8,128)} %copy-done.24) | copy-start | bytes 98308
  205.3 70.5 %reduce-scatter.5.cloned.1.call-start = ((), (), s32[]{:S(2)}) async-start(), calls=%async_computation.12 | async-start | bytes 2211840 | tf_op jit(solution)/shard_map/reduce_scatter | solution.py:287
  212.0 17.7 %copy-start.30 = (f32[256]{0:T(256)S(1)}, f32[256]{0:T(256)}, u32[]{:S(2)}) copy-start(f32[256]{0:T(256)} %copy-done.29) | copy-start | bytes 3076
  228.9 11.3 %copy-start.10 = (bf16[256,768]{1,0:T(8,128)(2,1)}, bf16[256,768]{1,0:T(8,128)(2,1)S(1)}, u32[]{:S(2)}) copy-start(bf16[256,768]{1,0:T(8,128)(2,1)S(1)} %fusion.10) | copy-start | bytes 1179652
  228.9 7.9 %collective-permute-start.3 = (bf16[256,768]{1,0:T(8,128)(2,1)S(1)}, bf16[256,768]{1,0:T(8,128)(2,1)S(1)}, u32[]{:S(2)}, u32[]{:S(2)}) collective-permute-start(bf16[256,768]{1,0:T(8,128)(2,1)S(1)} %fusion.10), channel_id=1, source_target_pairs={{0,8},{8,0},{1,9},{9,1},{2,10},{10,2},{3,11},{11,3},{4,12},{12,4},... | collective-permute-start | bytes 1179656 | tf_op jit(solution)/shard_map/ppermute | solution.py:72
  236.7 3.5 %copy-start.12 = (bf16[256,768]{1,0:T(8,128)(2,1)}, bf16[256,768]{1,0:T(8,128)(2,1)S(1)}, u32[]{:S(2)}) copy-start(bf16[256,768]{1,0:T(8,128)(2,1)S(1)} %collective-permute-done.3) | copy-start | bytes 1179652
  254.2 16.8 %copy-start.36 = (f32[256]{0:T(256)S(1)}, f32[256]{0:T(256)}, u32[]{:S(2)}) copy-start(f32[256]{0:T(256)} %get-tuple-element.69) | copy-start | bytes 3076
  254.3 29.6 %copy-start.35 = (f32[256]{0:T(256)S(1)}, f32[256]{0:T(256)}, u32[]{:S(2)}) copy-start(f32[256]{0:T(256)} %get-tuple-element.70) | copy-start | bytes 3076
  267.3 30.0 %copy-start.11 = (bf16[256,768]{1,0:T(8,128)(2,1)S(1)}, bf16[256,768]{1,0:T(8,128)(2,1)}, u32[]{:S(2)}) copy-start(bf16[256,768]{1,0:T(8,128)(2,1)} %copy-done.10) | copy-start | bytes 1179652
  267.3 30.0 %copy-start.13 = (bf16[256,768]{1,0:T(8,128)(2,1)S(1)}, bf16[256,768]{1,0:T(8,128)(2,1)}, u32[]{:S(2)}) copy-start(bf16[256,768]{1,0:T(8,128)(2,1)} %copy-done.12) | copy-start | bytes 1179652
  277.5 15.6 %all-to-all-start.3 = ((bf16[8,12,1153]{2,1,0:T(8,128)(2,1)}), bf16[8,12,1153]{2,1,0:T(8,128)(2,1)S(1)}, u32[]{:S(2)}, u32[]{:S(2)}) async-start(bf16[8,12,1153]{2,1,0:T(8,128)(2,1)} %reshape.261), calls=%async_computation.5 | async-start | bytes 655360 | tf_op jit(solution)/shard_map/all_to_all | solution.py:86
  293.9 12.5 %all-to-all-start.4 = ((bf16[8,12,1153]{2,1,0:T(8,128)(2,1)}), bf16[8,12,1153]{2,1,0:T(8,128)(2,1)S(1)}, u32[]{:S(2)}, u32[]{:S(2)}) async-start(bf16[8,12,1153]{2,1,0:T(8,128)(2,1)} %broadcast_in_dim.108), calls=%async_computation.6 | async-start | bytes 655360 | tf_op jit(solution)/shard_map/all_to_all | solution.py:79
  (3 other events, 5.6 us)
Sparse Core Ops, SparseCore 0:
  10.7 27.3 all-gather.2
  54.9 29.0 all-gather.4
  158.5 34.3 reduce-scatter.2
  240.3 35.3 reduce-scatter.4
